TPU v7x, 512 devices: a whole 4x4x16 slice. The times are simulated.
512 devices in a mesh: grp: 4 (over z_hi, core), row: 4 (over x), col: 32 (over y, z_lo).
Axes of the slice: x: 4, y: 4, z: 16 (z_hi: 2, z_lo: 8; z = z_hi * 8 + z_lo), core: 2. Of those that a mesh axis runs over, the one named last changes fastest.
Arguments:
- acts: bfloat16 [768, 8192], P('grp', 'col'), may hold values from -6 to 6
- grads: bfloat16 [768, 28672], P('grp', ('row', 'col')), may hold values from -6 to 6
- basis_in: bfloat16 [8192, 4096], P('col', 'row'), may hold values from -0.0625 to 0.0625
- basis_out: bfloat16 [4, 7168, 14336], P('row', 'grp', 'col'), may hold values from -0.03125 to 0.03125
- lengths: int32 [4, 2], P('grp'), may hold values from 1 to 96, 144 in all within a row
Outputs:
- eigenvalues: float32 [14336, 4096], P('col', 'row')
Inputs may be any that keep to these rules, and one draw needn't show every extreme that they name: The 2 lengths of each index of grp sum to exactly 144, and none exceeds 96.
All inputs are finite; a program needn't handle non-finite values.
Results may differ from a plain program's by a relative error of at most 0.006.
Values may be sent and summed in bfloat16 or wider, within the bound.
No kernel may reach another device: no remote copies, remote signals or barrier semaphores. Data moves between devices by JAX's collectives and lax.ppermute only.
A program may use at most 64 MiB of HBM per device.

v0:
```python
import jax
import jax.numpy as jnp
from jax import lax
from jax.sharding import PartitionSpec as P

LEN = 96
VALID = 144


def rows_for(lines, size):
    spare = -len(lines) % size
    return jnp.pad(lines, [(0, spare)] + [(0, 0)] * (lines.ndim - 1))


def sum_by_parts(value, axis):
    lines = value.reshape(-1, *value.shape[1:][-1:])
    own = lax.psum_scatter(
        rows_for(lines, lax.axis_size(axis)), axis, scatter_dimension=0, tiled=True
    )
    whole = lax.all_gather(own, axis).reshape(-1, *lines.shape[1:])
    return lax.slice_in_dim(whole, 0, len(lines)).reshape(value.shape)


def outer_square(left, right):
    block = lax.dot_general(
        left, right, (((0,), (0,)), ((), ())), preferred_element_type=jnp.float32
    )
    return block * block


def per_device(acts, grads, basis_in, basis_out, lengths):
    seq_lens = lengths[0]
    count = seq_lens.shape[0]
    partial_in = jnp.dot(acts, basis_in, preferred_element_type=jnp.float32)
    proj_in = lax.psum(partial_in, "col").astype(jnp.bfloat16)
    ends = jnp.cumsum(seq_lens)
    starts = ends - seq_lens
    slot_ids = jnp.arange(VALID, dtype=jnp.int32)
    segment = jnp.sum((slot_ids[:, None] >= ends[None, :]).astype(jnp.int32), axis=1)
    member = segment[:, None] == jnp.arange(count, dtype=jnp.int32)[None, :]
    offset = jnp.sum(jnp.where(member, starts[None, :], 0), axis=1)
    source = segment * LEN + slot_ids - offset
    packed = jnp.take(grads, source, axis=0)
    gathered = lax.all_gather(packed, "col", axis=1, tiled=True)
    proj_in = jnp.take(proj_in, source, axis=0)
    partial_out = jnp.dot(
        gathered,
        lax.all_gather(basis_out, "grp", axis=1, tiled=True)[0],
        preferred_element_type=jnp.float32,
    )
    proj_out = lax.psum(partial_out, "row").astype(jnp.bfloat16)
    slot_pos = jnp.arange(LEN, dtype=jnp.int32)
    total = jnp.zeros((proj_out.shape[1], proj_in.shape[1]), jnp.float32)
    padded_out = jnp.concatenate(
        [proj_out, jnp.zeros((LEN, proj_out.shape[1]), jnp.bfloat16)], axis=0
    )
    padded_in = jnp.concatenate([proj_in, jnp.zeros((LEN, proj_in.shape[1]), jnp.bfloat16)], axis=0)
    for seq in range(count):
        keep = (slot_pos < seq_lens[seq]).astype(jnp.bfloat16)
        piece_out = lax.dynamic_slice_in_dim(padded_out, starts[seq], LEN, 0)
        piece_in = lax.dynamic_slice_in_dim(padded_in, starts[seq], LEN, 0)
        total = total + outer_square(piece_out * keep[:, None], piece_in)
    summed = sum_by_parts(total.astype(jnp.bfloat16), "grp").astype(jnp.float32)
    return summed / (lax.axis_size("grp") * count * LEN)


def solution(mesh):
    in_specs = (
        P("grp", "col"),
        P("grp", ("row", "col")),
        P("col", "row"),
        P("row", "grp", "col"),
        P("grp", None),
    )
    out_specs = P("col", "row")
    return jax.shard_map(
        per_device, mesh=mesh, in_specs=in_specs, out_specs=out_specs, check_vma=False
    )
```

profile of v0, /device:TPU:1, one launch (start us, length us, event | category | flops | bytes accessed | tf_op | source)
XLA Modules:
  0.0 539.5 jit_solution(12668688378372334434)
XLA Ops:
  6.5 0.9 reduce-window.4
  7.4 0.7 fusion.13
  8.2 0.1 fusion.10
  8.3 1.7 gather_fusion
  10.0 0.7 select_bitcast_fusion
  10.8 0.7 all-gather.5.cloned.1.call-update
  11.6 0.6 fusion.17
  14.6 0.3 fusion.18
  14.9 227.9 %all-reduce.5 = bf16[192,1024]{1,0:T(8,128)(2,1)S(1)} all-reduce(f32[192,1024]{1,0:T(8,128)S(1)} %fusion.18), channel_id=1, replica_groups=mesh['grp'=4,'row'=4,'col'=32] {'col'}, use_global_device_ids=true, to_apply=%region_4.5 | all-reduce | flops 196608 | bytes 1179648 | tf_op jit(solution)/shard_map/psum | solution.py:35
  242.7 0.9 gather_fusion.1
  244.8 0.6 fusion.16
  245.5 0.6 compare_convert_fusion.2
  246.0 0.6 compare_convert_fusion.1
  246.7 0.1 broadcast_select_fusion
  246.8 2.5 copy.8
  249.3 5.0 reshape.92
  254.2 158.1 %all-gather.5.cloned.1.call-done = bf16[1,7168,448]{1,2,0:T(8,128)(2,1)} async-done(((bf16[1,1792,448]{1,2,0:T(8,128)(2,1)}), bf16[1,7168,448]{1,2,0:T(8,128)(2,1)}) %all-gather.5.cloned.1.call-update) | async-done | bytes 6422544 | tf_op jit(solution)/shard_map/all_gather | solution.py:48
  412.3 5.5 %fusion = f32[144,448]{1,0:T(8,128)S(1)} fusion(bf16[7168,144]{0,1:T(8,128)(2,1)} %reshape.92, bf16[1,7168,448]{1,2,0:T(8,128)(2,1)} %all-gather.5.cloned.1.call-done), kind=kOutput, calls=%fused_computation.2 | convolution fusion | flops 924844032 | bytes 8744960 | tf_op jit(solution)/shard_map/dot_general | solution.py:46
  417.8 21.2 %all-reduce.4 = bf16[144,448]{1,0:T(8,128)(2,1)S(1)} all-reduce(f32[144,448]{1,0:T(8,128)S(1)} %fusion), channel_id=1, replica_groups=mesh['grp'=4,'row'=4,'col'=32] {'row'}, use_global_device_ids=true, to_apply=%region_3.4 | all-reduce | flops 64512 | bytes 387072 | tf_op jit(solution)/shard_map/psum | solution.py:51
  439.1 0.5 fusion.2
  439.6 1.4 add_convert_fusion
  441.0 63.2 %reduce-scatter.2.cloned.1.call-done = bf16[112,1024]{1,0:T(8,128)(2,1)} async-done(((bf16[448,1024]{1,0:T(8,128)(2,1)}), bf16[112,1024]{1,0:T(8,128)(2,1)}) %reduce-scatter.2.cloned.1.call-update) | async-done | bytes 229392 | tf_op jit(solution)/shard_map/reduce_scatter | solution.py:17
  504.3 27.2 %all-gather = bf16[448,1024]{1,0:T(8,128)(2,1)S(1)} all-gather(bf16[112,1024]{1,0:T(8,128)(2,1)} %reduce-scatter.2.cloned.1.call-done), channel_id=2, replica_groups=mesh['grp'=4,'row'=4,'col'=32] {'grp'}, dimensions={0}, use_global_device_ids=true | all-gather | bytes 1146880 | tf_op jit(solution)/shard_map/all_gather | solution.py:20
  531.5 1.5 convert_multiply_fusion
  (18 shorter events, 0.3 us)
Async XLA Ops:
  6.5 8.0 %copy-start = (bf16[256,1024]{1,0:T(8,128)(2,1)S(1)}, bf16[256,1024]{1,0:T(8,128)(2,1)}, u32[]{:S(2)}) copy-start(bf16[256,1024]{1,0:T(8,128)(2,1)} %param.7) | copy-start | bytes 1572868
  6.5 5.0 copy-start.2
  6.5 8.1 %copy-start.1 = (bf16[192,256]{1,0:T(8,128)(2,1)S(1)}, bf16[192,256]{1,0:T(8,128)(2,1)}, u32[]{:S(2)}) copy-start(bf16[192,256]{1,0:T(8,128)(2,1)} %param.5) | copy-start | bytes 294916
  6.5 240.2 %all-gather.7.cloned.1.call-start = ((), (), s32[]{:S(2)}) async-start(), calls=%async_computation.3 | async-start | bytes 2433024 | tf_op jit(solution)/shard_map/all_gather | solution.py:44
  10.8 401.6 %all-gather.5.cloned.1.call-start = ((), (), s32[]{:S(2)}) async-start(), calls=%async_computation.1 | async-start | bytes 8028160 | tf_op jit(solution)/shard_map/all_gather | solution.py:48
  11.5 492.7 %reduce-scatter.2.cloned.1.call-start = ((), (), s32[]{:S(2)}) async-start(), calls=%async_computation.2 | async-start | bytes 1146880 | tf_op jit(solution)/shard_map/reduce_scatter | solution.py:17
Sparse Core Ops, SparseCore 0:
  10.9 216.3 all-gather.6
  229.4 182.9 all-gather.4
  441.1 63.0 reduce-scatter.1
where the time goes:
time: 543 us; the launch traced here: 539 us
  blocking collectives  276 us (51%)
  waiting for transfers between devices  222 us (41%)
  between operations  16.8 us (3%)
  local copies, waits for them, and re-layouts  11.3 us (2%)
  matrix products  7.65 us (1%)
    psum x1, blocking collectives, per_device(): proj_in = lax.psum(partial_in, 'col').astype(jnp.bfloat16)  228 us
    all_gather x1, waiting for transfers between devices, per_device(): lax.all_gather(basis_out, 'grp', axis=1, tiled=True)[0]  158 us
    reduce_scatter x1, waiting for transfers between devices, sum_by_parts(): lax.psum_scatter(rows_for(lines, lax.axis_size(axis)), axis, scatter_dime...  63.2 us
    all_gather x1, blocking collectives, sum_by_parts(): whole = lax.all_gather(own, axis).reshape(-1, *lines.shape[1:])  27.2 us
    psum x1, blocking collectives, per_device(): proj_out = lax.psum(partial_out, 'row').astype(jnp.bfloat16)  21.2 us
  transfers between devices with their start and end apart: 3, of which 2 were waited for; matrix products, arithmetic and copies ran while one was open for 2% of the time, Pallas kernels for 0%

commit v1 on v0

v1 whole, which is shorter than its diff:
```python
import jax
import jax.numpy as jnp
from jax import lax
from jax.experimental import pallas as pl
from jax.experimental.pallas import tpu as pltpu
from jax.sharding import Mesh, PartitionSpec as P

LEN = 96
VALID = 144
BF = jnp.bfloat16
F32 = jnp.float32
PLANE = ("zhi", "core", "y", "zlo")


def transposed():
    def place(zhi, core, y, zlo):
        return ((zhi * 2 + core) * 4 + y) * 8 + zlo

    pairs = []
    for g in range(4):
        for y in range(4):
            for z in range(8):
                to = 7 - z if g >> 1 != y >> 1 else z
                pairs.append((place(g >> 1, g & 1, y, z), place(y >> 1, y & 1, g, to)))
    return pairs


def exchange(x, axis):
    return lax.all_to_all(x, axis, 0, 0, tiled=True)


def everywhere(x, axis):
    n = lax.axis_size(axis)
    return lax.all_to_all(jnp.broadcast_to(x[None], (n,) + x.shape), axis, 0, 0, tiled=True)


def swap(x, axis, by):
    n = lax.axis_size(axis)
    return lax.ppermute(x, axis, [(i, i ^ by) for i in range(n)])


def project_kernel(lines_ref, basis_ref, out_ref):
    for t in range(4):
        total = jnp.zeros((VALID, basis_ref.shape[1]), F32)
        for z in range(8):
            total += jnp.dot(
                lines_ref[t, z, :, :224],
                basis_ref[z * 224 : (z + 1) * 224, :],
                preferred_element_type=F32,
            )
        out_ref[t] = total.astype(BF)


def square_kernel(out_ref, in_ref, mask_ref, eig_ref):
    total = jnp.zeros(eig_ref.shape, F32)
    for g in range(4):
        first = out_ref[g] * mask_ref[g]
        for left in (first, out_ref[g] - first):
            block = lax.dot_general(
                left, in_ref[g], (((0,), (0,)), ((), ())), preferred_element_type=F32
            )
            total += block * block
    eig_ref[...] = total / 768.0


def project(lines, basis):
    return pl.pallas_call(
        project_kernel,
        out_shape=jax.ShapeDtypeStruct((4, VALID, basis.shape[1]), BF),
        compiler_params=pltpu.CompilerParams(vmem_limit_bytes=40 << 20),
    )(lines, basis)


def squares(proj_out, proj_in, mask):
    cols, wide = proj_out.shape[2], proj_in.shape[2]
    tile = 256
    return pl.pallas_call(
        square_kernel,
        grid=(wide // tile,),
        in_specs=[
            pl.BlockSpec((4, VALID, cols), lambda i: (0, 0, 0)),
            pl.BlockSpec((4, VALID, tile), lambda i: (0, 0, i)),
            pl.BlockSpec((4, VALID, 1), lambda i: (0, 0, 0)),
        ],
        out_specs=pl.BlockSpec((cols, tile), lambda i: (0, i)),
        out_shape=jax.ShapeDtypeStruct((cols, wide), F32),
        compiler_params=pltpu.CompilerParams(vmem_limit_bytes=40 << 20),
    )(proj_out, proj_in, mask)


def per_device(acts, grads, basis_in, basis_out, lengths):
    first = lengths[0, 0]
    slot = jnp.arange(VALID, dtype=jnp.int32)
    source = jnp.where(slot < first, slot, slot - first + LEN)
    mask = (slot < first).astype(BF)
    lines = jnp.take(grads, source, axis=0)
    lines = jnp.concatenate([lines, jnp.broadcast_to(mask[:, None], (VALID, 32))], axis=1)
    lines = lax.ppermute(lines, PLANE, transposed())
    partial = jnp.dot(jnp.take(acts, source, axis=0), basis_in, preferred_element_type=F32)
    partial = partial.astype(BF).reshape(VALID, 8, 4, 32).transpose(2, 0, 1, 3)
    partial = exchange(partial.reshape(4, VALID, 256), "y")
    partial = jnp.sum(partial.astype(F32), axis=0).astype(BF)
    both = jnp.concatenate(
        [
            jnp.broadcast_to(lines[None, :, :224], (8, VALID, 224)),
            partial.reshape(VALID, 8, 32).transpose(1, 0, 2),
        ],
        axis=2,
    )
    both = exchange(both, "zlo")
    proj_in = jnp.sum(both[:, :, 224:].astype(F32), axis=0).astype(BF)
    mirrored = (lax.axis_index("zhi") != lax.axis_index("y") // 2)
    feats = both[:, :, :224]
    feats = jnp.where(mirrored, feats[::-1], feats)
    spare = jnp.concatenate(
        [proj_in[None], jnp.broadcast_to(lines[None, :, 224:], (7, VALID, 32))], axis=0
    )
    whole = everywhere(jnp.concatenate([feats, spare], axis=2), "y")
    part = project(whole, basis_out[0])
    masks = whole[:, 1, :, 224:225]
    proj_in = whole[:, 0, :, 224:].transpose(1, 0, 2).reshape(VALID, 128)
    ins = jnp.stack([proj_in, swap(proj_in, "zhi", 1)])
    ins = jnp.where(lax.axis_index("zhi") == 0, ins, ins[::-1])
    zlo = lax.axis_index("zlo")
    for by in (4, 2, 1):
        other = swap(ins, "zlo", by)
        low = (zlo // by) % 2 == 0
        ins = jnp.where(
            low, jnp.concatenate([ins, other], axis=2), jnp.concatenate([other, ins], axis=2)
        )
    wide = ins.shape[2]
    ins = ins.reshape(2, VALID, 2, 2, 2, 128).transpose(0, 1, 4, 3, 2, 5).reshape(2, VALID, wide)
    other = swap(ins, "core", 1)
    core0 = lax.axis_index("core") == 0
    ins = jnp.where(core0, jnp.stack([ins, other], axis=1), jnp.stack([other, ins], axis=1))
    ins = ins.reshape(4, VALID, wide)
    cols = part.shape[2]
    half = exchange(part.reshape(2, 2 * VALID, cols), "core").astype(F32).sum(0).astype(BF)
    own = exchange(half.reshape(4, VALID // 2, cols), "x").astype(F32).sum(0).astype(BF)
    own = (own.astype(F32) + swap(own, "zhi", 1).astype(F32)).astype(BF)
    half = everywhere(own, "x").reshape(2 * VALID, cols)
    outs = everywhere(half, "core").reshape(4, VALID, cols)
    return squares(outs, ins, masks)


def solution(mesh):
    fine = Mesh(mesh.devices.reshape(2, 2, 4, 4, 8), ("zhi", "core", "x", "y", "zlo"))
    grp, row, col = ("zhi", "core"), "x", ("y", "zlo")
    in_specs = (
        P(grp, col),
        P(grp, (row, *col)),
        P(col, row),
        P(row, grp, col),
        P(grp, None),
    )
    return jax.shard_map(
        per_device, mesh=fine, in_specs=in_specs, out_specs=P(col, row), check_vma=False
    )
```

time: 543 us -> 213 us (0.39)
  blocking collectives: 276 us -> 34.9 us
  waiting for transfers between devices: 222 us -> 48.9 us
  starting transfers between devices: 0.08 us -> 91.9 us
  between operations: 16.8 us -> 0.44 us
  matrix products: 7.65 us -> 0.28 us
  Pallas kernels: 0 us -> 6.64 us
  local copies, waits for them, and re-layouts: 11.3 us -> 17.8 us
    psum x2 -> x0, blocking collectives: 249 us -> none  [the longest x1 228 us: per_device(): proj_in = lax.psum(partial_in, 'col').astype(jnp.bfloat16)]
    all_gather x2 -> x0, waiting for transfers between devices: 158 us -> none  [the longest x1 158 us: per_device(): lax.all_gather(basis_out, 'grp', axis=1, tiled=True)[0]]
    ppermute x0 -> x7, starting transfers between devices: none -> 64.5 us  [the longest x6 55.7 us: swap(): return lax.ppermute(x, axis, [(i, i ^ by) for i in range(n)])]
    reduce_scatter x1 -> x0, waiting for transfers between devices: 63.2 us -> none  [sum_by_parts(): lax.psum_scatter(rows_for(lines, lax.axis_size(axis)), axis, scatter_dime...]
    all_to_all x0 -> x2, blocking collectives: none -> 34.9 us  [the longest x1 29.5 us: everywhere(): lax.all_to_all(jnp.broadcast_to(x[None], (n,) + x.shape), axis, 0, 0, til...]
    all_to_all x0 -> x5, waiting for transfers between devices: none -> 28.4 us  [the longest x3 22.7 us: exchange(): return lax.all_to_all(x, axis, 0, 0, tiled=True)]
    all_to_all x0 -> x5, starting transfers between devices: none -> 27.4 us  [the longest x3 17 us: exchange(): return lax.all_to_all(x, axis, 0, 0, tiled=True)]
    all_gather x1 -> x0, blocking collectives: 27.2 us -> none  [sum_by_parts(): whole = lax.all_gather(own, axis).reshape(-1, *lines.shape[1:])]
  transfers between devices with their start and end apart: 3 -> 12, of which waited for: 2 -> 7; matrix products, arithmetic and copies ran while one was open for 2% -> 9% of each run, Pallas kernels for 0% -> 1%
where the time goes in v1:
time: 213 us; the launch traced here: 210 us
  starting transfers between devices  91.9 us (43%)
  waiting for transfers between devices  48.9 us (23%)
  blocking collectives  34.9 us (16%)
  local copies, waits for them, and re-layouts  17.8 us (8%)
  other arithmetic  9.26 us (4%)
  Pallas kernels  6.64 us (3%)
    ppermute x6, starting transfers between devices, swap(): return lax.ppermute(x, axis, [(i, i ^ by) for i in range(n)])  55.7 us
    all_to_all x1, blocking collectives, everywhere(): lax.all_to_all(jnp.broadcast_to(x[None], (n,) + x.shape), axis, 0, 0, til...  29.5 us
    all_to_all x3, waiting for transfers between devices, exchange(): return lax.all_to_all(x, axis, 0, 0, tiled=True)  22.7 us
    ppermute x6, waiting for transfers between devices, swap(): return lax.ppermute(x, axis, [(i, i ^ by) for i in range(n)])  18.9 us
    all_to_all x3, starting transfers between devices, exchange(): return lax.all_to_all(x, axis, 0, 0, tiled=True)  17 us
    all_to_all x2, starting transfers between devices, everywhere(): lax.all_to_all(jnp.broadcast_to(x[None], (n,) + x.shape), axis, 0, 0, til...  10.4 us
    ppermute x1, starting transfers between devices, per_device(): lines = lax.ppermute(lines, PLANE, transposed())  8.82 us
    all_to_all x2, waiting for transfers between devices, everywhere(): lax.all_to_all(jnp.broadcast_to(x[None], (n,) + x.shape), axis, 0, 0, til...  5.71 us
  transfers between devices with their start and end apart: 12, of which 7 were waited for; matrix products, arithmetic and copies ran while one was open for 9% of the time, Pallas kernels for 1%

profile of v1, /device:TPU:1, one launch (start us, length us, event | category | flops | bytes accessed | tf_op | source)
XLA Modules:
  0.0 210.0 jit_solution(8339159671139294109)
XLA Ops:
  1.4 1.7 gather_fusion.1
  4.6 5.0 %all-to-all-start = ((bf16[4,144,256]{2,1,0:T(8,128)(2,1)}), bf16[4,144,256]{2,1,0:T(8,128)(2,1)S(1)}, u32[]{:S(2)}, u32[]{:S(2)}) async-start(bf16[4,144,256]{2,1,0:T(8,128)(2,1)} %copy.64), calls=%async_computation | async-start | bytes 589824 | tf_op jit(solution)/shard_map/all_to_all | solution.py:29
  10.8 8.8 %collective-permute-start = (bf16[144,256]{1,0:T(8,128)(2,1)S(1)}, bf16[144,256]{1,0:T(8,128)(2,1)S(1)}, u32[]{:S(2)}, u32[]{:S(2)}) collective-permute-start(bf16[144,256]{1,0:T(8,128)(2,1)S(1)} %pad_maximum_fusion.2), channel_id=1, source_target_pairs={{0,0},{1,1},{2,2},{3,3},{4,4},{5,5},{6,6},{7,7},{8,128},{9,129},{1... | collective-permute-start | bytes 221192 | tf_op jit(solution)/shard_map/ppermute | solution.py:98
  22.7 7.9 %all-to-all-start.1 = ((bf16[8,144,256]{2,1,0:T(8,128)(2,1)}), bf16[8,144,256]{2,1,0:T(8,128)(2,1)S(1)}, u32[]{:S(2)}, u32[]{:S(2)}) async-start(bf16[8,144,256]{2,1,0:T(8,128)(2,1)} %pad_maximum_fusion), calls=%async_computation.1 | async-start | bytes 1179648 | tf_op jit(solution)/shard_map/all_to_all | solution.py:29
  30.7 22.6 %all-to-all-done.1 = bf16[8,144,256]{2,1,0:T(8,128)(2,1)S(1)} async-done(((bf16[8,144,256]{2,1,0:T(8,128)(2,1)}), bf16[8,144,256]{2,1,0:T(8,128)(2,1)S(1)}, u32[]{:S(2)}, u32[]{:S(2)}) %all-to-all-start.1) | async-done | bytes 589856 | tf_op jit(solution)/shard_map/all_to_all | solution.py:29
  54.0 29.5 %all_to_all.35.lines_ref = bf16[4,8,144,256]{3,2,1,0:T(8,128)(2,1)S(1)} all-to-all(bf16[4,8,144,256]{3,2,1,0:T(8,128)(2,1)S(1)} %broadcast_in_dim.68), channel_id=1, replica_groups=mesh['zhi'=2,'core'=2,'x'=4,'y'=4,'zlo'=8] {'y'}, dimensions={0} | all-to-all | bytes 4718592 | tf_op jit(solution)/shard_map/all_to_all | solution.py:34
  83.8 11.5 %collective-permute-start.2 = (bf16[144,128]{0,1:T(8,128)(2,1)S(1)}, bf16[144,128]{0,1:T(8,128)(2,1)S(1)}, u32[]{:S(2)}, u32[]{:S(2)}) collective-permute-start(bf16[144,128]{0,1:T(8,128)(2,1)S(1)} %bitcast.43), channel_id=1, source_target_pairs={{0,256},{256,0},{1,257},{257,1},{2,258},{258,2},{3,259},{259,3},{4... | collective-permute-start | bytes 110600 | tf_op jit(solution)/shard_map/ppermute | solution.py:39
  95.2 2.3 %collective-permute-done.2 = bf16[144,128]{0,1:T(8,128)(2,1)S(1)} collective-permute-done((bf16[144,128]{0,1:T(8,128)(2,1)S(1)}, bf16[144,128]{0,1:T(8,128)(2,1)S(1)}, u32[]{:S(2)}, u32[]{:S(2)}) %collective-permute-start.2) | collective-permute-done | bytes 36896 | tf_op jit(solution)/shard_map/ppermute | solution.py:39
  97.5 13.6 %collective-permute-start.3 = (bf16[2,144,128]{1,2,0:T(8,128)(2,1)S(1)}, bf16[2,144,128]{1,2,0:T(8,128)(2,1)S(1)}, u32[]{:S(2)}, u32[]{:S(2)}) collective-permute-start(bf16[2,144,128]{1,2,0:T(8,128)(2,1)S(1)} %reverse_select_fusion.1), channel_id=1, source_target_pairs={{0,4},{1,5},{2,6},{3,7},{4,0},{5,1},{6,2},{7,3},{8,12},{9,13},{10,... | collective-permute-start | bytes 221192 | tf_op jit(solution)/shard_map/ppermute | solution.py:39
  111.2 4.3 %collective-permute-done.3 = bf16[2,144,128]{1,2,0:T(8,128)(2,1)S(1)} collective-permute-done((bf16[2,144,128]{1,2,0:T(8,128)(2,1)S(1)}, bf16[2,144,128]{1,2,0:T(8,128)(2,1)S(1)}, u32[]{:S(2)}, u32[]{:S(2)}) %collective-permute-start.3) | collective-permute-done | bytes 73760 | tf_op jit(solution)/shard_map/ppermute | solution.py:39
  115.5 11.9 %collective-permute-start.4 = (bf16[2,144,256]{1,2,0:T(8,128)(2,1)S(1)}, bf16[2,144,256]{1,2,0:T(8,128)(2,1)S(1)}, u32[]{:S(2)}, u32[]{:S(2)}) collective-permute-start(bf16[2,144,256]{1,2,0:T(8,128)(2,1)S(1)} %maximum_select_fusion.2), channel_id=1, source_target_pairs={{0,2},{1,3},{2,0},{3,1},{4,6},{5,7},{6,4},{7,5},{8,10},{9,11},{10,... | collective-permute-start | bytes 442376 | tf_op jit(solution)/shard_map/ppermute | solution.py:39
  127.5 5.2 %collective-permute-done.4 = bf16[2,144,256]{1,2,0:T(8,128)(2,1)S(1)} collective-permute-done((bf16[2,144,256]{1,2,0:T(8,128)(2,1)S(1)}, bf16[2,144,256]{1,2,0:T(8,128)(2,1)S(1)}, u32[]{:S(2)}, u32[]{:S(2)}) %collective-permute-start.4) | collective-permute-done | bytes 147488 | tf_op jit(solution)/shard_map/ppermute | solution.py:39
  133.7 8.8 %collective-permute-start.5 = (bf16[2,144,512]{1,2,0:T(8,128)(2,1)}, bf16[2,144,512]{1,2,0:T(8,128)(2,1)}, u32[]{:S(2)}, u32[]{:S(2)}) collective-permute-start(bf16[2,144,512]{1,2,0:T(8,128)(2,1)} %maximum_select_fusion.1), channel_id=1, source_target_pairs={{0,1},{1,0},{2,3},{3,2},{4,5},{5,4},{6,7},{7,6},{8,9},{9,8},{10,11... | collective-permute-start | bytes 884744 | tf_op jit(solution)/shard_map/ppermute | solution.py:39
  142.5 3.7 %copy.67 = bf16[1,1792,448]{2,1,0:T(8,128)(2,1)} copy(bf16[1,1792,448]{1,2,0:T(8,128)(2,1)} %param.8) | data formatting | bytes 3211264 | tf_op args[3]
  149.1 5.3 %all_to_all.36 = bf16[2,288,448]{2,1,0:T(8,128)(2,1)S(1)} all-to-all(bf16[2,288,448]{2,1,0:T(8,128)(2,1)S(1)} %bitcast.36), channel_id=1, replica_groups=mesh['zhi'=2,'core'=2,'x'=4,'y'=4,'zlo'=8] {'core'}, dimensions={0} | all-to-all | bytes 1032192 | tf_op jit(solution)/shard_map/all_to_all | solution.py:29
  155.3 4.1 %all-to-all-start.4 = ((bf16[4,72,448]{2,1,0:T(8,128)(2,1)}), bf16[4,72,448]{2,1,0:T(8,128)(2,1)}, u32[]{:S(2)}, u32[]{:S(2)}) async-start(bf16[4,72,448]{2,1,0:T(8,128)(2,1)} %bitcast.41), calls=%async_computation.4 | async-start | bytes 589824 | tf_op jit(solution)/shard_map/all_to_all | solution.py:29
  165.1 2.5 %collective-permute-start.6 = (bf16[2,144,1024]{2,1,0:T(8,128)(2,1)}, bf16[2,144,1024]{2,1,0:T(8,128)(2,1)}, u32[]{:S(2)}, u32[]{:S(2)}) collective-permute-start(bf16[2,144,1024]{2,1,0:T(8,128)(2,1)} %reshape.99), channel_id=1, source_target_pairs={{0,128},{128,0},{1,129},{129,1},{2,130},{130,2},{3,131},{131,3},{4... | collective-permute-start | bytes 1769480 | tf_op jit(solution)/shard_map/ppermute | solution.py:39
  168.6 7.4 %collective-permute-start.1 = (bf16[72,448]{1,0:T(8,128)(2,1)S(1)}, bf16[72,448]{1,0:T(8,128)(2,1)}, u32[]{:S(2)}, u32[]{:S(2)}) collective-permute-start(bf16[72,448]{1,0:T(8,128)(2,1)S(1)} %reduce_sum.51), channel_id=1, source_target_pairs={{0,256},{256,0},{1,257},{257,1},{2,258},{258,2},{3,259},{259,3},{4... | collective-permute-start | bytes 193544 | tf_op jit(solution)/shard_map/ppermute | solution.py:39
  176.0 7.1 %collective-permute-done.1 = bf16[72,448]{1,0:T(8,128)(2,1)} collective-permute-done((bf16[72,448]{1,0:T(8,128)(2,1)S(1)}, bf16[72,448]{1,0:T(8,128)(2,1)}, u32[]{:S(2)}, u32[]{:S(2)}) %collective-permute-start.1) | collective-permute-done | bytes 64544 | tf_op jit(solution)/shard_map/ppermute | solution.py:39
  184.8 4.5 %all-to-all-start.5 = ((bf16[4,72,448]{2,1,0:T(8,128)(2,1)}), bf16[4,72,448]{2,1,0:T(8,128)(2,1)}, u32[]{:S(2)}, u32[]{:S(2)}) async-start(bf16[4,72,448]{2,1,0:T(8,128)(2,1)} %broadcast_in_dim.69), calls=%async_computation.5 | async-start | bytes 589824 | tf_op jit(solution)/shard_map/all_to_all | solution.py:34
  189.4 5.7 %all-to-all-done.5 = bf16[4,72,448]{2,1,0:T(8,128)(2,1)} async-done(((bf16[4,72,448]{2,1,0:T(8,128)(2,1)}), bf16[4,72,448]{2,1,0:T(8,128)(2,1)}, u32[]{:S(2)}, u32[]{:S(2)}) %all-to-all-start.5) | async-done | bytes 258080 | tf_op jit(solution)/shard_map/all_to_all | solution.py:34
  195.1 1.8 broadcast_in_dim.71
  197.0 5.8 %all-to-all-start.6 = ((bf16[2,288,448]{2,1,0:T(8,128)(2,1)}), bf16[2,288,448]{2,1,0:T(8,128)(2,1)S(1)}, u32[]{:S(2)}, u32[]{:S(2)}) async-start(bf16[2,288,448]{2,1,0:T(8,128)(2,1)} %broadcast_in_dim.71), calls=%async_computation.6 | async-start | bytes 1179648 | tf_op jit(solution)/shard_map/all_to_all | solution.py:34
  204.8 5.3 %shard_map.56 = f32[448,1024]{1,0:T(8,128)} custom-call(bf16[4,144,448]{2,1,0:T(8,128)(2,1)S(1)} %bitcast.37, bf16[4,144,1024]{2,1,0:T(8,128)(2,1)S(1)} %bitcast.35, bf16[4,144,1]{2,1,0:T(8,128)(2,1)S(1)} %slice_bitcast_fusion.mask_ref), custom_call_target="tpu_custom_call" | custom-call | tf_op jit(solution)/shard_map/pallas_call | solution.py:77
  (58 shorter events, 23.1 us)
Async XLA Ops:
  0.0 3.1 %copy-start = (bf16[256,1024]{1,0:T(8,128)(2,1)S(1)}, bf16[256,1024]{1,0:T(8,128)(2,1)}, u32[]{:S(2)}) copy-start(bf16[256,1024]{1,0:T(8,128)(2,1)} %param.7) | copy-start | bytes 1572868
  3.6 6.0 %copy-start.4 = (bf16[192,224]{1,0:T(8,128)(2,1)S(1)}, bf16[192,224]{1,0:T(8,128)(2,1)}, u32[]{:S(2)}) copy-start(bf16[192,224]{1,0:T(8,128)(2,1)} %param.6) | copy-start | bytes 258052
  4.6 15.0 %all-to-all-start = ((bf16[4,144,256]{2,1,0:T(8,128)(2,1)}), bf16[4,144,256]{2,1,0:T(8,128)(2,1)S(1)}, u32[]{:S(2)}, u32[]{:S(2)}) async-start(bf16[4,144,256]{2,1,0:T(8,128)(2,1)} %copy.64), calls=%async_computation | async-start | bytes 589824 | tf_op jit(solution)/shard_map/all_to_all | solution.py:29
  10.8 10.9 %collective-permute-start = (bf16[144,256]{1,0:T(8,128)(2,1)S(1)}, bf16[144,256]{1,0:T(8,128)(2,1)S(1)}, u32[]{:S(2)}, u32[]{:S(2)}) collective-permute-start(bf16[144,256]{1,0:T(8,128)(2,1)S(1)} %pad_maximum_fusion.2), channel_id=1, source_target_pairs={{0,0},{1,1},{2,2},{3,3},{4,4},{5,5},{6,6},{7,7},{8,128},{9,129},{1... | collective-permute-start | bytes 221192 | tf_op jit(solution)/shard_map/ppermute | solution.py:98
  22.7 30.6 %all-to-all-start.1 = ((bf16[8,144,256]{2,1,0:T(8,128)(2,1)}), bf16[8,144,256]{2,1,0:T(8,128)(2,1)S(1)}, u32[]{:S(2)}, u32[]{:S(2)}) async-start(bf16[8,144,256]{2,1,0:T(8,128)(2,1)} %pad_maximum_fusion), calls=%async_computation.1 | async-start | bytes 1179648 | tf_op jit(solution)/shard_map/all_to_all | solution.py:29
  83.8 13.7 %collective-permute-start.2 = (bf16[144,128]{0,1:T(8,128)(2,1)S(1)}, bf16[144,128]{0,1:T(8,128)(2,1)S(1)}, u32[]{:S(2)}, u32[]{:S(2)}) collective-permute-start(bf16[144,128]{0,1:T(8,128)(2,1)S(1)} %bitcast.43), channel_id=1, source_target_pairs={{0,256},{256,0},{1,257},{257,1},{2,258},{258,2},{3,259},{259,3},{4... | collective-permute-start | bytes 110600 | tf_op jit(solution)/shard_map/ppermute | solution.py:39
  97.5 17.9 %collective-permute-start.3 = (bf16[2,144,128]{1,2,0:T(8,128)(2,1)S(1)}, bf16[2,144,128]{1,2,0:T(8,128)(2,1)S(1)}, u32[]{:S(2)}, u32[]{:S(2)}) collective-permute-start(bf16[2,144,128]{1,2,0:T(8,128)(2,1)S(1)} %reverse_select_fusion.1), channel_id=1, source_target_pairs={{0,4},{1,5},{2,6},{3,7},{4,0},{5,1},{6,2},{7,3},{8,12},{9,13},{10,... | collective-permute-start | bytes 221192 | tf_op jit(solution)/shard_map/ppermute | solution.py:39
  115.5 17.2 %collective-permute-start.4 = (bf16[2,144,256]{1,2,0:T(8,128)(2,1)S(1)}, bf16[2,144,256]{1,2,0:T(8,128)(2,1)S(1)}, u32[]{:S(2)}, u32[]{:S(2)}) collective-permute-start(bf16[2,144,256]{1,2,0:T(8,128)(2,1)S(1)} %maximum_select_fusion.2), channel_id=1, source_target_pairs={{0,2},{1,3},{2,0},{3,1},{4,6},{5,7},{6,4},{7,5},{8,10},{9,11},{10,... | collective-permute-start | bytes 442376 | tf_op jit(solution)/shard_map/ppermute | solution.py:39
  133.7 27.1 %collective-permute-start.5 = (bf16[2,144,512]{1,2,0:T(8,128)(2,1)}, bf16[2,144,512]{1,2,0:T(8,128)(2,1)}, u32[]{:S(2)}, u32[]{:S(2)}) collective-permute-start(bf16[2,144,512]{1,2,0:T(8,128)(2,1)} %maximum_select_fusion.1), channel_id=1, source_target_pairs={{0,1},{1,0},{2,3},{3,2},{4,5},{5,4},{6,7},{7,6},{8,9},{9,8},{10,11... | collective-permute-start | bytes 884744 | tf_op jit(solution)/shard_map/ppermute | solution.py:39
  146.2 1.5 copy-start.1
  155.3 12.2 %all-to-all-start.4 = ((bf16[4,72,448]{2,1,0:T(8,128)(2,1)}), bf16[4,72,448]{2,1,0:T(8,128)(2,1)}, u32[]{:S(2)}, u32[]{:S(2)}) async-start(bf16[4,72,448]{2,1,0:T(8,128)(2,1)} %bitcast.41), calls=%async_computation.4 | async-start | bytes 589824 | tf_op jit(solution)/shard_map/all_to_all | solution.py:29
  163.8 21.0 %copy-start.2 = (bf16[2,144,2,2,2,128]{5,4,3,2,1,0:T(2,128)(2,1)}, bf16[2,144,2,2,2,128]{5,4,3,2,1,0:T(2,128)(2,1)S(1)}, u32[]{:S(2)}) copy-start(bf16[2,144,2,2,2,128]{5,4,3,2,1,0:T(2,128)(2,1)S(1)} %copy.72) | copy-start | bytes 1769476
  165.1 38.2 %collective-permute-start.6 = (bf16[2,144,1024]{2,1,0:T(8,128)(2,1)}, bf16[2,144,1024]{2,1,0:T(8,128)(2,1)}, u32[]{:S(2)}, u32[]{:S(2)}) collective-permute-start(bf16[2,144,1024]{2,1,0:T(8,128)(2,1)} %reshape.99), channel_id=1, source_target_pairs={{0,128},{128,0},{1,129},{129,1},{2,130},{130,2},{3,131},{131,3},{4... | collective-permute-start | bytes 1769480 | tf_op jit(solution)/shard_map/ppermute | solution.py:39
  168.6 14.6 %collective-permute-start.1 = (bf16[72,448]{1,0:T(8,128)(2,1)S(1)}, bf16[72,448]{1,0:T(8,128)(2,1)}, u32[]{:S(2)}, u32[]{:S(2)}) collective-permute-start(bf16[72,448]{1,0:T(8,128)(2,1)S(1)} %reduce_sum.51), channel_id=1, source_target_pairs={{0,256},{256,0},{1,257},{257,1},{2,258},{258,2},{3,259},{259,3},{4... | collective-permute-start | bytes 193544 | tf_op jit(solution)/shard_map/ppermute | solution.py:39
  184.8 10.3 %all-to-all-start.5 = ((bf16[4,72,448]{2,1,0:T(8,128)(2,1)}), bf16[4,72,448]{2,1,0:T(8,128)(2,1)}, u32[]{:S(2)}, u32[]{:S(2)}) async-start(bf16[4,72,448]{2,1,0:T(8,128)(2,1)} %broadcast_in_dim.69), calls=%async_computation.5 | async-start | bytes 589824 | tf_op jit(solution)/shard_map/all_to_all | solution.py:34
  189.4 13.4 %copy-start.3 = (bf16[2,144,2,2,2,128]{5,4,3,2,1,0:T(2,128)(2,1)S(1)}, bf16[2,144,2,2,2,128]{5,4,3,2,1,0:T(2,128)(2,1)}, u32[]{:S(2)}) copy-start(bf16[2,144,2,2,2,128]{5,4,3,2,1,0:T(2,128)(2,1)} %copy-done.2) | copy-start | bytes 1769476
  197.0 7.8 %all-to-all-start.6 = ((bf16[2,288,448]{2,1,0:T(8,128)(2,1)}), bf16[2,288,448]{2,1,0:T(8,128)(2,1)S(1)}, u32[]{:S(2)}, u32[]{:S(2)}) async-start(bf16[2,288,448]{2,1,0:T(8,128)(2,1)} %broadcast_in_dim.71), calls=%async_computation.6 | async-start | bytes 1179648 | tf_op jit(solution)/shard_map/all_to_all | solution.py:34

commit v2 on v0

v2 whole, which is shorter than its diff:
```python
import jax
import jax.numpy as jnp
from jax import lax
from jax.experimental import pallas as pl
from jax.experimental.pallas import tpu as pltpu
from jax.sharding import Mesh, PartitionSpec as P

LEN = 96
VALID = 144
FEAT = 224
WIDE = 256
BF = jnp.bfloat16
F32 = jnp.float32
PLANE = ("zhi", "core", "y", "zh", "zq")
PARAMS = pltpu.CompilerParams(vmem_limit_bytes=48 << 20)


def to_basis(flip):
    def place(zhi, core, y, zlo):
        return ((zhi * 2 + core) * 4 + y) * 8 + zlo

    pairs = []
    for zhi in range(2):
        for core in range(2):
            for y in range(4):
                for z in range(8):
                    to = 7 - z if zhi != y >> 1 else z
                    there = place(y >> 1, zhi, core * 2 + (y & 1), to ^ flip)
                    pairs.append((place(zhi, core, y, z), there))
    return pairs


def exchange(x, axis):
    return lax.all_to_all(x, axis, 0, 0, tiled=True)


def everywhere(x, axis):
    return exchange(jnp.broadcast_to(x[None], (lax.axis_size(axis),) + x.shape), axis)


def swap(x, axis):
    return lax.ppermute(x, axis, [(0, 1), (1, 0)])


def across(left, right):
    return lax.dot_general(left, right, (((1,), (1,)), ((), ())), preferred_element_type=F32)


def chosen(first):
    slot = lax.broadcasted_iota(jnp.int32, (VALID, 2 * LEN), 0)
    line = lax.broadcasted_iota(jnp.int32, (VALID, 2 * LEN), 1)
    source = jnp.where(slot < first, slot, slot - first + LEN)
    return (source == line).astype(F32).astype(BF)


def start_kernel(len_ref, grads_ref, acts_ref, basis_ref, lines_ref, part_ref):
    pick = chosen(len_ref[0, 0])
    lines_ref[:, :FEAT] = jnp.dot(pick, grads_ref[...], preferred_element_type=F32).astype(BF)
    lines_ref[:, FEAT:] = jnp.zeros((VALID, WIDE - FEAT), BF)
    lines = jnp.dot(pick, acts_ref[...], preferred_element_type=F32).astype(BF)
    for y in range(4):
        part_ref[y] = jnp.dot(
            lines, basis_ref[:, y * WIDE : (y + 1) * WIDE], preferred_element_type=F32
        ).astype(BF)


def join_kernel(near_ref, far_ref, parts_ref, out_ref):
    total = parts_ref[0].astype(F32)
    for y in range(1, 4):
        total += parts_ref[y].astype(F32)
    total = total.astype(BF)
    for d in range(4):
        for w, ref in enumerate((near_ref, far_ref)):
            at = d * 64 + w * 32
            out_ref[d, w] = jnp.concatenate([ref[:, :FEAT], total[:, at : at + 32]], axis=1)


def sort_kernel(where_ref, both_ref, out_ref, in_ref):
    zh, mirrored = where_ref[0], where_ref[1]
    for f in range(8):
        at = jnp.where(mirrored == 1, 7 - f, f)
        far = (at // 4 != zh).astype(jnp.int32)
        block = both_ref[at % 4, far][:, :FEAT]
        for copy in range(4):
            out_ref[copy, :, f * FEAT : (f + 1) * FEAT] = block
    sums = []
    for w in range(2):
        total = both_ref[0, w][:, FEAT:].astype(F32)
        for q in range(1, 4):
            total += both_ref[q, w][:, FEAT:].astype(F32)
        sums.append(total)
    slot = lax.broadcasted_iota(jnp.int32, (VALID, 64), 0)
    mask = (slot < where_ref[2]).astype(F32)
    in_ref[...] = jnp.concatenate(sums + [mask], axis=1).astype(BF)


def project_kernel(where_ref, lines_ref, own_ref, other_ref, out_ref):
    core = where_ref[3]
    for t in range(2):
        total = across(lines_ref[2 * t + core], own_ref[...])
        total += across(lines_ref[2 * t + 1 - core], other_ref[...])
        for h in range(2):
            out_ref[2 * t + h] = total[h * 72 : (h + 1) * 72].astype(BF)


def sum_kernel(parts_ref, out_ref):
    total = parts_ref[0].astype(F32)
    for x in range(1, 4):
        total += parts_ref[x].astype(F32)
    out_ref[...] = total.astype(BF)


def spread_kernel(one_ref, two_ref, out_ref):
    total = (one_ref[...].astype(F32) + two_ref[...].astype(F32)).astype(BF)
    for x in range(4):
        out_ref[x] = total


def arrange_kernel(where_ref, own_ref, other_ref, own_mask_ref, other_mask_ref, out_ref, mask_ref):
    core, zq = where_ref[3], where_ref[4]
    for zhi in range(2):
        for c in range(2):
            mine = core == c
            g = zhi * 2 + c
            for y in range(4):
                for q in range(4):
                    at = y * WIDE + q * 64
                    block = jnp.where(mine, own_ref[y, q ^ zq], other_ref[y, q ^ zq])
                    out_ref[g, :, at : at + 64] = block[:, zhi * 64 : zhi * 64 + 64]
            mask_ref[g] = jnp.where(mine, own_mask_ref[zhi], other_mask_ref[zhi])


def square_kernel(where_ref, own_ref, other_ref, in_ref, mask_ref, eig_ref, left_ref):
    core = where_ref[3]
    for g in range(4):
        mine = core == g // 2
        lines = jnp.where(mine, own_ref[g % 2], other_ref[g % 2])
        first = lines * mask_ref[g][:, :1]
        left_ref[2 * g] = first.T
        left_ref[2 * g + 1] = (lines - first).T
    rows, cols = 112, 256
    for o in range(448 // rows):
        for i in range(1024 // cols):
            total = jnp.zeros((rows, cols), F32)
            for s in range(8):
                block = jnp.dot(
                    left_ref[s, o * rows : (o + 1) * rows, :],
                    in_ref[s // 2, :, i * cols : (i + 1) * cols],
                    preferred_element_type=F32,
                )
                total += block * block
            eig_ref[o * rows : (o + 1) * rows, i * cols : (i + 1) * cols] = total / 768.0


def call(kernel, out, *args, scalars=1, scratch=()):
    single = not isinstance(out, (list, tuple))
    smem = pl.BlockSpec(memory_space=pltpu.SMEM)
    vmem = pl.BlockSpec(memory_space=pltpu.VMEM)
    outs = [out] if single else list(out)
    got = pl.pallas_call(
        kernel,
        in_specs=[smem] * scalars + [vmem] * (len(args) - scalars),
        out_specs=[vmem] * len(outs),
        out_shape=outs,
        scratch_shapes=scratch,
        compiler_params=PARAMS,
    )(*args)
    return got[0] if single else got


def like(*shape, dtype=BF):
    return jax.ShapeDtypeStruct(shape, dtype)


def per_device(acts, grads, basis_in, basis_out, lengths):
    zhi, core, zh, zq = (lax.axis_index(a) for a in ("zhi", "core", "zh", "zq"))
    where = jnp.stack([zh, (core != zhi).astype(jnp.int32), lengths[0, 0], core, zq])
    lines, partial = call(
        start_kernel,
        [like(VALID, WIDE), like(4, VALID, WIDE)],
        lengths,
        grads,
        acts,
        basis_in,
    )
    near = lax.ppermute(lines, PLANE, to_basis(0))
    far = lax.ppermute(lines, PLANE, to_basis(4))
    basis = basis_out[0].T
    other_basis = swap(basis, "core")
    partial = exchange(partial, "y")
    both = call(join_kernel, like(4, 2, VALID, WIDE), near, far, partial, scalars=0)
    both = exchange(both, "zq")
    lines, ins = call(sort_kernel, [like(4, VALID, 8 * FEAT), like(VALID, 128)], where, both)
    lines = exchange(lines, "y")
    sums = ins.astype(F32) + swap(ins, "zh").astype(F32)
    ins = jnp.concatenate([sums[:, :64].astype(BF), ins[:, 64:]], axis=1)
    pair = swap(ins, "zhi")
    low = zhi == 0
    pair = jnp.where(low, jnp.stack([ins, pair]), jnp.stack([pair, ins]))
    masks = pair[:, :, 64:]
    ins = jnp.concatenate([pair[0, :, :64], pair[1, :, :64]], axis=1)
    ins, masks, other_masks, lines = lax.optimization_barrier(
        (ins, masks, swap(masks, "core"), lines)
    )
    ins = jnp.stack([ins] + [lax.ppermute(ins, "zq", [(i, i ^ k) for i in range(4)]) for k in (1, 2, 3)])
    cols = basis.shape[0]
    part = call(project_kernel, like(4, 72, cols), where, lines, basis, other_basis)
    part = exchange(part, "x")
    part = call(sum_kernel, like(72, cols), part, scalars=0)
    part, ins = lax.optimization_barrier((part, ins))
    ins = everywhere(ins, "y").reshape(4, 4, VALID, 128)
    part = call(spread_kernel, like(4, 72, cols), part, swap(part, "zhi"), scalars=0)
    part, ins = lax.optimization_barrier((part, ins))
    outs = exchange(part, "x").reshape(2, VALID, cols)
    ins, masks = call(
        arrange_kernel,
        [like(4, VALID, 1024), like(4, VALID, 64)],
        where,
        ins,
        swap(ins, "core"),
        masks,
        other_masks,
    )
    return call(
        square_kernel,
        like(cols, 1024, dtype=F32),
        where,
        outs,
        swap(outs, "core"),
        ins,
        masks,
        scratch=[pltpu.VMEM((8, cols, VALID), BF)],
    )


def solution(mesh):
    axes = ("zhi", "core", "x", "y", "zh", "zq")
    fine = Mesh(mesh.devices.reshape(2, 2, 4, 4, 2, 4), axes)
    grp, row, col = ("zhi", "core"), "x", ("y", "zh", "zq")
    in_specs = (
        P(grp, col),
        P(grp, (row, *col)),
        P(col, row),
        P(row, grp, col),
        P(grp, None),
    )
    return jax.shard_map(
        per_device, mesh=fine, in_specs=in_specs, out_specs=P(col, row), check_vma=False
    )
```

time: 543 us -> 163 us (0.30)
  blocking collectives: 276 us -> 10.8 us
  waiting for transfers between devices: 222 us -> 40.4 us
  starting transfers between devices: 0.08 us -> 89.6 us
  between operations: 16.8 us -> 0.26 us
  Pallas kernels: 0 us -> 13.8 us
  matrix products: 7.65 us -> 0 us
    psum x2 -> x0, blocking collectives: 249 us -> none  [the longest x1 228 us: per_device(): proj_in = lax.psum(partial_in, 'col').astype(jnp.bfloat16)]
    all_gather x2 -> x0, waiting for transfers between devices: 158 us -> none  [the longest x1 158 us: per_device(): lax.all_gather(basis_out, 'grp', axis=1, tiled=True)[0]]
    reduce_scatter x1 -> x0, waiting for transfers between devices: 63.2 us -> none  [sum_by_parts(): lax.psum_scatter(rows_for(lines, lax.axis_size(axis)), axis, scatter_dime...]
    ppermute x0 -> x12, starting transfers between devices: none -> 56.7 us  [the longest x7 27.6 us: swap(): return lax.ppermute(x, axis, [(0, 1), (1, 0)])]
    all_to_all x0 -> x5, starting transfers between devices: none -> 32.9 us  [exchange(): return lax.all_to_all(x, axis, 0, 0, tiled=True)]
    ppermute x0 -> x12, waiting for transfers between devices: none -> 30.3 us  [the longest x7 26.6 us: swap(): return lax.ppermute(x, axis, [(0, 1), (1, 0)])]
    all_gather x1 -> x0, blocking collectives: 27.2 us -> none  [sum_by_parts(): whole = lax.all_gather(own, axis).reshape(-1, *lines.shape[1:])]
    pallas_call x0 -> x8, Pallas kernels: none -> 13.8 us  [call(): pl.pallas_call(kernel, in_specs=[smem] * scalars + [vmem] * (len(args) -...]
  transfers between devices with their start and end apart: 3 -> 17, of which waited for: 2 -> 7; matrix products, arithmetic and copies ran while one was open for 2% -> 0% of each run, Pallas kernels for 0% -> 1%
where the time goes in v2:
time: 163 us; the launch traced here: 161 us
  starting transfers between devices  89.6 us (55%)
  waiting for transfers between devices  40.4 us (25%)
  Pallas kernels  13.8 us (8%)
  blocking collectives  10.8 us (7%)
  local copies, waits for them, and re-layouts  5.99 us (4%)
    all_to_all x5, starting transfers between devices, exchange(): return lax.all_to_all(x, axis, 0, 0, tiled=True)  32.9 us
    ppermute x7, starting transfers between devices, swap(): return lax.ppermute(x, axis, [(0, 1), (1, 0)])  27.6 us
    ppermute x7, waiting for transfers between devices, swap(): return lax.ppermute(x, axis, [(0, 1), (1, 0)])  26.6 us
    pallas_call x8, Pallas kernels, call(): pl.pallas_call(kernel, in_specs=[smem] * scalars + [vmem] * (len(args) -...  13.8 us
    ppermute x1, starting transfers between devices, per_device(): far = lax.ppermute(lines, PLANE, to_basis(4))  12.6 us
    all_to_all x1, blocking collectives, exchange(): return lax.all_to_all(x, axis, 0, 0, tiled=True)  10.8 us
    all_to_all x5, waiting for transfers between devices, exchange(): return lax.all_to_all(x, axis, 0, 0, tiled=True)  10.1 us
    ppermute x3, starting transfers between devices, per_device(): lax.ppermute(ins, 'zq', [(i, i ^ k) for i in range(4)])  9.26 us
  transfers between devices with their start and end apart: 17, of which 7 were waited for; matrix products, arithmetic and copies ran while one was open for 0% of the time, Pallas kernels for 1%

profile of v2, /device:TPU:1, one launch (start us, length us, event | category | flops | bytes accessed | tf_op | source)
XLA Modules:
  0.0 161.2 jit_solution(14557485197712177830)
XLA Ops:
  5.1 5.0 %all-to-all-start = ((bf16[4,144,256]{2,1,0:T(8,128)(2,1)}), bf16[4,144,256]{2,1,0:T(8,128)(2,1)S(1)}, u32[]{:S(2)}, u32[]{:S(2)}) async-start(bf16[4,144,256]{2,1,0:T(8,128)(2,1)} %get-tuple-element.20), calls=%async_computation | async-start | bytes 589824 | tf_op jit(solution)/shard_map/all_to_all | solution.py:34
  10.1 12.6 %collective-permute-start.1 = (bf16[144,256]{1,0:T(8,128)(2,1)S(1)}, bf16[144,256]{1,0:T(8,128)(2,1)S(1)}, u32[]{:S(2)}, u32[]{:S(2)}) collective-permute-start(bf16[144,256]{1,0:T(8,128)(2,1)S(1)} %get-tuple-element.19), channel_id=1, source_target_pairs={{0,4},{1,5},{2,6},{3,7},{4,0},{5,1},{6,2},{7,3},{8,12},{9,13},{10,... | collective-permute-start | bytes 221192 | tf_op jit(solution)/shard_map/ppermute | solution.py:187
  22.7 7.2 %collective-permute-start = (bf16[144,256]{1,0:T(8,128)(2,1)S(1)}, bf16[144,256]{1,0:T(8,128)(2,1)S(1)}, u32[]{:S(2)}, u32[]{:S(2)}) collective-permute-start(bf16[144,256]{1,0:T(8,128)(2,1)S(1)} %get-tuple-element.19), channel_id=1, source_target_pairs={{0,0},{1,1},{2,2},{3,3},{4,4},{5,5},{6,6},{7,7},{8,8},{9,9},{10,10... | collective-permute-start | bytes 221192 | tf_op jit(solution)/shard_map/ppermute | solution.py:186
  29.9 2.4 %collective-permute-done.near_ref = bf16[144,256]{1,0:T(8,128)(2,1)S(1)} collective-permute-done((bf16[144,256]{1,0:T(8,128)(2,1)S(1)}, bf16[144,256]{1,0:T(8,128)(2,1)S(1)}, u32[]{:S(2)}, u32[]{:S(2)}) %collective-permute-start) | collective-permute-done | bytes 73760 | tf_op jit(solution)/shard_map/ppermute | solution.py:186
  33.3 8.3 %all-to-all-start.1 = ((bf16[4,2,144,256]{3,2,1,0:T(8,128)(2,1)}), bf16[4,2,144,256]{3,2,1,0:T(8,128)(2,1)S(1)}, u32[]{:S(2)}, u32[]{:S(2)}) async-start(bf16[4,2,144,256]{3,2,1,0:T(8,128)(2,1)} %shard_map.56), calls=%async_computation.1 | async-start | bytes 1179648 | tf_op jit(solution)/shard_map/all_to_all | solution.py:34
  43.7 10.1 %all-to-all-done.1.both_ref = bf16[4,2,144,256]{3,2,1,0:T(8,128)(2,1)S(1)} async-done(((bf16[4,2,144,256]{3,2,1,0:T(8,128)(2,1)}), bf16[4,2,144,256]{3,2,1,0:T(8,128)(2,1)S(1)}, u32[]{:S(2)}, u32[]{:S(2)}) %all-to-all-start.1) | async-done | bytes 589856 | tf_op jit(solution)/shard_map/all_to_all | solution.py:34
  56.1 10.0 %all-to-all-start.2 = ((bf16[4,144,1792]{2,1,0:T(8,128)(2,1)}), bf16[4,144,1792]{2,1,0:T(8,128)(2,1)S(1)}, u32[]{:S(2)}, u32[]{:S(2)}) async-start(bf16[4,144,1792]{2,1,0:T(8,128)(2,1)} %copy-done), calls=%async_computation.2 | async-start | bytes 4128768 | tf_op jit(solution)/shard_map/all_to_all | solution.py:34
  66.1 4.5 %collective-permute-start.2 = (bf16[144,128]{1,0:T(8,128)(2,1)S(1)}, bf16[144,128]{1,0:T(8,128)(2,1)S(1)}, u32[]{:S(2)}, u32[]{:S(2)}) collective-permute-start(bf16[144,128]{1,0:T(8,128)(2,1)S(1)} %get-tuple-element.21), channel_id=1, source_target_pairs={{0,4},{4,0},{1,5},{5,1},{2,6},{6,2},{3,7},{7,3},{8,12},{12,8},{9,1... | collective-permute-start | bytes 110600 | tf_op jit(solution)/shard_map/ppermute | solution.py:42
  70.7 4.0 %collective-permute-done.2 = bf16[144,128]{1,0:T(8,128)(2,1)S(1)} collective-permute-done((bf16[144,128]{1,0:T(8,128)(2,1)S(1)}, bf16[144,128]{1,0:T(8,128)(2,1)S(1)}, u32[]{:S(2)}, u32[]{:S(2)}) %collective-permute-start.2) | collective-permute-done | bytes 36896 | tf_op jit(solution)/shard_map/ppermute | solution.py:42
  74.9 1.9 %collective-permute-start.3 = (bf16[144,128]{1,0:T(8,128)(2,1)S(1)}, bf16[144,128]{1,0:T(8,128)(2,1)S(1)}, u32[]{:S(2)}, u32[]{:S(2)}) collective-permute-start(bf16[144,128]{1,0:T(8,128)(2,1)S(1)} %pad_maximum_fusion.1), channel_id=1, source_target_pairs={{0,256},{256,0},{1,257},{257,1},{2,258},{258,2},{3,259},{259,3},{4... | collective-permute-start | bytes 110600 | tf_op jit(solution)/shard_map/ppermute | solution.py:42
  76.9 11.6 %collective-permute-done.3 = bf16[144,128]{1,0:T(8,128)(2,1)S(1)} collective-permute-done((bf16[144,128]{1,0:T(8,128)(2,1)S(1)}, bf16[144,128]{1,0:T(8,128)(2,1)S(1)}, u32[]{:S(2)}, u32[]{:S(2)}) %collective-permute-start.3) | collective-permute-done | bytes 36896 | tf_op jit(solution)/shard_map/ppermute | solution.py:42
  88.6 4.9 %collective-permute-start.4 = (bf16[2,144,64]{2,1,0:T(8,128)(2,1)S(1)}, bf16[2,144,64]{2,1,0:T(8,128)(2,1)S(1)}, u32[]{:S(2)}, u32[]{:S(2)}) collective-permute-start(bf16[2,144,64]{2,1,0:T(8,128)(2,1)S(1)} %slice.29.own_mask_ref), channel_id=1, source_target_pairs={{0,128},{128,0},{1,129},{129,1},{2,130},{130,2},{3,131},{131,3},{4... | collective-permute-start | bytes 110600 | tf_op jit(solution)/shard_map/ppermute | solution.py:42
  94.5 4.6 %shard_map.58 = bf16[4,72,448]{2,1,0:T(8,128)(2,1)} custom-call(s32[5]{0:T(128)S(1)} %stack.52.where_ref, bf16[4,144,1792]{2,1,0:T(8,128)(2,1)S(1)} %all-to-all-done.2.lines_ref, bf16[448,1792]{1,0:T(8,128)(2,1)} %bitcast.10.own_ref, bf16[448,1792]{1,0:T(8,128)(2,1)} %collective-permute-done.5.other_ref), custom_call_target="tpu_custom_call" | custom-call | tf_op jit(solution)/shard_map/pallas_call | solution.py:160
  99.1 5.0 %all-to-all-start.3 = ((bf16[4,72,448]{2,1,0:T(8,128)(2,1)}), bf16[4,72,448]{2,1,0:T(8,128)(2,1)S(1)}, u32[]{:S(2)}, u32[]{:S(2)}) async-start(bf16[4,72,448]{2,1,0:T(8,128)(2,1)} %shard_map.58), calls=%async_computation.3 | async-start | bytes 589824 | tf_op jit(solution)/shard_map/all_to_all | solution.py:34
  104.1 2.3 %collective-permute-start.8 = (bf16[144,128]{1,0:T(8,128)(2,1)S(1)}, bf16[144,128]{1,0:T(8,128)(2,1)S(1)}, u32[]{:S(2)}, u32[]{:S(2)}) collective-permute-start(bf16[144,128]{1,0:T(8,128)(2,1)S(1)} %pad_maximum_fusion.2), channel_id=1, source_target_pairs={{0,3},{1,2},{2,1},{3,0},{4,7},{5,6},{6,5},{7,4},{8,11},{9,10},{10,... | collective-permute-start | bytes 110600 | tf_op jit(solution)/shard_map/ppermute | solution.py:205
  106.4 1.9 %collective-permute-start.7 = (bf16[144,128]{1,0:T(8,128)(2,1)S(1)}, bf16[144,128]{1,0:T(8,128)(2,1)S(1)}, u32[]{:S(2)}, u32[]{:S(2)}) collective-permute-start(bf16[144,128]{1,0:T(8,128)(2,1)S(1)} %pad_maximum_fusion.2), channel_id=1, source_target_pairs={{0,2},{1,3},{2,0},{3,1},{4,6},{5,7},{6,4},{7,5},{8,10},{9,11},{10,... | collective-permute-start | bytes 110600 | tf_op jit(solution)/shard_map/ppermute | solution.py:205
  108.3 5.1 %collective-permute-start.6 = (bf16[144,128]{1,0:T(8,128)(2,1)S(1)}, bf16[144,128]{1,0:T(8,128)(2,1)S(1)}, u32[]{:S(2)}, u32[]{:S(2)}) collective-permute-start(bf16[144,128]{1,0:T(8,128)(2,1)S(1)} %pad_maximum_fusion.2), channel_id=1, source_target_pairs={{0,1},{1,0},{2,3},{3,2},{4,5},{5,4},{6,7},{7,6},{8,9},{9,8},{10,11... | collective-permute-start | bytes 110600 | tf_op jit(solution)/shard_map/ppermute | solution.py:205
  115.7 4.5 %all-to-all-start.4 = ((bf16[4,4,144,128]{3,2,1,0:T(8,128)(2,1)}), bf16[4,4,144,128]{3,2,1,0:T(8,128)(2,1)S(1)}, u32[]{:S(2)}, u32[]{:S(2)}) async-start(bf16[4,4,144,128]{3,2,1,0:T(8,128)(2,1)} %broadcast_in_dim.2), calls=%async_computation.4 | async-start | bytes 1179648 | tf_op jit(solution)/shard_map/all_to_all | solution.py:34
  120.2 4.4 %collective-permute-start.9 = (bf16[72,448]{1,0:T(8,128)(2,1)S(1)}, bf16[72,448]{1,0:T(8,128)(2,1)S(1)}, u32[]{:S(2)}, u32[]{:S(2)}) collective-permute-start(bf16[72,448]{1,0:T(8,128)(2,1)S(1)} %shard_map.59.one_ref), channel_id=1, source_target_pairs={{0,256},{256,0},{1,257},{257,1},{2,258},{258,2},{3,259},{259,3},{4... | collective-permute-start | bytes 193544 | tf_op jit(solution)/shard_map/ppermute | solution.py:42
  124.5 10.2 %collective-permute-done.9.two_ref = bf16[72,448]{1,0:T(8,128)(2,1)S(1)} collective-permute-done((bf16[72,448]{1,0:T(8,128)(2,1)S(1)}, bf16[72,448]{1,0:T(8,128)(2,1)S(1)}, u32[]{:S(2)}, u32[]{:S(2)}) %collective-permute-start.9) | collective-permute-done | bytes 64544 | tf_op jit(solution)/shard_map/ppermute | solution.py:42
  134.8 6.7 %collective-permute-start.11 = (bf16[4,4,144,128]{3,2,1,0:T(8,128)(2,1)S(1)}, bf16[4,4,144,128]{3,2,1,0:T(8,128)(2,1)S(1)}, u32[]{:S(2)}, u32[]{:S(2)}) collective-permute-start(bf16[4,4,144,128]{3,2,1,0:T(8,128)(2,1)S(1)} %all-to-all-done.4.own_ref), channel_id=1, source_target_pairs={{0,128},{128,0},{1,129},{129,1},{2,130},{130,2},{3,131},{131,3},{4... | collective-permute-start | bytes 1769480 | tf_op jit(solution)/shard_map/ppermute | solution.py:42
  141.4 10.8 %all_to_all.30 = bf16[4,72,448]{2,1,0:T(8,128)(2,1)S(1)} all-to-all(bf16[4,72,448]{2,1,0:T(8,128)(2,1)S(1)} %shard_map.60), channel_id=1, replica_groups=mesh['zhi'=2,'core'=2,'x'=4,'y'=4,'zh'=2,'zq'=4] {'x'}, dimensions={0} | all-to-all | bytes 516096 | tf_op jit(solution)/shard_map/all_to_all | solution.py:34
  152.3 3.3 %collective-permute-start.10 = (bf16[2,144,448]{2,1,0:T(8,128)(2,1)S(1)}, bf16[2,144,448]{2,1,0:T(8,128)(2,1)S(1)}, u32[]{:S(2)}, u32[]{:S(2)}) collective-permute-start(bf16[2,144,448]{2,1,0:T(8,128)(2,1)S(1)} %bitcast.21), channel_id=1, source_target_pairs={{0,128},{128,0},{1,129},{129,1},{2,130},{130,2},{3,131},{131,3},{4... | collective-permute-start | bytes 774152 | tf_op jit(solution)/shard_map/ppermute | solution.py:42
  156.9 4.2 %shard_map.62 = f32[448,1024]{1,0:T(8,128)} custom-call(s32[5]{0:T(128)S(1)} %stack.52.where_ref, bf16[2,144,448]{2,1,0:T(8,128)(2,1)S(1)} %bitcast.22, bf16[2,144,448]{2,1,0:T(8,128)(2,1)S(1)} %collective-permute-done.10.other_ref, bf16[4,144,1024]{2,1,0:T(8,128)(2,1)S(1)} %get-tuple-element.31.in_ref, bf16[4,144,64]{2,1,0:T(8,128)(2,1)S(1)} %get-tuple-element.32.mask_ref), custom_call_target="tpu_custom_call" | custom-call | tf_op jit(solution)/shard_map/pallas_call | solution.py:160
  (42 shorter events, 15.3 us)
Async XLA Ops:
  0.0 1.0 copy-start.1
  1.0 0.9 copy-start.2
  1.9 0.9 copy-start.3
  2.8 0.7 copy-start.4
  3.5 40.1 %copy-start.5 = (s32[1,2]{1,0:T(1,128)S(1)}, s32[1,2]{1,0:T(1,128)}, u32[]{:S(2)}) copy-start(s32[1,2]{1,0:T(1,128)} %len_ref.1) | copy-start | bytes 28
  5.1 27.2 %all-to-all-start = ((bf16[4,144,256]{2,1,0:T(8,128)(2,1)}), bf16[4,144,256]{2,1,0:T(8,128)(2,1)S(1)}, u32[]{:S(2)}, u32[]{:S(2)}) async-start(bf16[4,144,256]{2,1,0:T(8,128)(2,1)} %get-tuple-element.20), calls=%async_computation | async-start | bytes 589824 | tf_op jit(solution)/shard_map/all_to_all | solution.py:34
  10.1 19.8 %collective-permute-start.1 = (bf16[144,256]{1,0:T(8,128)(2,1)S(1)}, bf16[144,256]{1,0:T(8,128)(2,1)S(1)}, u32[]{:S(2)}, u32[]{:S(2)}) collective-permute-start(bf16[144,256]{1,0:T(8,128)(2,1)S(1)} %get-tuple-element.19), channel_id=1, source_target_pairs={{0,4},{1,5},{2,6},{3,7},{4,0},{5,1},{6,2},{7,3},{8,12},{9,13},{10,... | collective-permute-start | bytes 221192 | tf_op jit(solution)/shard_map/ppermute | solution.py:187
  22.7 9.6 %collective-permute-start = (bf16[144,256]{1,0:T(8,128)(2,1)S(1)}, bf16[144,256]{1,0:T(8,128)(2,1)S(1)}, u32[]{:S(2)}, u32[]{:S(2)}) collective-permute-start(bf16[144,256]{1,0:T(8,128)(2,1)S(1)} %get-tuple-element.19), channel_id=1, source_target_pairs={{0,0},{1,1},{2,2},{3,3},{4,4},{5,5},{6,6},{7,7},{8,8},{9,9},{10,10... | collective-permute-start | bytes 221192 | tf_op jit(solution)/shard_map/ppermute | solution.py:186
  33.3 20.5 %all-to-all-start.1 = ((bf16[4,2,144,256]{3,2,1,0:T(8,128)(2,1)}), bf16[4,2,144,256]{3,2,1,0:T(8,128)(2,1)S(1)}, u32[]{:S(2)}, u32[]{:S(2)}) async-start(bf16[4,2,144,256]{3,2,1,0:T(8,128)(2,1)} %shard_map.56), calls=%async_computation.1 | async-start | bytes 1179648 | tf_op jit(solution)/shard_map/all_to_all | solution.py:34
  41.6 52.8 %collective-permute-start.5 = (bf16[448,1792]{1,0:T(8,128)(2,1)}, bf16[448,1792]{1,0:T(8,128)(2,1)}, u32[]{:S(2)}, u32[]{:S(2)}) collective-permute-start(bf16[448,1792]{1,0:T(8,128)(2,1)} %bitcast.10.own_ref), channel_id=1, source_target_pairs={{0,128},{128,0},{1,129},{129,1},{2,130},{130,2},{3,131},{131,3},{4... | collective-permute-start | bytes 4816904 | tf_op jit(solution)/shard_map/ppermute | solution.py:42
  54.8 1.3 copy-start
  56.1 38.3 %all-to-all-start.2 = ((bf16[4,144,1792]{2,1,0:T(8,128)(2,1)}), bf16[4,144,1792]{2,1,0:T(8,128)(2,1)S(1)}, u32[]{:S(2)}, u32[]{:S(2)}) async-start(bf16[4,144,1792]{2,1,0:T(8,128)(2,1)} %copy-done), calls=%async_computation.2 | async-start | bytes 4128768 | tf_op jit(solution)/shard_map/all_to_all | solution.py:34
  66.1 8.6 %collective-permute-start.2 = (bf16[144,128]{1,0:T(8,128)(2,1)S(1)}, bf16[144,128]{1,0:T(8,128)(2,1)S(1)}, u32[]{:S(2)}, u32[]{:S(2)}) collective-permute-start(bf16[144,128]{1,0:T(8,128)(2,1)S(1)} %get-tuple-element.21), channel_id=1, source_target_pairs={{0,4},{4,0},{1,5},{5,1},{2,6},{6,2},{3,7},{7,3},{8,12},{12,8},{9,1... | collective-permute-start | bytes 110600 | tf_op jit(solution)/shard_map/ppermute | solution.py:42
  74.9 13.6 %collective-permute-start.3 = (bf16[144,128]{1,0:T(8,128)(2,1)S(1)}, bf16[144,128]{1,0:T(8,128)(2,1)S(1)}, u32[]{:S(2)}, u32[]{:S(2)}) collective-permute-start(bf16[144,128]{1,0:T(8,128)(2,1)S(1)} %pad_maximum_fusion.1), channel_id=1, source_target_pairs={{0,256},{256,0},{1,257},{257,1},{2,258},{258,2},{3,259},{259,3},{4... | collective-permute-start | bytes 110600 | tf_op jit(solution)/shard_map/ppermute | solution.py:42
  88.6 5.8 %collective-permute-start.4 = (bf16[2,144,64]{2,1,0:T(8,128)(2,1)S(1)}, bf16[2,144,64]{2,1,0:T(8,128)(2,1)S(1)}, u32[]{:S(2)}, u32[]{:S(2)}) collective-permute-start(bf16[2,144,64]{2,1,0:T(8,128)(2,1)S(1)} %slice.29.own_mask_ref), channel_id=1, source_target_pairs={{0,128},{128,0},{1,129},{129,1},{2,130},{130,2},{3,131},{131,3},{4... | collective-permute-start | bytes 110600 | tf_op jit(solution)/shard_map/ppermute | solution.py:42
  99.1 15.7 %all-to-all-start.3 = ((bf16[4,72,448]{2,1,0:T(8,128)(2,1)}), bf16[4,72,448]{2,1,0:T(8,128)(2,1)S(1)}, u32[]{:S(2)}, u32[]{:S(2)}) async-start(bf16[4,72,448]{2,1,0:T(8,128)(2,1)} %shard_map.58), calls=%async_computation.3 | async-start | bytes 589824 | tf_op jit(solution)/shard_map/all_to_all | solution.py:34
  104.1 9.3 %collective-permute-start.8 = (bf16[144,128]{1,0:T(8,128)(2,1)S(1)}, bf16[144,128]{1,0:T(8,128)(2,1)S(1)}, u32[]{:S(2)}, u32[]{:S(2)}) collective-permute-start(bf16[144,128]{1,0:T(8,128)(2,1)S(1)} %pad_maximum_fusion.2), channel_id=1, source_target_pairs={{0,3},{1,2},{2,1},{3,0},{4,7},{5,6},{6,5},{7,4},{8,11},{9,10},{10,... | collective-permute-start | bytes 110600 | tf_op jit(solution)/shard_map/ppermute | solution.py:205
  106.4 7.0 %collective-permute-start.7 = (bf16[144,128]{1,0:T(8,128)(2,1)S(1)}, bf16[144,128]{1,0:T(8,128)(2,1)S(1)}, u32[]{:S(2)}, u32[]{:S(2)}) collective-permute-start(bf16[144,128]{1,0:T(8,128)(2,1)S(1)} %pad_maximum_fusion.2), channel_id=1, source_target_pairs={{0,2},{1,3},{2,0},{3,1},{4,6},{5,7},{6,4},{7,5},{8,10},{9,11},{10,... | collective-permute-start | bytes 110600 | tf_op jit(solution)/shard_map/ppermute | solution.py:205
  108.3 6.4 %collective-permute-start.6 = (bf16[144,128]{1,0:T(8,128)(2,1)S(1)}, bf16[144,128]{1,0:T(8,128)(2,1)S(1)}, u32[]{:S(2)}, u32[]{:S(2)}) collective-permute-start(bf16[144,128]{1,0:T(8,128)(2,1)S(1)} %pad_maximum_fusion.2), channel_id=1, source_target_pairs={{0,1},{1,0},{2,3},{3,2},{4,5},{5,4},{6,7},{7,6},{8,9},{9,8},{10,11... | collective-permute-start | bytes 110600 | tf_op jit(solution)/shard_map/ppermute | solution.py:205
  115.7 19.1 %all-to-all-start.4 = ((bf16[4,4,144,128]{3,2,1,0:T(8,128)(2,1)}), bf16[4,4,144,128]{3,2,1,0:T(8,128)(2,1)S(1)}, u32[]{:S(2)}, u32[]{:S(2)}) async-start(bf16[4,4,144,128]{3,2,1,0:T(8,128)(2,1)} %broadcast_in_dim.2), calls=%async_computation.4 | async-start | bytes 1179648 | tf_op jit(solution)/shard_map/all_to_all | solution.py:34
  120.2 14.5 %collective-permute-start.9 = (bf16[72,448]{1,0:T(8,128)(2,1)S(1)}, bf16[72,448]{1,0:T(8,128)(2,1)S(1)}, u32[]{:S(2)}, u32[]{:S(2)}) collective-permute-start(bf16[72,448]{1,0:T(8,128)(2,1)S(1)} %shard_map.59.one_ref), channel_id=1, source_target_pairs={{0,256},{256,0},{1,257},{257,1},{2,258},{258,2},{3,259},{259,3},{4... | collective-permute-start | bytes 193544 | tf_op jit(solution)/shard_map/ppermute | solution.py:42
  134.8 20.8 %collective-permute-start.11 = (bf16[4,4,144,128]{3,2,1,0:T(8,128)(2,1)S(1)}, bf16[4,4,144,128]{3,2,1,0:T(8,128)(2,1)S(1)}, u32[]{:S(2)}, u32[]{:S(2)}) collective-permute-start(bf16[4,4,144,128]{3,2,1,0:T(8,128)(2,1)S(1)} %all-to-all-done.4.own_ref), channel_id=1, source_target_pairs={{0,128},{128,0},{1,129},{129,1},{2,130},{130,2},{3,131},{131,3},{4... | collective-permute-start | bytes 1769480 | tf_op jit(solution)/shard_map/ppermute | solution.py:42
  152.3 4.6 %collective-permute-start.10 = (bf16[2,144,448]{2,1,0:T(8,128)(2,1)S(1)}, bf16[2,144,448]{2,1,0:T(8,128)(2,1)S(1)}, u32[]{:S(2)}, u32[]{:S(2)}) collective-permute-start(bf16[2,144,448]{2,1,0:T(8,128)(2,1)S(1)} %bitcast.21), channel_id=1, source_target_pairs={{0,128},{128,0},{1,129},{129,1},{2,130},{130,2},{3,131},{131,3},{4... | collective-permute-start | bytes 774152 | tf_op jit(solution)/shard_map/ppermute | solution.py:42

commit v3 on v2

--- a/solution.py
+++ b/solution.py
@@ -53,21 +53,27 @@
     return (source == line).astype(F32).astype(BF)
 
 
-def start_kernel(len_ref, grads_ref, acts_ref, basis_ref, lines_ref, part_ref):
+def pack_kernel(len_ref, grads_ref, out_ref):
     pick = chosen(len_ref[0, 0])
-    lines_ref[:, :FEAT] = jnp.dot(pick, grads_ref[...], preferred_element_type=F32).astype(BF)
-    lines_ref[:, FEAT:] = jnp.zeros((VALID, WIDE - FEAT), BF)
+    out_ref[:, :FEAT] = jnp.dot(pick, grads_ref[...], preferred_element_type=F32).astype(BF)
+    out_ref[:, FEAT:] = jnp.zeros((VALID, WIDE - FEAT), BF)
+
+
+def inputs_kernel(where_ref, acts_ref, basis_ref, *out_refs):
+    pick = chosen(where_ref[2])
     lines = jnp.dot(pick, acts_ref[...], preferred_element_type=F32).astype(BF)
-    for y in range(4):
-        part_ref[y] = jnp.dot(
-            lines, basis_ref[:, y * WIDE : (y + 1) * WIDE], preferred_element_type=F32
+    for k in range(4):
+        at = pl.multiple_of((where_ref[5] ^ k) * WIDE, WIDE)
+        out_refs[k][...] = jnp.dot(
+            lines, basis_ref[:, pl.ds(at, WIDE)], preferred_element_type=F32
         ).astype(BF)
 
 
-def join_kernel(near_ref, far_ref, parts_ref, out_ref):
-    total = parts_ref[0].astype(F32)
-    for y in range(1, 4):
-        total += parts_ref[y].astype(F32)
+def join_kernel(near_ref, far_ref, *refs):
+    parts, out_ref = refs[:4], refs[4]
+    total = parts[0][...].astype(F32)
+    for k in range(1, 4):
+        total += parts[k][...].astype(F32)
     total = total.astype(BF)
     for d in range(4):
         for w, ref in enumerate((near_ref, far_ref)):
@@ -80,25 +86,46 @@
     for f in range(8):
         at = jnp.where(mirrored == 1, 7 - f, f)
         far = (at // 4 != zh).astype(jnp.int32)
-        block = both_ref[at % 4, far][:, :FEAT]
-        for copy in range(4):
-            out_ref[copy, :, f * FEAT : (f + 1) * FEAT] = block
+        out_ref[:, f * FEAT : (f + 1) * FEAT] = both_ref[at % 4, far][:, :FEAT]
     sums = []
     for w in range(2):
         total = both_ref[0, w][:, FEAT:].astype(F32)
         for q in range(1, 4):
             total += both_ref[q, w][:, FEAT:].astype(F32)
         sums.append(total)
-    slot = lax.broadcasted_iota(jnp.int32, (VALID, 64), 0)
-    mask = (slot < where_ref[2]).astype(F32)
-    in_ref[...] = jnp.concatenate(sums + [mask], axis=1).astype(BF)
-
-
-def project_kernel(where_ref, lines_ref, own_ref, other_ref, out_ref):
-    core = where_ref[3]
-    for t in range(2):
-        total = across(lines_ref[2 * t + core], own_ref[...])
-        total += across(lines_ref[2 * t + 1 - core], other_ref[...])
+    half = VALID // 2
+    packed = jnp.concatenate([x[i : i + half] for i in (0, half) for x in sums], axis=1)
+    count = jnp.full((8, 128), where_ref[2], jnp.int32).astype(F32).astype(BF)
+    for copy in range(16):
+        in_ref[copy, :half] = packed.astype(BF)
+        in_ref[copy, half:] = count
+
+
+def merge_kernel(parts_ref, out_ref):
+    half = VALID // 2
+    for zhi in range(2):
+        for q in range(4):
+            at = zhi * 8 + q
+            total = parts_ref[at, :half].astype(F32) + parts_ref[at + 4, :half].astype(F32)
+            total = total.astype(BF)
+            out_ref[zhi, :half, q * 64 : q * 64 + 64] = total[:, :64]
+            out_ref[zhi, half:VALID, q * 64 : q * 64 + 64] = total[:, 64:]
+        for h in range(2):
+            out_ref[zhi, VALID:, h * 128 : h * 128 + 128] = parts_ref[zhi * 8, half:]
+
+
+def order_kernel(where_ref, own_ref, other_ref, one_ref, two_ref):
+    same = where_ref[3] == where_ref[6]
+    own, other = own_ref[...], other_ref[...]
+    one_ref[...] = jnp.where(same, own, other).T
+    two_ref[...] = jnp.where(same, other, own).T
+
+
+def project_kernel(where_ref, a_ref, b_ref, c_ref, d_ref, one_ref, two_ref, out_ref):
+    yh = where_ref[7]
+    for left, right, t in ((a_ref, b_ref, yh), (c_ref, d_ref, 1 - yh)):
+        total = jnp.dot(left[...], one_ref[...], preferred_element_type=F32)
+        total += jnp.dot(right[...], two_ref[...], preferred_element_type=F32)
         for h in range(2):
             out_ref[2 * t + h] = total[h * 72 : (h + 1) * 72].astype(BF)
 
@@ -116,18 +143,19 @@
         out_ref[x] = total
 
 
-def arrange_kernel(where_ref, own_ref, other_ref, own_mask_ref, other_mask_ref, out_ref, mask_ref):
-    core, zq = where_ref[3], where_ref[4]
+def arrange_kernel(where_ref, own_ref, other_ref, out_ref, mask_ref):
+    core = where_ref[3]
+    slot = lax.broadcasted_iota(jnp.int32, (VALID, 128), 0).astype(F32)
     for zhi in range(2):
         for c in range(2):
             mine = core == c
             g = zhi * 2 + c
             for y in range(4):
-                for q in range(4):
-                    at = y * WIDE + q * 64
-                    block = jnp.where(mine, own_ref[y, q ^ zq], other_ref[y, q ^ zq])
-                    out_ref[g, :, at : at + 64] = block[:, zhi * 64 : zhi * 64 + 64]
-            mask_ref[g] = jnp.where(mine, own_mask_ref[zhi], other_mask_ref[zhi])
+                k = y ^ where_ref[5]
+                block = jnp.where(mine, own_ref[k, zhi], other_ref[k, zhi])
+                out_ref[g, :, y * WIDE : (y + 1) * WIDE] = block[:VALID]
+            count = block[VALID : VALID + 1, :128].astype(F32)
+            mask_ref[g] = (slot < count).astype(F32).astype(BF)
 
 
 def square_kernel(where_ref, own_ref, other_ref, in_ref, mask_ref, eig_ref, left_ref):
@@ -172,54 +200,47 @@
     return jax.ShapeDtypeStruct(shape, dtype)
 
 
+def others(x, axis):
+    n = lax.axis_size(axis)
+    return [lax.ppermute(x, axis, [(i, i ^ k) for i in range(n)]) for k in range(1, n)]
+
+
 def per_device(acts, grads, basis_in, basis_out, lengths):
-    zhi, core, zh, zq = (lax.axis_index(a) for a in ("zhi", "core", "zh", "zq"))
-    where = jnp.stack([zh, (core != zhi).astype(jnp.int32), lengths[0, 0], core, zq])
-    lines, partial = call(
-        start_kernel,
-        [like(VALID, WIDE), like(4, VALID, WIDE)],
-        lengths,
-        grads,
-        acts,
-        basis_in,
-    )
+    zhi, core, y, zh, zq = (lax.axis_index(a) for a in ("zhi", "core", "y", "zh", "zq"))
+    crossed = (core != zhi).astype(jnp.int32)
+    where = jnp.stack([zh, crossed, lengths[0, 0], core, zq, y, y & 1, y >> 1])
+    lines = call(pack_kernel, like(VALID, WIDE), lengths, grads)
     near = lax.ppermute(lines, PLANE, to_basis(0))
     far = lax.ppermute(lines, PLANE, to_basis(4))
+    partial = call(inputs_kernel, [like(VALID, WIDE)] * 4, where, acts, basis_in)
+    partial = [partial[0]] + [
+        lax.ppermute(partial[k], "y", [(i, i ^ k) for i in range(4)]) for k in (1, 2, 3)
+    ]
     basis = basis_out[0].T
+    cols, rows = basis.shape
     other_basis = swap(basis, "core")
-    partial = exchange(partial, "y")
-    both = call(join_kernel, like(4, 2, VALID, WIDE), near, far, partial, scalars=0)
+    both = call(join_kernel, like(4, 2, VALID, WIDE), near, far, *partial, scalars=0)
     both = exchange(both, "zq")
-    lines, ins = call(sort_kernel, [like(4, VALID, 8 * FEAT), like(VALID, 128)], where, both)
-    lines = exchange(lines, "y")
-    sums = ins.astype(F32) + swap(ins, "zh").astype(F32)
-    ins = jnp.concatenate([sums[:, :64].astype(BF), ins[:, 64:]], axis=1)
-    pair = swap(ins, "zhi")
-    low = zhi == 0
-    pair = jnp.where(low, jnp.stack([ins, pair]), jnp.stack([pair, ins]))
-    masks = pair[:, :, 64:]
-    ins = jnp.concatenate([pair[0, :, :64], pair[1, :, :64]], axis=1)
-    ins, masks, other_masks, lines = lax.optimization_barrier(
-        (ins, masks, swap(masks, "core"), lines)
-    )
-    ins = jnp.stack([ins] + [lax.ppermute(ins, "zq", [(i, i ^ k) for i in range(4)]) for k in (1, 2, 3)])
-    cols = basis.shape[0]
-    part = call(project_kernel, like(4, 72, cols), where, lines, basis, other_basis)
+    lines, ins = call(sort_kernel, [like(VALID, 8 * FEAT), like(16, 80, 128)], where, both)
+    one, two = call(order_kernel, [like(rows, cols)] * 2, where, basis, other_basis)
+    lines = [lines] + others(lines, "y")
+    ins = exchange(ins, ("zhi", "zh", "zq"))
+    ins = call(merge_kernel, like(2, VALID + 8, WIDE), ins, scalars=0)
+    ins, lines, one, two = lax.optimization_barrier((ins, lines, one, two))
+    part = call(project_kernel, like(4, 72, cols), where, *lines, one, two)
     part = exchange(part, "x")
     part = call(sum_kernel, like(72, cols), part, scalars=0)
     part, ins = lax.optimization_barrier((part, ins))
-    ins = everywhere(ins, "y").reshape(4, 4, VALID, 128)
+    ins = jnp.stack([ins] + others(ins, "y"))
     part = call(spread_kernel, like(4, 72, cols), part, swap(part, "zhi"), scalars=0)
     part, ins = lax.optimization_barrier((part, ins))
     outs = exchange(part, "x").reshape(2, VALID, cols)
     ins, masks = call(
         arrange_kernel,
-        [like(4, VALID, 1024), like(4, VALID, 64)],
+        [like(4, VALID, 1024), like(4, VALID, 128)],
         where,
         ins,
         swap(ins, "core"),
-        masks,
-        other_masks,
     )
     return call(
         square_kernel,

time: 163 us -> 161 us (0.988)
  waiting for transfers between devices: 40.4 us -> 31.9 us
  blocking collectives: 10.8 us -> 19.1 us
  starting transfers between devices: 89.6 us -> 86 us
  Pallas kernels: 13.8 us -> 17.1 us
    ppermute x7 -> x4, waiting for transfers between devices: 26.6 us -> 2.89 us  [swap(): return lax.ppermute(x, axis, [(0, 1), (1, 0)])]
    all_to_all x5 -> x2, starting transfers between devices: 32.9 us -> 11.3 us  [exchange(): return lax.all_to_all(x, axis, 0, 0, tiled=True)]
    ppermute x3 -> x9, starting transfers between devices: 9.26 us -> 28.3 us  [the longest x6 18.7 us: others(): lax.ppermute(x, axis, [(i, i ^ k) for i in range(n)])]
    ppermute x3 -> x9, waiting for transfers between devices: 1.32 us -> 16.4 us  [the longest x6 14.3 us: others(): lax.ppermute(x, axis, [(i, i ^ k) for i in range(n)])]
    all_to_all x1 -> x2, blocking collectives: 10.8 us -> 19.1 us  [exchange(): return lax.all_to_all(x, axis, 0, 0, tiled=True)]
    pallas_call x8 -> x11, Pallas kernels: 13.8 us -> 17.1 us  [call(): pl.pallas_call(kernel, in_specs=[smem] * scalars + [vmem] * (len(args) -...]
    all_to_all x5 -> x2, waiting for transfers between devices: 10.1 us -> 12.5 us  [exchange(): return lax.all_to_all(x, axis, 0, 0, tiled=True)]
    ppermute x1, waiting for transfers between devices: 2.38 us -> 0.01 us  [per_device(): near = lax.ppermute(lines, PLANE, to_basis(0))]
  transfers between devices with their start and end apart: 17 -> 17, of which waited for: 7 -> 8; matrix products, arithmetic and copies ran while one was open for 0% -> 0% of each run, Pallas kernels for 1% -> 5%
where the time goes in v3:
time: 161 us; the launch traced here: 160 us
  starting transfers between devices  86 us (53%)
  waiting for transfers between devices  31.9 us (20%)
  blocking collectives  19.1 us (12%)
  Pallas kernels  17.1 us (11%)
  local copies, waits for them, and re-layouts  5.72 us (4%)
    ppermute x4, starting transfers between devices, swap(): return lax.ppermute(x, axis, [(0, 1), (1, 0)])  26 us
    all_to_all x2, blocking collectives, exchange(): return lax.all_to_all(x, axis, 0, 0, tiled=True)  19.1 us
    ppermute x6, starting transfers between devices, others(): lax.ppermute(x, axis, [(i, i ^ k) for i in range(n)])  18.7 us
    pallas_call x11, Pallas kernels, call(): pl.pallas_call(kernel, in_specs=[smem] * scalars + [vmem] * (len(args) -...  17.1 us
    ppermute x6, waiting for transfers between devices, others(): lax.ppermute(x, axis, [(i, i ^ k) for i in range(n)])  14.3 us
    ppermute x1, starting transfers between devices, per_device(): far = lax.ppermute(lines, PLANE, to_basis(4))  12.8 us
    all_to_all x2, waiting for transfers between devices, exchange(): return lax.all_to_all(x, axis, 0, 0, tiled=True)  12.5 us
    all_to_all x2, starting transfers between devices, exchange(): return lax.all_to_all(x, axis, 0, 0, tiled=True)  11.3 us
  transfers between devices with their start and end apart: 17, of which 8 were waited for; matrix products, arithmetic and copies ran while one was open for 0% of the time, Pallas kernels for 5%

profile of v3, /device:TPU:1, one launch (start us, length us, event | category | flops | bytes accessed | tf_op | source)
XLA Modules:
  0.0 160.0 jit_solution(16074729593865250113)
XLA Ops:
  2.3 12.8 %collective-permute-start.1 = (bf16[144,256]{1,0:T(8,128)(2,1)S(1)}, bf16[144,256]{1,0:T(8,128)(2,1)S(1)}, u32[]{:S(2)}, u32[]{:S(2)}) collective-permute-start(bf16[144,256]{1,0:T(8,128)(2,1)S(1)} %shard_map.55), channel_id=1, source_target_pairs={{0,4},{1,5},{2,6},{3,7},{4,0},{5,1},{6,2},{7,3},{8,12},{9,13},{10,... | collective-permute-start | bytes 221192 | tf_op jit(solution)/shard_map/ppermute | solution.py:214
  15.1 7.5 %collective-permute-start = (bf16[144,256]{1,0:T(8,128)(2,1)S(1)}, bf16[144,256]{1,0:T(8,128)(2,1)S(1)}, u32[]{:S(2)}, u32[]{:S(2)}) collective-permute-start(bf16[144,256]{1,0:T(8,128)(2,1)S(1)} %shard_map.55), channel_id=1, source_target_pairs={{0,0},{1,1},{2,2},{3,3},{4,4},{5,5},{6,6},{7,7},{8,8},{9,9},{10,10... | collective-permute-start | bytes 221192 | tf_op jit(solution)/shard_map/ppermute | solution.py:213
  26.2 3.2 %collective-permute-start.2 = (bf16[144,256]{1,0:T(8,128)(2,1)S(1)}, bf16[144,256]{1,0:T(8,128)(2,1)S(1)}, u32[]{:S(2)}, u32[]{:S(2)}) collective-permute-start(bf16[144,256]{1,0:T(8,128)(2,1)S(1)} %get-tuple-element.27), channel_id=1, source_target_pairs={{0,8},{8,0},{16,24},{24,16},{1,9},{9,1},{17,25},{25,17},{2,10},{10... | collective-permute-start | bytes 221192 | tf_op jit(solution)/shard_map/ppermute | solution.py:217
  29.4 2.2 %collective-permute-start.3 = (bf16[144,256]{1,0:T(8,128)(2,1)S(1)}, bf16[144,256]{1,0:T(8,128)(2,1)S(1)}, u32[]{:S(2)}, u32[]{:S(2)}) collective-permute-start(bf16[144,256]{1,0:T(8,128)(2,1)S(1)} %get-tuple-element.28), channel_id=1, source_target_pairs={{0,16},{8,24},{16,0},{24,8},{1,17},{9,25},{17,1},{25,9},{2,18},{10... | collective-permute-start | bytes 221192 | tf_op jit(solution)/shard_map/ppermute | solution.py:217
  31.7 4.1 %collective-permute-start.4 = (bf16[144,256]{1,0:T(8,128)(2,1)S(1)}, bf16[144,256]{1,0:T(8,128)(2,1)S(1)}, u32[]{:S(2)}, u32[]{:S(2)}) collective-permute-start(bf16[144,256]{1,0:T(8,128)(2,1)S(1)} %get-tuple-element.29), channel_id=1, source_target_pairs={{0,24},{8,16},{16,8},{24,0},{1,25},{9,17},{17,9},{25,1},{2,26},{10... | collective-permute-start | bytes 221192 | tf_op jit(solution)/shard_map/ppermute | solution.py:217
  39.0 5.6 %all-to-all-start = ((bf16[4,2,144,256]{3,2,1,0:T(8,128)(2,1)}), bf16[4,2,144,256]{3,2,1,0:T(8,128)(2,1)S(1)}, u32[]{:S(2)}, u32[]{:S(2)}) async-start(bf16[4,2,144,256]{3,2,1,0:T(8,128)(2,1)} %shard_map.57), calls=%async_computation | async-start | bytes 1179648 | tf_op jit(solution)/shard_map/all_to_all | solution.py:34
  44.6 3.8 %collective-permute-start.8 = (bf16[448,1792]{1,0:T(8,128)(2,1)S(1)}, bf16[448,1792]{1,0:T(8,128)(2,1)}, u32[]{:S(2)}, u32[]{:S(2)}) collective-permute-start(bf16[448,1792]{1,0:T(8,128)(2,1)S(1)} %bitcast.17), channel_id=1, source_target_pairs={{0,128},{128,0},{1,129},{129,1},{2,130},{130,2},{3,131},{131,3},{4... | collective-permute-start | bytes 4816904 | tf_op jit(solution)/shard_map/ppermute | solution.py:42
  48.4 11.6 %all-to-all-done.both_ref = bf16[4,2,144,256]{3,2,1,0:T(8,128)(2,1)S(1)} async-done(((bf16[4,2,144,256]{3,2,1,0:T(8,128)(2,1)}), bf16[4,2,144,256]{3,2,1,0:T(8,128)(2,1)S(1)}, u32[]{:S(2)}, u32[]{:S(2)}) %all-to-all-start) | async-done | bytes 589856 | tf_op jit(solution)/shard_map/all_to_all | solution.py:34
  61.7 5.7 %all-to-all-start.1 = ((bf16[16,80,128]{2,1,0:T(8,128)(2,1)}), bf16[16,80,128]{2,1,0:T(8,128)(2,1)}, u32[]{:S(2)}, u32[]{:S(2)}) async-start(bf16[16,80,128]{2,1,0:T(8,128)(2,1)} %get-tuple-element.30), calls=%async_computation.1 | async-start | bytes 655360 | tf_op jit(solution)/shard_map/all_to_all | solution.py:34
  67.5 5.1 %collective-permute-start.7 = (bf16[144,1792]{1,0:T(8,128)(2,1)}, bf16[144,1792]{1,0:T(8,128)(2,1)}, u32[]{:S(2)}, u32[]{:S(2)}) collective-permute-start(bf16[144,1792]{1,0:T(8,128)(2,1)} %get-tuple-element.34.a_ref), channel_id=1, source_target_pairs={{0,24},{8,16},{16,8},{24,0},{1,25},{9,17},{17,9},{25,1},{2,26},{10... | collective-permute-start | bytes 1548296 | tf_op jit(solution)/shard_map/ppermute | solution.py:205
  74.5 2.5 %collective-permute-start.5 = (bf16[144,1792]{1,0:T(8,128)(2,1)}, bf16[144,1792]{1,0:T(8,128)(2,1)}, u32[]{:S(2)}, u32[]{:S(2)}) collective-permute-start(bf16[144,1792]{1,0:T(8,128)(2,1)} %get-tuple-element.34.a_ref), channel_id=1, source_target_pairs={{0,8},{8,0},{16,24},{24,16},{1,9},{9,1},{17,25},{25,17},{2,10},{10... | collective-permute-start | bytes 1548296 | tf_op jit(solution)/shard_map/ppermute | solution.py:205
  77.0 3.8 %shard_map.60 = (bf16[1792,448]{1,0:T(8,128)(2,1)S(1)}, bf16[1792,448]{1,0:T(8,128)(2,1)}) custom-call(s32[8]{0:T(128)S(1)} %stack.50.where_ref, bf16[448,1792]{1,0:T(8,128)(2,1)S(1)} %bitcast.18, bf16[448,1792]{1,0:T(8,128)(2,1)} %collective-permute-done.8.other_ref), custom_call_target="tpu_custom_call" | custom-call | tf_op jit(solution)/shard_map/pallas_call | solution.py:188
  82.9 12.0 %collective-permute-done.7.d_ref = bf16[144,1792]{1,0:T(8,128)(2,1)} collective-permute-done((bf16[144,1792]{1,0:T(8,128)(2,1)}, bf16[144,1792]{1,0:T(8,128)(2,1)}, u32[]{:S(2)}, u32[]{:S(2)}) %collective-permute-start.7) | collective-permute-done | bytes 516128 | tf_op jit(solution)/shard_map/ppermute | solution.py:205
  94.9 2.3 %collective-permute-done.5.b_ref = bf16[144,1792]{1,0:T(8,128)(2,1)} collective-permute-done((bf16[144,1792]{1,0:T(8,128)(2,1)}, bf16[144,1792]{1,0:T(8,128)(2,1)}, u32[]{:S(2)}, u32[]{:S(2)}) %collective-permute-start.5) | collective-permute-done | bytes 516128 | tf_op jit(solution)/shard_map/ppermute | solution.py:205
  98.7 2.7 %shard_map.61 = bf16[4,72,448]{2,1,0:T(8,128)(2,1)S(1)} custom-call(s32[8]{0:T(128)S(1)} %stack.50.where_ref, bf16[144,1792]{1,0:T(8,128)(2,1)} %get-tuple-element.34.a_ref, bf16[144,1792]{1,0:T(8,128)(2,1)} %collective-permute-done.5.b_ref, bf16[144,1792]{1,0:T(8,128)(2,1)} %collective-permute-done.6.c_ref, bf16[144,1792]{1,0:T(8,128)(2,1)} %collective-permute-done.7.d_ref, ...), custom_call_target="tpu_custom_call" | custom-call | tf_op jit(solution)/shard_map/pallas_call | solution.py:188
  101.5 9.5 %all_to_all.20.parts_ref = bf16[4,72,448]{2,1,0:T(8,128)(2,1)S(1)} all-to-all(bf16[4,72,448]{2,1,0:T(8,128)(2,1)S(1)} %shard_map.61), channel_id=1, replica_groups=mesh['zhi'=2,'core'=2,'x'=4,'y'=4,'zh'=2,'zq'=4] {'x'}, dimensions={0} | all-to-all | bytes 516096 | tf_op jit(solution)/shard_map/all_to_all | solution.py:34
  111.0 4.7 %collective-permute-start.12 = (bf16[2,152,256]{2,1,0:T(8,128)(2,1)S(1)}, bf16[2,152,256]{2,1,0:T(8,128)(2,1)S(1)}, u32[]{:S(2)}, u32[]{:S(2)}) collective-permute-start(bf16[2,152,256]{2,1,0:T(8,128)(2,1)S(1)} %shard_map.59), channel_id=1, source_target_pairs={{0,24},{8,16},{16,8},{24,0},{1,25},{9,17},{17,9},{25,1},{2,26},{10... | collective-permute-start | bytes 466952 | tf_op jit(solution)/shard_map/ppermute | solution.py:205
  115.8 2.2 %collective-permute-start.11 = (bf16[2,152,256]{2,1,0:T(8,128)(2,1)S(1)}, bf16[2,152,256]{2,1,0:T(8,128)(2,1)S(1)}, u32[]{:S(2)}, u32[]{:S(2)}) collective-permute-start(bf16[2,152,256]{2,1,0:T(8,128)(2,1)S(1)} %shard_map.59), channel_id=1, source_target_pairs={{0,16},{8,24},{16,0},{24,8},{1,17},{9,25},{17,1},{25,9},{2,18},{10... | collective-permute-start | bytes 466952 | tf_op jit(solution)/shard_map/ppermute | solution.py:205
  120.2 11.6 %collective-permute-start.9 = (bf16[72,448]{1,0:T(8,128)(2,1)S(1)}, bf16[72,448]{1,0:T(8,128)(2,1)S(1)}, u32[]{:S(2)}, u32[]{:S(2)}) collective-permute-start(bf16[72,448]{1,0:T(8,128)(2,1)S(1)} %shard_map.62.one_ref), channel_id=1, source_target_pairs={{0,256},{256,0},{1,257},{257,1},{2,258},{258,2},{3,259},{259,3},{4... | collective-permute-start | bytes 193544 | tf_op jit(solution)/shard_map/ppermute | solution.py:42
  131.8 2.5 %collective-permute-done.9.two_ref = bf16[72,448]{1,0:T(8,128)(2,1)S(1)} collective-permute-done((bf16[72,448]{1,0:T(8,128)(2,1)S(1)}, bf16[72,448]{1,0:T(8,128)(2,1)S(1)}, u32[]{:S(2)}, u32[]{:S(2)}) %collective-permute-start.9) | collective-permute-done | bytes 64544 | tf_op jit(solution)/shard_map/ppermute | solution.py:42
  134.5 7.8 %collective-permute-start.14 = (bf16[4,2,152,256]{3,2,1,0:T(8,128)(2,1)S(1)}, bf16[4,2,152,256]{3,2,1,0:T(8,128)(2,1)S(1)}, u32[]{:S(2)}, u32[]{:S(2)}) collective-permute-start(bf16[4,2,152,256]{3,2,1,0:T(8,128)(2,1)S(1)} %pad_maximum_fusion.own_ref), channel_id=1, source_target_pairs={{0,128},{128,0},{1,129},{129,1},{2,130},{130,2},{3,131},{131,3},{4... | collective-permute-start | bytes 1867784 | tf_op jit(solution)/shard_map/ppermute | solution.py:42
  142.3 9.5 %all_to_all.21 = bf16[4,72,448]{2,1,0:T(8,128)(2,1)S(1)} all-to-all(bf16[4,72,448]{2,1,0:T(8,128)(2,1)S(1)} %shard_map.63), channel_id=1, replica_groups=mesh['zhi'=2,'core'=2,'x'=4,'y'=4,'zh'=2,'zq'=4] {'x'}, dimensions={0} | all-to-all | bytes 516096 | tf_op jit(solution)/shard_map/all_to_all | solution.py:34
  151.8 2.7 %collective-permute-start.13 = (bf16[2,144,448]{2,1,0:T(8,128)(2,1)S(1)}, bf16[2,144,448]{2,1,0:T(8,128)(2,1)S(1)}, u32[]{:S(2)}, u32[]{:S(2)}) collective-permute-start(bf16[2,144,448]{2,1,0:T(8,128)(2,1)S(1)} %bitcast.19), channel_id=1, source_target_pairs={{0,128},{128,0},{1,129},{129,1},{2,130},{130,2},{3,131},{131,3},{4... | collective-permute-start | bytes 774152 | tf_op jit(solution)/shard_map/ppermute | solution.py:42
  155.7 4.3 %shard_map.65 = f32[448,1024]{1,0:T(8,128)} custom-call(s32[8]{0:T(128)S(1)} %stack.50.where_ref, bf16[2,144,448]{2,1,0:T(8,128)(2,1)S(1)} %bitcast.20, bf16[2,144,448]{2,1,0:T(8,128)(2,1)S(1)} %collective-permute-done.13.other_ref, bf16[4,144,1024]{2,1,0:T(8,128)(2,1)S(1)} %get-tuple-element.45.in_ref, bf16[4,144,128]{2,1,0:T(8,128)(2,1)S(1)} %get-tuple-element.46.mask_ref), custom_call_target="tpu_custom_call" | custom-call | tf_op jit(solution)/shard_map/pallas_call | solution.py:188
  (37 shorter events, 19.7 us)
Async XLA Ops:
  0.0 0.9 copy-start.3
  0.9 0.7 copy-start.5
  1.5 43.0 %copy-start.1 = (bf16[1,1792,448]{1,2,0:T(8,128)(2,1)S(1)}, bf16[1,1792,448]{1,2,0:T(8,128)(2,1)}, u32[]{:S(2)}) copy-start(bf16[1,1792,448]{1,2,0:T(8,128)(2,1)} %param.8) | copy-start | bytes 4816900
  2.3 33.6 %collective-permute-start.1 = (bf16[144,256]{1,0:T(8,128)(2,1)S(1)}, bf16[144,256]{1,0:T(8,128)(2,1)S(1)}, u32[]{:S(2)}, u32[]{:S(2)}) collective-permute-start(bf16[144,256]{1,0:T(8,128)(2,1)S(1)} %shard_map.55), channel_id=1, source_target_pairs={{0,4},{1,5},{2,6},{3,7},{4,0},{5,1},{6,2},{7,3},{8,12},{9,13},{10,... | collective-permute-start | bytes 221192 | tf_op jit(solution)/shard_map/ppermute | solution.py:214
  15.1 20.8 %collective-permute-start = (bf16[144,256]{1,0:T(8,128)(2,1)S(1)}, bf16[144,256]{1,0:T(8,128)(2,1)S(1)}, u32[]{:S(2)}, u32[]{:S(2)}) collective-permute-start(bf16[144,256]{1,0:T(8,128)(2,1)S(1)} %shard_map.55), channel_id=1, source_target_pairs={{0,0},{1,1},{2,2},{3,3},{4,4},{5,5},{6,6},{7,7},{8,8},{9,9},{10,10... | collective-permute-start | bytes 221192 | tf_op jit(solution)/shard_map/ppermute | solution.py:213
  23.4 1.0 copy-start.2
  24.4 0.9 copy-start.4
  26.2 9.6 %collective-permute-start.2 = (bf16[144,256]{1,0:T(8,128)(2,1)S(1)}, bf16[144,256]{1,0:T(8,128)(2,1)S(1)}, u32[]{:S(2)}, u32[]{:S(2)}) collective-permute-start(bf16[144,256]{1,0:T(8,128)(2,1)S(1)} %get-tuple-element.27), channel_id=1, source_target_pairs={{0,8},{8,0},{16,24},{24,16},{1,9},{9,1},{17,25},{25,17},{2,10},{10... | collective-permute-start | bytes 221192 | tf_op jit(solution)/shard_map/ppermute | solution.py:217
  29.4 6.6 %collective-permute-start.3 = (bf16[144,256]{1,0:T(8,128)(2,1)S(1)}, bf16[144,256]{1,0:T(8,128)(2,1)S(1)}, u32[]{:S(2)}, u32[]{:S(2)}) collective-permute-start(bf16[144,256]{1,0:T(8,128)(2,1)S(1)} %get-tuple-element.28), channel_id=1, source_target_pairs={{0,16},{8,24},{16,0},{24,8},{1,17},{9,25},{17,1},{25,9},{2,18},{10... | collective-permute-start | bytes 221192 | tf_op jit(solution)/shard_map/ppermute | solution.py:217
  31.7 6.3 %collective-permute-start.4 = (bf16[144,256]{1,0:T(8,128)(2,1)S(1)}, bf16[144,256]{1,0:T(8,128)(2,1)S(1)}, u32[]{:S(2)}, u32[]{:S(2)}) collective-permute-start(bf16[144,256]{1,0:T(8,128)(2,1)S(1)} %get-tuple-element.29), channel_id=1, source_target_pairs={{0,24},{8,16},{16,8},{24,0},{1,25},{9,17},{17,9},{25,1},{2,26},{10... | collective-permute-start | bytes 221192 | tf_op jit(solution)/shard_map/ppermute | solution.py:217
  39.0 21.0 %all-to-all-start = ((bf16[4,2,144,256]{3,2,1,0:T(8,128)(2,1)}), bf16[4,2,144,256]{3,2,1,0:T(8,128)(2,1)S(1)}, u32[]{:S(2)}, u32[]{:S(2)}) async-start(bf16[4,2,144,256]{3,2,1,0:T(8,128)(2,1)} %shard_map.57), calls=%async_computation | async-start | bytes 1179648 | tf_op jit(solution)/shard_map/all_to_all | solution.py:34
  44.6 32.5 %collective-permute-start.8 = (bf16[448,1792]{1,0:T(8,128)(2,1)S(1)}, bf16[448,1792]{1,0:T(8,128)(2,1)}, u32[]{:S(2)}, u32[]{:S(2)}) collective-permute-start(bf16[448,1792]{1,0:T(8,128)(2,1)S(1)} %bitcast.17), channel_id=1, source_target_pairs={{0,128},{128,0},{1,129},{129,1},{2,130},{130,2},{3,131},{131,3},{4... | collective-permute-start | bytes 4816904 | tf_op jit(solution)/shard_map/ppermute | solution.py:42
  61.7 20.1 %all-to-all-start.1 = ((bf16[16,80,128]{2,1,0:T(8,128)(2,1)}), bf16[16,80,128]{2,1,0:T(8,128)(2,1)}, u32[]{:S(2)}, u32[]{:S(2)}) async-start(bf16[16,80,128]{2,1,0:T(8,128)(2,1)} %get-tuple-element.30), calls=%async_computation.1 | async-start | bytes 655360 | tf_op jit(solution)/shard_map/all_to_all | solution.py:34
  67.5 27.5 %collective-permute-start.7 = (bf16[144,1792]{1,0:T(8,128)(2,1)}, bf16[144,1792]{1,0:T(8,128)(2,1)}, u32[]{:S(2)}, u32[]{:S(2)}) collective-permute-start(bf16[144,1792]{1,0:T(8,128)(2,1)} %get-tuple-element.34.a_ref), channel_id=1, source_target_pairs={{0,24},{8,16},{16,8},{24,0},{1,25},{9,17},{17,9},{25,1},{2,26},{10... | collective-permute-start | bytes 1548296 | tf_op jit(solution)/shard_map/ppermute | solution.py:205
  72.6 22.3 %collective-permute-start.6 = (bf16[144,1792]{1,0:T(8,128)(2,1)}, bf16[144,1792]{1,0:T(8,128)(2,1)}, u32[]{:S(2)}, u32[]{:S(2)}) collective-permute-start(bf16[144,1792]{1,0:T(8,128)(2,1)} %get-tuple-element.34.a_ref), channel_id=1, source_target_pairs={{0,16},{8,24},{16,0},{24,8},{1,17},{9,25},{17,1},{25,9},{2,18},{10... | collective-permute-start | bytes 1548296 | tf_op jit(solution)/shard_map/ppermute | solution.py:205
  74.5 22.7 %collective-permute-start.5 = (bf16[144,1792]{1,0:T(8,128)(2,1)}, bf16[144,1792]{1,0:T(8,128)(2,1)}, u32[]{:S(2)}, u32[]{:S(2)}) collective-permute-start(bf16[144,1792]{1,0:T(8,128)(2,1)} %get-tuple-element.34.a_ref), channel_id=1, source_target_pairs={{0,8},{8,0},{16,24},{24,16},{1,9},{9,1},{17,25},{25,17},{2,10},{10... | collective-permute-start | bytes 1548296 | tf_op jit(solution)/shard_map/ppermute | solution.py:205
  97.2 1.5 copy-start
  111.0 23.3 %collective-permute-start.12 = (bf16[2,152,256]{2,1,0:T(8,128)(2,1)S(1)}, bf16[2,152,256]{2,1,0:T(8,128)(2,1)S(1)}, u32[]{:S(2)}, u32[]{:S(2)}) collective-permute-start(bf16[2,152,256]{2,1,0:T(8,128)(2,1)S(1)} %shard_map.59), channel_id=1, source_target_pairs={{0,24},{8,16},{16,8},{24,0},{1,25},{9,17},{17,9},{25,1},{2,26},{10... | collective-permute-start | bytes 466952 | tf_op jit(solution)/shard_map/ppermute | solution.py:205
  115.8 18.6 %collective-permute-start.11 = (bf16[2,152,256]{2,1,0:T(8,128)(2,1)S(1)}, bf16[2,152,256]{2,1,0:T(8,128)(2,1)S(1)}, u32[]{:S(2)}, u32[]{:S(2)}) collective-permute-start(bf16[2,152,256]{2,1,0:T(8,128)(2,1)S(1)} %shard_map.59), channel_id=1, source_target_pairs={{0,16},{8,24},{16,0},{24,8},{1,17},{9,25},{17,1},{25,9},{2,18},{10... | collective-permute-start | bytes 466952 | tf_op jit(solution)/shard_map/ppermute | solution.py:205
  118.0 16.3 %collective-permute-start.10 = (bf16[2,152,256]{2,1,0:T(8,128)(2,1)S(1)}, bf16[2,152,256]{2,1,0:T(8,128)(2,1)S(1)}, u32[]{:S(2)}, u32[]{:S(2)}) collective-permute-start(bf16[2,152,256]{2,1,0:T(8,128)(2,1)S(1)} %shard_map.59), channel_id=1, source_target_pairs={{0,8},{8,0},{16,24},{24,16},{1,9},{9,1},{17,25},{25,17},{2,10},{10... | collective-permute-start | bytes 466952 | tf_op jit(solution)/shard_map/ppermute | solution.py:205
  120.2 14.1 %collective-permute-start.9 = (bf16[72,448]{1,0:T(8,128)(2,1)S(1)}, bf16[72,448]{1,0:T(8,128)(2,1)S(1)}, u32[]{:S(2)}, u32[]{:S(2)}) collective-permute-start(bf16[72,448]{1,0:T(8,128)(2,1)S(1)} %shard_map.62.one_ref), channel_id=1, source_target_pairs={{0,256},{256,0},{1,257},{257,1},{2,258},{258,2},{3,259},{259,3},{4... | collective-permute-start | bytes 193544 | tf_op jit(solution)/shard_map/ppermute | solution.py:42
  134.5 20.1 %collective-permute-start.14 = (bf16[4,2,152,256]{3,2,1,0:T(8,128)(2,1)S(1)}, bf16[4,2,152,256]{3,2,1,0:T(8,128)(2,1)S(1)}, u32[]{:S(2)}, u32[]{:S(2)}) collective-permute-start(bf16[4,2,152,256]{3,2,1,0:T(8,128)(2,1)S(1)} %pad_maximum_fusion.own_ref), channel_id=1, source_target_pairs={{0,128},{128,0},{1,129},{129,1},{2,130},{130,2},{3,131},{131,3},{4... | collective-permute-start | bytes 1867784 | tf_op jit(solution)/shard_map/ppermute | solution.py:42
  151.8 3.9 %collective-permute-start.13 = (bf16[2,144,448]{2,1,0:T(8,128)(2,1)S(1)}, bf16[2,144,448]{2,1,0:T(8,128)(2,1)S(1)}, u32[]{:S(2)}, u32[]{:S(2)}) collective-permute-start(bf16[2,144,448]{2,1,0:T(8,128)(2,1)S(1)} %bitcast.19), channel_id=1, source_target_pairs={{0,128},{128,0},{1,129},{129,1},{2,130},{130,2},{3,131},{131,3},{4... | collective-permute-start | bytes 774152 | tf_op jit(solution)/shard_map/ppermute | solution.py:42

commit v4 on v3

--- a/solution.py
+++ b/solution.py
@@ -12,7 +12,7 @@
 BF = jnp.bfloat16
 F32 = jnp.float32
 PLANE = ("zhi", "core", "y", "zh", "zq")
-PARAMS = pltpu.CompilerParams(vmem_limit_bytes=48 << 20)
+PARAMS = pltpu.CompilerParams(vmem_limit_bytes=16 << 20)
 
 
 def to_basis(flip):
@@ -101,7 +101,8 @@
         in_ref[copy, half:] = count
 
 
-def merge_kernel(parts_ref, out_ref):
+def merge_kernel(parts_ref, spread_ref):
+    out_ref = spread_ref.at[0]
     half = VALID // 2
     for zhi in range(2):
         for q in range(4):
@@ -112,20 +113,16 @@
             out_ref[zhi, half:VALID, q * 64 : q * 64 + 64] = total[:, 64:]
         for h in range(2):
             out_ref[zhi, VALID:, h * 128 : h * 128 + 128] = parts_ref[zhi * 8, half:]
-
-
-def order_kernel(where_ref, own_ref, other_ref, one_ref, two_ref):
-    same = where_ref[3] == where_ref[6]
-    own, other = own_ref[...], other_ref[...]
-    one_ref[...] = jnp.where(same, own, other).T
-    two_ref[...] = jnp.where(same, other, own).T
-
-
-def project_kernel(where_ref, a_ref, b_ref, c_ref, d_ref, one_ref, two_ref, out_ref):
-    yh = where_ref[7]
-    for left, right, t in ((a_ref, b_ref, yh), (c_ref, d_ref, 1 - yh)):
-        total = jnp.dot(left[...], one_ref[...], preferred_element_type=F32)
-        total += jnp.dot(right[...], two_ref[...], preferred_element_type=F32)
+    for copy in range(1, 4):
+        spread_ref[copy] = out_ref[...]
+
+
+def project_kernel(where_ref, a_ref, b_ref, c_ref, d_ref, own_ref, other_ref, out_ref):
+    yh, same = where_ref[7], where_ref[3] == where_ref[6]
+    for left_ref, right_ref, t in ((a_ref, b_ref, yh), (c_ref, d_ref, 1 - yh)):
+        left, right = left_ref[...], right_ref[...]
+        total = across(jnp.where(same, left, right), own_ref[...])
+        total += across(jnp.where(same, right, left), other_ref[...])
         for h in range(2):
             out_ref[2 * t + h] = total[h * 72 : (h + 1) * 72].astype(BF)
 
@@ -151,8 +148,7 @@
             mine = core == c
             g = zhi * 2 + c
             for y in range(4):
-                k = y ^ where_ref[5]
-                block = jnp.where(mine, own_ref[k, zhi], other_ref[k, zhi])
+                block = jnp.where(mine, own_ref[y, zhi], other_ref[y, zhi])
                 out_ref[g, :, y * WIDE : (y + 1) * WIDE] = block[:VALID]
             count = block[VALID : VALID + 1, :128].astype(F32)
             mask_ref[g] = (slot < count).astype(F32).astype(BF)
@@ -217,30 +213,30 @@
         lax.ppermute(partial[k], "y", [(i, i ^ k) for i in range(4)]) for k in (1, 2, 3)
     ]
     basis = basis_out[0].T
-    cols, rows = basis.shape
+    cols = basis.shape[0]
     other_basis = swap(basis, "core")
     both = call(join_kernel, like(4, 2, VALID, WIDE), near, far, *partial, scalars=0)
     both = exchange(both, "zq")
     lines, ins = call(sort_kernel, [like(VALID, 8 * FEAT), like(16, 80, 128)], where, both)
-    one, two = call(order_kernel, [like(rows, cols)] * 2, where, basis, other_basis)
     lines = [lines] + others(lines, "y")
     ins = exchange(ins, ("zhi", "zh", "zq"))
-    ins = call(merge_kernel, like(2, VALID + 8, WIDE), ins, scalars=0)
-    ins, lines, one, two = lax.optimization_barrier((ins, lines, one, two))
-    part = call(project_kernel, like(4, 72, cols), where, *lines, one, two)
+    ins = call(merge_kernel, like(4, 2, VALID + 8, WIDE), ins, scalars=0)
+    ins = exchange(ins, "y")
+    ins, lines = lax.optimization_barrier((ins, lines))
+    part = call(project_kernel, like(4, 72, cols), where, *lines, basis, other_basis)
     part = exchange(part, "x")
     part = call(sum_kernel, like(72, cols), part, scalars=0)
     part, ins = lax.optimization_barrier((part, ins))
-    ins = jnp.stack([ins] + others(ins, "y"))
+    other_ins = swap(ins, "core")
     part = call(spread_kernel, like(4, 72, cols), part, swap(part, "zhi"), scalars=0)
-    part, ins = lax.optimization_barrier((part, ins))
+    part, ins, other_ins = lax.optimization_barrier((part, ins, other_ins))
     outs = exchange(part, "x").reshape(2, VALID, cols)
     ins, masks = call(
         arrange_kernel,
         [like(4, VALID, 1024), like(4, VALID, 128)],
         where,
         ins,
-        swap(ins, "core"),
+        other_ins,
     )
     return call(
         square_kernel,

time: 161 us -> 162 us (level)
  blocking collectives: 19.1 us -> 37.9 us
  starting transfers between devices: 86 us -> 76.7 us
  Pallas kernels: 17.1 us -> 13.2 us
  waiting for transfers between devices: 31.9 us -> 29.3 us
    all_to_all x2 -> x3, blocking collectives: 19.1 us -> 37.9 us  [exchange(): return lax.all_to_all(x, axis, 0, 0, tiled=True)]
    ppermute x6 -> x3, starting transfers between devices: 18.7 us -> 8.98 us  [others(): lax.ppermute(x, axis, [(i, i ^ k) for i in range(n)])]
    pallas_call x11 -> x10, Pallas kernels: 17.1 us -> 13.2 us  [call(): pl.pallas_call(kernel, in_specs=[smem] * scalars + [vmem] * (len(args) -...]
    ppermute x6 -> x3, waiting for transfers between devices: 14.3 us -> 12.1 us  [others(): lax.ppermute(x, axis, [(i, i ^ k) for i in range(n)])]
    unnamed x12 -> x10, local copies, waits for them, and re-layouts: 4.99 us -> 3.49 us
  transfers between devices with their start and end apart: 17 -> 14, of which waited for: 8 -> 8; matrix products, arithmetic and copies ran while one was open for 0% -> 0% of each run, Pallas kernels for 5% -> 2%
where the time goes in v4:
time: 162 us
  starting transfers between devices  76.7 us (47%)
  blocking collectives  37.9 us (23%)
  waiting for transfers between devices  29.3 us (18%)
  Pallas kernels  13.2 us (8%)
  local copies, waits for them, and re-layouts  4.22 us (3%)
    all_to_all x3, blocking collectives, exchange(): return lax.all_to_all(x, axis, 0, 0, tiled=True)  37.9 us
    ppermute x4, starting transfers between devices, swap(): return lax.ppermute(x, axis, [(0, 1), (1, 0)])  27.4 us
    pallas_call x10, Pallas kernels, call(): pl.pallas_call(kernel, in_specs=[smem] * scalars + [vmem] * (len(args) -...  13.2 us
    ppermute x1, starting transfers between devices, per_device(): far = lax.ppermute(lines, PLANE, to_basis(4))  12.8 us
    all_to_all x2, waiting for transfers between devices, exchange(): return lax.all_to_all(x, axis, 0, 0, tiled=True)  12.1 us
    ppermute x3, waiting for transfers between devices, others(): lax.ppermute(x, axis, [(i, i ^ k) for i in range(n)])  12.1 us
    all_to_all x2, starting transfers between devices, exchange(): return lax.all_to_all(x, axis, 0, 0, tiled=True)  10.4 us
    ppermute x3, starting transfers between devices, per_device(): lax.ppermute(partial[k], 'y', [(i, i ^ k) for i in range(4)])  9.58 us
  transfers between devices with their start and end apart: 14, of which 8 were waited for; matrix products, arithmetic and copies ran while one was open for 0% of the time, Pallas kernels for 2%

profile of v4, /device:TPU:1, one launch (start us, length us, event | category | flops | bytes accessed | tf_op | source)
XLA Modules:
  0.0 161.5 jit_solution(13990984604042575121)
XLA Ops:
  2.3 12.8 %collective-permute-start.1 = (bf16[144,256]{1,0:T(8,128)(2,1)S(1)}, bf16[144,256]{1,0:T(8,128)(2,1)S(1)}, u32[]{:S(2)}, u32[]{:S(2)}) collective-permute-start(bf16[144,256]{1,0:T(8,128)(2,1)S(1)} %shard_map.55), channel_id=1, source_target_pairs={{0,4},{1,5},{2,6},{3,7},{4,0},{5,1},{6,2},{7,3},{8,12},{9,13},{10,... | collective-permute-start | bytes 221192 | tf_op jit(solution)/shard_map/ppermute | solution.py:210
  15.1 7.5 %collective-permute-start = (bf16[144,256]{1,0:T(8,128)(2,1)S(1)}, bf16[144,256]{1,0:T(8,128)(2,1)S(1)}, u32[]{:S(2)}, u32[]{:S(2)}) collective-permute-start(bf16[144,256]{1,0:T(8,128)(2,1)S(1)} %shard_map.55), channel_id=1, source_target_pairs={{0,0},{1,1},{2,2},{3,3},{4,4},{5,5},{6,6},{7,7},{8,8},{9,9},{10,10... | collective-permute-start | bytes 221192 | tf_op jit(solution)/shard_map/ppermute | solution.py:209
  26.2 3.2 %collective-permute-start.2 = (bf16[144,256]{1,0:T(8,128)(2,1)S(1)}, bf16[144,256]{1,0:T(8,128)(2,1)S(1)}, u32[]{:S(2)}, u32[]{:S(2)}) collective-permute-start(bf16[144,256]{1,0:T(8,128)(2,1)S(1)} %get-tuple-element.24), channel_id=1, source_target_pairs={{0,8},{8,0},{16,24},{24,16},{1,9},{9,1},{17,25},{25,17},{2,10},{10... | collective-permute-start | bytes 221192 | tf_op jit(solution)/shard_map/ppermute | solution.py:213
  29.4 2.2 %collective-permute-start.3 = (bf16[144,256]{1,0:T(8,128)(2,1)S(1)}, bf16[144,256]{1,0:T(8,128)(2,1)S(1)}, u32[]{:S(2)}, u32[]{:S(2)}) collective-permute-start(bf16[144,256]{1,0:T(8,128)(2,1)S(1)} %get-tuple-element.25), channel_id=1, source_target_pairs={{0,16},{8,24},{16,0},{24,8},{1,17},{9,25},{17,1},{25,9},{2,18},{10... | collective-permute-start | bytes 221192 | tf_op jit(solution)/shard_map/ppermute | solution.py:213
  31.7 4.1 %collective-permute-start.4 = (bf16[144,256]{1,0:T(8,128)(2,1)S(1)}, bf16[144,256]{1,0:T(8,128)(2,1)S(1)}, u32[]{:S(2)}, u32[]{:S(2)}) collective-permute-start(bf16[144,256]{1,0:T(8,128)(2,1)S(1)} %get-tuple-element.26), channel_id=1, source_target_pairs={{0,24},{8,16},{16,8},{24,0},{1,25},{9,17},{17,9},{25,1},{2,26},{10... | collective-permute-start | bytes 221192 | tf_op jit(solution)/shard_map/ppermute | solution.py:213
  36.0 2.0 %collective-permute-done.4.refs_3_ = bf16[144,256]{1,0:T(8,128)(2,1)S(1)} collective-permute-done((bf16[144,256]{1,0:T(8,128)(2,1)S(1)}, bf16[144,256]{1,0:T(8,128)(2,1)S(1)}, u32[]{:S(2)}, u32[]{:S(2)}) %collective-permute-start.4) | collective-permute-done | bytes 73760 | tf_op jit(solution)/shard_map/ppermute | solution.py:213
  38.2 20.3 %all_to_all.25.both_ref = bf16[4,2,144,256]{3,2,1,0:T(8,128)(2,1)S(1)} all-to-all(bf16[4,2,144,256]{3,2,1,0:T(8,128)(2,1)S(1)} %shard_map.57), channel_id=1, replica_groups=mesh['zhi'=2,'core'=2,'x'=4,'y'=4,'zh'=2,'zq'=4] {'zq'}, dimensions={0} | all-to-all | bytes 1179648 | tf_op jit(solution)/shard_map/all_to_all | solution.py:34
  60.1 5.8 %all-to-all-start.1 = ((bf16[16,80,128]{2,1,0:T(8,128)(2,1)}), bf16[16,80,128]{2,1,0:T(8,128)(2,1)S(1)}, u32[]{:S(2)}, u32[]{:S(2)}) async-start(bf16[16,80,128]{2,1,0:T(8,128)(2,1)} %get-tuple-element.27), calls=%async_computation.1 | async-start | bytes 655360 | tf_op jit(solution)/shard_map/all_to_all | solution.py:34
  66.0 2.9 %collective-permute-start.8 = (bf16[448,1792]{1,0:T(8,128)(2,1)S(1)}, bf16[448,1792]{1,0:T(8,128)(2,1)}, u32[]{:S(2)}, u32[]{:S(2)}) collective-permute-start(bf16[448,1792]{1,0:T(8,128)(2,1)S(1)} %bitcast.13), channel_id=1, source_target_pairs={{0,128},{128,0},{1,129},{129,1},{2,130},{130,2},{3,131},{131,3},{4... | collective-permute-start | bytes 4816904 | tf_op jit(solution)/shard_map/ppermute | solution.py:42
  68.9 4.5 %collective-permute-start.7 = (bf16[144,1792]{1,0:T(8,128)(2,1)S(1)}, bf16[144,1792]{1,0:T(8,128)(2,1)S(1)}, u32[]{:S(2)}, u32[]{:S(2)}) collective-permute-start(bf16[144,1792]{1,0:T(8,128)(2,1)S(1)} %get-tuple-element.29.a_ref), channel_id=1, source_target_pairs={{0,24},{8,16},{16,8},{24,0},{1,25},{9,17},{17,9},{25,1},{2,26},{10... | collective-permute-start | bytes 1548296 | tf_op jit(solution)/shard_map/ppermute | solution.py:201
  75.3 2.6 %collective-permute-start.5 = (bf16[144,1792]{1,0:T(8,128)(2,1)S(1)}, bf16[144,1792]{1,0:T(8,128)(2,1)}, u32[]{:S(2)}, u32[]{:S(2)}) collective-permute-start(bf16[144,1792]{1,0:T(8,128)(2,1)S(1)} %get-tuple-element.29.a_ref), channel_id=1, source_target_pairs={{0,8},{8,0},{16,24},{24,16},{1,9},{9,1},{17,25},{25,17},{2,10},{10... | collective-permute-start | bytes 1548296 | tf_op jit(solution)/shard_map/ppermute | solution.py:201
  77.9 3.3 %all-to-all-done.1.parts_ref = bf16[16,80,128]{2,1,0:T(8,128)(2,1)S(1)} async-done(((bf16[16,80,128]{2,1,0:T(8,128)(2,1)}), bf16[16,80,128]{2,1,0:T(8,128)(2,1)S(1)}, u32[]{:S(2)}, u32[]{:S(2)}) %all-to-all-start.1) | async-done | bytes 327712 | tf_op jit(solution)/shard_map/all_to_all | solution.py:34
  82.2 4.5 %all-to-all-start.2 = ((bf16[4,2,152,256]{3,2,1,0:T(8,128)(2,1)}), bf16[4,2,152,256]{3,2,1,0:T(8,128)(2,1)S(1)}, u32[]{:S(2)}, u32[]{:S(2)}) async-start(bf16[4,2,152,256]{3,2,1,0:T(8,128)(2,1)} %shard_map.59), calls=%async_computation.2 | async-start | bytes 1245184 | tf_op jit(solution)/shard_map/all_to_all | solution.py:34
  86.7 9.7 %collective-permute-done.7.d_ref = bf16[144,1792]{1,0:T(8,128)(2,1)S(1)} collective-permute-done((bf16[144,1792]{1,0:T(8,128)(2,1)S(1)}, bf16[144,1792]{1,0:T(8,128)(2,1)S(1)}, u32[]{:S(2)}, u32[]{:S(2)}) %collective-permute-start.7) | collective-permute-done | bytes 516128 | tf_op jit(solution)/shard_map/ppermute | solution.py:201
  96.4 2.3 %collective-permute-done.5.b_ref = bf16[144,1792]{1,0:T(8,128)(2,1)} collective-permute-done((bf16[144,1792]{1,0:T(8,128)(2,1)S(1)}, bf16[144,1792]{1,0:T(8,128)(2,1)}, u32[]{:S(2)}, u32[]{:S(2)}) %collective-permute-start.5) | collective-permute-done | bytes 516128 | tf_op jit(solution)/shard_map/ppermute | solution.py:201
  98.8 8.8 %all-to-all-done.2.own_ref = bf16[4,2,152,256]{3,2,1,0:T(8,128)(2,1)S(1)} async-done(((bf16[4,2,152,256]{3,2,1,0:T(8,128)(2,1)}), bf16[4,2,152,256]{3,2,1,0:T(8,128)(2,1)S(1)}, u32[]{:S(2)}, u32[]{:S(2)}) %all-to-all-start.2) | async-done | bytes 622624 | tf_op jit(solution)/shard_map/all_to_all | solution.py:34
  107.6 3.7 %shard_map.60 = bf16[4,72,448]{2,1,0:T(8,128)(2,1)S(1)} custom-call(s32[8]{0:T(128)S(1)} %stack.35.where_ref, bf16[144,1792]{1,0:T(8,128)(2,1)S(1)} %get-tuple-element.29.a_ref, bf16[144,1792]{1,0:T(8,128)(2,1)} %collective-permute-done.5.b_ref, bf16[144,1792]{1,0:T(8,128)(2,1)} %collective-permute-done.6.c_ref, ...), custom_call_target="tpu_custom_call" | custom-call | tf_op jit(solution)/shard_map/pallas_call | solution.py:184
  111.3 9.5 %all_to_all.26.parts_ref = bf16[4,72,448]{2,1,0:T(8,128)(2,1)S(1)} all-to-all(bf16[4,72,448]{2,1,0:T(8,128)(2,1)S(1)} %shard_map.60), channel_id=1, replica_groups=mesh['zhi'=2,'core'=2,'x'=4,'y'=4,'zh'=2,'zq'=4] {'x'}, dimensions={0} | all-to-all | bytes 516096 | tf_op jit(solution)/shard_map/all_to_all | solution.py:34
  120.9 4.4 %collective-permute-start.10 = (bf16[4,2,152,256]{3,2,1,0:T(8,128)(2,1)S(1)}, bf16[4,2,152,256]{3,2,1,0:T(8,128)(2,1)S(1)}, u32[]{:S(2)}, u32[]{:S(2)}) collective-permute-start(bf16[4,2,152,256]{3,2,1,0:T(8,128)(2,1)S(1)} %all-to-all-done.2.own_ref), channel_id=1, source_target_pairs={{0,128},{128,0},{1,129},{129,1},{2,130},{130,2},{3,131},{131,3},{4... | collective-permute-start | bytes 1867784 | tf_op jit(solution)/shard_map/ppermute | solution.py:42
  125.4 12.3 %collective-permute-start.9 = (bf16[72,448]{1,0:T(8,128)(2,1)S(1)}, bf16[72,448]{1,0:T(8,128)(2,1)S(1)}, u32[]{:S(2)}, u32[]{:S(2)}) collective-permute-start(bf16[72,448]{1,0:T(8,128)(2,1)S(1)} %shard_map.61.one_ref), channel_id=1, source_target_pairs={{0,256},{256,0},{1,257},{257,1},{2,258},{258,2},{3,259},{259,3},{4... | collective-permute-start | bytes 193544 | tf_op jit(solution)/shard_map/ppermute | solution.py:42
  137.6 2.5 %collective-permute-done.9.two_ref = bf16[72,448]{1,0:T(8,128)(2,1)S(1)} collective-permute-done((bf16[72,448]{1,0:T(8,128)(2,1)S(1)}, bf16[72,448]{1,0:T(8,128)(2,1)S(1)}, u32[]{:S(2)}, u32[]{:S(2)}) %collective-permute-start.9) | collective-permute-done | bytes 64544 | tf_op jit(solution)/shard_map/ppermute | solution.py:42
  140.2 8.1 %all_to_all.27 = bf16[4,72,448]{2,1,0:T(8,128)(2,1)S(1)} all-to-all(bf16[4,72,448]{2,1,0:T(8,128)(2,1)S(1)} %shard_map.62), channel_id=1, replica_groups=mesh['zhi'=2,'core'=2,'x'=4,'y'=4,'zh'=2,'zq'=4] {'x'}, dimensions={0} | all-to-all | bytes 516096 | tf_op jit(solution)/shard_map/all_to_all | solution.py:34
  148.3 7.7 %collective-permute-start.11 = (bf16[2,144,448]{2,1,0:T(8,128)(2,1)S(1)}, bf16[2,144,448]{2,1,0:T(8,128)(2,1)S(1)}, u32[]{:S(2)}, u32[]{:S(2)}) collective-permute-start(bf16[2,144,448]{2,1,0:T(8,128)(2,1)S(1)} %bitcast.15), channel_id=1, source_target_pairs={{0,128},{128,0},{1,129},{129,1},{2,130},{130,2},{3,131},{131,3},{4... | collective-permute-start | bytes 774152 | tf_op jit(solution)/shard_map/ppermute | solution.py:42
  157.2 4.3 %shard_map.64 = f32[448,1024]{1,0:T(8,128)} custom-call(s32[8]{0:T(128)S(1)} %stack.35.where_ref, bf16[2,144,448]{2,1,0:T(8,128)(2,1)S(1)} %bitcast.16, bf16[2,144,448]{2,1,0:T(8,128)(2,1)S(1)} %collective-permute-done.11.other_ref, bf16[4,144,1024]{2,1,0:T(8,128)(2,1)S(1)} %get-tuple-element.39.in_ref, bf16[4,144,128]{2,1,0:T(8,128)(2,1)S(1)} %get-tuple-element.40.mask_ref), custom_call_target="tpu_custom_call" | custom-call | tf_op jit(solution)/shard_map/pallas_call | solution.py:184
  (28 shorter events, 12.0 us)
Async XLA Ops:
  0.0 0.9 copy-start.2
  0.9 0.7 copy-start.4
  2.3 33.6 %collective-permute-start.1 = (bf16[144,256]{1,0:T(8,128)(2,1)S(1)}, bf16[144,256]{1,0:T(8,128)(2,1)S(1)}, u32[]{:S(2)}, u32[]{:S(2)}) collective-permute-start(bf16[144,256]{1,0:T(8,128)(2,1)S(1)} %shard_map.55), channel_id=1, source_target_pairs={{0,4},{1,5},{2,6},{3,7},{4,0},{5,1},{6,2},{7,3},{8,12},{9,13},{10,... | collective-permute-start | bytes 221192 | tf_op jit(solution)/shard_map/ppermute | solution.py:210
  15.1 20.8 %collective-permute-start = (bf16[144,256]{1,0:T(8,128)(2,1)S(1)}, bf16[144,256]{1,0:T(8,128)(2,1)S(1)}, u32[]{:S(2)}, u32[]{:S(2)}) collective-permute-start(bf16[144,256]{1,0:T(8,128)(2,1)S(1)} %shard_map.55), channel_id=1, source_target_pairs={{0,0},{1,1},{2,2},{3,3},{4,4},{5,5},{6,6},{7,7},{8,8},{9,9},{10,10... | collective-permute-start | bytes 221192 | tf_op jit(solution)/shard_map/ppermute | solution.py:209
  23.4 1.0 copy-start.1
  24.4 0.9 copy-start.3
  26.2 9.6 %collective-permute-start.2 = (bf16[144,256]{1,0:T(8,128)(2,1)S(1)}, bf16[144,256]{1,0:T(8,128)(2,1)S(1)}, u32[]{:S(2)}, u32[]{:S(2)}) collective-permute-start(bf16[144,256]{1,0:T(8,128)(2,1)S(1)} %get-tuple-element.24), channel_id=1, source_target_pairs={{0,8},{8,0},{16,24},{24,16},{1,9},{9,1},{17,25},{25,17},{2,10},{10... | collective-permute-start | bytes 221192 | tf_op jit(solution)/shard_map/ppermute | solution.py:213
  29.4 6.6 %collective-permute-start.3 = (bf16[144,256]{1,0:T(8,128)(2,1)S(1)}, bf16[144,256]{1,0:T(8,128)(2,1)S(1)}, u32[]{:S(2)}, u32[]{:S(2)}) collective-permute-start(bf16[144,256]{1,0:T(8,128)(2,1)S(1)} %get-tuple-element.25), channel_id=1, source_target_pairs={{0,16},{8,24},{16,0},{24,8},{1,17},{9,25},{17,1},{25,9},{2,18},{10... | collective-permute-start | bytes 221192 | tf_op jit(solution)/shard_map/ppermute | solution.py:213
  31.7 6.3 %collective-permute-start.4 = (bf16[144,256]{1,0:T(8,128)(2,1)S(1)}, bf16[144,256]{1,0:T(8,128)(2,1)S(1)}, u32[]{:S(2)}, u32[]{:S(2)}) collective-permute-start(bf16[144,256]{1,0:T(8,128)(2,1)S(1)} %get-tuple-element.26), channel_id=1, source_target_pairs={{0,24},{8,16},{16,8},{24,0},{1,25},{9,17},{17,9},{25,1},{2,26},{10... | collective-permute-start | bytes 221192 | tf_op jit(solution)/shard_map/ppermute | solution.py:213
  38.0 28.0 %copy-start = (bf16[1,1792,448]{1,2,0:T(8,128)(2,1)S(1)}, bf16[1,1792,448]{1,2,0:T(8,128)(2,1)}, u32[]{:S(2)}) copy-start(bf16[1,1792,448]{1,2,0:T(8,128)(2,1)} %param.8) | copy-start | bytes 4816900
  60.1 21.1 %all-to-all-start.1 = ((bf16[16,80,128]{2,1,0:T(8,128)(2,1)}), bf16[16,80,128]{2,1,0:T(8,128)(2,1)S(1)}, u32[]{:S(2)}, u32[]{:S(2)}) async-start(bf16[16,80,128]{2,1,0:T(8,128)(2,1)} %get-tuple-element.27), calls=%async_computation.1 | async-start | bytes 655360 | tf_op jit(solution)/shard_map/all_to_all | solution.py:34
  66.0 41.6 %collective-permute-start.8 = (bf16[448,1792]{1,0:T(8,128)(2,1)S(1)}, bf16[448,1792]{1,0:T(8,128)(2,1)}, u32[]{:S(2)}, u32[]{:S(2)}) collective-permute-start(bf16[448,1792]{1,0:T(8,128)(2,1)S(1)} %bitcast.13), channel_id=1, source_target_pairs={{0,128},{128,0},{1,129},{129,1},{2,130},{130,2},{3,131},{131,3},{4... | collective-permute-start | bytes 4816904 | tf_op jit(solution)/shard_map/ppermute | solution.py:42
  68.9 27.5 %collective-permute-start.7 = (bf16[144,1792]{1,0:T(8,128)(2,1)S(1)}, bf16[144,1792]{1,0:T(8,128)(2,1)S(1)}, u32[]{:S(2)}, u32[]{:S(2)}) collective-permute-start(bf16[144,1792]{1,0:T(8,128)(2,1)S(1)} %get-tuple-element.29.a_ref), channel_id=1, source_target_pairs={{0,24},{8,16},{16,8},{24,0},{1,25},{9,17},{17,9},{25,1},{2,26},{10... | collective-permute-start | bytes 1548296 | tf_op jit(solution)/shard_map/ppermute | solution.py:201
  73.4 23.1 %collective-permute-start.6 = (bf16[144,1792]{1,0:T(8,128)(2,1)S(1)}, bf16[144,1792]{1,0:T(8,128)(2,1)}, u32[]{:S(2)}, u32[]{:S(2)}) collective-permute-start(bf16[144,1792]{1,0:T(8,128)(2,1)S(1)} %get-tuple-element.29.a_ref), channel_id=1, source_target_pairs={{0,16},{8,24},{16,0},{24,8},{1,17},{9,25},{17,1},{25,9},{2,18},{10... | collective-permute-start | bytes 1548296 | tf_op jit(solution)/shard_map/ppermute | solution.py:201
  75.3 23.5 %collective-permute-start.5 = (bf16[144,1792]{1,0:T(8,128)(2,1)S(1)}, bf16[144,1792]{1,0:T(8,128)(2,1)}, u32[]{:S(2)}, u32[]{:S(2)}) collective-permute-start(bf16[144,1792]{1,0:T(8,128)(2,1)S(1)} %get-tuple-element.29.a_ref), channel_id=1, source_target_pairs={{0,8},{8,0},{16,24},{24,16},{1,9},{9,1},{17,25},{25,17},{2,10},{10... | collective-permute-start | bytes 1548296 | tf_op jit(solution)/shard_map/ppermute | solution.py:201
  82.2 25.4 %all-to-all-start.2 = ((bf16[4,2,152,256]{3,2,1,0:T(8,128)(2,1)}), bf16[4,2,152,256]{3,2,1,0:T(8,128)(2,1)S(1)}, u32[]{:S(2)}, u32[]{:S(2)}) async-start(bf16[4,2,152,256]{3,2,1,0:T(8,128)(2,1)} %shard_map.59), calls=%async_computation.2 | async-start | bytes 1245184 | tf_op jit(solution)/shard_map/all_to_all | solution.py:34
  120.9 19.3 %collective-permute-start.10 = (bf16[4,2,152,256]{3,2,1,0:T(8,128)(2,1)S(1)}, bf16[4,2,152,256]{3,2,1,0:T(8,128)(2,1)S(1)}, u32[]{:S(2)}, u32[]{:S(2)}) collective-permute-start(bf16[4,2,152,256]{3,2,1,0:T(8,128)(2,1)S(1)} %all-to-all-done.2.own_ref), channel_id=1, source_target_pairs={{0,128},{128,0},{1,129},{129,1},{2,130},{130,2},{3,131},{131,3},{4... | collective-permute-start | bytes 1867784 | tf_op jit(solution)/shard_map/ppermute | solution.py:42
  125.4 14.8 %collective-permute-start.9 = (bf16[72,448]{1,0:T(8,128)(2,1)S(1)}, bf16[72,448]{1,0:T(8,128)(2,1)S(1)}, u32[]{:S(2)}, u32[]{:S(2)}) collective-permute-start(bf16[72,448]{1,0:T(8,128)(2,1)S(1)} %shard_map.61.one_ref), channel_id=1, source_target_pairs={{0,256},{256,0},{1,257},{257,1},{2,258},{258,2},{3,259},{259,3},{4... | collective-permute-start | bytes 193544 | tf_op jit(solution)/shard_map/ppermute | solution.py:42
  148.3 8.9 %collective-permute-start.11 = (bf16[2,144,448]{2,1,0:T(8,128)(2,1)S(1)}, bf16[2,144,448]{2,1,0:T(8,128)(2,1)S(1)}, u32[]{:S(2)}, u32[]{:S(2)}) collective-permute-start(bf16[2,144,448]{2,1,0:T(8,128)(2,1)S(1)} %bitcast.15), channel_id=1, source_target_pairs={{0,128},{128,0},{1,129},{129,1},{2,130},{130,2},{3,131},{131,3},{4... | collective-permute-start | bytes 774152 | tf_op jit(solution)/shard_map/ppermute | solution.py:42

commit v5 on v4

--- a/solution.py
+++ b/solution.py
@@ -11,6 +11,8 @@
 WIDE = 256
 BF = jnp.bfloat16
 F32 = jnp.float32
+HINT = pl.CostEstimate(flops=int(5e9), bytes_accessed=int(1e6), transcendentals=0)
+LONG = pl.CostEstimate(flops=int(3e10), bytes_accessed=int(1e6), transcendentals=0)
 PLANE = ("zhi", "core", "y", "zh", "zq")
 PARAMS = pltpu.CompilerParams(vmem_limit_bytes=16 << 20)
 
@@ -59,26 +61,31 @@
     out_ref[:, FEAT:] = jnp.zeros((VALID, WIDE - FEAT), BF)
 
 
-def inputs_kernel(where_ref, acts_ref, basis_ref, *out_refs):
+def inputs_kernel(where_ref, acts_ref, basis_ref, out_ref):
     pick = chosen(where_ref[2])
     lines = jnp.dot(pick, acts_ref[...], preferred_element_type=F32).astype(BF)
-    for k in range(4):
-        at = pl.multiple_of((where_ref[5] ^ k) * WIDE, WIDE)
-        out_refs[k][...] = jnp.dot(
-            lines, basis_ref[:, pl.ds(at, WIDE)], preferred_element_type=F32
+    for y in range(4):
+        out_ref[y] = jnp.dot(
+            lines, basis_ref[:, y * WIDE : (y + 1) * WIDE], preferred_element_type=F32
         ).astype(BF)
 
 
-def join_kernel(near_ref, far_ref, *refs):
-    parts, out_ref = refs[:4], refs[4]
-    total = parts[0][...].astype(F32)
-    for k in range(1, 4):
-        total += parts[k][...].astype(F32)
+def pair_kernel(near_ref, far_ref, out_ref):
+    out_ref[0] = near_ref[...]
+    out_ref[1] = far_ref[...]
+
+
+def join_kernel(pair_ref, parts_ref, out_ref):
+    total = parts_ref[0].astype(F32)
+    for y in range(1, 4):
+        total += parts_ref[y].astype(F32)
     total = total.astype(BF)
     for d in range(4):
-        for w, ref in enumerate((near_ref, far_ref)):
+        for w in range(2):
             at = d * 64 + w * 32
-            out_ref[d, w] = jnp.concatenate([ref[:, :FEAT], total[:, at : at + 32]], axis=1)
+            out_ref[d, w] = jnp.concatenate(
+                [pair_ref[w][:, :FEAT], total[:, at : at + 32]], axis=1
+            )
 
 
 def sort_kernel(where_ref, both_ref, out_ref, in_ref):
@@ -176,7 +183,7 @@
             eig_ref[o * rows : (o + 1) * rows, i * cols : (i + 1) * cols] = total / 768.0
 
 
-def call(kernel, out, *args, scalars=1, scratch=()):
+def call(kernel, out, *args, scalars=1, scratch=(), cost=None):
     single = not isinstance(out, (list, tuple))
     smem = pl.BlockSpec(memory_space=pltpu.SMEM)
     vmem = pl.BlockSpec(memory_space=pltpu.VMEM)
@@ -187,6 +194,7 @@
         out_specs=[vmem] * len(outs),
         out_shape=outs,
         scratch_shapes=scratch,
+        cost_estimate=cost,
         compiler_params=PARAMS,
     )(*args)
     return got[0] if single else got
@@ -208,28 +216,27 @@
     lines = call(pack_kernel, like(VALID, WIDE), lengths, grads)
     near = lax.ppermute(lines, PLANE, to_basis(0))
     far = lax.ppermute(lines, PLANE, to_basis(4))
-    partial = call(inputs_kernel, [like(VALID, WIDE)] * 4, where, acts, basis_in)
-    partial = [partial[0]] + [
-        lax.ppermute(partial[k], "y", [(i, i ^ k) for i in range(4)]) for k in (1, 2, 3)
-    ]
+    partial = call(inputs_kernel, like(4, VALID, WIDE), where, acts, basis_in)
+    partial = exchange(partial, "y")
     basis = basis_out[0].T
     cols = basis.shape[0]
     other_basis = swap(basis, "core")
-    both = call(join_kernel, like(4, 2, VALID, WIDE), near, far, *partial, scalars=0)
+    both = call(pair_kernel, like(2, VALID, WIDE), near, far, scalars=0, cost=HINT)
+    both = call(join_kernel, like(4, 2, VALID, WIDE), both, partial, scalars=0)
     both = exchange(both, "zq")
     lines, ins = call(sort_kernel, [like(VALID, 8 * FEAT), like(16, 80, 128)], where, both)
     lines = [lines] + others(lines, "y")
     ins = exchange(ins, ("zhi", "zh", "zq"))
+    part = call(project_kernel, like(4, 72, cols), where, *lines, basis, other_basis, cost=LONG)
+    part, ins = lax.optimization_barrier((part, ins))
     ins = call(merge_kernel, like(4, 2, VALID + 8, WIDE), ins, scalars=0)
-    ins = exchange(ins, "y")
-    ins, lines = lax.optimization_barrier((ins, lines))
-    part = call(project_kernel, like(4, 72, cols), where, *lines, basis, other_basis)
     part = exchange(part, "x")
     part = call(sum_kernel, like(72, cols), part, scalars=0)
     part, ins = lax.optimization_barrier((part, ins))
+    ins = exchange(ins, "y")
+    part = call(spread_kernel, like(4, 72, cols), part, swap(part, "zhi"), scalars=0, cost=HINT)
+    part, ins = lax.optimization_barrier((part, ins))
     other_ins = swap(ins, "core")
-    part = call(spread_kernel, like(4, 72, cols), part, swap(part, "zhi"), scalars=0)
-    part, ins, other_ins = lax.optimization_barrier((part, ins, other_ins))
     outs = exchange(part, "x").reshape(2, VALID, cols)
     ins, masks = call(
         arrange_kernel,

time: 162 us -> 147 us (0.907)
  blocking collectives: 37.9 us -> 9.54 us
  waiting for transfers between devices: 29.3 us -> 44.6 us
  starting transfers between devices: 76.7 us -> 72.4 us
  Pallas kernels: 13.2 us -> 15.5 us
    all_to_all x3 -> x1, blocking collectives: 37.9 us -> 9.54 us  [exchange(): return lax.all_to_all(x, axis, 0, 0, tiled=True)]
    all_to_all x2 -> x5, waiting for transfers between devices: 12.1 us -> 31.2 us  [exchange(): return lax.all_to_all(x, axis, 0, 0, tiled=True)]
    all_to_all x2 -> x5, starting transfers between devices: 10.4 us -> 21.7 us  [exchange(): return lax.all_to_all(x, axis, 0, 0, tiled=True)]
    ppermute x3 -> x0, starting transfers between devices: 9.58 us -> none  [per_device(): lax.ppermute(partial[k], 'y', [(i, i ^ k) for i in range(4)])]
    ppermute x4, starting transfers between devices: 27.4 us -> 21.4 us  [swap(): return lax.ppermute(x, axis, [(0, 1), (1, 0)])]
    pallas_call x10 -> x11, Pallas kernels: 13.2 us -> 15.5 us  [call(): pl.pallas_call(kernel, in_specs=[smem] * scalars + [vmem] * (len(args) -...]
    ppermute x4, waiting for transfers between devices: 3.01 us -> 0.74 us  [swap(): return lax.ppermute(x, axis, [(0, 1), (1, 0)])]
    ppermute x3 -> x0, waiting for transfers between devices: 2.13 us -> none  [per_device(): lax.ppermute(partial[k], 'y', [(i, i ^ k) for i in range(4)])]
  transfers between devices with their start and end apart: 14 -> 14, of which waited for: 8 -> 8; matrix products, arithmetic and copies ran while one was open for 0% -> 0% of each run, Pallas kernels for 2% -> 7%
where the time goes in v5:
time: 147 us
  starting transfers between devices  72.4 us (49%)
  waiting for transfers between devices  44.6 us (30%)
  Pallas kernels  15.5 us (11%)
  blocking collectives  9.54 us (6%)
  local copies, waits for them, and re-layouts  4.22 us (3%)
    all_to_all x5, waiting for transfers between devices, exchange(): return lax.all_to_all(x, axis, 0, 0, tiled=True)  31.2 us
    all_to_all x5, starting transfers between devices, exchange(): return lax.all_to_all(x, axis, 0, 0, tiled=True)  21.7 us
    ppermute x4, starting transfers between devices, swap(): return lax.ppermute(x, axis, [(0, 1), (1, 0)])  21.4 us
    pallas_call x11, Pallas kernels, call(): pl.pallas_call(kernel, in_specs=[smem] * scalars + [vmem] * (len(args) -...  15.5 us
    ppermute x1, starting transfers between devices, per_device(): far = lax.ppermute(lines, PLANE, to_basis(4))  12.8 us
    ppermute x3, waiting for transfers between devices, others(): lax.ppermute(x, axis, [(i, i ^ k) for i in range(n)])  12.7 us
    all_to_all x1, blocking collectives, exchange(): return lax.all_to_all(x, axis, 0, 0, tiled=True)  9.54 us
    ppermute x3, starting transfers between devices, others(): lax.ppermute(x, axis, [(i, i ^ k) for i in range(n)])  8.97 us
  transfers between devices with their start and end apart: 14, of which 8 were waited for; matrix products, arithmetic and copies ran while one was open for 0% of the time, Pallas kernels for 7%

profile of v5, /device:TPU:1, one launch (start us, length us, event | category | flops | bytes accessed | tf_op | source)
XLA Modules:
  0.0 146.5 jit_solution(16490775118118106872)
XLA Ops:
  2.3 12.8 %collective-permute-start.1 = (bf16[144,256]{1,0:T(8,128)(2,1)S(1)}, bf16[144,256]{1,0:T(8,128)(2,1)S(1)}, u32[]{:S(2)}, u32[]{:S(2)}) collective-permute-start(bf16[144,256]{1,0:T(8,128)(2,1)S(1)} %shard_map.55), channel_id=1, source_target_pairs={{0,4},{1,5},{2,6},{3,7},{4,0},{5,1},{6,2},{7,3},{8,12},{9,13},{10,... | collective-permute-start | bytes 221192 | tf_op jit(solution)/shard_map/ppermute | solution.py:218
  15.1 7.5 %collective-permute-start = (bf16[144,256]{1,0:T(8,128)(2,1)S(1)}, bf16[144,256]{1,0:T(8,128)(2,1)S(1)}, u32[]{:S(2)}, u32[]{:S(2)}) collective-permute-start(bf16[144,256]{1,0:T(8,128)(2,1)S(1)} %shard_map.55), channel_id=1, source_target_pairs={{0,0},{1,1},{2,2},{3,3},{4,4},{5,5},{6,6},{7,7},{8,8},{9,9},{10,10... | collective-permute-start | bytes 221192 | tf_op jit(solution)/shard_map/ppermute | solution.py:217
  26.9 3.5 %all-to-all-start = ((bf16[4,144,256]{2,1,0:T(8,128)(2,1)}), bf16[4,144,256]{2,1,0:T(8,128)(2,1)S(1)}, u32[]{:S(2)}, u32[]{:S(2)}) async-start(bf16[4,144,256]{2,1,0:T(8,128)(2,1)} %shard_map.57), calls=%async_computation | async-start | bytes 589824 | tf_op jit(solution)/shard_map/all_to_all | solution.py:36
  30.5 6.6 %all-to-all-done.parts_ref = bf16[4,144,256]{2,1,0:T(8,128)(2,1)S(1)} async-done(((bf16[4,144,256]{2,1,0:T(8,128)(2,1)}), bf16[4,144,256]{2,1,0:T(8,128)(2,1)S(1)}, u32[]{:S(2)}, u32[]{:S(2)}) %all-to-all-start) | async-done | bytes 294944 | tf_op jit(solution)/shard_map/all_to_all | solution.py:36
  38.0 4.1 %all-to-all-start.1 = ((bf16[4,2,144,256]{3,2,1,0:T(8,128)(2,1)}), bf16[4,2,144,256]{3,2,1,0:T(8,128)(2,1)S(1)}, u32[]{:S(2)}, u32[]{:S(2)}) async-start(bf16[4,2,144,256]{3,2,1,0:T(8,128)(2,1)} %shard_map.58), calls=%async_computation.1 | async-start | bytes 1179648 | tf_op jit(solution)/shard_map/all_to_all | solution.py:36
  42.2 3.2 %collective-permute-start.5 = (bf16[448,1792]{1,0:T(8,128)(2,1)S(1)}, bf16[448,1792]{1,0:T(8,128)(2,1)}, u32[]{:S(2)}, u32[]{:S(2)}) collective-permute-start(bf16[448,1792]{1,0:T(8,128)(2,1)S(1)} %bitcast.16), channel_id=1, source_target_pairs={{0,128},{128,0},{1,129},{129,1},{2,130},{130,2},{3,131},{131,3},{4... | collective-permute-start | bytes 4816904 | tf_op jit(solution)/shard_map/ppermute | solution.py:44
  45.4 12.2 %all-to-all-done.1.both_ref = bf16[4,2,144,256]{3,2,1,0:T(8,128)(2,1)S(1)} async-done(((bf16[4,2,144,256]{3,2,1,0:T(8,128)(2,1)}), bf16[4,2,144,256]{3,2,1,0:T(8,128)(2,1)S(1)}, u32[]{:S(2)}, u32[]{:S(2)}) %all-to-all-start.1) | async-done | bytes 589856 | tf_op jit(solution)/shard_map/all_to_all | solution.py:36
  57.5 1.7 %shard_map.59 = (bf16[144,1792]{1,0:T(8,128)(2,1)S(1)}, bf16[16,80,128]{2,1,0:T(8,128)(2,1)}) custom-call(s32[8]{0:T(128)S(1)} %stack.35.where_ref, bf16[4,2,144,256]{3,2,1,0:T(8,128)(2,1)S(1)} %all-to-all-done.1.both_ref), custom_call_target="tpu_custom_call" | custom-call | tf_op jit(solution)/shard_map/pallas_call | solution.py:191
  59.2 2.8 %collective-permute-start.4 = (bf16[144,1792]{1,0:T(8,128)(2,1)S(1)}, bf16[144,1792]{1,0:T(8,128)(2,1)S(1)}, u32[]{:S(2)}, u32[]{:S(2)}) collective-permute-start(bf16[144,1792]{1,0:T(8,128)(2,1)S(1)} %get-tuple-element.15.a_ref), channel_id=1, source_target_pairs={{0,24},{8,16},{16,8},{24,0},{1,25},{9,17},{17,9},{25,1},{2,26},{10... | collective-permute-start | bytes 1548296 | tf_op jit(solution)/shard_map/ppermute | solution.py:209
  62.0 3.1 %collective-permute-start.3 = (bf16[144,1792]{1,0:T(8,128)(2,1)S(1)}, bf16[144,1792]{1,0:T(8,128)(2,1)}, u32[]{:S(2)}, u32[]{:S(2)}) collective-permute-start(bf16[144,1792]{1,0:T(8,128)(2,1)S(1)} %get-tuple-element.15.a_ref), channel_id=1, source_target_pairs={{0,16},{8,24},{16,0},{24,8},{1,17},{9,25},{17,1},{25,9},{2,18},{10... | collective-permute-start | bytes 1548296 | tf_op jit(solution)/shard_map/ppermute | solution.py:209
  65.1 3.1 %collective-permute-start.2 = (bf16[144,1792]{1,0:T(8,128)(2,1)S(1)}, bf16[144,1792]{1,0:T(8,128)(2,1)}, u32[]{:S(2)}, u32[]{:S(2)}) collective-permute-start(bf16[144,1792]{1,0:T(8,128)(2,1)S(1)} %get-tuple-element.15.a_ref), channel_id=1, source_target_pairs={{0,8},{8,0},{16,24},{24,16},{1,9},{9,1},{17,25},{25,17},{2,10},{10... | collective-permute-start | bytes 1548296 | tf_op jit(solution)/shard_map/ppermute | solution.py:209
  68.2 6.6 %all-to-all-start.2 = ((bf16[16,80,128]{2,1,0:T(8,128)(2,1)}), bf16[16,80,128]{2,1,0:T(8,128)(2,1)S(1)}, u32[]{:S(2)}, u32[]{:S(2)}) async-start(bf16[16,80,128]{2,1,0:T(8,128)(2,1)} %get-tuple-element.16), calls=%async_computation.2 | async-start | bytes 655360 | tf_op jit(solution)/shard_map/all_to_all | solution.py:36
  74.9 10.3 %collective-permute-done.4.d_ref = bf16[144,1792]{1,0:T(8,128)(2,1)S(1)} collective-permute-done((bf16[144,1792]{1,0:T(8,128)(2,1)S(1)}, bf16[144,1792]{1,0:T(8,128)(2,1)S(1)}, u32[]{:S(2)}, u32[]{:S(2)}) %collective-permute-start.4) | collective-permute-done | bytes 516128 | tf_op jit(solution)/shard_map/ppermute | solution.py:209
  85.2 2.4 %collective-permute-done.2.b_ref = bf16[144,1792]{1,0:T(8,128)(2,1)} collective-permute-done((bf16[144,1792]{1,0:T(8,128)(2,1)S(1)}, bf16[144,1792]{1,0:T(8,128)(2,1)}, u32[]{:S(2)}, u32[]{:S(2)}) %collective-permute-start.2) | collective-permute-done | bytes 516128 | tf_op jit(solution)/shard_map/ppermute | solution.py:209
  87.6 4.5 %shard_map.60 = bf16[4,72,448]{2,1,0:T(8,128)(2,1)} custom-call(s32[8]{0:T(128)S(1)} %stack.35.where_ref, bf16[144,1792]{1,0:T(8,128)(2,1)S(1)} %get-tuple-element.15.a_ref, bf16[144,1792]{1,0:T(8,128)(2,1)} %collective-permute-done.2.b_ref, bf16[144,1792]{1,0:T(8,128)(2,1)} %collective-permute-done.3.c_ref, ...), custom_call_target="tpu_custom_call" | custom-call | flops 30000001024 | bytes 1000000 | tf_op jit(solution)/shard_map/pallas_call | solution.py:191
  92.1 4.0 %all-to-all-start.3 = ((bf16[4,72,448]{2,1,0:T(8,128)(2,1)}), bf16[4,72,448]{2,1,0:T(8,128)(2,1)S(1)}, u32[]{:S(2)}, u32[]{:S(2)}) async-start(bf16[4,72,448]{2,1,0:T(8,128)(2,1)} %shard_map.60), calls=%async_computation.3 | async-start | bytes 589824 | tf_op jit(solution)/shard_map/all_to_all | solution.py:36
  97.1 4.7 %all-to-all-done.3.parts_ref = bf16[4,72,448]{2,1,0:T(8,128)(2,1)S(1)} async-done(((bf16[4,72,448]{2,1,0:T(8,128)(2,1)}), bf16[4,72,448]{2,1,0:T(8,128)(2,1)S(1)}, u32[]{:S(2)}, u32[]{:S(2)}) %all-to-all-start.3) | async-done | bytes 258080 | tf_op jit(solution)/shard_map/all_to_all | solution.py:36
  101.8 10.1 %collective-permute-start.6 = (bf16[72,448]{1,0:T(8,128)(2,1)S(1)}, bf16[72,448]{1,0:T(8,128)(2,1)S(1)}, u32[]{:S(2)}, u32[]{:S(2)}) collective-permute-start(bf16[72,448]{1,0:T(8,128)(2,1)S(1)} %shard_map.61.one_ref), channel_id=1, source_target_pairs={{0,256},{256,0},{1,257},{257,1},{2,258},{258,2},{3,259},{259,3},{4... | collective-permute-start | bytes 193544 | tf_op jit(solution)/shard_map/ppermute | solution.py:44
  112.0 3.5 %all-to-all-start.4 = ((bf16[4,2,152,256]{3,2,1,0:T(8,128)(2,1)}), bf16[4,2,152,256]{3,2,1,0:T(8,128)(2,1)S(1)}, u32[]{:S(2)}, u32[]{:S(2)}) async-start(bf16[4,2,152,256]{3,2,1,0:T(8,128)(2,1)} %shard_map.62), calls=%async_computation.4 | async-start | bytes 1245184 | tf_op jit(solution)/shard_map/all_to_all | solution.py:36
  115.8 7.7 %all-to-all-done.4.own_ref = bf16[4,2,152,256]{3,2,1,0:T(8,128)(2,1)S(1)} async-done(((bf16[4,2,152,256]{3,2,1,0:T(8,128)(2,1)}), bf16[4,2,152,256]{3,2,1,0:T(8,128)(2,1)S(1)}, u32[]{:S(2)}, u32[]{:S(2)}) %all-to-all-start.4) | async-done | bytes 622624 | tf_op jit(solution)/shard_map/all_to_all | solution.py:36
  123.4 5.4 %collective-permute-start.8 = (bf16[4,2,152,256]{3,2,1,0:T(8,128)(2,1)S(1)}, bf16[4,2,152,256]{3,2,1,0:T(8,128)(2,1)S(1)}, u32[]{:S(2)}, u32[]{:S(2)}) collective-permute-start(bf16[4,2,152,256]{3,2,1,0:T(8,128)(2,1)S(1)} %all-to-all-done.4.own_ref), channel_id=1, source_target_pairs={{0,128},{128,0},{1,129},{129,1},{2,130},{130,2},{3,131},{131,3},{4... | collective-permute-start | bytes 1867784 | tf_op jit(solution)/shard_map/ppermute | solution.py:44
  128.8 9.5 %all_to_all.30 = bf16[4,72,448]{2,1,0:T(8,128)(2,1)S(1)} all-to-all(bf16[4,72,448]{2,1,0:T(8,128)(2,1)S(1)} %shard_map.63), channel_id=1, replica_groups=mesh['zhi'=2,'core'=2,'x'=4,'y'=4,'zh'=2,'zq'=4] {'x'}, dimensions={0} | all-to-all | bytes 516096 | tf_op jit(solution)/shard_map/all_to_all | solution.py:36
  138.4 2.7 %collective-permute-start.7 = (bf16[2,144,448]{2,1,0:T(8,128)(2,1)S(1)}, bf16[2,144,448]{2,1,0:T(8,128)(2,1)S(1)}, u32[]{:S(2)}, u32[]{:S(2)}) collective-permute-start(bf16[2,144,448]{2,1,0:T(8,128)(2,1)S(1)} %bitcast.13), channel_id=1, source_target_pairs={{0,128},{128,0},{1,129},{129,1},{2,130},{130,2},{3,131},{131,3},{4... | collective-permute-start | bytes 774152 | tf_op jit(solution)/shard_map/ppermute | solution.py:44
  142.2 4.3 %shard_map.65 = f32[448,1024]{1,0:T(8,128)} custom-call(s32[8]{0:T(128)S(1)} %stack.35.where_ref, bf16[2,144,448]{2,1,0:T(8,128)(2,1)S(1)} %bitcast.14, bf16[2,144,448]{2,1,0:T(8,128)(2,1)S(1)} %collective-permute-done.7.other_ref, bf16[4,144,1024]{2,1,0:T(8,128)(2,1)S(1)} %get-tuple-element.23.in_ref, bf16[4,144,128]{2,1,0:T(8,128)(2,1)S(1)} %get-tuple-element.24.mask_ref), custom_call_target="tpu_custom_call" | custom-call | tf_op jit(solution)/shard_map/pallas_call | solution.py:191
  (27 shorter events, 10.0 us)
Async XLA Ops:
  0.0 0.9 copy-start.2
  0.9 0.7 copy-start.3
  2.3 28.2 %collective-permute-start.1 = (bf16[144,256]{1,0:T(8,128)(2,1)S(1)}, bf16[144,256]{1,0:T(8,128)(2,1)S(1)}, u32[]{:S(2)}, u32[]{:S(2)}) collective-permute-start(bf16[144,256]{1,0:T(8,128)(2,1)S(1)} %shard_map.55), channel_id=1, source_target_pairs={{0,4},{1,5},{2,6},{3,7},{4,0},{5,1},{6,2},{7,3},{8,12},{9,13},{10,... | collective-permute-start | bytes 221192 | tf_op jit(solution)/shard_map/ppermute | solution.py:218
  15.1 15.3 %collective-permute-start = (bf16[144,256]{1,0:T(8,128)(2,1)S(1)}, bf16[144,256]{1,0:T(8,128)(2,1)S(1)}, u32[]{:S(2)}, u32[]{:S(2)}) collective-permute-start(bf16[144,256]{1,0:T(8,128)(2,1)S(1)} %shard_map.55), channel_id=1, source_target_pairs={{0,0},{1,1},{2,2},{3,3},{4,4},{5,5},{6,6},{7,7},{8,8},{9,9},{10,10... | collective-permute-start | bytes 221192 | tf_op jit(solution)/shard_map/ppermute | solution.py:217
  23.4 1.0 copy-start
  24.4 0.9 copy-start.1
  26.9 10.1 %all-to-all-start = ((bf16[4,144,256]{2,1,0:T(8,128)(2,1)}), bf16[4,144,256]{2,1,0:T(8,128)(2,1)S(1)}, u32[]{:S(2)}, u32[]{:S(2)}) async-start(bf16[4,144,256]{2,1,0:T(8,128)(2,1)} %shard_map.57), calls=%async_computation | async-start | bytes 589824 | tf_op jit(solution)/shard_map/all_to_all | solution.py:36
  30.4 11.7 %copy-start.4 = (bf16[1,1792,448]{1,2,0:T(8,128)(2,1)S(1)}, bf16[1,1792,448]{1,2,0:T(8,128)(2,1)}, u32[]{:S(2)}) copy-start(bf16[1,1792,448]{1,2,0:T(8,128)(2,1)} %param.8) | copy-start | bytes 4816900
  38.0 19.5 %all-to-all-start.1 = ((bf16[4,2,144,256]{3,2,1,0:T(8,128)(2,1)}), bf16[4,2,144,256]{3,2,1,0:T(8,128)(2,1)S(1)}, u32[]{:S(2)}, u32[]{:S(2)}) async-start(bf16[4,2,144,256]{3,2,1,0:T(8,128)(2,1)} %shard_map.58), calls=%async_computation.1 | async-start | bytes 1179648 | tf_op jit(solution)/shard_map/all_to_all | solution.py:36
  42.2 32.7 %collective-permute-start.5 = (bf16[448,1792]{1,0:T(8,128)(2,1)S(1)}, bf16[448,1792]{1,0:T(8,128)(2,1)}, u32[]{:S(2)}, u32[]{:S(2)}) collective-permute-start(bf16[448,1792]{1,0:T(8,128)(2,1)S(1)} %bitcast.16), channel_id=1, source_target_pairs={{0,128},{128,0},{1,129},{129,1},{2,130},{130,2},{3,131},{131,3},{4... | collective-permute-start | bytes 4816904 | tf_op jit(solution)/shard_map/ppermute | solution.py:44
  59.2 25.9 %collective-permute-start.4 = (bf16[144,1792]{1,0:T(8,128)(2,1)S(1)}, bf16[144,1792]{1,0:T(8,128)(2,1)S(1)}, u32[]{:S(2)}, u32[]{:S(2)}) collective-permute-start(bf16[144,1792]{1,0:T(8,128)(2,1)S(1)} %get-tuple-element.15.a_ref), channel_id=1, source_target_pairs={{0,24},{8,16},{16,8},{24,0},{1,25},{9,17},{17,9},{25,1},{2,26},{10... | collective-permute-start | bytes 1548296 | tf_op jit(solution)/shard_map/ppermute | solution.py:209
  62.0 23.1 %collective-permute-start.3 = (bf16[144,1792]{1,0:T(8,128)(2,1)S(1)}, bf16[144,1792]{1,0:T(8,128)(2,1)}, u32[]{:S(2)}, u32[]{:S(2)}) collective-permute-start(bf16[144,1792]{1,0:T(8,128)(2,1)S(1)} %get-tuple-element.15.a_ref), channel_id=1, source_target_pairs={{0,16},{8,24},{16,0},{24,8},{1,17},{9,25},{17,1},{25,9},{2,18},{10... | collective-permute-start | bytes 1548296 | tf_op jit(solution)/shard_map/ppermute | solution.py:209
  65.1 22.4 %collective-permute-start.2 = (bf16[144,1792]{1,0:T(8,128)(2,1)S(1)}, bf16[144,1792]{1,0:T(8,128)(2,1)}, u32[]{:S(2)}, u32[]{:S(2)}) collective-permute-start(bf16[144,1792]{1,0:T(8,128)(2,1)S(1)} %get-tuple-element.15.a_ref), channel_id=1, source_target_pairs={{0,8},{8,0},{16,24},{24,16},{1,9},{9,1},{17,25},{25,17},{2,10},{10... | collective-permute-start | bytes 1548296 | tf_op jit(solution)/shard_map/ppermute | solution.py:209
  68.2 23.8 %all-to-all-start.2 = ((bf16[16,80,128]{2,1,0:T(8,128)(2,1)}), bf16[16,80,128]{2,1,0:T(8,128)(2,1)S(1)}, u32[]{:S(2)}, u32[]{:S(2)}) async-start(bf16[16,80,128]{2,1,0:T(8,128)(2,1)} %get-tuple-element.16), calls=%async_computation.2 | async-start | bytes 655360 | tf_op jit(solution)/shard_map/all_to_all | solution.py:36
  92.1 9.7 %all-to-all-start.3 = ((bf16[4,72,448]{2,1,0:T(8,128)(2,1)}), bf16[4,72,448]{2,1,0:T(8,128)(2,1)S(1)}, u32[]{:S(2)}, u32[]{:S(2)}) async-start(bf16[4,72,448]{2,1,0:T(8,128)(2,1)} %shard_map.60), calls=%async_computation.3 | async-start | bytes 589824 | tf_op jit(solution)/shard_map/all_to_all | solution.py:36
  101.8 13.9 %collective-permute-start.6 = (bf16[72,448]{1,0:T(8,128)(2,1)S(1)}, bf16[72,448]{1,0:T(8,128)(2,1)S(1)}, u32[]{:S(2)}, u32[]{:S(2)}) collective-permute-start(bf16[72,448]{1,0:T(8,128)(2,1)S(1)} %shard_map.61.one_ref), channel_id=1, source_target_pairs={{0,256},{256,0},{1,257},{257,1},{2,258},{258,2},{3,259},{259,3},{4... | collective-permute-start | bytes 193544 | tf_op jit(solution)/shard_map/ppermute | solution.py:44
  112.0 11.5 %all-to-all-start.4 = ((bf16[4,2,152,256]{3,2,1,0:T(8,128)(2,1)}), bf16[4,2,152,256]{3,2,1,0:T(8,128)(2,1)S(1)}, u32[]{:S(2)}, u32[]{:S(2)}) async-start(bf16[4,2,152,256]{3,2,1,0:T(8,128)(2,1)} %shard_map.62), calls=%async_computation.4 | async-start | bytes 1245184 | tf_op jit(solution)/shard_map/all_to_all | solution.py:36
  123.4 17.6 %collective-permute-start.8 = (bf16[4,2,152,256]{3,2,1,0:T(8,128)(2,1)S(1)}, bf16[4,2,152,256]{3,2,1,0:T(8,128)(2,1)S(1)}, u32[]{:S(2)}, u32[]{:S(2)}) collective-permute-start(bf16[4,2,152,256]{3,2,1,0:T(8,128)(2,1)S(1)} %all-to-all-done.4.own_ref), channel_id=1, source_target_pairs={{0,128},{128,0},{1,129},{129,1},{2,130},{130,2},{3,131},{131,3},{4... | collective-permute-start | bytes 1867784 | tf_op jit(solution)/shard_map/ppermute | solution.py:44
  138.4 3.9 %collective-permute-start.7 = (bf16[2,144,448]{2,1,0:T(8,128)(2,1)S(1)}, bf16[2,144,448]{2,1,0:T(8,128)(2,1)S(1)}, u32[]{:S(2)}, u32[]{:S(2)}) collective-permute-start(bf16[2,144,448]{2,1,0:T(8,128)(2,1)S(1)} %bitcast.13), channel_id=1, source_target_pairs={{0,128},{128,0},{1,129},{129,1},{2,130},{130,2},{3,131},{131,3},{4... | collective-permute-start | bytes 774152 | tf_op jit(solution)/shard_map/ppermute | solution.py:44

commit v6 on v5

--- a/solution.py
+++ b/solution.py
@@ -17,7 +17,7 @@
 PARAMS = pltpu.CompilerParams(vmem_limit_bytes=16 << 20)
 
 
-def to_basis(flip):
+def to_basis(far):
     def place(zhi, core, y, zlo):
         return ((zhi * 2 + core) * 4 + y) * 8 + zlo
 
@@ -26,8 +26,9 @@
         for core in range(2):
             for y in range(4):
                 for z in range(8):
-                    to = 7 - z if zhi != y >> 1 else z
-                    there = place(y >> 1, zhi, core * 2 + (y & 1), to ^ flip)
+                    crossed = zhi != y >> 1
+                    to = (z ^ 3 if far else z ^ 4) if crossed else (z ^ 4 if far else z)
+                    there = place(y >> 1, zhi, core * 2 + (y & 1), to)
                     pairs.append((place(zhi, core, y, z), there))
     return pairs
 
@@ -89,11 +90,11 @@
 
 
 def sort_kernel(where_ref, both_ref, out_ref, in_ref):
-    zh, mirrored = where_ref[0], where_ref[1]
+    zh, crossed = where_ref[0], where_ref[1]
     for f in range(8):
-        at = jnp.where(mirrored == 1, 7 - f, f)
-        far = (at // 4 != zh).astype(jnp.int32)
-        out_ref[:, f * FEAT : (f + 1) * FEAT] = both_ref[at % 4, far][:, :FEAT]
+        far = (jnp.int32(f // 4) != zh).astype(jnp.int32) ^ crossed
+        at = (f % 4) ^ (3 * (far & crossed))
+        out_ref[:, f * FEAT : (f + 1) * FEAT] = both_ref[at, far][:, :FEAT]
     sums = []
     for w in range(2):
         total = both_ref[0, w][:, FEAT:].astype(F32)
@@ -108,8 +109,7 @@
         in_ref[copy, half:] = count
 
 
-def merge_kernel(parts_ref, spread_ref):
-    out_ref = spread_ref.at[0]
+def merge_kernel(parts_ref, out_ref):
     half = VALID // 2
     for zhi in range(2):
         for q in range(4):
@@ -120,18 +120,19 @@
             out_ref[zhi, half:VALID, q * 64 : q * 64 + 64] = total[:, 64:]
         for h in range(2):
             out_ref[zhi, VALID:, h * 128 : h * 128 + 128] = parts_ref[zhi * 8, half:]
-    for copy in range(1, 4):
-        spread_ref[copy] = out_ref[...]
-
-
-def project_kernel(where_ref, a_ref, b_ref, c_ref, d_ref, own_ref, other_ref, out_ref):
+
+
+def project_kernel(where_ref, a_ref, b_ref, c_ref, d_ref, own_ref, other_ref, out_ref, held):
     yh, same = where_ref[7], where_ref[3] == where_ref[6]
     for left_ref, right_ref, t in ((a_ref, b_ref, yh), (c_ref, d_ref, 1 - yh)):
         left, right = left_ref[...], right_ref[...]
-        total = across(jnp.where(same, left, right), own_ref[...])
-        total += across(jnp.where(same, right, left), other_ref[...])
-        for h in range(2):
-            out_ref[2 * t + h] = total[h * 72 : (h + 1) * 72].astype(BF)
+        held[0, t] = jnp.where(same, left, right)
+        held[1, t] = jnp.where(same, right, left)
+    rows = (2 * VALID, held.shape[3])
+    total = across(held[0].reshape(rows), own_ref[...])
+    total += across(held[1].reshape(rows), other_ref[...])
+    for h in range(4):
+        out_ref[h] = total[h * 72 : (h + 1) * 72].astype(BF)
 
 
 def sum_kernel(parts_ref, out_ref):
@@ -149,29 +150,37 @@
 
 def arrange_kernel(where_ref, own_ref, other_ref, out_ref, mask_ref):
     core = where_ref[3]
-    slot = lax.broadcasted_iota(jnp.int32, (VALID, 128), 0).astype(F32)
+    slot = lax.broadcasted_iota(jnp.int32, (8, VALID), 1).astype(F32)
     for zhi in range(2):
         for c in range(2):
             mine = core == c
             g = zhi * 2 + c
             for y in range(4):
-                block = jnp.where(mine, own_ref[y, zhi], other_ref[y, zhi])
+                k = y ^ where_ref[5]
+                block = jnp.where(mine, own_ref[k, zhi], other_ref[k, zhi])
                 out_ref[g, :, y * WIDE : (y + 1) * WIDE] = block[:VALID]
-            count = block[VALID : VALID + 1, :128].astype(F32)
+            count = block[VALID:, :VALID].astype(F32)
             mask_ref[g] = (slot < count).astype(F32).astype(BF)
+
+
+def left_kernel(lines_ref, left_ref):
+    for t in range(2):
+        left_ref[t] = lines_ref[t].T
 
 
 def square_kernel(where_ref, own_ref, other_ref, in_ref, mask_ref, eig_ref, left_ref):
     core = where_ref[3]
-    for g in range(4):
-        mine = core == g // 2
-        lines = jnp.where(mine, own_ref[g % 2], other_ref[g % 2])
-        first = lines * mask_ref[g][:, :1]
-        left_ref[2 * g] = first.T
-        left_ref[2 * g + 1] = (lines - first).T
-    rows, cols = 112, 256
-    for o in range(448 // rows):
-        for i in range(1024 // cols):
+    for t in range(2):
+        for at, lines in (
+            (2 * core + t, own_ref[t]),
+            (2 * (1 - core) + t, other_ref[t].T),
+        ):
+            first = lines * mask_ref[at][:1]
+            left_ref[2 * at] = first
+            left_ref[2 * at + 1] = lines - first
+    rows, cols = 224, 256
+    for i in range(1024 // cols):
+        for o in range(448 // rows):
             total = jnp.zeros((rows, cols), F32)
             for s in range(8):
                 block = jnp.dot(
@@ -206,7 +215,8 @@
 
 def others(x, axis):
     n = lax.axis_size(axis)
-    return [lax.ppermute(x, axis, [(i, i ^ k) for i in range(n)]) for k in range(1, n)]
+    sent = {k: lax.ppermute(x, axis, [(i, i ^ k) for i in range(n)]) for k in (1, 3, 2)}
+    return [sent[k] for k in (1, 2, 3)]
 
 
 def per_device(acts, grads, basis_in, basis_out, lengths):
@@ -214,8 +224,8 @@
     crossed = (core != zhi).astype(jnp.int32)
     where = jnp.stack([zh, crossed, lengths[0, 0], core, zq, y, y & 1, y >> 1])
     lines = call(pack_kernel, like(VALID, WIDE), lengths, grads)
-    near = lax.ppermute(lines, PLANE, to_basis(0))
-    far = lax.ppermute(lines, PLANE, to_basis(4))
+    near = lax.ppermute(lines, PLANE, to_basis(False))
+    far = lax.ppermute(lines, PLANE, to_basis(True))
     partial = call(inputs_kernel, like(4, VALID, WIDE), where, acts, basis_in)
     partial = exchange(partial, "y")
     basis = basis_out[0].T
@@ -227,29 +237,40 @@
     lines, ins = call(sort_kernel, [like(VALID, 8 * FEAT), like(16, 80, 128)], where, both)
     lines = [lines] + others(lines, "y")
     ins = exchange(ins, ("zhi", "zh", "zq"))
-    part = call(project_kernel, like(4, 72, cols), where, *lines, basis, other_basis, cost=LONG)
+    part = call(
+        project_kernel,
+        like(4, 72, cols),
+        where,
+        *lines,
+        basis,
+        other_basis,
+        cost=LONG,
+        scratch=[pltpu.VMEM((2, 2, VALID, 8 * FEAT), BF)],
+    )
     part, ins = lax.optimization_barrier((part, ins))
-    ins = call(merge_kernel, like(4, 2, VALID + 8, WIDE), ins, scalars=0)
+    ins = call(merge_kernel, like(2, VALID + 8, WIDE), ins, scalars=0)
     part = exchange(part, "x")
     part = call(sum_kernel, like(72, cols), part, scalars=0)
     part, ins = lax.optimization_barrier((part, ins))
-    ins = exchange(ins, "y")
+    ins = [ins] + others(ins, "y")
     part = call(spread_kernel, like(4, 72, cols), part, swap(part, "zhi"), scalars=0, cost=HINT)
     part, ins = lax.optimization_barrier((part, ins))
+    ins = jnp.stack(ins)
     other_ins = swap(ins, "core")
     outs = exchange(part, "x").reshape(2, VALID, cols)
     ins, masks = call(
         arrange_kernel,
-        [like(4, VALID, 1024), like(4, VALID, 128)],
+        [like(4, VALID, 1024), like(4, 8, VALID)],
         where,
         ins,
         other_ins,
     )
+    left = call(left_kernel, like(2, cols, VALID), outs, scalars=0, cost=HINT)
     return call(
         square_kernel,
         like(cols, 1024, dtype=F32),
         where,
-        outs,
+        left,
         swap(outs, "core"),
         ins,
         masks,

time: 147 us -> 148 us (level)
  starting transfers between devices: 72.4 us -> 84.2 us
  blocking collectives: 9.54 us -> 0 us
  waiting for transfers between devices: 44.6 us -> 43.1 us
    all_to_all x1 -> x0, blocking collectives: 9.54 us -> none  [exchange(): return lax.all_to_all(x, axis, 0, 0, tiled=True)]
    ppermute x3 -> x6, starting transfers between devices: 8.97 us -> 17.9 us  [others(): lax.ppermute(x, axis, [(i, i ^ k) for i in range(n)])]
    all_to_all x5, waiting for transfers between devices: 31.2 us -> 25.9 us  [exchange(): return lax.all_to_all(x, axis, 0, 0, tiled=True)]
    ppermute x3 -> x6, waiting for transfers between devices: 12.7 us -> 16.9 us  [others(): lax.ppermute(x, axis, [(i, i ^ k) for i in range(n)])]
    ppermute x4, starting transfers between devices: 21.4 us -> 24.7 us  [swap(): return lax.ppermute(x, axis, [(0, 1), (1, 0)])]
    pallas_call x11 -> x12, Pallas kernels: 15.5 us -> 14.8 us  [call(): pl.pallas_call(kernel, in_specs=[smem] * scalars + [vmem] * (len(args) -...]
  transfers between devices with their start and end apart: 14 -> 17, of which waited for: 8 -> 9; matrix products, arithmetic and copies ran while one was open for 0% -> 1% of each run, Pallas kernels for 7% -> 6%
where the time goes in v6:
time: 148 us; the launch traced here: 147 us
  starting transfers between devices  84.2 us (57%)
  waiting for transfers between devices  43.1 us (29%)
  Pallas kernels  14.8 us (10%)
  local copies, waits for them, and re-layouts  4.22 us (3%)
    all_to_all x5, waiting for transfers between devices, exchange(): return lax.all_to_all(x, axis, 0, 0, tiled=True)  25.9 us
    ppermute x4, starting transfers between devices, swap(): return lax.ppermute(x, axis, [(0, 1), (1, 0)])  24.7 us
    all_to_all x5, starting transfers between devices, exchange(): return lax.all_to_all(x, axis, 0, 0, tiled=True)  21.2 us
    ppermute x6, starting transfers between devices, others(): lax.ppermute(x, axis, [(i, i ^ k) for i in range(n)])  17.9 us
    ppermute x6, waiting for transfers between devices, others(): lax.ppermute(x, axis, [(i, i ^ k) for i in range(n)])  16.9 us
    pallas_call x12, Pallas kernels, call(): pl.pallas_call(kernel, in_specs=[smem] * scalars + [vmem] * (len(args) -...  14.8 us
    ppermute x1, starting transfers between devices, per_device(): far = lax.ppermute(lines, PLANE, to_basis(True))  12.8 us
    ppermute x1, starting transfers between devices, per_device(): near = lax.ppermute(lines, PLANE, to_basis(False))  7.54 us
  transfers between devices with their start and end apart: 17, of which 9 were waited for; matrix products, arithmetic and copies ran while one was open for 1% of the time, Pallas kernels for 6%

profile of v6, /device:TPU:1, one launch (start us, length us, event | category | flops | bytes accessed | tf_op | source)
XLA Modules:
  0.0 146.7 jit_solution(13109874645095533923)
XLA Ops:
  2.3 12.8 %collective-permute-start.1 = (bf16[144,256]{1,0:T(8,128)(2,1)S(1)}, bf16[144,256]{1,0:T(8,128)(2,1)S(1)}, u32[]{:S(2)}, u32[]{:S(2)}) collective-permute-start(bf16[144,256]{1,0:T(8,128)(2,1)S(1)} %shard_map.55), channel_id=1, source_target_pairs={{0,4},{1,5},{2,6},{3,7},{4,0},{5,1},{6,2},{7,3},{8,12},{9,13},{10,... | collective-permute-start | bytes 221192 | tf_op jit(solution)/shard_map/ppermute | solution.py:228
  15.1 7.5 %collective-permute-start = (bf16[144,256]{1,0:T(8,128)(2,1)S(1)}, bf16[144,256]{1,0:T(8,128)(2,1)S(1)}, u32[]{:S(2)}, u32[]{:S(2)}) collective-permute-start(bf16[144,256]{1,0:T(8,128)(2,1)S(1)} %shard_map.55), channel_id=1, source_target_pairs={{0,0},{1,1},{2,2},{3,3},{4,4},{5,5},{6,6},{7,7},{8,8},{9,9},{10,10... | collective-permute-start | bytes 221192 | tf_op jit(solution)/shard_map/ppermute | solution.py:227
  26.9 3.5 %all-to-all-start = ((bf16[4,144,256]{2,1,0:T(8,128)(2,1)}), bf16[4,144,256]{2,1,0:T(8,128)(2,1)S(1)}, u32[]{:S(2)}, u32[]{:S(2)}) async-start(bf16[4,144,256]{2,1,0:T(8,128)(2,1)} %shard_map.57), calls=%async_computation | async-start | bytes 589824 | tf_op jit(solution)/shard_map/all_to_all | solution.py:37
  30.5 7.2 %all-to-all-done.parts_ref = bf16[4,144,256]{2,1,0:T(8,128)(2,1)S(1)} async-done(((bf16[4,144,256]{2,1,0:T(8,128)(2,1)}), bf16[4,144,256]{2,1,0:T(8,128)(2,1)S(1)}, u32[]{:S(2)}, u32[]{:S(2)}) %all-to-all-start) | async-done | bytes 294944 | tf_op jit(solution)/shard_map/all_to_all | solution.py:37
  38.6 3.5 %all-to-all-start.1 = ((bf16[4,2,144,256]{3,2,1,0:T(8,128)(2,1)}), bf16[4,2,144,256]{3,2,1,0:T(8,128)(2,1)S(1)}, u32[]{:S(2)}, u32[]{:S(2)}) async-start(bf16[4,2,144,256]{3,2,1,0:T(8,128)(2,1)} %shard_map.58), calls=%async_computation.1 | async-start | bytes 1179648 | tf_op jit(solution)/shard_map/all_to_all | solution.py:37
  42.1 2.6 %collective-permute-start.5 = (bf16[448,1792]{1,0:T(8,128)(2,1)S(1)}, bf16[448,1792]{1,0:T(8,128)(2,1)}, u32[]{:S(2)}, u32[]{:S(2)}) collective-permute-start(bf16[448,1792]{1,0:T(8,128)(2,1)S(1)} %bitcast.21), channel_id=1, source_target_pairs={{0,128},{128,0},{1,129},{129,1},{2,130},{130,2},{3,131},{131,3},{4... | collective-permute-start | bytes 4816904 | tf_op jit(solution)/shard_map/ppermute | solution.py:45
  44.7 12.8 %all-to-all-done.1.both_ref = bf16[4,2,144,256]{3,2,1,0:T(8,128)(2,1)S(1)} async-done(((bf16[4,2,144,256]{3,2,1,0:T(8,128)(2,1)}), bf16[4,2,144,256]{3,2,1,0:T(8,128)(2,1)S(1)}, u32[]{:S(2)}, u32[]{:S(2)}) %all-to-all-start.1) | async-done | bytes 589856 | tf_op jit(solution)/shard_map/all_to_all | solution.py:37
  59.2 2.8 %collective-permute-start.4 = (bf16[144,1792]{1,0:T(8,128)(2,1)S(1)}, bf16[144,1792]{1,0:T(8,128)(2,1)S(1)}, u32[]{:S(2)}, u32[]{:S(2)}) collective-permute-start(bf16[144,1792]{1,0:T(8,128)(2,1)S(1)} %get-tuple-element.18.a_ref), channel_id=1, source_target_pairs={{0,24},{8,16},{16,8},{24,0},{1,25},{9,17},{17,9},{25,1},{2,26},{10... | collective-permute-start | bytes 1548296 | tf_op jit(solution)/shard_map/ppermute | solution.py:218
  62.0 3.1 %collective-permute-start.3 = (bf16[144,1792]{1,0:T(8,128)(2,1)S(1)}, bf16[144,1792]{1,0:T(8,128)(2,1)}, u32[]{:S(2)}, u32[]{:S(2)}) collective-permute-start(bf16[144,1792]{1,0:T(8,128)(2,1)S(1)} %get-tuple-element.18.a_ref), channel_id=1, source_target_pairs={{0,16},{8,24},{16,0},{24,8},{1,17},{9,25},{17,1},{25,9},{2,18},{10... | collective-permute-start | bytes 1548296 | tf_op jit(solution)/shard_map/ppermute | solution.py:218
  65.1 3.1 %collective-permute-start.2 = (bf16[144,1792]{1,0:T(8,128)(2,1)S(1)}, bf16[144,1792]{1,0:T(8,128)(2,1)}, u32[]{:S(2)}, u32[]{:S(2)}) collective-permute-start(bf16[144,1792]{1,0:T(8,128)(2,1)S(1)} %get-tuple-element.18.a_ref), channel_id=1, source_target_pairs={{0,8},{8,0},{16,24},{24,16},{1,9},{9,1},{17,25},{25,17},{2,10},{10... | collective-permute-start | bytes 1548296 | tf_op jit(solution)/shard_map/ppermute | solution.py:218
  68.2 6.8 %all-to-all-start.2 = ((bf16[16,80,128]{2,1,0:T(8,128)(2,1)}), bf16[16,80,128]{2,1,0:T(8,128)(2,1)S(1)}, u32[]{:S(2)}, u32[]{:S(2)}) async-start(bf16[16,80,128]{2,1,0:T(8,128)(2,1)} %get-tuple-element.19), calls=%async_computation.2 | async-start | bytes 655360 | tf_op jit(solution)/shard_map/all_to_all | solution.py:37
  75.0 10.2 %collective-permute-done.4.d_ref = bf16[144,1792]{1,0:T(8,128)(2,1)S(1)} collective-permute-done((bf16[144,1792]{1,0:T(8,128)(2,1)S(1)}, bf16[144,1792]{1,0:T(8,128)(2,1)S(1)}, u32[]{:S(2)}, u32[]{:S(2)}) %collective-permute-start.4) | collective-permute-done | bytes 516128 | tf_op jit(solution)/shard_map/ppermute | solution.py:218
  85.2 2.4 %collective-permute-done.2.b_ref = bf16[144,1792]{1,0:T(8,128)(2,1)} collective-permute-done((bf16[144,1792]{1,0:T(8,128)(2,1)S(1)}, bf16[144,1792]{1,0:T(8,128)(2,1)}, u32[]{:S(2)}, u32[]{:S(2)}) %collective-permute-start.2) | collective-permute-done | bytes 516128 | tf_op jit(solution)/shard_map/ppermute | solution.py:218
  87.6 4.0 %shard_map.60 = bf16[4,72,448]{2,1,0:T(8,128)(2,1)} custom-call(s32[8]{0:T(128)S(1)} %stack.50.where_ref, bf16[144,1792]{1,0:T(8,128)(2,1)S(1)} %get-tuple-element.18.a_ref, bf16[144,1792]{1,0:T(8,128)(2,1)} %collective-permute-done.2.b_ref, bf16[144,1792]{1,0:T(8,128)(2,1)} %collective-permute-done.3.c_ref, ...), custom_call_target="tpu_custom_call" | custom-call | flops 30000001024 | bytes 1000000 | tf_op jit(solution)/shard_map/pallas_call | solution.py:200
  91.5 4.0 %all-to-all-start.3 = ((bf16[4,72,448]{2,1,0:T(8,128)(2,1)}), bf16[4,72,448]{2,1,0:T(8,128)(2,1)S(1)}, u32[]{:S(2)}, u32[]{:S(2)}) async-start(bf16[4,72,448]{2,1,0:T(8,128)(2,1)} %shard_map.60), calls=%async_computation.3 | async-start | bytes 589824 | tf_op jit(solution)/shard_map/all_to_all | solution.py:37
  95.7 5.6 %all-to-all-done.3.parts_ref = bf16[4,72,448]{2,1,0:T(8,128)(2,1)S(1)} async-done(((bf16[4,72,448]{2,1,0:T(8,128)(2,1)}), bf16[4,72,448]{2,1,0:T(8,128)(2,1)S(1)}, u32[]{:S(2)}, u32[]{:S(2)}) %all-to-all-start.3) | async-done | bytes 258080 | tf_op jit(solution)/shard_map/all_to_all | solution.py:37
  101.3 10.6 %collective-permute-start.6 = (bf16[72,448]{1,0:T(8,128)(2,1)S(1)}, bf16[72,448]{1,0:T(8,128)(2,1)S(1)}, u32[]{:S(2)}, u32[]{:S(2)}) collective-permute-start(bf16[72,448]{1,0:T(8,128)(2,1)S(1)} %shard_map.61.one_ref), channel_id=1, source_target_pairs={{0,256},{256,0},{1,257},{257,1},{2,258},{258,2},{3,259},{259,3},{4... | collective-permute-start | bytes 193544 | tf_op jit(solution)/shard_map/ppermute | solution.py:45
  111.9 2.5 %collective-permute-start.9 = (bf16[2,152,256]{2,1,0:T(8,128)(2,1)S(1)}, bf16[2,152,256]{2,1,0:T(8,128)(2,1)S(1)}, u32[]{:S(2)}, u32[]{:S(2)}) collective-permute-start(bf16[2,152,256]{2,1,0:T(8,128)(2,1)S(1)} %shard_map.62), channel_id=1, source_target_pairs={{0,24},{8,16},{16,8},{24,0},{1,25},{9,17},{17,9},{25,1},{2,26},{10... | collective-permute-start | bytes 466952 | tf_op jit(solution)/shard_map/ppermute | solution.py:218
  114.4 4.1 %collective-permute-start.8 = (bf16[2,152,256]{2,1,0:T(8,128)(2,1)S(1)}, bf16[2,152,256]{2,1,0:T(8,128)(2,1)S(1)}, u32[]{:S(2)}, u32[]{:S(2)}) collective-permute-start(bf16[2,152,256]{2,1,0:T(8,128)(2,1)S(1)} %shard_map.62), channel_id=1, source_target_pairs={{0,16},{8,24},{16,0},{24,8},{1,17},{9,25},{17,1},{25,9},{2,18},{10... | collective-permute-start | bytes 466952 | tf_op jit(solution)/shard_map/ppermute | solution.py:218
  122.2 3.7 %collective-permute-done.7 = bf16[2,152,256]{2,1,0:T(8,128)(2,1)S(1)} collective-permute-done((bf16[2,152,256]{2,1,0:T(8,128)(2,1)S(1)}, bf16[2,152,256]{2,1,0:T(8,128)(2,1)S(1)}, u32[]{:S(2)}, u32[]{:S(2)}) %collective-permute-start.7) | collective-permute-done | bytes 155680 | tf_op jit(solution)/shard_map/ppermute | solution.py:218
  125.9 3.5 %all-to-all-start.4 = ((bf16[4,72,448]{2,1,0:T(8,128)(2,1)}), bf16[4,72,448]{2,1,0:T(8,128)(2,1)S(1)}, u32[]{:S(2)}, u32[]{:S(2)}) async-start(bf16[4,72,448]{2,1,0:T(8,128)(2,1)} %shard_map.63), calls=%async_computation.4 | async-start | bytes 589824 | tf_op jit(solution)/shard_map/all_to_all | solution.py:37
  129.5 5.2 %collective-permute-start.11 = (bf16[4,2,152,256]{3,2,1,0:T(8,128)(2,1)S(1)}, bf16[4,2,152,256]{3,2,1,0:T(8,128)(2,1)S(1)}, u32[]{:S(2)}, u32[]{:S(2)}) collective-permute-start(bf16[4,2,152,256]{3,2,1,0:T(8,128)(2,1)S(1)} %pad_maximum_fusion.own_ref), channel_id=1, source_target_pairs={{0,128},{128,0},{1,129},{129,1},{2,130},{130,2},{3,131},{131,3},{4... | collective-permute-start | bytes 1867784 | tf_op jit(solution)/shard_map/ppermute | solution.py:45
  135.1 6.3 %collective-permute-start.10 = (bf16[2,144,448]{2,1,0:T(8,128)(2,1)S(1)}, bf16[2,144,448]{2,1,0:T(8,128)(2,1)S(1)}, u32[]{:S(2)}, u32[]{:S(2)}) collective-permute-start(bf16[2,144,448]{2,1,0:T(8,128)(2,1)S(1)} %bitcast.18), channel_id=1, source_target_pairs={{0,128},{128,0},{1,129},{129,1},{2,130},{130,2},{3,131},{131,3},{4... | collective-permute-start | bytes 774152 | tf_op jit(solution)/shard_map/ppermute | solution.py:45
  142.6 4.1 %shard_map.66 = f32[448,1024]{1,0:T(8,128)} custom-call(s32[8]{0:T(128)S(1)} %stack.50.where_ref, bf16[2,448,144]{2,1,0:T(8,128)(2,1)S(1)} %shard_map.64.own_ref, bf16[2,144,448]{2,1,0:T(8,128)(2,1)S(1)} %collective-permute-done.10.other_ref, bf16[4,144,1024]{2,1,0:T(8,128)(2,1)S(1)} %get-tuple-element.29.in_ref, ...), custom_call_target="tpu_custom_call" | custom-call | tf_op jit(solution)/shard_map/pallas_call | solution.py:200
  (34 shorter events, 14.7 us)
Async XLA Ops:
  0.0 0.9 copy-start.2
  0.9 0.7 copy-start.3
  2.3 28.2 %collective-permute-start.1 = (bf16[144,256]{1,0:T(8,128)(2,1)S(1)}, bf16[144,256]{1,0:T(8,128)(2,1)S(1)}, u32[]{:S(2)}, u32[]{:S(2)}) collective-permute-start(bf16[144,256]{1,0:T(8,128)(2,1)S(1)} %shard_map.55), channel_id=1, source_target_pairs={{0,4},{1,5},{2,6},{3,7},{4,0},{5,1},{6,2},{7,3},{8,12},{9,13},{10,... | collective-permute-start | bytes 221192 | tf_op jit(solution)/shard_map/ppermute | solution.py:228
  15.1 15.3 %collective-permute-start = (bf16[144,256]{1,0:T(8,128)(2,1)S(1)}, bf16[144,256]{1,0:T(8,128)(2,1)S(1)}, u32[]{:S(2)}, u32[]{:S(2)}) collective-permute-start(bf16[144,256]{1,0:T(8,128)(2,1)S(1)} %shard_map.55), channel_id=1, source_target_pairs={{0,0},{1,1},{2,2},{3,3},{4,4},{5,5},{6,6},{7,7},{8,8},{9,9},{10,10... | collective-permute-start | bytes 221192 | tf_op jit(solution)/shard_map/ppermute | solution.py:227
  23.4 1.0 copy-start
  24.4 0.9 copy-start.1
  26.9 10.7 %all-to-all-start = ((bf16[4,144,256]{2,1,0:T(8,128)(2,1)}), bf16[4,144,256]{2,1,0:T(8,128)(2,1)S(1)}, u32[]{:S(2)}, u32[]{:S(2)}) async-start(bf16[4,144,256]{2,1,0:T(8,128)(2,1)} %shard_map.57), calls=%async_computation | async-start | bytes 589824 | tf_op jit(solution)/shard_map/all_to_all | solution.py:37
  30.4 11.6 %copy-start.4 = (bf16[1,1792,448]{1,2,0:T(8,128)(2,1)S(1)}, bf16[1,1792,448]{1,2,0:T(8,128)(2,1)}, u32[]{:S(2)}) copy-start(bf16[1,1792,448]{1,2,0:T(8,128)(2,1)} %param.8) | copy-start | bytes 4816900
  38.6 18.9 %all-to-all-start.1 = ((bf16[4,2,144,256]{3,2,1,0:T(8,128)(2,1)}), bf16[4,2,144,256]{3,2,1,0:T(8,128)(2,1)S(1)}, u32[]{:S(2)}, u32[]{:S(2)}) async-start(bf16[4,2,144,256]{3,2,1,0:T(8,128)(2,1)} %shard_map.58), calls=%async_computation.1 | async-start | bytes 1179648 | tf_op jit(solution)/shard_map/all_to_all | solution.py:37
  42.1 32.9 %collective-permute-start.5 = (bf16[448,1792]{1,0:T(8,128)(2,1)S(1)}, bf16[448,1792]{1,0:T(8,128)(2,1)}, u32[]{:S(2)}, u32[]{:S(2)}) collective-permute-start(bf16[448,1792]{1,0:T(8,128)(2,1)S(1)} %bitcast.21), channel_id=1, source_target_pairs={{0,128},{128,0},{1,129},{129,1},{2,130},{130,2},{3,131},{131,3},{4... | collective-permute-start | bytes 4816904 | tf_op jit(solution)/shard_map/ppermute | solution.py:45
  59.2 26.0 %collective-permute-start.4 = (bf16[144,1792]{1,0:T(8,128)(2,1)S(1)}, bf16[144,1792]{1,0:T(8,128)(2,1)S(1)}, u32[]{:S(2)}, u32[]{:S(2)}) collective-permute-start(bf16[144,1792]{1,0:T(8,128)(2,1)S(1)} %get-tuple-element.18.a_ref), channel_id=1, source_target_pairs={{0,24},{8,16},{16,8},{24,0},{1,25},{9,17},{17,9},{25,1},{2,26},{10... | collective-permute-start | bytes 1548296 | tf_op jit(solution)/shard_map/ppermute | solution.py:218
  62.0 23.2 %collective-permute-start.3 = (bf16[144,1792]{1,0:T(8,128)(2,1)S(1)}, bf16[144,1792]{1,0:T(8,128)(2,1)}, u32[]{:S(2)}, u32[]{:S(2)}) collective-permute-start(bf16[144,1792]{1,0:T(8,128)(2,1)S(1)} %get-tuple-element.18.a_ref), channel_id=1, source_target_pairs={{0,16},{8,24},{16,0},{24,8},{1,17},{9,25},{17,1},{25,9},{2,18},{10... | collective-permute-start | bytes 1548296 | tf_op jit(solution)/shard_map/ppermute | solution.py:218
  65.1 22.5 %collective-permute-start.2 = (bf16[144,1792]{1,0:T(8,128)(2,1)S(1)}, bf16[144,1792]{1,0:T(8,128)(2,1)}, u32[]{:S(2)}, u32[]{:S(2)}) collective-permute-start(bf16[144,1792]{1,0:T(8,128)(2,1)S(1)} %get-tuple-element.18.a_ref), channel_id=1, source_target_pairs={{0,8},{8,0},{16,24},{24,16},{1,9},{9,1},{17,25},{25,17},{2,10},{10... | collective-permute-start | bytes 1548296 | tf_op jit(solution)/shard_map/ppermute | solution.py:218
  68.2 23.4 %all-to-all-start.2 = ((bf16[16,80,128]{2,1,0:T(8,128)(2,1)}), bf16[16,80,128]{2,1,0:T(8,128)(2,1)S(1)}, u32[]{:S(2)}, u32[]{:S(2)}) async-start(bf16[16,80,128]{2,1,0:T(8,128)(2,1)} %get-tuple-element.19), calls=%async_computation.2 | async-start | bytes 655360 | tf_op jit(solution)/shard_map/all_to_all | solution.py:37
  91.5 9.7 %all-to-all-start.3 = ((bf16[4,72,448]{2,1,0:T(8,128)(2,1)}), bf16[4,72,448]{2,1,0:T(8,128)(2,1)S(1)}, u32[]{:S(2)}, u32[]{:S(2)}) async-start(bf16[4,72,448]{2,1,0:T(8,128)(2,1)} %shard_map.60), calls=%async_computation.3 | async-start | bytes 589824 | tf_op jit(solution)/shard_map/all_to_all | solution.py:37
  101.3 19.6 %collective-permute-start.6 = (bf16[72,448]{1,0:T(8,128)(2,1)S(1)}, bf16[72,448]{1,0:T(8,128)(2,1)S(1)}, u32[]{:S(2)}, u32[]{:S(2)}) collective-permute-start(bf16[72,448]{1,0:T(8,128)(2,1)S(1)} %shard_map.61.one_ref), channel_id=1, source_target_pairs={{0,256},{256,0},{1,257},{257,1},{2,258},{258,2},{3,259},{259,3},{4... | collective-permute-start | bytes 193544 | tf_op jit(solution)/shard_map/ppermute | solution.py:45
  111.9 9.8 %collective-permute-start.9 = (bf16[2,152,256]{2,1,0:T(8,128)(2,1)S(1)}, bf16[2,152,256]{2,1,0:T(8,128)(2,1)S(1)}, u32[]{:S(2)}, u32[]{:S(2)}) collective-permute-start(bf16[2,152,256]{2,1,0:T(8,128)(2,1)S(1)} %shard_map.62), channel_id=1, source_target_pairs={{0,24},{8,16},{16,8},{24,0},{1,25},{9,17},{17,9},{25,1},{2,26},{10... | collective-permute-start | bytes 466952 | tf_op jit(solution)/shard_map/ppermute | solution.py:218
  114.4 7.8 %collective-permute-start.8 = (bf16[2,152,256]{2,1,0:T(8,128)(2,1)S(1)}, bf16[2,152,256]{2,1,0:T(8,128)(2,1)S(1)}, u32[]{:S(2)}, u32[]{:S(2)}) collective-permute-start(bf16[2,152,256]{2,1,0:T(8,128)(2,1)S(1)} %shard_map.62), channel_id=1, source_target_pairs={{0,16},{8,24},{16,0},{24,8},{1,17},{9,25},{17,1},{25,9},{2,18},{10... | collective-permute-start | bytes 466952 | tf_op jit(solution)/shard_map/ppermute | solution.py:218
  118.5 7.4 %collective-permute-start.7 = (bf16[2,152,256]{2,1,0:T(8,128)(2,1)S(1)}, bf16[2,152,256]{2,1,0:T(8,128)(2,1)S(1)}, u32[]{:S(2)}, u32[]{:S(2)}) collective-permute-start(bf16[2,152,256]{2,1,0:T(8,128)(2,1)S(1)} %shard_map.62), channel_id=1, source_target_pairs={{0,8},{8,0},{16,24},{24,16},{1,9},{9,1},{17,25},{25,17},{2,10},{10... | collective-permute-start | bytes 466952 | tf_op jit(solution)/shard_map/ppermute | solution.py:218
  125.9 9.1 %all-to-all-start.4 = ((bf16[4,72,448]{2,1,0:T(8,128)(2,1)}), bf16[4,72,448]{2,1,0:T(8,128)(2,1)S(1)}, u32[]{:S(2)}, u32[]{:S(2)}) async-start(bf16[4,72,448]{2,1,0:T(8,128)(2,1)} %shard_map.63), calls=%async_computation.4 | async-start | bytes 589824 | tf_op jit(solution)/shard_map/all_to_all | solution.py:37
  129.5 12.1 %collective-permute-start.11 = (bf16[4,2,152,256]{3,2,1,0:T(8,128)(2,1)S(1)}, bf16[4,2,152,256]{3,2,1,0:T(8,128)(2,1)S(1)}, u32[]{:S(2)}, u32[]{:S(2)}) collective-permute-start(bf16[4,2,152,256]{3,2,1,0:T(8,128)(2,1)S(1)} %pad_maximum_fusion.own_ref), channel_id=1, source_target_pairs={{0,128},{128,0},{1,129},{129,1},{2,130},{130,2},{3,131},{131,3},{4... | collective-permute-start | bytes 1867784 | tf_op jit(solution)/shard_map/ppermute | solution.py:45
  135.1 7.5 %collective-permute-start.10 = (bf16[2,144,448]{2,1,0:T(8,128)(2,1)S(1)}, bf16[2,144,448]{2,1,0:T(8,128)(2,1)S(1)}, u32[]{:S(2)}, u32[]{:S(2)}) collective-permute-start(bf16[2,144,448]{2,1,0:T(8,128)(2,1)S(1)} %bitcast.18), channel_id=1, source_target_pairs={{0,128},{128,0},{1,129},{129,1},{2,130},{130,2},{3,131},{131,3},{4... | collective-permute-start | bytes 774152 | tf_op jit(solution)/shard_map/ppermute | solution.py:45

commit v7 on v6

--- a/solution.py
+++ b/solution.py
@@ -56,37 +56,37 @@
     return (source == line).astype(F32).astype(BF)
 
 
-def pack_kernel(len_ref, grads_ref, out_ref):
+def start_kernel(len_ref, grads_hbm, acts_hbm, basis_hbm, lines_ref, part_ref, *scratch):
+    held, sems = scratch[:3], scratch[3:]
+    copies = [
+        pltpu.make_async_copy(source, ref, sem)
+        for source, ref, sem in zip((acts_hbm, basis_hbm, grads_hbm), held, sems)
+    ]
+    for copy in copies:
+        copy.start()
+    acts_ref, basis_ref, grads_ref = held
     pick = chosen(len_ref[0, 0])
-    out_ref[:, :FEAT] = jnp.dot(pick, grads_ref[...], preferred_element_type=F32).astype(BF)
-    out_ref[:, FEAT:] = jnp.zeros((VALID, WIDE - FEAT), BF)
-
-
-def inputs_kernel(where_ref, acts_ref, basis_ref, out_ref):
-    pick = chosen(where_ref[2])
+    copies[0].wait()
     lines = jnp.dot(pick, acts_ref[...], preferred_element_type=F32).astype(BF)
+    copies[1].wait()
     for y in range(4):
-        out_ref[y] = jnp.dot(
+        part_ref[y] = jnp.dot(
             lines, basis_ref[:, y * WIDE : (y + 1) * WIDE], preferred_element_type=F32
         ).astype(BF)
-
-
-def pair_kernel(near_ref, far_ref, out_ref):
-    out_ref[0] = near_ref[...]
-    out_ref[1] = far_ref[...]
-
-
-def join_kernel(pair_ref, parts_ref, out_ref):
+    copies[2].wait()
+    lines_ref[:, :FEAT] = jnp.dot(pick, grads_ref[...], preferred_element_type=F32).astype(BF)
+    lines_ref[:, FEAT:] = jnp.zeros((VALID, WIDE - FEAT), BF)
+
+
+def join_kernel(near_ref, far_ref, parts_ref, out_ref):
     total = parts_ref[0].astype(F32)
     for y in range(1, 4):
         total += parts_ref[y].astype(F32)
     total = total.astype(BF)
     for d in range(4):
-        for w in range(2):
+        for w, ref in enumerate((near_ref, far_ref)):
             at = d * 64 + w * 32
-            out_ref[d, w] = jnp.concatenate(
-                [pair_ref[w][:, :FEAT], total[:, at : at + 32]], axis=1
-            )
+            out_ref[d, w] = jnp.concatenate([ref[:, :FEAT], total[:, at : at + 32]], axis=1)
 
 
 def sort_kernel(where_ref, both_ref, out_ref, in_ref):
@@ -223,16 +223,22 @@
     zhi, core, y, zh, zq = (lax.axis_index(a) for a in ("zhi", "core", "y", "zh", "zq"))
     crossed = (core != zhi).astype(jnp.int32)
     where = jnp.stack([zh, crossed, lengths[0, 0], core, zq, y, y & 1, y >> 1])
-    lines = call(pack_kernel, like(VALID, WIDE), lengths, grads)
+    lines, partial = pl.pallas_call(
+        start_kernel,
+        in_specs=[pl.BlockSpec(memory_space=pltpu.SMEM)] + [pl.BlockSpec(memory_space=pl.ANY)] * 3,
+        out_specs=[pl.BlockSpec(memory_space=pltpu.VMEM)] * 2,
+        out_shape=[like(VALID, WIDE), like(4, VALID, WIDE)],
+        scratch_shapes=[pltpu.VMEM(x.shape, BF) for x in (acts, basis_in, grads)]
+        + [pltpu.SemaphoreType.DMA] * 3,
+        compiler_params=pltpu.CompilerParams(vmem_limit_bytes=60 << 20),
+    )(lengths, grads, acts, basis_in)
     near = lax.ppermute(lines, PLANE, to_basis(False))
     far = lax.ppermute(lines, PLANE, to_basis(True))
-    partial = call(inputs_kernel, like(4, VALID, WIDE), where, acts, basis_in)
     partial = exchange(partial, "y")
     basis = basis_out[0].T
     cols = basis.shape[0]
     other_basis = swap(basis, "core")
-    both = call(pair_kernel, like(2, VALID, WIDE), near, far, scalars=0, cost=HINT)
-    both = call(join_kernel, like(4, 2, VALID, WIDE), both, partial, scalars=0)
+    both = call(join_kernel, like(4, 2, VALID, WIDE), near, far, partial, scalars=0)
     both = exchange(both, "zq")
     lines, ins = call(sort_kernel, [like(VALID, 8 * FEAT), like(16, 80, 128)], where, both)
     lines = [lines] + others(lines, "y")
@@ -254,7 +260,6 @@
     part, ins = lax.optimization_barrier((part, ins))
     ins = [ins] + others(ins, "y")
     part = call(spread_kernel, like(4, 72, cols), part, swap(part, "zhi"), scalars=0, cost=HINT)
-    part, ins = lax.optimization_barrier((part, ins))
     ins = jnp.stack(ins)
     other_ins = swap(ins, "core")
     outs = exchange(part, "x").reshape(2, VALID, cols)

time: 148 us -> 140 us (0.946)
  waiting for transfers between devices: 43.1 us -> 35.6 us
  local copies, waits for them, and re-layouts: 4.22 us -> 0.13 us
  starting transfers between devices: 84.2 us -> 87.7 us
    all_to_all x5, waiting for transfers between devices: 25.9 us -> 17.4 us  [exchange(): return lax.all_to_all(x, axis, 0, 0, tiled=True)]
    ppermute x6, starting transfers between devices: 17.9 us -> 23.8 us  [others(): lax.ppermute(x, axis, [(i, i ^ k) for i in range(n)])]
    ppermute x4, starting transfers between devices: 24.7 us -> 20.5 us  [swap(): return lax.ppermute(x, axis, [(0, 1), (1, 0)])]
    unnamed x10 -> x4, local copies, waits for them, and re-layouts: 3.49 us -> 0.01 us
    pallas_call x0 -> x1, Pallas kernels: none -> 2.97 us  [per_device(): pl.pallas_call(start_kernel, in_specs=[pl.BlockSpec(memory_space=pltpu.SM...]
    ppermute x1, waiting for transfers between devices: 0.01 us -> 2.61 us  [per_device(): near = lax.ppermute(lines, PLANE, to_basis(False))]
    all_to_all x5, starting transfers between devices: 21.2 us -> 23.6 us  [exchange(): return lax.all_to_all(x, axis, 0, 0, tiled=True)]
    pallas_call x12 -> x9, Pallas kernels: 14.8 us -> 12.6 us  [call(): pl.pallas_call(kernel, in_specs=[smem] * scalars + [vmem] * (len(args) -...]
  transfers between devices with their start and end apart: 17 -> 17, of which waited for: 9 -> 7; matrix products, arithmetic and copies ran while one was open for 1% -> 0% of each run, Pallas kernels for 6% -> 5%
where the time goes in v7:
time: 140 us; the launch traced here: 139 us
  starting transfers between devices  87.7 us (63%)
  waiting for transfers between devices  35.6 us (25%)
  Pallas kernels  15.6 us (11%)
    ppermute x6, starting transfers between devices, others(): lax.ppermute(x, axis, [(i, i ^ k) for i in range(n)])  23.8 us
    all_to_all x5, starting transfers between devices, exchange(): return lax.all_to_all(x, axis, 0, 0, tiled=True)  23.6 us
    ppermute x4, starting transfers between devices, swap(): return lax.ppermute(x, axis, [(0, 1), (1, 0)])  20.5 us
    all_to_all x5, waiting for transfers between devices, exchange(): return lax.all_to_all(x, axis, 0, 0, tiled=True)  17.4 us
    ppermute x6, waiting for transfers between devices, others(): lax.ppermute(x, axis, [(i, i ^ k) for i in range(n)])  15 us
    pallas_call x9, Pallas kernels, call(): pl.pallas_call(kernel, in_specs=[smem] * scalars + [vmem] * (len(args) -...  12.6 us
    ppermute x1, starting transfers between devices, per_device(): far = lax.ppermute(lines, PLANE, to_basis(True))  12.6 us
    ppermute x1, starting transfers between devices, per_device(): near = lax.ppermute(lines, PLANE, to_basis(False))  7.21 us
  transfers between devices with their start and end apart: 17, of which 7 were waited for; matrix products, arithmetic and copies ran while one was open for 0% of the time, Pallas kernels for 5%

profile of v7, /device:TPU:1, one launch (start us, length us, event | category | flops | bytes accessed | tf_op | source)
XLA Modules:
  0.0 139.4 jit_solution(12165162210424565733)
XLA Ops:
  0.0 3.0 %shard_map.55 = (bf16[144,256]{1,0:T(8,128)(2,1)}, bf16[4,144,256]{2,1,0:T(8,128)(2,1)}) custom-call(s32[1,2]{1,0:T(1,128)} %len_ref.1, bf16[192,224]{1,0:T(8,128)(2,1)} %grads_hbm.1, bf16[192,256]{1,0:T(8,128)(2,1)} %acts_hbm.1, bf16[256,1024]{1,0:T(8,128)(2,1)} %basis_hbm.1), custom_call_target="tpu_custom_call" | custom-call | tf_op jit(solution)/shard_map/pallas_call | solution.py:226
  3.0 5.0 %all-to-all-start = ((bf16[4,144,256]{2,1,0:T(8,128)(2,1)}), bf16[4,144,256]{2,1,0:T(8,128)(2,1)S(1)}, u32[]{:S(2)}, u32[]{:S(2)}) async-start(bf16[4,144,256]{2,1,0:T(8,128)(2,1)} %get-tuple-element.16), calls=%async_computation | async-start | bytes 589824 | tf_op jit(solution)/shard_map/all_to_all | solution.py:37
  8.0 12.6 %collective-permute-start.1 = (bf16[144,256]{1,0:T(8,128)(2,1)}, bf16[144,256]{1,0:T(8,128)(2,1)S(1)}, u32[]{:S(2)}, u32[]{:S(2)}) collective-permute-start(bf16[144,256]{1,0:T(8,128)(2,1)} %get-tuple-element.15), channel_id=1, source_target_pairs={{0,4},{1,5},{2,6},{3,7},{4,0},{5,1},{6,2},{7,3},{8,12},{9,13},{10,... | collective-permute-start | bytes 221192 | tf_op jit(solution)/shard_map/ppermute | solution.py:236
  20.6 7.2 %collective-permute-start = (bf16[144,256]{1,0:T(8,128)(2,1)}, bf16[144,256]{1,0:T(8,128)(2,1)S(1)}, u32[]{:S(2)}, u32[]{:S(2)}) collective-permute-start(bf16[144,256]{1,0:T(8,128)(2,1)} %get-tuple-element.15), channel_id=1, source_target_pairs={{0,0},{1,1},{2,2},{3,3},{4,4},{5,5},{6,6},{7,7},{8,8},{9,9},{10,10... | collective-permute-start | bytes 221192 | tf_op jit(solution)/shard_map/ppermute | solution.py:235
  27.9 2.6 %collective-permute-done.near_ref = bf16[144,256]{1,0:T(8,128)(2,1)S(1)} collective-permute-done((bf16[144,256]{1,0:T(8,128)(2,1)}, bf16[144,256]{1,0:T(8,128)(2,1)S(1)}, u32[]{:S(2)}, u32[]{:S(2)}) %collective-permute-start) | collective-permute-done | bytes 73760 | tf_op jit(solution)/shard_map/ppermute | solution.py:235
  31.4 6.6 %all-to-all-start.1 = ((bf16[4,2,144,256]{3,2,1,0:T(8,128)(2,1)}), bf16[4,2,144,256]{3,2,1,0:T(8,128)(2,1)S(1)}, u32[]{:S(2)}, u32[]{:S(2)}) async-start(bf16[4,2,144,256]{3,2,1,0:T(8,128)(2,1)} %shard_map.56), calls=%async_computation.1 | async-start | bytes 1179648 | tf_op jit(solution)/shard_map/all_to_all | solution.py:37
  40.1 11.8 %all-to-all-done.1.both_ref = bf16[4,2,144,256]{3,2,1,0:T(8,128)(2,1)S(1)} async-done(((bf16[4,2,144,256]{3,2,1,0:T(8,128)(2,1)}), bf16[4,2,144,256]{3,2,1,0:T(8,128)(2,1)S(1)}, u32[]{:S(2)}, u32[]{:S(2)}) %all-to-all-start.1) | async-done | bytes 589856 | tf_op jit(solution)/shard_map/all_to_all | solution.py:37
  53.6 9.0 %collective-permute-start.4 = (bf16[144,1792]{1,0:T(8,128)(2,1)S(1)}, bf16[144,1792]{1,0:T(8,128)(2,1)}, u32[]{:S(2)}, u32[]{:S(2)}) collective-permute-start(bf16[144,1792]{1,0:T(8,128)(2,1)S(1)} %get-tuple-element.17.a_ref), channel_id=1, source_target_pairs={{0,24},{8,16},{16,8},{24,0},{1,25},{9,17},{17,9},{25,1},{2,26},{10... | collective-permute-start | bytes 1548296 | tf_op jit(solution)/shard_map/ppermute | solution.py:218
  62.6 2.6 %collective-permute-start.3 = (bf16[144,1792]{1,0:T(8,128)(2,1)S(1)}, bf16[144,1792]{1,0:T(8,128)(2,1)}, u32[]{:S(2)}, u32[]{:S(2)}) collective-permute-start(bf16[144,1792]{1,0:T(8,128)(2,1)S(1)} %get-tuple-element.17.a_ref), channel_id=1, source_target_pairs={{0,16},{8,24},{16,0},{24,8},{1,17},{9,25},{17,1},{25,9},{2,18},{10... | collective-permute-start | bytes 1548296 | tf_op jit(solution)/shard_map/ppermute | solution.py:218
  65.2 1.9 %collective-permute-start.2 = (bf16[144,1792]{1,0:T(8,128)(2,1)S(1)}, bf16[144,1792]{1,0:T(8,128)(2,1)}, u32[]{:S(2)}, u32[]{:S(2)}) collective-permute-start(bf16[144,1792]{1,0:T(8,128)(2,1)S(1)} %get-tuple-element.17.a_ref), channel_id=1, source_target_pairs={{0,8},{8,0},{16,24},{24,16},{1,9},{9,1},{17,25},{25,17},{2,10},{10... | collective-permute-start | bytes 1548296 | tf_op jit(solution)/shard_map/ppermute | solution.py:218
  67.1 4.6 %all-to-all-start.2 = ((bf16[16,80,128]{2,1,0:T(8,128)(2,1)}), bf16[16,80,128]{2,1,0:T(8,128)(2,1)S(1)}, u32[]{:S(2)}, u32[]{:S(2)}) async-start(bf16[16,80,128]{2,1,0:T(8,128)(2,1)} %get-tuple-element.18), calls=%async_computation.2 | async-start | bytes 655360 | tf_op jit(solution)/shard_map/all_to_all | solution.py:37
  71.7 12.7 %collective-permute-done.4.d_ref = bf16[144,1792]{1,0:T(8,128)(2,1)} collective-permute-done((bf16[144,1792]{1,0:T(8,128)(2,1)S(1)}, bf16[144,1792]{1,0:T(8,128)(2,1)}, u32[]{:S(2)}, u32[]{:S(2)}) %collective-permute-start.4) | collective-permute-done | bytes 516128 | tf_op jit(solution)/shard_map/ppermute | solution.py:218
  84.4 2.3 %collective-permute-done.2.b_ref = bf16[144,1792]{1,0:T(8,128)(2,1)} collective-permute-done((bf16[144,1792]{1,0:T(8,128)(2,1)S(1)}, bf16[144,1792]{1,0:T(8,128)(2,1)}, u32[]{:S(2)}, u32[]{:S(2)}) %collective-permute-start.2) | collective-permute-done | bytes 516128 | tf_op jit(solution)/shard_map/ppermute | solution.py:218
  86.7 4.1 %shard_map.58 = bf16[4,72,448]{2,1,0:T(8,128)(2,1)} custom-call(s32[8]{0:T(128)S(1)} %stack.50.where_ref, bf16[144,1792]{1,0:T(8,128)(2,1)S(1)} %get-tuple-element.17.a_ref, bf16[144,1792]{1,0:T(8,128)(2,1)} %collective-permute-done.2.b_ref, bf16[144,1792]{1,0:T(8,128)(2,1)} %collective-permute-done.3.c_ref, bf16[144,1792]{1,0:T(8,128)(2,1)} %collective-permute-done.4.d_ref, ...), custom_call_target="tpu_custom_call" | custom-call | flops 30000001024 | bytes 1000000 | tf_op jit(solution)/shard_map/pallas_call | solution.py:200
  90.8 4.0 %all-to-all-start.3 = ((bf16[4,72,448]{2,1,0:T(8,128)(2,1)}), bf16[4,72,448]{2,1,0:T(8,128)(2,1)S(1)}, u32[]{:S(2)}, u32[]{:S(2)}) async-start(bf16[4,72,448]{2,1,0:T(8,128)(2,1)} %shard_map.58), calls=%async_computation.3 | async-start | bytes 589824 | tf_op jit(solution)/shard_map/all_to_all | solution.py:37
  94.9 5.6 %all-to-all-done.3.parts_ref = bf16[4,72,448]{2,1,0:T(8,128)(2,1)S(1)} async-done(((bf16[4,72,448]{2,1,0:T(8,128)(2,1)}), bf16[4,72,448]{2,1,0:T(8,128)(2,1)S(1)}, u32[]{:S(2)}, u32[]{:S(2)}) %all-to-all-start.3) | async-done | bytes 258080 | tf_op jit(solution)/shard_map/all_to_all | solution.py:37
  100.5 4.7 %collective-permute-start.6 = (bf16[72,448]{1,0:T(8,128)(2,1)S(1)}, bf16[72,448]{1,0:T(8,128)(2,1)S(1)}, u32[]{:S(2)}, u32[]{:S(2)}) collective-permute-start(bf16[72,448]{1,0:T(8,128)(2,1)S(1)} %shard_map.59.one_ref), channel_id=1, source_target_pairs={{0,256},{256,0},{1,257},{257,1},{2,258},{258,2},{3,259},{259,3},{4... | collective-permute-start | bytes 193544 | tf_op jit(solution)/shard_map/ppermute | solution.py:45
  105.2 5.4 %collective-permute-start.10 = (bf16[2,152,256]{2,1,0:T(8,128)(2,1)S(1)}, bf16[2,152,256]{2,1,0:T(8,128)(2,1)S(1)}, u32[]{:S(2)}, u32[]{:S(2)}) collective-permute-start(bf16[2,152,256]{2,1,0:T(8,128)(2,1)S(1)} %shard_map.60), channel_id=1, source_target_pairs={{0,24},{8,16},{16,8},{24,0},{1,25},{9,17},{17,9},{25,1},{2,26},{10... | collective-permute-start | bytes 466952 | tf_op jit(solution)/shard_map/ppermute | solution.py:218
  110.6 3.0 %collective-permute-start.9 = (bf16[2,152,256]{2,1,0:T(8,128)(2,1)S(1)}, bf16[2,152,256]{2,1,0:T(8,128)(2,1)S(1)}, u32[]{:S(2)}, u32[]{:S(2)}) collective-permute-start(bf16[2,152,256]{2,1,0:T(8,128)(2,1)S(1)} %shard_map.60), channel_id=1, source_target_pairs={{0,16},{8,24},{16,0},{24,8},{1,17},{9,25},{17,1},{25,9},{2,18},{10... | collective-permute-start | bytes 466952 | tf_op jit(solution)/shard_map/ppermute | solution.py:218
  113.6 1.9 %collective-permute-start.8 = (bf16[2,152,256]{2,1,0:T(8,128)(2,1)S(1)}, bf16[2,152,256]{2,1,0:T(8,128)(2,1)S(1)}, u32[]{:S(2)}, u32[]{:S(2)}) collective-permute-start(bf16[2,152,256]{2,1,0:T(8,128)(2,1)S(1)} %shard_map.60), channel_id=1, source_target_pairs={{0,8},{8,0},{16,24},{24,16},{1,9},{9,1},{17,25},{25,17},{2,10},{10... | collective-permute-start | bytes 466952 | tf_op jit(solution)/shard_map/ppermute | solution.py:218
  116.6 3.5 %all-to-all-start.4 = ((bf16[4,72,448]{2,1,0:T(8,128)(2,1)}), bf16[4,72,448]{2,1,0:T(8,128)(2,1)S(1)}, u32[]{:S(2)}, u32[]{:S(2)}) async-start(bf16[4,72,448]{2,1,0:T(8,128)(2,1)} %shard_map.61), calls=%async_computation.4 | async-start | bytes 589824 | tf_op jit(solution)/shard_map/all_to_all | solution.py:37
  120.2 7.9 %collective-permute-start.11 = (bf16[4,2,152,256]{3,2,1,0:T(8,128)(2,1)S(1)}, bf16[4,2,152,256]{3,2,1,0:T(8,128)(2,1)S(1)}, u32[]{:S(2)}, u32[]{:S(2)}) collective-permute-start(bf16[4,2,152,256]{3,2,1,0:T(8,128)(2,1)S(1)} %pad_maximum_fusion.own_ref), channel_id=1, source_target_pairs={{0,128},{128,0},{1,129},{129,1},{2,130},{130,2},{3,131},{131,3},{4... | collective-permute-start | bytes 1867784 | tf_op jit(solution)/shard_map/ppermute | solution.py:45
  128.1 6.0 %collective-permute-start.7 = (bf16[2,144,448]{2,1,0:T(8,128)(2,1)S(1)}, bf16[2,144,448]{2,1,0:T(8,128)(2,1)S(1)}, u32[]{:S(2)}, u32[]{:S(2)}) collective-permute-start(bf16[2,144,448]{2,1,0:T(8,128)(2,1)S(1)} %bitcast.18), channel_id=1, source_target_pairs={{0,128},{128,0},{1,129},{129,1},{2,130},{130,2},{3,131},{131,3},{4... | collective-permute-start | bytes 774152 | tf_op jit(solution)/shard_map/ppermute | solution.py:45
  135.3 4.1 %shard_map.64 = f32[448,1024]{1,0:T(8,128)} custom-call(s32[8]{0:T(128)S(1)} %stack.50.where_ref, bf16[2,448,144]{2,1,0:T(8,128)(2,1)S(1)} %shard_map.62.own_ref, bf16[2,144,448]{2,1,0:T(8,128)(2,1)S(1)} %collective-permute-done.7.other_ref, bf16[4,144,1024]{2,1,0:T(8,128)(2,1)S(1)} %get-tuple-element.23.in_ref, ...), custom_call_target="tpu_custom_call" | custom-call | tf_op jit(solution)/shard_map/pallas_call | solution.py:200
  (26 shorter events, 7.2 us)
Async XLA Ops:
  0.0 38.0 %copy-start = (bf16[1,1792,448]{1,2,0:T(8,128)(2,1)S(1)}, bf16[1,1792,448]{1,2,0:T(8,128)(2,1)}, u32[]{:S(2)}) copy-start(bf16[1,1792,448]{1,2,0:T(8,128)(2,1)} %param.8) | copy-start | bytes 4816900
  3.0 37.0 %copy-start.1 = (s32[1,2]{1,0:T(1,128)S(1)}, s32[1,2]{1,0:T(1,128)}, u32[]{:S(2)}) copy-start(s32[1,2]{1,0:T(1,128)} %len_ref.1) | copy-start | bytes 28
  3.0 27.5 %all-to-all-start = ((bf16[4,144,256]{2,1,0:T(8,128)(2,1)}), bf16[4,144,256]{2,1,0:T(8,128)(2,1)S(1)}, u32[]{:S(2)}, u32[]{:S(2)}) async-start(bf16[4,144,256]{2,1,0:T(8,128)(2,1)} %get-tuple-element.16), calls=%async_computation | async-start | bytes 589824 | tf_op jit(solution)/shard_map/all_to_all | solution.py:37
  8.0 19.8 %collective-permute-start.1 = (bf16[144,256]{1,0:T(8,128)(2,1)}, bf16[144,256]{1,0:T(8,128)(2,1)S(1)}, u32[]{:S(2)}, u32[]{:S(2)}) collective-permute-start(bf16[144,256]{1,0:T(8,128)(2,1)} %get-tuple-element.15), channel_id=1, source_target_pairs={{0,4},{1,5},{2,6},{3,7},{4,0},{5,1},{6,2},{7,3},{8,12},{9,13},{10,... | collective-permute-start | bytes 221192 | tf_op jit(solution)/shard_map/ppermute | solution.py:236
  20.6 9.8 %collective-permute-start = (bf16[144,256]{1,0:T(8,128)(2,1)}, bf16[144,256]{1,0:T(8,128)(2,1)S(1)}, u32[]{:S(2)}, u32[]{:S(2)}) collective-permute-start(bf16[144,256]{1,0:T(8,128)(2,1)} %get-tuple-element.15), channel_id=1, source_target_pairs={{0,0},{1,1},{2,2},{3,3},{4,4},{5,5},{6,6},{7,7},{8,8},{9,9},{10,10... | collective-permute-start | bytes 221192 | tf_op jit(solution)/shard_map/ppermute | solution.py:235
  31.4 20.5 %all-to-all-start.1 = ((bf16[4,2,144,256]{3,2,1,0:T(8,128)(2,1)}), bf16[4,2,144,256]{3,2,1,0:T(8,128)(2,1)S(1)}, u32[]{:S(2)}, u32[]{:S(2)}) async-start(bf16[4,2,144,256]{3,2,1,0:T(8,128)(2,1)} %shard_map.56), calls=%async_computation.1 | async-start | bytes 1179648 | tf_op jit(solution)/shard_map/all_to_all | solution.py:37
  38.0 33.7 %collective-permute-start.5 = (bf16[448,1792]{1,0:T(8,128)(2,1)S(1)}, bf16[448,1792]{1,0:T(8,128)(2,1)}, u32[]{:S(2)}, u32[]{:S(2)}) collective-permute-start(bf16[448,1792]{1,0:T(8,128)(2,1)S(1)} %bitcast.20), channel_id=1, source_target_pairs={{0,128},{128,0},{1,129},{129,1},{2,130},{130,2},{3,131},{131,3},{4... | collective-permute-start | bytes 4816904 | tf_op jit(solution)/shard_map/ppermute | solution.py:45
  53.6 30.8 %collective-permute-start.4 = (bf16[144,1792]{1,0:T(8,128)(2,1)S(1)}, bf16[144,1792]{1,0:T(8,128)(2,1)}, u32[]{:S(2)}, u32[]{:S(2)}) collective-permute-start(bf16[144,1792]{1,0:T(8,128)(2,1)S(1)} %get-tuple-element.17.a_ref), channel_id=1, source_target_pairs={{0,24},{8,16},{16,8},{24,0},{1,25},{9,17},{17,9},{25,1},{2,26},{10... | collective-permute-start | bytes 1548296 | tf_op jit(solution)/shard_map/ppermute | solution.py:218
  62.6 21.7 %collective-permute-start.3 = (bf16[144,1792]{1,0:T(8,128)(2,1)S(1)}, bf16[144,1792]{1,0:T(8,128)(2,1)}, u32[]{:S(2)}, u32[]{:S(2)}) collective-permute-start(bf16[144,1792]{1,0:T(8,128)(2,1)S(1)} %get-tuple-element.17.a_ref), channel_id=1, source_target_pairs={{0,16},{8,24},{16,0},{24,8},{1,17},{9,25},{17,1},{25,9},{2,18},{10... | collective-permute-start | bytes 1548296 | tf_op jit(solution)/shard_map/ppermute | solution.py:218
  65.2 21.5 %collective-permute-start.2 = (bf16[144,1792]{1,0:T(8,128)(2,1)S(1)}, bf16[144,1792]{1,0:T(8,128)(2,1)}, u32[]{:S(2)}, u32[]{:S(2)}) collective-permute-start(bf16[144,1792]{1,0:T(8,128)(2,1)S(1)} %get-tuple-element.17.a_ref), channel_id=1, source_target_pairs={{0,8},{8,0},{16,24},{24,16},{1,9},{9,1},{17,25},{25,17},{2,10},{10... | collective-permute-start | bytes 1548296 | tf_op jit(solution)/shard_map/ppermute | solution.py:218
  67.1 23.6 %all-to-all-start.2 = ((bf16[16,80,128]{2,1,0:T(8,128)(2,1)}), bf16[16,80,128]{2,1,0:T(8,128)(2,1)S(1)}, u32[]{:S(2)}, u32[]{:S(2)}) async-start(bf16[16,80,128]{2,1,0:T(8,128)(2,1)} %get-tuple-element.18), calls=%async_computation.2 | async-start | bytes 655360 | tf_op jit(solution)/shard_map/all_to_all | solution.py:37
  90.8 9.7 %all-to-all-start.3 = ((bf16[4,72,448]{2,1,0:T(8,128)(2,1)}), bf16[4,72,448]{2,1,0:T(8,128)(2,1)S(1)}, u32[]{:S(2)}, u32[]{:S(2)}) async-start(bf16[4,72,448]{2,1,0:T(8,128)(2,1)} %shard_map.58), calls=%async_computation.3 | async-start | bytes 589824 | tf_op jit(solution)/shard_map/all_to_all | solution.py:37
  100.5 15.4 %collective-permute-start.6 = (bf16[72,448]{1,0:T(8,128)(2,1)S(1)}, bf16[72,448]{1,0:T(8,128)(2,1)S(1)}, u32[]{:S(2)}, u32[]{:S(2)}) collective-permute-start(bf16[72,448]{1,0:T(8,128)(2,1)S(1)} %shard_map.59.one_ref), channel_id=1, source_target_pairs={{0,256},{256,0},{1,257},{257,1},{2,258},{258,2},{3,259},{259,3},{4... | collective-permute-start | bytes 193544 | tf_op jit(solution)/shard_map/ppermute | solution.py:45
  105.2 14.9 %collective-permute-start.10 = (bf16[2,152,256]{2,1,0:T(8,128)(2,1)S(1)}, bf16[2,152,256]{2,1,0:T(8,128)(2,1)S(1)}, u32[]{:S(2)}, u32[]{:S(2)}) collective-permute-start(bf16[2,152,256]{2,1,0:T(8,128)(2,1)S(1)} %shard_map.60), channel_id=1, source_target_pairs={{0,24},{8,16},{16,8},{24,0},{1,25},{9,17},{17,9},{25,1},{2,26},{10... | collective-permute-start | bytes 466952 | tf_op jit(solution)/shard_map/ppermute | solution.py:218
  110.6 9.5 %collective-permute-start.9 = (bf16[2,152,256]{2,1,0:T(8,128)(2,1)S(1)}, bf16[2,152,256]{2,1,0:T(8,128)(2,1)S(1)}, u32[]{:S(2)}, u32[]{:S(2)}) collective-permute-start(bf16[2,152,256]{2,1,0:T(8,128)(2,1)S(1)} %shard_map.60), channel_id=1, source_target_pairs={{0,16},{8,24},{16,0},{24,8},{1,17},{9,25},{17,1},{25,9},{2,18},{10... | collective-permute-start | bytes 466952 | tf_op jit(solution)/shard_map/ppermute | solution.py:218
  113.6 6.5 %collective-permute-start.8 = (bf16[2,152,256]{2,1,0:T(8,128)(2,1)S(1)}, bf16[2,152,256]{2,1,0:T(8,128)(2,1)S(1)}, u32[]{:S(2)}, u32[]{:S(2)}) collective-permute-start(bf16[2,152,256]{2,1,0:T(8,128)(2,1)S(1)} %shard_map.60), channel_id=1, source_target_pairs={{0,8},{8,0},{16,24},{24,16},{1,9},{9,1},{17,25},{25,17},{2,10},{10... | collective-permute-start | bytes 466952 | tf_op jit(solution)/shard_map/ppermute | solution.py:218
  116.6 11.5 %all-to-all-start.4 = ((bf16[4,72,448]{2,1,0:T(8,128)(2,1)}), bf16[4,72,448]{2,1,0:T(8,128)(2,1)S(1)}, u32[]{:S(2)}, u32[]{:S(2)}) async-start(bf16[4,72,448]{2,1,0:T(8,128)(2,1)} %shard_map.61), calls=%async_computation.4 | async-start | bytes 589824 | tf_op jit(solution)/shard_map/all_to_all | solution.py:37
  120.2 14.1 %collective-permute-start.11 = (bf16[4,2,152,256]{3,2,1,0:T(8,128)(2,1)S(1)}, bf16[4,2,152,256]{3,2,1,0:T(8,128)(2,1)S(1)}, u32[]{:S(2)}, u32[]{:S(2)}) collective-permute-start(bf16[4,2,152,256]{3,2,1,0:T(8,128)(2,1)S(1)} %pad_maximum_fusion.own_ref), channel_id=1, source_target_pairs={{0,128},{128,0},{1,129},{129,1},{2,130},{130,2},{3,131},{131,3},{4... | collective-permute-start | bytes 1867784 | tf_op jit(solution)/shard_map/ppermute | solution.py:45
  128.1 7.2 %collective-permute-start.7 = (bf16[2,144,448]{2,1,0:T(8,128)(2,1)S(1)}, bf16[2,144,448]{2,1,0:T(8,128)(2,1)S(1)}, u32[]{:S(2)}, u32[]{:S(2)}) collective-permute-start(bf16[2,144,448]{2,1,0:T(8,128)(2,1)S(1)} %bitcast.18), channel_id=1, source_target_pairs={{0,128},{128,0},{1,129},{129,1},{2,130},{130,2},{3,131},{131,3},{4... | collective-permute-start | bytes 774152 | tf_op jit(solution)/shard_map/ppermute | solution.py:45

commit v8 on v7

--- a/solution.py
+++ b/solution.py
@@ -28,7 +28,8 @@
                 for z in range(8):
                     crossed = zhi != y >> 1
                     to = (z ^ 3 if far else z ^ 4) if crossed else (z ^ 4 if far else z)
-                    there = place(y >> 1, zhi, core * 2 + (y & 1), to)
+                    to_y = 2 * (core ^ (y >> 1)) + ((y & 1) ^ core)
+                    there = place(y >> 1, zhi, to_y, to)
                     pairs.append((place(zhi, core, y, z), there))
     return pairs
 
@@ -89,12 +90,15 @@
             out_ref[d, w] = jnp.concatenate([ref[:, :FEAT], total[:, at : at + 32]], axis=1)
 
 
-def sort_kernel(where_ref, both_ref, out_ref, in_ref):
+def sort_kernel(where_ref, both_ref, out_ref):
     zh, crossed = where_ref[0], where_ref[1]
     for f in range(8):
         far = (jnp.int32(f // 4) != zh).astype(jnp.int32) ^ crossed
         at = (f % 4) ^ (3 * (far & crossed))
         out_ref[:, f * FEAT : (f + 1) * FEAT] = both_ref[at, far][:, :FEAT]
+
+
+def pack_kernel(where_ref, both_ref, in_ref):
     sums = []
     for w in range(2):
         total = both_ref[0, w][:, FEAT:].astype(F32)
@@ -122,17 +126,48 @@
             out_ref[zhi, VALID:, h * 128 : h * 128 + 128] = parts_ref[zhi * 8, half:]
 
 
-def project_kernel(where_ref, a_ref, b_ref, c_ref, d_ref, own_ref, other_ref, out_ref, held):
-    yh, same = where_ref[7], where_ref[3] == where_ref[6]
-    for left_ref, right_ref, t in ((a_ref, b_ref, yh), (c_ref, d_ref, 1 - yh)):
+def project_kernel(
+    where_ref, a_ref, b_ref, c_ref, d_ref, own_ref, other_ref, out_ref, held, total_ref
+):
+    step = pl.program_id(0)
+    tokens, same = where_ref[7], where_ref[3] == where_ref[6]
+    for left_ref, right_ref, t in ((a_ref, b_ref, tokens), (d_ref, c_ref, 1 - tokens)):
         left, right = left_ref[...], right_ref[...]
         held[0, t] = jnp.where(same, left, right)
         held[1, t] = jnp.where(same, right, left)
     rows = (2 * VALID, held.shape[3])
     total = across(held[0].reshape(rows), own_ref[...])
     total += across(held[1].reshape(rows), other_ref[...])
-    for h in range(4):
-        out_ref[h] = total[h * 72 : (h + 1) * 72].astype(BF)
+
+    @pl.when(step == 0)
+    def _():
+        total_ref[...] = total
+
+    @pl.when(step > 0)
+    def _():
+        total_ref[...] += total
+
+    @pl.when(step == pl.num_programs(0) - 1)
+    def _():
+        for h in range(4):
+            out_ref[h] = total_ref[h * 72 : (h + 1) * 72].astype(BF)
+
+
+def project(where, lines, basis, other_basis):
+    cols, rows = basis.shape
+    deep = rows // 2
+    line = pl.BlockSpec((VALID, deep), lambda k: (0, k))
+    rotated = pl.BlockSpec((cols, deep), lambda k: (0, k))
+    return pl.pallas_call(
+        project_kernel,
+        grid=(rows // deep,),
+        in_specs=[pl.BlockSpec(memory_space=pltpu.SMEM)] + [line] * 4 + [rotated] * 2,
+        out_specs=pl.BlockSpec((4, 72, cols), lambda k: (0, 0, 0)),
+        out_shape=like(4, 72, cols),
+        scratch_shapes=[pltpu.VMEM((2, 2, VALID, deep), BF), pltpu.VMEM((2 * VALID, cols), F32)],
+        compiler_params=PARAMS,
+        cost_estimate=LONG,
+    )(where, *lines, basis, other_basis)
 
 
 def sum_kernel(parts_ref, out_ref):
@@ -170,26 +205,49 @@
 
 def square_kernel(where_ref, own_ref, other_ref, in_ref, mask_ref, eig_ref, left_ref):
     core = where_ref[3]
-    for t in range(2):
-        for at, lines in (
-            (2 * core + t, own_ref[t]),
-            (2 * (1 - core) + t, other_ref[t].T),
-        ):
-            first = lines * mask_ref[at][:1]
-            left_ref[2 * at] = first
-            left_ref[2 * at + 1] = lines - first
-    rows, cols = 224, 256
-    for i in range(1024 // cols):
-        for o in range(448 // rows):
-            total = jnp.zeros((rows, cols), F32)
-            for s in range(8):
-                block = jnp.dot(
-                    left_ref[s, o * rows : (o + 1) * rows, :],
-                    in_ref[s // 2, :, i * cols : (i + 1) * cols],
-                    preferred_element_type=F32,
-                )
-                total += block * block
-            eig_ref[o * rows : (o + 1) * rows, i * cols : (i + 1) * cols] = total / 768.0
+
+    @pl.when(pl.program_id(0) == 0)
+    def _():
+        for t in range(2):
+            for at, lines in (
+                (2 * core + t, own_ref[t]),
+                (2 * (1 - core) + t, other_ref[t].T),
+            ):
+                first = lines * mask_ref[at][:1]
+                left_ref[2 * at] = first
+                left_ref[2 * at + 1] = lines - first
+
+    rows = 224
+    for o in range(448 // rows):
+        total = jnp.zeros((rows, eig_ref.shape[1]), F32)
+        for s in range(8):
+            block = jnp.dot(
+                left_ref[s, o * rows : (o + 1) * rows, :],
+                in_ref[s // 2],
+                preferred_element_type=F32,
+            )
+            total += block * block
+        eig_ref[o * rows : (o + 1) * rows] = total / 768.0
+
+
+def squares(where, left, other, ins, masks):
+    cols, wide, tile = left.shape[1], ins.shape[2], 256
+    whole = lambda x: pl.BlockSpec(x.shape, lambda i: (0, 0, 0))
+    return pl.pallas_call(
+        square_kernel,
+        grid=(wide // tile,),
+        in_specs=[
+            pl.BlockSpec(memory_space=pltpu.SMEM),
+            whole(left),
+            whole(other),
+            pl.BlockSpec((4, VALID, tile), lambda i: (0, 0, i)),
+            whole(masks),
+        ],
+        out_specs=pl.BlockSpec((cols, tile), lambda i: (0, i)),
+        out_shape=like(cols, wide, dtype=F32),
+        scratch_shapes=[pltpu.VMEM((8, cols, VALID), BF)],
+        compiler_params=PARAMS,
+    )(where, left, other, ins, masks)
 
 
 def call(kernel, out, *args, scalars=1, scratch=(), cost=None):
@@ -222,7 +280,8 @@
 def per_device(acts, grads, basis_in, basis_out, lengths):
     zhi, core, y, zh, zq = (lax.axis_index(a) for a in ("zhi", "core", "y", "zh", "zq"))
     crossed = (core != zhi).astype(jnp.int32)
-    where = jnp.stack([zh, crossed, lengths[0, 0], core, zq, y, y & 1, y >> 1])
+    tokens = (y >> 1) ^ zhi
+    where = jnp.stack([zh, crossed, lengths[0, 0], core, zq, y, (y & 1) ^ tokens, tokens])
     lines, partial = pl.pallas_call(
         start_kernel,
         in_specs=[pl.BlockSpec(memory_space=pltpu.SMEM)] + [pl.BlockSpec(memory_space=pl.ANY)] * 3,
@@ -240,19 +299,11 @@
     other_basis = swap(basis, "core")
     both = call(join_kernel, like(4, 2, VALID, WIDE), near, far, partial, scalars=0)
     both = exchange(both, "zq")
-    lines, ins = call(sort_kernel, [like(VALID, 8 * FEAT), like(16, 80, 128)], where, both)
+    lines = call(sort_kernel, like(VALID, 8 * FEAT), where, both)
+    ins = call(pack_kernel, like(16, 80, 128), where, both)
     lines = [lines] + others(lines, "y")
     ins = exchange(ins, ("zhi", "zh", "zq"))
-    part = call(
-        project_kernel,
-        like(4, 72, cols),
-        where,
-        *lines,
-        basis,
-        other_basis,
-        cost=LONG,
-        scratch=[pltpu.VMEM((2, 2, VALID, 8 * FEAT), BF)],
-    )
+    part = project(where, lines, basis, other_basis)
     part, ins = lax.optimization_barrier((part, ins))
     ins = call(merge_kernel, like(2, VALID + 8, WIDE), ins, scalars=0)
     part = exchange(part, "x")
@@ -271,16 +322,7 @@
         other_ins,
     )
     left = call(left_kernel, like(2, cols, VALID), outs, scalars=0, cost=HINT)
-    return call(
-        square_kernel,
-        like(cols, 1024, dtype=F32),
-        where,
-        left,
-        swap(outs, "core"),
-        ins,
-        masks,
-        scratch=[pltpu.VMEM((8, cols, VALID), BF)],
-    )
+    return squares(where, left, swap(outs, "core"), ins, masks)
 
 
 def solution(mesh):

time: 140 us -> 140 us (level)
    pallas_call x0 -> x2, Pallas kernels: none -> 8.52 us  [the longest x1 4.32 us: squares(): pl.pallas_call(square_kernel, grid=(wide // tile,), in_specs=[pl.BlockSpe...]
    pallas_call x9 -> x8, Pallas kernels: 12.6 us -> 5.07 us  [call(): pl.pallas_call(kernel, in_specs=[smem] * scalars + [vmem] * (len(args) -...]
  transfers between devices with their start and end apart: 17 -> 17, of which waited for: 7 -> 7; matrix products, arithmetic and copies ran while one was open for 0% -> 0% of each run, Pallas kernels for 5% -> 6%
where the time goes in v8:
time: 140 us; the launch traced here: 139 us
  starting transfers between devices  87.7 us (63%)
  waiting for transfers between devices  34.4 us (25%)
  Pallas kernels  16.6 us (12%)
    ppermute x6, starting transfers between devices, others(): lax.ppermute(x, axis, [(i, i ^ k) for i in range(n)])  23.6 us
    all_to_all x5, starting transfers between devices, exchange(): return lax.all_to_all(x, axis, 0, 0, tiled=True)  22.9 us
    ppermute x4, starting transfers between devices, swap(): return lax.ppermute(x, axis, [(0, 1), (1, 0)])  21.1 us
    all_to_all x5, waiting for transfers between devices, exchange(): return lax.all_to_all(x, axis, 0, 0, tiled=True)  17.1 us
    ppermute x6, waiting for transfers between devices, others(): lax.ppermute(x, axis, [(i, i ^ k) for i in range(n)])  14.3 us
    ppermute x1, starting transfers between devices, per_device(): far = lax.ppermute(lines, PLANE, to_basis(True))  12.3 us
    ppermute x1, starting transfers between devices, per_device(): near = lax.ppermute(lines, PLANE, to_basis(False))  7.77 us
    pallas_call x8, Pallas kernels, call(): pl.pallas_call(kernel, in_specs=[smem] * scalars + [vmem] * (len(args) -...  5.07 us
  transfers between devices with their start and end apart: 17, of which 7 were waited for; matrix products, arithmetic and copies ran while one was open for 0% of the time, Pallas kernels for 6%

profile of v8, /device:TPU:1, one launch (start us, length us, event | category | flops | bytes accessed | tf_op | source)
XLA Modules:
  0.0 139.1 jit_solution(7880438569169606780)
XLA Ops:
  0.0 3.0 %shard_map.55 = (bf16[144,256]{1,0:T(8,128)(2,1)}, bf16[4,144,256]{2,1,0:T(8,128)(2,1)}) custom-call(s32[1,2]{1,0:T(1,128)} %len_ref.1, bf16[192,224]{1,0:T(8,128)(2,1)} %grads_hbm.1, bf16[192,256]{1,0:T(8,128)(2,1)} %acts_hbm.1, bf16[256,1024]{1,0:T(8,128)(2,1)} %basis_hbm.1), custom_call_target="tpu_custom_call" | custom-call | tf_op jit(solution)/shard_map/pallas_call | solution.py:285
  3.0 5.0 %all-to-all-start = ((bf16[4,144,256]{2,1,0:T(8,128)(2,1)}), bf16[4,144,256]{2,1,0:T(8,128)(2,1)S(1)}, u32[]{:S(2)}, u32[]{:S(2)}) async-start(bf16[4,144,256]{2,1,0:T(8,128)(2,1)} %get-tuple-element.14), calls=%async_computation | async-start | bytes 589824 | tf_op jit(solution)/shard_map/all_to_all | solution.py:38
  8.0 12.3 %collective-permute-start.1 = (bf16[144,256]{1,0:T(8,128)(2,1)}, bf16[144,256]{1,0:T(8,128)(2,1)S(1)}, u32[]{:S(2)}, u32[]{:S(2)}) collective-permute-start(bf16[144,256]{1,0:T(8,128)(2,1)} %get-tuple-element.13), channel_id=1, source_target_pairs={{0,4},{1,5},{2,6},{3,7},{4,0},{5,1},{6,2},{7,3},{8,12},{9,13},{10,... | collective-permute-start | bytes 221192 | tf_op jit(solution)/shard_map/ppermute | solution.py:295
  20.3 7.8 %collective-permute-start = (bf16[144,256]{1,0:T(8,128)(2,1)}, bf16[144,256]{1,0:T(8,128)(2,1)S(1)}, u32[]{:S(2)}, u32[]{:S(2)}) collective-permute-start(bf16[144,256]{1,0:T(8,128)(2,1)} %get-tuple-element.13), channel_id=1, source_target_pairs={{0,0},{1,1},{2,2},{3,3},{4,4},{5,5},{6,6},{7,7},{8,8},{9,9},{10,10... | collective-permute-start | bytes 221192 | tf_op jit(solution)/shard_map/ppermute | solution.py:294
  28.1 2.1 %collective-permute-done.near_ref = bf16[144,256]{1,0:T(8,128)(2,1)S(1)} collective-permute-done((bf16[144,256]{1,0:T(8,128)(2,1)}, bf16[144,256]{1,0:T(8,128)(2,1)S(1)}, u32[]{:S(2)}, u32[]{:S(2)}) %collective-permute-start) | collective-permute-done | bytes 73760 | tf_op jit(solution)/shard_map/ppermute | solution.py:294
  31.1 6.9 %all-to-all-start.1 = ((bf16[4,2,144,256]{3,2,1,0:T(8,128)(2,1)}), bf16[4,2,144,256]{3,2,1,0:T(8,128)(2,1)S(1)}, u32[]{:S(2)}, u32[]{:S(2)}) async-start(bf16[4,2,144,256]{3,2,1,0:T(8,128)(2,1)} %shard_map.56), calls=%async_computation.1 | async-start | bytes 1179648 | tf_op jit(solution)/shard_map/all_to_all | solution.py:38
  40.1 11.5 %all-to-all-done.1.both_ref = bf16[4,2,144,256]{3,2,1,0:T(8,128)(2,1)S(1)} async-done(((bf16[4,2,144,256]{3,2,1,0:T(8,128)(2,1)}), bf16[4,2,144,256]{3,2,1,0:T(8,128)(2,1)S(1)}, u32[]{:S(2)}, u32[]{:S(2)}) %all-to-all-start.1) | async-done | bytes 589856 | tf_op jit(solution)/shard_map/all_to_all | solution.py:38
  52.3 8.8 %collective-permute-start.4 = (bf16[144,1792]{1,0:T(8,128)(2,1)S(1)}, bf16[144,1792]{1,0:T(8,128)(2,1)}, u32[]{:S(2)}, u32[]{:S(2)}) collective-permute-start(bf16[144,1792]{1,0:T(8,128)(2,1)S(1)} %shard_map.57.a_ref), channel_id=1, source_target_pairs={{0,24},{8,16},{16,8},{24,0},{1,25},{9,17},{17,9},{25,1},{2,26},{10... | collective-permute-start | bytes 1548296 | tf_op jit(solution)/shard_map/ppermute | solution.py:276
  61.1 3.0 %collective-permute-start.3 = (bf16[144,1792]{1,0:T(8,128)(2,1)S(1)}, bf16[144,1792]{1,0:T(8,128)(2,1)}, u32[]{:S(2)}, u32[]{:S(2)}) collective-permute-start(bf16[144,1792]{1,0:T(8,128)(2,1)S(1)} %shard_map.57.a_ref), channel_id=1, source_target_pairs={{0,16},{8,24},{16,0},{24,8},{1,17},{9,25},{17,1},{25,9},{2,18},{10... | collective-permute-start | bytes 1548296 | tf_op jit(solution)/shard_map/ppermute | solution.py:276
  64.1 1.9 %collective-permute-start.2 = (bf16[144,1792]{1,0:T(8,128)(2,1)S(1)}, bf16[144,1792]{1,0:T(8,128)(2,1)}, u32[]{:S(2)}, u32[]{:S(2)}) collective-permute-start(bf16[144,1792]{1,0:T(8,128)(2,1)S(1)} %shard_map.57.a_ref), channel_id=1, source_target_pairs={{0,8},{8,0},{16,24},{24,16},{1,9},{9,1},{17,25},{25,17},{2,10},{10... | collective-permute-start | bytes 1548296 | tf_op jit(solution)/shard_map/ppermute | solution.py:276
  67.6 3.6 %all-to-all-start.2 = ((bf16[16,80,128]{2,1,0:T(8,128)(2,1)}), bf16[16,80,128]{2,1,0:T(8,128)(2,1)S(1)}, u32[]{:S(2)}, u32[]{:S(2)}) async-start(bf16[16,80,128]{2,1,0:T(8,128)(2,1)} %shard_map.59), calls=%async_computation.2 | async-start | bytes 655360 | tf_op jit(solution)/shard_map/all_to_all | solution.py:38
  71.2 11.7 %collective-permute-done.4.d_ref = bf16[144,1792]{1,0:T(8,128)(2,1)} collective-permute-done((bf16[144,1792]{1,0:T(8,128)(2,1)S(1)}, bf16[144,1792]{1,0:T(8,128)(2,1)}, u32[]{:S(2)}, u32[]{:S(2)}) %collective-permute-start.4) | collective-permute-done | bytes 516128 | tf_op jit(solution)/shard_map/ppermute | solution.py:276
  82.9 2.6 %collective-permute-done.2.b_ref = bf16[144,1792]{1,0:T(8,128)(2,1)} collective-permute-done((bf16[144,1792]{1,0:T(8,128)(2,1)S(1)}, bf16[144,1792]{1,0:T(8,128)(2,1)}, u32[]{:S(2)}, u32[]{:S(2)}) %collective-permute-start.2) | collective-permute-done | bytes 516128 | tf_op jit(solution)/shard_map/ppermute | solution.py:276
  85.5 4.2 %shard_map.58 = bf16[4,72,448]{2,1,0:T(8,128)(2,1)} custom-call(s32[8]{0:T(128)S(1)} %stack.50.where_ref, bf16[144,1792]{1,0:T(8,128)(2,1)S(1)} %shard_map.57.a_ref, bf16[144,1792]{1,0:T(8,128)(2,1)} %collective-permute-done.2.b_ref, bf16[144,1792]{1,0:T(8,128)(2,1)} %collective-permute-done.3.c_ref, bf16[144,1792]{1,0:T(8,128)(2,1)} %collective-permute-done.4.d_ref, ...), custom_call_target="tpu_custom_call" | custom-call | flops 30000001024 | bytes 1000000 | tf_op jit(solution)/shard_map/pallas_call | solution.py:161
  89.7 4.0 %all-to-all-start.3 = ((bf16[4,72,448]{2,1,0:T(8,128)(2,1)}), bf16[4,72,448]{2,1,0:T(8,128)(2,1)S(1)}, u32[]{:S(2)}, u32[]{:S(2)}) async-start(bf16[4,72,448]{2,1,0:T(8,128)(2,1)} %shard_map.58), calls=%async_computation.3 | async-start | bytes 589824 | tf_op jit(solution)/shard_map/all_to_all | solution.py:38
  93.8 5.6 %all-to-all-done.3.parts_ref = bf16[4,72,448]{2,1,0:T(8,128)(2,1)S(1)} async-done(((bf16[4,72,448]{2,1,0:T(8,128)(2,1)}), bf16[4,72,448]{2,1,0:T(8,128)(2,1)S(1)}, u32[]{:S(2)}, u32[]{:S(2)}) %all-to-all-start.3) | async-done | bytes 258080 | tf_op jit(solution)/shard_map/all_to_all | solution.py:38
  99.5 5.3 %collective-permute-start.6 = (bf16[72,448]{1,0:T(8,128)(2,1)S(1)}, bf16[72,448]{1,0:T(8,128)(2,1)S(1)}, u32[]{:S(2)}, u32[]{:S(2)}) collective-permute-start(bf16[72,448]{1,0:T(8,128)(2,1)S(1)} %shard_map.60.one_ref), channel_id=1, source_target_pairs={{0,256},{256,0},{1,257},{257,1},{2,258},{258,2},{3,259},{259,3},{4... | collective-permute-start | bytes 193544 | tf_op jit(solution)/shard_map/ppermute | solution.py:46
  104.7 5.1 %collective-permute-start.10 = (bf16[2,152,256]{2,1,0:T(8,128)(2,1)S(1)}, bf16[2,152,256]{2,1,0:T(8,128)(2,1)S(1)}, u32[]{:S(2)}, u32[]{:S(2)}) collective-permute-start(bf16[2,152,256]{2,1,0:T(8,128)(2,1)S(1)} %shard_map.61), channel_id=1, source_target_pairs={{0,24},{8,16},{16,8},{24,0},{1,25},{9,17},{17,9},{25,1},{2,26},{10... | collective-permute-start | bytes 466952 | tf_op jit(solution)/shard_map/ppermute | solution.py:276
  109.9 2.9 %collective-permute-start.9 = (bf16[2,152,256]{2,1,0:T(8,128)(2,1)S(1)}, bf16[2,152,256]{2,1,0:T(8,128)(2,1)S(1)}, u32[]{:S(2)}, u32[]{:S(2)}) collective-permute-start(bf16[2,152,256]{2,1,0:T(8,128)(2,1)S(1)} %shard_map.61), channel_id=1, source_target_pairs={{0,16},{8,24},{16,0},{24,8},{1,17},{9,25},{17,1},{25,9},{2,18},{10... | collective-permute-start | bytes 466952 | tf_op jit(solution)/shard_map/ppermute | solution.py:276
  112.8 1.9 %collective-permute-start.8 = (bf16[2,152,256]{2,1,0:T(8,128)(2,1)S(1)}, bf16[2,152,256]{2,1,0:T(8,128)(2,1)S(1)}, u32[]{:S(2)}, u32[]{:S(2)}) collective-permute-start(bf16[2,152,256]{2,1,0:T(8,128)(2,1)S(1)} %shard_map.61), channel_id=1, source_target_pairs={{0,8},{8,0},{16,24},{24,16},{1,9},{9,1},{17,25},{25,17},{2,10},{10... | collective-permute-start | bytes 466952 | tf_op jit(solution)/shard_map/ppermute | solution.py:276
  116.1 3.5 %all-to-all-start.4 = ((bf16[4,72,448]{2,1,0:T(8,128)(2,1)}), bf16[4,72,448]{2,1,0:T(8,128)(2,1)S(1)}, u32[]{:S(2)}, u32[]{:S(2)}) async-start(bf16[4,72,448]{2,1,0:T(8,128)(2,1)} %shard_map.62), calls=%async_computation.4 | async-start | bytes 589824 | tf_op jit(solution)/shard_map/all_to_all | solution.py:38
  119.7 7.8 %collective-permute-start.11 = (bf16[4,2,152,256]{3,2,1,0:T(8,128)(2,1)S(1)}, bf16[4,2,152,256]{3,2,1,0:T(8,128)(2,1)S(1)}, u32[]{:S(2)}, u32[]{:S(2)}) collective-permute-start(bf16[4,2,152,256]{3,2,1,0:T(8,128)(2,1)S(1)} %pad_maximum_fusion.own_ref), channel_id=1, source_target_pairs={{0,128},{128,0},{1,129},{129,1},{2,130},{130,2},{3,131},{131,3},{4... | collective-permute-start | bytes 1867784 | tf_op jit(solution)/shard_map/ppermute | solution.py:46
  127.5 6.1 %collective-permute-start.7 = (bf16[2,144,448]{2,1,0:T(8,128)(2,1)S(1)}, bf16[2,144,448]{2,1,0:T(8,128)(2,1)S(1)}, u32[]{:S(2)}, u32[]{:S(2)}) collective-permute-start(bf16[2,144,448]{2,1,0:T(8,128)(2,1)S(1)} %bitcast.18), channel_id=1, source_target_pairs={{0,128},{128,0},{1,129},{129,1},{2,130},{130,2},{3,131},{131,3},{4... | collective-permute-start | bytes 774152 | tf_op jit(solution)/shard_map/ppermute | solution.py:46
  134.8 4.3 %shard_map.65 = f32[448,1024]{1,0:T(8,128)} custom-call(s32[8]{0:T(128)S(1)} %stack.50.where_ref, bf16[2,448,144]{2,1,0:T(8,128)(2,1)S(1)} %shard_map.63.own_ref, bf16[2,144,448]{2,1,0:T(8,128)(2,1)S(1)} %collective-permute-done.7.other_ref, bf16[4,144,1024]{2,1,0:T(8,128)(2,1)S(1)} %get-tuple-element.19.in_ref, ...), custom_call_target="tpu_custom_call" | custom-call | tf_op jit(solution)/shard_map/pallas_call | solution.py:236
  (27 shorter events, 8.1 us)
Async XLA Ops:
  0.0 38.0 %copy-start = (bf16[1,1792,448]{1,2,0:T(8,128)(2,1)S(1)}, bf16[1,1792,448]{1,2,0:T(8,128)(2,1)}, u32[]{:S(2)}) copy-start(bf16[1,1792,448]{1,2,0:T(8,128)(2,1)} %param.8) | copy-start | bytes 4816900
  3.0 37.0 %copy-start.1 = (s32[1,2]{1,0:T(1,128)S(1)}, s32[1,2]{1,0:T(1,128)}, u32[]{:S(2)}) copy-start(s32[1,2]{1,0:T(1,128)} %len_ref.1) | copy-start | bytes 28
  3.0 27.2 %all-to-all-start = ((bf16[4,144,256]{2,1,0:T(8,128)(2,1)}), bf16[4,144,256]{2,1,0:T(8,128)(2,1)S(1)}, u32[]{:S(2)}, u32[]{:S(2)}) async-start(bf16[4,144,256]{2,1,0:T(8,128)(2,1)} %get-tuple-element.14), calls=%async_computation | async-start | bytes 589824 | tf_op jit(solution)/shard_map/all_to_all | solution.py:38
  8.0 20.1 %collective-permute-start.1 = (bf16[144,256]{1,0:T(8,128)(2,1)}, bf16[144,256]{1,0:T(8,128)(2,1)S(1)}, u32[]{:S(2)}, u32[]{:S(2)}) collective-permute-start(bf16[144,256]{1,0:T(8,128)(2,1)} %get-tuple-element.13), channel_id=1, source_target_pairs={{0,4},{1,5},{2,6},{3,7},{4,0},{5,1},{6,2},{7,3},{8,12},{9,13},{10,... | collective-permute-start | bytes 221192 | tf_op jit(solution)/shard_map/ppermute | solution.py:295
  20.3 9.8 %collective-permute-start = (bf16[144,256]{1,0:T(8,128)(2,1)}, bf16[144,256]{1,0:T(8,128)(2,1)S(1)}, u32[]{:S(2)}, u32[]{:S(2)}) collective-permute-start(bf16[144,256]{1,0:T(8,128)(2,1)} %get-tuple-element.13), channel_id=1, source_target_pairs={{0,0},{1,1},{2,2},{3,3},{4,4},{5,5},{6,6},{7,7},{8,8},{9,9},{10,10... | collective-permute-start | bytes 221192 | tf_op jit(solution)/shard_map/ppermute | solution.py:294
  31.1 20.5 %all-to-all-start.1 = ((bf16[4,2,144,256]{3,2,1,0:T(8,128)(2,1)}), bf16[4,2,144,256]{3,2,1,0:T(8,128)(2,1)S(1)}, u32[]{:S(2)}, u32[]{:S(2)}) async-start(bf16[4,2,144,256]{3,2,1,0:T(8,128)(2,1)} %shard_map.56), calls=%async_computation.1 | async-start | bytes 1179648 | tf_op jit(solution)/shard_map/all_to_all | solution.py:38
  38.0 33.2 %collective-permute-start.5 = (bf16[448,1792]{1,0:T(8,128)(2,1)S(1)}, bf16[448,1792]{1,0:T(8,128)(2,1)}, u32[]{:S(2)}, u32[]{:S(2)}) collective-permute-start(bf16[448,1792]{1,0:T(8,128)(2,1)S(1)} %bitcast.20), channel_id=1, source_target_pairs={{0,128},{128,0},{1,129},{129,1},{2,130},{130,2},{3,131},{131,3},{4... | collective-permute-start | bytes 4816904 | tf_op jit(solution)/shard_map/ppermute | solution.py:46
  52.3 30.6 %collective-permute-start.4 = (bf16[144,1792]{1,0:T(8,128)(2,1)S(1)}, bf16[144,1792]{1,0:T(8,128)(2,1)}, u32[]{:S(2)}, u32[]{:S(2)}) collective-permute-start(bf16[144,1792]{1,0:T(8,128)(2,1)S(1)} %shard_map.57.a_ref), channel_id=1, source_target_pairs={{0,24},{8,16},{16,8},{24,0},{1,25},{9,17},{17,9},{25,1},{2,26},{10... | collective-permute-start | bytes 1548296 | tf_op jit(solution)/shard_map/ppermute | solution.py:276
  61.1 21.8 %collective-permute-start.3 = (bf16[144,1792]{1,0:T(8,128)(2,1)S(1)}, bf16[144,1792]{1,0:T(8,128)(2,1)}, u32[]{:S(2)}, u32[]{:S(2)}) collective-permute-start(bf16[144,1792]{1,0:T(8,128)(2,1)S(1)} %shard_map.57.a_ref), channel_id=1, source_target_pairs={{0,16},{8,24},{16,0},{24,8},{1,17},{9,25},{17,1},{25,9},{2,18},{10... | collective-permute-start | bytes 1548296 | tf_op jit(solution)/shard_map/ppermute | solution.py:276
  64.1 21.4 %collective-permute-start.2 = (bf16[144,1792]{1,0:T(8,128)(2,1)S(1)}, bf16[144,1792]{1,0:T(8,128)(2,1)}, u32[]{:S(2)}, u32[]{:S(2)}) collective-permute-start(bf16[144,1792]{1,0:T(8,128)(2,1)S(1)} %shard_map.57.a_ref), channel_id=1, source_target_pairs={{0,8},{8,0},{16,24},{24,16},{1,9},{9,1},{17,25},{25,17},{2,10},{10... | collective-permute-start | bytes 1548296 | tf_op jit(solution)/shard_map/ppermute | solution.py:276
  67.6 22.1 %all-to-all-start.2 = ((bf16[16,80,128]{2,1,0:T(8,128)(2,1)}), bf16[16,80,128]{2,1,0:T(8,128)(2,1)S(1)}, u32[]{:S(2)}, u32[]{:S(2)}) async-start(bf16[16,80,128]{2,1,0:T(8,128)(2,1)} %shard_map.59), calls=%async_computation.2 | async-start | bytes 655360 | tf_op jit(solution)/shard_map/all_to_all | solution.py:38
  89.7 9.7 %all-to-all-start.3 = ((bf16[4,72,448]{2,1,0:T(8,128)(2,1)}), bf16[4,72,448]{2,1,0:T(8,128)(2,1)S(1)}, u32[]{:S(2)}, u32[]{:S(2)}) async-start(bf16[4,72,448]{2,1,0:T(8,128)(2,1)} %shard_map.58), calls=%async_computation.3 | async-start | bytes 589824 | tf_op jit(solution)/shard_map/all_to_all | solution.py:38
  99.5 15.9 %collective-permute-start.6 = (bf16[72,448]{1,0:T(8,128)(2,1)S(1)}, bf16[72,448]{1,0:T(8,128)(2,1)S(1)}, u32[]{:S(2)}, u32[]{:S(2)}) collective-permute-start(bf16[72,448]{1,0:T(8,128)(2,1)S(1)} %shard_map.60.one_ref), channel_id=1, source_target_pairs={{0,256},{256,0},{1,257},{257,1},{2,258},{258,2},{3,259},{259,3},{4... | collective-permute-start | bytes 193544 | tf_op jit(solution)/shard_map/ppermute | solution.py:46
  104.7 14.8 %collective-permute-start.10 = (bf16[2,152,256]{2,1,0:T(8,128)(2,1)S(1)}, bf16[2,152,256]{2,1,0:T(8,128)(2,1)S(1)}, u32[]{:S(2)}, u32[]{:S(2)}) collective-permute-start(bf16[2,152,256]{2,1,0:T(8,128)(2,1)S(1)} %shard_map.61), channel_id=1, source_target_pairs={{0,24},{8,16},{16,8},{24,0},{1,25},{9,17},{17,9},{25,1},{2,26},{10... | collective-permute-start | bytes 466952 | tf_op jit(solution)/shard_map/ppermute | solution.py:276
  109.9 9.7 %collective-permute-start.9 = (bf16[2,152,256]{2,1,0:T(8,128)(2,1)S(1)}, bf16[2,152,256]{2,1,0:T(8,128)(2,1)S(1)}, u32[]{:S(2)}, u32[]{:S(2)}) collective-permute-start(bf16[2,152,256]{2,1,0:T(8,128)(2,1)S(1)} %shard_map.61), channel_id=1, source_target_pairs={{0,16},{8,24},{16,0},{24,8},{1,17},{9,25},{17,1},{25,9},{2,18},{10... | collective-permute-start | bytes 466952 | tf_op jit(solution)/shard_map/ppermute | solution.py:276
  112.8 6.8 %collective-permute-start.8 = (bf16[2,152,256]{2,1,0:T(8,128)(2,1)S(1)}, bf16[2,152,256]{2,1,0:T(8,128)(2,1)S(1)}, u32[]{:S(2)}, u32[]{:S(2)}) collective-permute-start(bf16[2,152,256]{2,1,0:T(8,128)(2,1)S(1)} %shard_map.61), channel_id=1, source_target_pairs={{0,8},{8,0},{16,24},{24,16},{1,9},{9,1},{17,25},{25,17},{2,10},{10... | collective-permute-start | bytes 466952 | tf_op jit(solution)/shard_map/ppermute | solution.py:276
  116.1 11.4 %all-to-all-start.4 = ((bf16[4,72,448]{2,1,0:T(8,128)(2,1)}), bf16[4,72,448]{2,1,0:T(8,128)(2,1)S(1)}, u32[]{:S(2)}, u32[]{:S(2)}) async-start(bf16[4,72,448]{2,1,0:T(8,128)(2,1)} %shard_map.62), calls=%async_computation.4 | async-start | bytes 589824 | tf_op jit(solution)/shard_map/all_to_all | solution.py:38
  119.7 14.1 %collective-permute-start.11 = (bf16[4,2,152,256]{3,2,1,0:T(8,128)(2,1)S(1)}, bf16[4,2,152,256]{3,2,1,0:T(8,128)(2,1)S(1)}, u32[]{:S(2)}, u32[]{:S(2)}) collective-permute-start(bf16[4,2,152,256]{3,2,1,0:T(8,128)(2,1)S(1)} %pad_maximum_fusion.own_ref), channel_id=1, source_target_pairs={{0,128},{128,0},{1,129},{129,1},{2,130},{130,2},{3,131},{131,3},{4... | collective-permute-start | bytes 1867784 | tf_op jit(solution)/shard_map/ppermute | solution.py:46
  127.5 7.3 %collective-permute-start.7 = (bf16[2,144,448]{2,1,0:T(8,128)(2,1)S(1)}, bf16[2,144,448]{2,1,0:T(8,128)(2,1)S(1)}, u32[]{:S(2)}, u32[]{:S(2)}) collective-permute-start(bf16[2,144,448]{2,1,0:T(8,128)(2,1)S(1)} %bitcast.18), channel_id=1, source_target_pairs={{0,128},{128,0},{1,129},{129,1},{2,130},{130,2},{3,131},{131,3},{4... | collective-permute-start | bytes 774152 | tf_op jit(solution)/shard_map/ppermute | solution.py:46

commit v9 on v8

--- a/solution.py
+++ b/solution.py
@@ -12,7 +12,7 @@
 BF = jnp.bfloat16
 F32 = jnp.float32
 HINT = pl.CostEstimate(flops=int(5e9), bytes_accessed=int(1e6), transcendentals=0)
-LONG = pl.CostEstimate(flops=int(3e10), bytes_accessed=int(1e6), transcendentals=0)
+LONG = pl.CostEstimate(flops=int(8e9), bytes_accessed=int(1e6), transcendentals=0)
 PLANE = ("zhi", "core", "y", "zh", "zq")
 PARAMS = pltpu.CompilerParams(vmem_limit_bytes=16 << 20)
 
@@ -90,12 +90,14 @@
             out_ref[d, w] = jnp.concatenate([ref[:, :FEAT], total[:, at : at + 32]], axis=1)
 
 
-def sort_kernel(where_ref, both_ref, out_ref):
+def sort_kernel(where_ref, both_ref, out_ref, half_ref):
     zh, crossed = where_ref[0], where_ref[1]
     for f in range(8):
         far = (jnp.int32(f // 4) != zh).astype(jnp.int32) ^ crossed
         at = (f % 4) ^ (3 * (far & crossed))
         out_ref[:, f * FEAT : (f + 1) * FEAT] = both_ref[at, far][:, :FEAT]
+    half = VALID // 2
+    half_ref[...] = jnp.where(where_ref[4] % 2 == 0, out_ref[:half], out_ref[half:])
 
 
 def pack_kernel(where_ref, both_ref, in_ref):
@@ -127,12 +129,17 @@
 
 
 def project_kernel(
-    where_ref, a_ref, b_ref, c_ref, d_ref, own_ref, other_ref, out_ref, held, total_ref
+    where_ref, a_ref, b_ref, c_ref, e_ref, d_ref, own_ref, other_ref, out_ref, held, total_ref
 ):
     step = pl.program_id(0)
     tokens, same = where_ref[7], where_ref[3] == where_ref[6]
-    for left_ref, right_ref, t in ((a_ref, b_ref, tokens), (d_ref, c_ref, 1 - tokens)):
-        left, right = left_ref[...], right_ref[...]
+    even = where_ref[4] % 2 == 0
+    mine, next_ = c_ref[...], e_ref[...]
+    far = jnp.concatenate([jnp.where(even, mine, next_), jnp.where(even, next_, mine)], axis=0)
+    for left, right, t in (
+        (a_ref[...], b_ref[...], tokens),
+        (d_ref[...], far, 1 - tokens),
+    ):
         held[0, t] = jnp.where(same, left, right)
         held[1, t] = jnp.where(same, right, left)
     rows = (2 * VALID, held.shape[3])
@@ -156,12 +163,12 @@
 def project(where, lines, basis, other_basis):
     cols, rows = basis.shape
     deep = rows // 2
-    line = pl.BlockSpec((VALID, deep), lambda k: (0, k))
+    line = [pl.BlockSpec((x.shape[0], deep), lambda k: (0, k)) for x in lines]
     rotated = pl.BlockSpec((cols, deep), lambda k: (0, k))
     return pl.pallas_call(
         project_kernel,
         grid=(rows // deep,),
-        in_specs=[pl.BlockSpec(memory_space=pltpu.SMEM)] + [line] * 4 + [rotated] * 2,
+        in_specs=[pl.BlockSpec(memory_space=pltpu.SMEM)] + line + [rotated] * 2,
         out_specs=pl.BlockSpec((4, 72, cols), lambda k: (0, 0, 0)),
         out_shape=like(4, 72, cols),
         scratch_shapes=[pltpu.VMEM((2, 2, VALID, deep), BF), pltpu.VMEM((2 * VALID, cols), F32)],
@@ -227,7 +234,7 @@
                 preferred_element_type=F32,
             )
             total += block * block
-        eig_ref[o * rows : (o + 1) * rows] = total / 768.0
+        eig_ref[o * rows : (o + 1) * rows] = total * (1.0 / 768.0)
 
 
 def squares(where, left, other, ins, masks):
@@ -299,9 +306,13 @@
     other_basis = swap(basis, "core")
     both = call(join_kernel, like(4, 2, VALID, WIDE), near, far, partial, scalars=0)
     both = exchange(both, "zq")
-    lines = call(sort_kernel, like(VALID, 8 * FEAT), where, both)
+    lines, half = call(
+        sort_kernel, [like(VALID, 8 * FEAT), like(VALID // 2, 8 * FEAT)], where, both
+    )
     ins = call(pack_kernel, like(16, 80, 128), where, both)
-    lines = [lines] + others(lines, "y")
+    two = lax.ppermute(half, "y", [(i, i ^ 2) for i in range(4)])
+    one, three = (lax.ppermute(lines, "y", [(i, i ^ k) for i in range(4)]) for k in (1, 3))
+    lines = [lines, one, two, lax.ppermute(two, "zq", [(i, i ^ 1) for i in range(4)]), three]
     ins = exchange(ins, ("zhi", "zh", "zq"))
     part = project(where, lines, basis, other_basis)
     part, ins = lax.optimization_barrier((part, ins))

time: 140 us -> 150 us (1.071)
  starting transfers between devices: 87.7 us -> 93.2 us
  waiting for transfers between devices: 34.4 us -> 38.6 us
    ppermute x0 -> x4, waiting for transfers between devices: none -> 17.5 us  [the longest x1 17.5 us: per_device(): lax.ppermute(two, 'zq', [(i, i ^ 1) for i in range(4)])]
    ppermute x0 -> x4, starting transfers between devices: none -> 16.9 us  [the longest x1 9.83 us: per_device(): two = lax.ppermute(half, 'y', [(i, i ^ 2) for i in range(4)])]
    ppermute x6 -> x3, starting transfers between devices: 23.6 us -> 9.75 us  [others(): lax.ppermute(x, axis, [(i, i ^ k) for i in range(n)])]
    ppermute x6 -> x3, waiting for transfers between devices: 14.3 us -> 1.65 us  [others(): lax.ppermute(x, axis, [(i, i ^ k) for i in range(n)])]
    ppermute x4, starting transfers between devices: 21.1 us -> 23.5 us  [swap(): return lax.ppermute(x, axis, [(0, 1), (1, 0)])]
  transfers between devices with their start and end apart: 17 -> 18, of which waited for: 7 -> 6; matrix products, arithmetic and copies ran while one was open for 0% -> 0% of each run, Pallas kernels for 6% -> 6%
where the time goes in v9:
time: 150 us; the launch traced here: 149 us
  starting transfers between devices  93.2 us (62%)
  waiting for transfers between devices  38.6 us (26%)
  Pallas kernels  16.6 us (11%)
    ppermute x4, starting transfers between devices, swap(): return lax.ppermute(x, axis, [(0, 1), (1, 0)])  23.5 us
    all_to_all x5, starting transfers between devices, exchange(): return lax.all_to_all(x, axis, 0, 0, tiled=True)  22.9 us
    ppermute x1, waiting for transfers between devices, per_device(): lax.ppermute(two, 'zq', [(i, i ^ 1) for i in range(4)])  17.5 us
    all_to_all x5, waiting for transfers between devices, exchange(): return lax.all_to_all(x, axis, 0, 0, tiled=True)  17.1 us
    ppermute x1, starting transfers between devices, per_device(): far = lax.ppermute(lines, PLANE, to_basis(True))  12.3 us
    ppermute x1, starting transfers between devices, per_device(): two = lax.ppermute(half, 'y', [(i, i ^ 2) for i in range(4)])  9.83 us
    ppermute x3, starting transfers between devices, others(): lax.ppermute(x, axis, [(i, i ^ k) for i in range(n)])  9.75 us
    ppermute x1, starting transfers between devices, per_device(): near = lax.ppermute(lines, PLANE, to_basis(False))  7.77 us
  transfers between devices with their start and end apart: 18, of which 6 were waited for; matrix products, arithmetic and copies ran while one was open for 0% of the time, Pallas kernels for 6%

profile of v9, /device:TPU:1, one launch (start us, length us, event | category | flops | bytes accessed | tf_op | source)
XLA Modules:
  0.0 148.9 jit_solution(11628441953194151600)
XLA Ops:
  0.0 3.0 %shard_map.55 = (bf16[144,256]{1,0:T(8,128)(2,1)}, bf16[4,144,256]{2,1,0:T(8,128)(2,1)}) custom-call(s32[1,2]{1,0:T(1,128)} %len_ref.1, bf16[192,224]{1,0:T(8,128)(2,1)} %grads_hbm.1, bf16[192,256]{1,0:T(8,128)(2,1)} %acts_hbm.1, bf16[256,1024]{1,0:T(8,128)(2,1)} %basis_hbm.1), custom_call_target="tpu_custom_call" | custom-call | tf_op jit(solution)/shard_map/pallas_call | solution.py:292
  3.0 5.0 %all-to-all-start = ((bf16[4,144,256]{2,1,0:T(8,128)(2,1)}), bf16[4,144,256]{2,1,0:T(8,128)(2,1)S(1)}, u32[]{:S(2)}, u32[]{:S(2)}) async-start(bf16[4,144,256]{2,1,0:T(8,128)(2,1)} %get-tuple-element.16), calls=%async_computation | async-start | bytes 589824 | tf_op jit(solution)/shard_map/all_to_all | solution.py:38
  8.0 12.3 %collective-permute-start.1 = (bf16[144,256]{1,0:T(8,128)(2,1)}, bf16[144,256]{1,0:T(8,128)(2,1)S(1)}, u32[]{:S(2)}, u32[]{:S(2)}) collective-permute-start(bf16[144,256]{1,0:T(8,128)(2,1)} %get-tuple-element.15), channel_id=1, source_target_pairs={{0,4},{1,5},{2,6},{3,7},{4,0},{5,1},{6,2},{7,3},{8,12},{9,13},{10,... | collective-permute-start | bytes 221192 | tf_op jit(solution)/shard_map/ppermute | solution.py:302
  20.3 7.8 %collective-permute-start = (bf16[144,256]{1,0:T(8,128)(2,1)}, bf16[144,256]{1,0:T(8,128)(2,1)S(1)}, u32[]{:S(2)}, u32[]{:S(2)}) collective-permute-start(bf16[144,256]{1,0:T(8,128)(2,1)} %get-tuple-element.15), channel_id=1, source_target_pairs={{0,0},{1,1},{2,2},{3,3},{4,4},{5,5},{6,6},{7,7},{8,8},{9,9},{10,10... | collective-permute-start | bytes 221192 | tf_op jit(solution)/shard_map/ppermute | solution.py:301
  28.1 2.1 %collective-permute-done.near_ref = bf16[144,256]{1,0:T(8,128)(2,1)S(1)} collective-permute-done((bf16[144,256]{1,0:T(8,128)(2,1)}, bf16[144,256]{1,0:T(8,128)(2,1)S(1)}, u32[]{:S(2)}, u32[]{:S(2)}) %collective-permute-start) | collective-permute-done | bytes 73760 | tf_op jit(solution)/shard_map/ppermute | solution.py:301
  31.1 6.9 %all-to-all-start.1 = ((bf16[4,2,144,256]{3,2,1,0:T(8,128)(2,1)}), bf16[4,2,144,256]{3,2,1,0:T(8,128)(2,1)S(1)}, u32[]{:S(2)}, u32[]{:S(2)}) async-start(bf16[4,2,144,256]{3,2,1,0:T(8,128)(2,1)} %shard_map.56), calls=%async_computation.1 | async-start | bytes 1179648 | tf_op jit(solution)/shard_map/all_to_all | solution.py:38
  40.1 11.5 %all-to-all-done.1.both_ref = bf16[4,2,144,256]{3,2,1,0:T(8,128)(2,1)S(1)} async-done(((bf16[4,2,144,256]{3,2,1,0:T(8,128)(2,1)}), bf16[4,2,144,256]{3,2,1,0:T(8,128)(2,1)S(1)}, u32[]{:S(2)}, u32[]{:S(2)}) %all-to-all-start.1) | async-done | bytes 589856 | tf_op jit(solution)/shard_map/all_to_all | solution.py:38
  52.4 9.8 %collective-permute-start.3 = (bf16[72,1792]{1,0:T(8,128)(2,1)S(1)}, bf16[72,1792]{1,0:T(8,128)(2,1)S(1)}, u32[]{:S(2)}, u32[]{:S(2)}) collective-permute-start(bf16[72,1792]{1,0:T(8,128)(2,1)S(1)} %get-tuple-element.18), channel_id=1, source_target_pairs={{0,16},{8,24},{16,0},{24,8},{1,17},{9,25},{17,1},{25,9},{2,18},{10... | collective-permute-start | bytes 774152 | tf_op jit(solution)/shard_map/ppermute | solution.py:313
  62.2 1.9 %collective-permute-start.5 = (bf16[144,1792]{1,0:T(8,128)(2,1)S(1)}, bf16[144,1792]{1,0:T(8,128)(2,1)}, u32[]{:S(2)}, u32[]{:S(2)}) collective-permute-start(bf16[144,1792]{1,0:T(8,128)(2,1)S(1)} %get-tuple-element.17.a_ref), channel_id=1, source_target_pairs={{0,24},{8,16},{16,8},{24,0},{1,25},{9,17},{17,9},{25,1},{2,26},{10... | collective-permute-start | bytes 1548296 | tf_op jit(solution)/shard_map/ppermute | solution.py:314
  64.2 1.9 %collective-permute-start.2 = (bf16[144,1792]{1,0:T(8,128)(2,1)S(1)}, bf16[144,1792]{1,0:T(8,128)(2,1)}, u32[]{:S(2)}, u32[]{:S(2)}) collective-permute-start(bf16[144,1792]{1,0:T(8,128)(2,1)S(1)} %get-tuple-element.17.a_ref), channel_id=1, source_target_pairs={{0,8},{8,0},{16,24},{24,16},{1,9},{9,1},{17,25},{25,17},{2,10},{10... | collective-permute-start | bytes 1548296 | tf_op jit(solution)/shard_map/ppermute | solution.py:314
  67.7 3.6 %all-to-all-start.2 = ((bf16[16,80,128]{2,1,0:T(8,128)(2,1)}), bf16[16,80,128]{2,1,0:T(8,128)(2,1)S(1)}, u32[]{:S(2)}, u32[]{:S(2)}) async-start(bf16[16,80,128]{2,1,0:T(8,128)(2,1)} %shard_map.59), calls=%async_computation.2 | async-start | bytes 655360 | tf_op jit(solution)/shard_map/all_to_all | solution.py:38
  71.2 3.3 %collective-permute-start.4 = (bf16[72,1792]{1,0:T(8,128)(2,1)S(1)}, bf16[72,1792]{1,0:T(8,128)(2,1)S(1)}, u32[]{:S(2)}, u32[]{:S(2)}) collective-permute-start(bf16[72,1792]{1,0:T(8,128)(2,1)S(1)} %collective-permute-done.3.c_ref), channel_id=1, source_target_pairs={{0,1},{1,0},{2,3},{3,2},{4,5},{5,4},{6,7},{7,6},{8,9},{9,8},{10,11... | collective-permute-start | bytes 774152 | tf_op jit(solution)/shard_map/ppermute | solution.py:315
  74.5 17.5 %collective-permute-done.4.e_ref = bf16[72,1792]{1,0:T(8,128)(2,1)S(1)} collective-permute-done((bf16[72,1792]{1,0:T(8,128)(2,1)S(1)}, bf16[72,1792]{1,0:T(8,128)(2,1)S(1)}, u32[]{:S(2)}, u32[]{:S(2)}) %collective-permute-start.4) | collective-permute-done | bytes 258080 | tf_op jit(solution)/shard_map/ppermute | solution.py:315
  92.0 4.2 %shard_map.58 = bf16[4,72,448]{2,1,0:T(8,128)(2,1)} custom-call(s32[8]{0:T(128)S(1)} %stack.50.where_ref, bf16[144,1792]{1,0:T(8,128)(2,1)S(1)} %get-tuple-element.17.a_ref, bf16[144,1792]{1,0:T(8,128)(2,1)} %collective-permute-done.2.b_ref, bf16[72,1792]{1,0:T(8,128)(2,1)S(1)} %collective-permute-done.3.c_ref, ...), custom_call_target="tpu_custom_call" | custom-call | flops 8000000000 | bytes 1000000 | tf_op jit(solution)/shard_map/pallas_call | solution.py:168
  96.2 4.0 %all-to-all-start.3 = ((bf16[4,72,448]{2,1,0:T(8,128)(2,1)}), bf16[4,72,448]{2,1,0:T(8,128)(2,1)S(1)}, u32[]{:S(2)}, u32[]{:S(2)}) async-start(bf16[4,72,448]{2,1,0:T(8,128)(2,1)} %shard_map.58), calls=%async_computation.3 | async-start | bytes 589824 | tf_op jit(solution)/shard_map/all_to_all | solution.py:38
  100.4 5.6 %all-to-all-done.3.parts_ref = bf16[4,72,448]{2,1,0:T(8,128)(2,1)S(1)} async-done(((bf16[4,72,448]{2,1,0:T(8,128)(2,1)}), bf16[4,72,448]{2,1,0:T(8,128)(2,1)S(1)}, u32[]{:S(2)}, u32[]{:S(2)}) %all-to-all-start.3) | async-done | bytes 258080 | tf_op jit(solution)/shard_map/all_to_all | solution.py:38
  106.0 11.3 %collective-permute-start.7 = (bf16[72,448]{1,0:T(8,128)(2,1)S(1)}, bf16[72,448]{1,0:T(8,128)(2,1)S(1)}, u32[]{:S(2)}, u32[]{:S(2)}) collective-permute-start(bf16[72,448]{1,0:T(8,128)(2,1)S(1)} %shard_map.60.one_ref), channel_id=1, source_target_pairs={{0,256},{256,0},{1,257},{257,1},{2,258},{258,2},{3,259},{259,3},{4... | collective-permute-start | bytes 193544 | tf_op jit(solution)/shard_map/ppermute | solution.py:46
  117.4 5.0 %collective-permute-start.11 = (bf16[2,152,256]{2,1,0:T(8,128)(2,1)S(1)}, bf16[2,152,256]{2,1,0:T(8,128)(2,1)S(1)}, u32[]{:S(2)}, u32[]{:S(2)}) collective-permute-start(bf16[2,152,256]{2,1,0:T(8,128)(2,1)S(1)} %shard_map.61), channel_id=1, source_target_pairs={{0,24},{8,16},{16,8},{24,0},{1,25},{9,17},{17,9},{25,1},{2,26},{10... | collective-permute-start | bytes 466952 | tf_op jit(solution)/shard_map/ppermute | solution.py:283
  122.4 2.8 %collective-permute-start.10 = (bf16[2,152,256]{2,1,0:T(8,128)(2,1)S(1)}, bf16[2,152,256]{2,1,0:T(8,128)(2,1)S(1)}, u32[]{:S(2)}, u32[]{:S(2)}) collective-permute-start(bf16[2,152,256]{2,1,0:T(8,128)(2,1)S(1)} %shard_map.61), channel_id=1, source_target_pairs={{0,16},{8,24},{16,0},{24,8},{1,17},{9,25},{17,1},{25,9},{2,18},{10... | collective-permute-start | bytes 466952 | tf_op jit(solution)/shard_map/ppermute | solution.py:283
  125.2 1.9 %collective-permute-start.9 = (bf16[2,152,256]{2,1,0:T(8,128)(2,1)S(1)}, bf16[2,152,256]{2,1,0:T(8,128)(2,1)S(1)}, u32[]{:S(2)}, u32[]{:S(2)}) collective-permute-start(bf16[2,152,256]{2,1,0:T(8,128)(2,1)S(1)} %shard_map.61), channel_id=1, source_target_pairs={{0,8},{8,0},{16,24},{24,16},{1,9},{9,1},{17,25},{25,17},{2,10},{10... | collective-permute-start | bytes 466952 | tf_op jit(solution)/shard_map/ppermute | solution.py:283
  127.9 3.5 %all-to-all-start.4 = ((bf16[4,72,448]{2,1,0:T(8,128)(2,1)}), bf16[4,72,448]{2,1,0:T(8,128)(2,1)S(1)}, u32[]{:S(2)}, u32[]{:S(2)}) async-start(bf16[4,72,448]{2,1,0:T(8,128)(2,1)} %shard_map.62), calls=%async_computation.4 | async-start | bytes 589824 | tf_op jit(solution)/shard_map/all_to_all | solution.py:38
  133.1 4.5 %collective-permute-start.12 = (bf16[4,2,152,256]{3,2,1,0:T(8,128)(2,1)S(1)}, bf16[4,2,152,256]{3,2,1,0:T(8,128)(2,1)S(1)}, u32[]{:S(2)}, u32[]{:S(2)}) collective-permute-start(bf16[4,2,152,256]{3,2,1,0:T(8,128)(2,1)S(1)} %pad_maximum_fusion.own_ref), channel_id=1, source_target_pairs={{0,128},{128,0},{1,129},{129,1},{2,130},{130,2},{3,131},{131,3},{4... | collective-permute-start | bytes 1867784 | tf_op jit(solution)/shard_map/ppermute | solution.py:46
  137.6 5.8 %collective-permute-start.8 = (bf16[2,144,448]{2,1,0:T(8,128)(2,1)S(1)}, bf16[2,144,448]{2,1,0:T(8,128)(2,1)S(1)}, u32[]{:S(2)}, u32[]{:S(2)}) collective-permute-start(bf16[2,144,448]{2,1,0:T(8,128)(2,1)S(1)} %bitcast.18), channel_id=1, source_target_pairs={{0,128},{128,0},{1,129},{129,1},{2,130},{130,2},{3,131},{131,3},{4... | collective-permute-start | bytes 774152 | tf_op jit(solution)/shard_map/ppermute | solution.py:46
  144.6 4.3 %shard_map.65 = f32[448,1024]{1,0:T(8,128)} custom-call(s32[8]{0:T(128)S(1)} %stack.50.where_ref, bf16[2,448,144]{2,1,0:T(8,128)(2,1)S(1)} %shard_map.63.own_ref, bf16[2,144,448]{2,1,0:T(8,128)(2,1)S(1)} %collective-permute-done.8.other_ref, bf16[4,144,1024]{2,1,0:T(8,128)(2,1)S(1)} %get-tuple-element.23.in_ref, ...), custom_call_target="tpu_custom_call" | custom-call | tf_op jit(solution)/shard_map/pallas_call | solution.py:243
  (29 shorter events, 9.2 us)
Async XLA Ops:
  0.0 38.0 %copy-start = (bf16[1,1792,448]{1,2,0:T(8,128)(2,1)S(1)}, bf16[1,1792,448]{1,2,0:T(8,128)(2,1)}, u32[]{:S(2)}) copy-start(bf16[1,1792,448]{1,2,0:T(8,128)(2,1)} %param.8) | copy-start | bytes 4816900
  3.0 37.0 %copy-start.1 = (s32[1,2]{1,0:T(1,128)S(1)}, s32[1,2]{1,0:T(1,128)}, u32[]{:S(2)}) copy-start(s32[1,2]{1,0:T(1,128)} %len_ref.1) | copy-start | bytes 28
  3.0 27.2 %all-to-all-start = ((bf16[4,144,256]{2,1,0:T(8,128)(2,1)}), bf16[4,144,256]{2,1,0:T(8,128)(2,1)S(1)}, u32[]{:S(2)}, u32[]{:S(2)}) async-start(bf16[4,144,256]{2,1,0:T(8,128)(2,1)} %get-tuple-element.16), calls=%async_computation | async-start | bytes 589824 | tf_op jit(solution)/shard_map/all_to_all | solution.py:38
  8.0 20.1 %collective-permute-start.1 = (bf16[144,256]{1,0:T(8,128)(2,1)}, bf16[144,256]{1,0:T(8,128)(2,1)S(1)}, u32[]{:S(2)}, u32[]{:S(2)}) collective-permute-start(bf16[144,256]{1,0:T(8,128)(2,1)} %get-tuple-element.15), channel_id=1, source_target_pairs={{0,4},{1,5},{2,6},{3,7},{4,0},{5,1},{6,2},{7,3},{8,12},{9,13},{10,... | collective-permute-start | bytes 221192 | tf_op jit(solution)/shard_map/ppermute | solution.py:302
  20.3 9.8 %collective-permute-start = (bf16[144,256]{1,0:T(8,128)(2,1)}, bf16[144,256]{1,0:T(8,128)(2,1)S(1)}, u32[]{:S(2)}, u32[]{:S(2)}) collective-permute-start(bf16[144,256]{1,0:T(8,128)(2,1)} %get-tuple-element.15), channel_id=1, source_target_pairs={{0,0},{1,1},{2,2},{3,3},{4,4},{5,5},{6,6},{7,7},{8,8},{9,9},{10,10... | collective-permute-start | bytes 221192 | tf_op jit(solution)/shard_map/ppermute | solution.py:301
  31.1 20.5 %all-to-all-start.1 = ((bf16[4,2,144,256]{3,2,1,0:T(8,128)(2,1)}), bf16[4,2,144,256]{3,2,1,0:T(8,128)(2,1)S(1)}, u32[]{:S(2)}, u32[]{:S(2)}) async-start(bf16[4,2,144,256]{3,2,1,0:T(8,128)(2,1)} %shard_map.56), calls=%async_computation.1 | async-start | bytes 1179648 | tf_op jit(solution)/shard_map/all_to_all | solution.py:38
  38.0 36.5 %collective-permute-start.6 = (bf16[448,1792]{1,0:T(8,128)(2,1)S(1)}, bf16[448,1792]{1,0:T(8,128)(2,1)}, u32[]{:S(2)}, u32[]{:S(2)}) collective-permute-start(bf16[448,1792]{1,0:T(8,128)(2,1)S(1)} %bitcast.20), channel_id=1, source_target_pairs={{0,128},{128,0},{1,129},{129,1},{2,130},{130,2},{3,131},{131,3},{4... | collective-permute-start | bytes 4816904 | tf_op jit(solution)/shard_map/ppermute | solution.py:46
  52.4 18.8 %collective-permute-start.3 = (bf16[72,1792]{1,0:T(8,128)(2,1)S(1)}, bf16[72,1792]{1,0:T(8,128)(2,1)S(1)}, u32[]{:S(2)}, u32[]{:S(2)}) collective-permute-start(bf16[72,1792]{1,0:T(8,128)(2,1)S(1)} %get-tuple-element.18), channel_id=1, source_target_pairs={{0,16},{8,24},{16,0},{24,8},{1,17},{9,25},{17,1},{25,9},{2,18},{10... | collective-permute-start | bytes 774152 | tf_op jit(solution)/shard_map/ppermute | solution.py:313
  62.2 29.8 %collective-permute-start.5 = (bf16[144,1792]{1,0:T(8,128)(2,1)S(1)}, bf16[144,1792]{1,0:T(8,128)(2,1)}, u32[]{:S(2)}, u32[]{:S(2)}) collective-permute-start(bf16[144,1792]{1,0:T(8,128)(2,1)S(1)} %get-tuple-element.17.a_ref), channel_id=1, source_target_pairs={{0,24},{8,16},{16,8},{24,0},{1,25},{9,17},{17,9},{25,1},{2,26},{10... | collective-permute-start | bytes 1548296 | tf_op jit(solution)/shard_map/ppermute | solution.py:314
  64.2 27.9 %collective-permute-start.2 = (bf16[144,1792]{1,0:T(8,128)(2,1)S(1)}, bf16[144,1792]{1,0:T(8,128)(2,1)}, u32[]{:S(2)}, u32[]{:S(2)}) collective-permute-start(bf16[144,1792]{1,0:T(8,128)(2,1)S(1)} %get-tuple-element.17.a_ref), channel_id=1, source_target_pairs={{0,8},{8,0},{16,24},{24,16},{1,9},{9,1},{17,25},{25,17},{2,10},{10... | collective-permute-start | bytes 1548296 | tf_op jit(solution)/shard_map/ppermute | solution.py:314
  67.7 28.6 %all-to-all-start.2 = ((bf16[16,80,128]{2,1,0:T(8,128)(2,1)}), bf16[16,80,128]{2,1,0:T(8,128)(2,1)S(1)}, u32[]{:S(2)}, u32[]{:S(2)}) async-start(bf16[16,80,128]{2,1,0:T(8,128)(2,1)} %shard_map.59), calls=%async_computation.2 | async-start | bytes 655360 | tf_op jit(solution)/shard_map/all_to_all | solution.py:38
  71.2 20.8 %collective-permute-start.4 = (bf16[72,1792]{1,0:T(8,128)(2,1)S(1)}, bf16[72,1792]{1,0:T(8,128)(2,1)S(1)}, u32[]{:S(2)}, u32[]{:S(2)}) collective-permute-start(bf16[72,1792]{1,0:T(8,128)(2,1)S(1)} %collective-permute-done.3.c_ref), channel_id=1, source_target_pairs={{0,1},{1,0},{2,3},{3,2},{4,5},{5,4},{6,7},{7,6},{8,9},{9,8},{10,11... | collective-permute-start | bytes 774152 | tf_op jit(solution)/shard_map/ppermute | solution.py:315
  96.2 9.7 %all-to-all-start.3 = ((bf16[4,72,448]{2,1,0:T(8,128)(2,1)}), bf16[4,72,448]{2,1,0:T(8,128)(2,1)S(1)}, u32[]{:S(2)}, u32[]{:S(2)}) async-start(bf16[4,72,448]{2,1,0:T(8,128)(2,1)} %shard_map.58), calls=%async_computation.3 | async-start | bytes 589824 | tf_op jit(solution)/shard_map/all_to_all | solution.py:38
  106.0 21.1 %collective-permute-start.7 = (bf16[72,448]{1,0:T(8,128)(2,1)S(1)}, bf16[72,448]{1,0:T(8,128)(2,1)S(1)}, u32[]{:S(2)}, u32[]{:S(2)}) collective-permute-start(bf16[72,448]{1,0:T(8,128)(2,1)S(1)} %shard_map.60.one_ref), channel_id=1, source_target_pairs={{0,256},{256,0},{1,257},{257,1},{2,258},{258,2},{3,259},{259,3},{4... | collective-permute-start | bytes 193544 | tf_op jit(solution)/shard_map/ppermute | solution.py:46
  117.4 14.0 %collective-permute-start.11 = (bf16[2,152,256]{2,1,0:T(8,128)(2,1)S(1)}, bf16[2,152,256]{2,1,0:T(8,128)(2,1)S(1)}, u32[]{:S(2)}, u32[]{:S(2)}) collective-permute-start(bf16[2,152,256]{2,1,0:T(8,128)(2,1)S(1)} %shard_map.61), channel_id=1, source_target_pairs={{0,24},{8,16},{16,8},{24,0},{1,25},{9,17},{17,9},{25,1},{2,26},{10... | collective-permute-start | bytes 466952 | tf_op jit(solution)/shard_map/ppermute | solution.py:283
  122.4 8.9 %collective-permute-start.10 = (bf16[2,152,256]{2,1,0:T(8,128)(2,1)S(1)}, bf16[2,152,256]{2,1,0:T(8,128)(2,1)S(1)}, u32[]{:S(2)}, u32[]{:S(2)}) collective-permute-start(bf16[2,152,256]{2,1,0:T(8,128)(2,1)S(1)} %shard_map.61), channel_id=1, source_target_pairs={{0,16},{8,24},{16,0},{24,8},{1,17},{9,25},{17,1},{25,9},{2,18},{10... | collective-permute-start | bytes 466952 | tf_op jit(solution)/shard_map/ppermute | solution.py:283
  125.2 7.8 %collective-permute-start.9 = (bf16[2,152,256]{2,1,0:T(8,128)(2,1)S(1)}, bf16[2,152,256]{2,1,0:T(8,128)(2,1)S(1)}, u32[]{:S(2)}, u32[]{:S(2)}) collective-permute-start(bf16[2,152,256]{2,1,0:T(8,128)(2,1)S(1)} %shard_map.61), channel_id=1, source_target_pairs={{0,8},{8,0},{16,24},{24,16},{1,9},{9,1},{17,25},{25,17},{2,10},{10... | collective-permute-start | bytes 466952 | tf_op jit(solution)/shard_map/ppermute | solution.py:283
  127.9 9.7 %all-to-all-start.4 = ((bf16[4,72,448]{2,1,0:T(8,128)(2,1)}), bf16[4,72,448]{2,1,0:T(8,128)(2,1)S(1)}, u32[]{:S(2)}, u32[]{:S(2)}) async-start(bf16[4,72,448]{2,1,0:T(8,128)(2,1)} %shard_map.62), calls=%async_computation.4 | async-start | bytes 589824 | tf_op jit(solution)/shard_map/all_to_all | solution.py:38
  133.1 10.5 %collective-permute-start.12 = (bf16[4,2,152,256]{3,2,1,0:T(8,128)(2,1)S(1)}, bf16[4,2,152,256]{3,2,1,0:T(8,128)(2,1)S(1)}, u32[]{:S(2)}, u32[]{:S(2)}) collective-permute-start(bf16[4,2,152,256]{3,2,1,0:T(8,128)(2,1)S(1)} %pad_maximum_fusion.own_ref), channel_id=1, source_target_pairs={{0,128},{128,0},{1,129},{129,1},{2,130},{130,2},{3,131},{131,3},{4... | collective-permute-start | bytes 1867784 | tf_op jit(solution)/shard_map/ppermute | solution.py:46
  137.6 7.0 %collective-permute-start.8 = (bf16[2,144,448]{2,1,0:T(8,128)(2,1)S(1)}, bf16[2,144,448]{2,1,0:T(8,128)(2,1)S(1)}, u32[]{:S(2)}, u32[]{:S(2)}) collective-permute-start(bf16[2,144,448]{2,1,0:T(8,128)(2,1)S(1)} %bitcast.18), channel_id=1, source_target_pairs={{0,128},{128,0},{1,129},{129,1},{2,130},{130,2},{3,131},{131,3},{4... | collective-permute-start | bytes 774152 | tf_op jit(solution)/shard_map/ppermute | solution.py:46

commit v10 on v8

--- a/solution.py
+++ b/solution.py
@@ -79,15 +79,22 @@
     lines_ref[:, FEAT:] = jnp.zeros((VALID, WIDE - FEAT), BF)
 
 
-def join_kernel(near_ref, far_ref, parts_ref, out_ref):
+def pair_kernel(near_ref, far_ref, out_ref):
+    out_ref[0] = near_ref[...]
+    out_ref[1] = far_ref[...]
+
+
+def join_kernel(pair_ref, parts_ref, out_ref):
     total = parts_ref[0].astype(F32)
     for y in range(1, 4):
         total += parts_ref[y].astype(F32)
     total = total.astype(BF)
     for d in range(4):
-        for w, ref in enumerate((near_ref, far_ref)):
+        for w in range(2):
             at = d * 64 + w * 32
-            out_ref[d, w] = jnp.concatenate([ref[:, :FEAT], total[:, at : at + 32]], axis=1)
+            out_ref[d, w] = jnp.concatenate(
+                [pair_ref[w][:, :FEAT], total[:, at : at + 32]], axis=1
+            )
 
 
 def sort_kernel(where_ref, both_ref, out_ref):
@@ -297,7 +304,8 @@
     basis = basis_out[0].T
     cols = basis.shape[0]
     other_basis = swap(basis, "core")
-    both = call(join_kernel, like(4, 2, VALID, WIDE), near, far, partial, scalars=0)
+    both = call(pair_kernel, like(2, VALID, WIDE), near, far, scalars=0, cost=HINT)
+    both = call(join_kernel, like(4, 2, VALID, WIDE), both, partial, scalars=0)
     both = exchange(both, "zq")
     lines = call(sort_kernel, like(VALID, 8 * FEAT), where, both)
     ins = call(pack_kernel, like(16, 80, 128), where, both)

time: 140 us -> 140 us (level)
  waiting for transfers between devices: 34.4 us -> 37.5 us
  starting transfers between devices: 87.7 us -> 84.9 us
    all_to_all x5, waiting for transfers between devices: 17.1 us -> 25.6 us  [exchange(): return lax.all_to_all(x, axis, 0, 0, tiled=True)]
    ppermute x6, starting transfers between devices: 23.6 us -> 18 us  [others(): lax.ppermute(x, axis, [(i, i ^ k) for i in range(n)])]
    ppermute x4, starting transfers between devices: 21.1 us -> 26 us  [swap(): return lax.ppermute(x, axis, [(0, 1), (1, 0)])]
    ppermute x6, waiting for transfers between devices: 14.3 us -> 11.7 us  [others(): lax.ppermute(x, axis, [(i, i ^ k) for i in range(n)])]
    all_to_all x5, starting transfers between devices: 22.9 us -> 20.6 us  [exchange(): return lax.all_to_all(x, axis, 0, 0, tiled=True)]
    ppermute x1, waiting for transfers between devices: 2.05 us -> 0.01 us  [per_device(): near = lax.ppermute(lines, PLANE, to_basis(False))]
    pallas_call x8 -> x9, Pallas kernels: 5.07 us -> 5.08 us  [call(): pl.pallas_call(kernel, in_specs=[smem] * scalars + [vmem] * (len(args) -...]
  transfers between devices with their start and end apart: 17 -> 17, of which waited for: 7 -> 6; matrix products, arithmetic and copies ran while one was open for 0% -> 0% of each run, Pallas kernels for 6% -> 6%
where the time goes in v10:
time: 140 us; the launch traced here: 139 us
  starting transfers between devices  84.9 us (61%)
  waiting for transfers between devices  37.5 us (27%)
  Pallas kernels  16.4 us (12%)
    ppermute x4, starting transfers between devices, swap(): return lax.ppermute(x, axis, [(0, 1), (1, 0)])  26 us
    all_to_all x5, waiting for transfers between devices, exchange(): return lax.all_to_all(x, axis, 0, 0, tiled=True)  25.6 us
    all_to_all x5, starting transfers between devices, exchange(): return lax.all_to_all(x, axis, 0, 0, tiled=True)  20.6 us
    ppermute x6, starting transfers between devices, others(): lax.ppermute(x, axis, [(i, i ^ k) for i in range(n)])  18 us
    ppermute x1, starting transfers between devices, per_device(): far = lax.ppermute(lines, PLANE, to_basis(True))  12.7 us
    ppermute x6, waiting for transfers between devices, others(): lax.ppermute(x, axis, [(i, i ^ k) for i in range(n)])  11.7 us
    ppermute x1, starting transfers between devices, per_device(): near = lax.ppermute(lines, PLANE, to_basis(False))  7.77 us
    pallas_call x9, Pallas kernels, call(): pl.pallas_call(kernel, in_specs=[smem] * scalars + [vmem] * (len(args) -...  5.08 us
  transfers between devices with their start and end apart: 17, of which 6 were waited for; matrix products, arithmetic and copies ran while one was open for 0% of the time, Pallas kernels for 6%

profile of v10, /device:TPU:1, one launch (start us, length us, event | category | flops | bytes accessed | tf_op | source)
XLA Modules:
  0.0 139.4 jit_solution(9920939832451240483)
XLA Ops:
  0.0 2.8 %shard_map.55 = (bf16[144,256]{1,0:T(8,128)(2,1)}, bf16[4,144,256]{2,1,0:T(8,128)(2,1)}) custom-call(s32[1,2]{1,0:T(1,128)} %len_ref.1, bf16[192,224]{1,0:T(8,128)(2,1)} %grads_hbm.1, bf16[192,256]{1,0:T(8,128)(2,1)} %acts_hbm.1, bf16[256,1024]{1,0:T(8,128)(2,1)} %basis_hbm.1), custom_call_target="tpu_custom_call" | custom-call | tf_op jit(solution)/shard_map/pallas_call | solution.py:292
  2.8 12.7 %collective-permute-start.1 = (bf16[144,256]{1,0:T(8,128)(2,1)}, bf16[144,256]{1,0:T(8,128)(2,1)S(1)}, u32[]{:S(2)}, u32[]{:S(2)}) collective-permute-start(bf16[144,256]{1,0:T(8,128)(2,1)} %get-tuple-element.13), channel_id=1, source_target_pairs={{0,4},{1,5},{2,6},{3,7},{4,0},{5,1},{6,2},{7,3},{8,12},{9,13},{10,... | collective-permute-start | bytes 221192 | tf_op jit(solution)/shard_map/ppermute | solution.py:302
  15.5 7.8 %collective-permute-start = (bf16[144,256]{1,0:T(8,128)(2,1)}, bf16[144,256]{1,0:T(8,128)(2,1)S(1)}, u32[]{:S(2)}, u32[]{:S(2)}) collective-permute-start(bf16[144,256]{1,0:T(8,128)(2,1)} %get-tuple-element.13), channel_id=1, source_target_pairs={{0,0},{1,1},{2,2},{3,3},{4,4},{5,5},{6,6},{7,7},{8,8},{9,9},{10,10... | collective-permute-start | bytes 221192 | tf_op jit(solution)/shard_map/ppermute | solution.py:301
  23.3 3.5 %all-to-all-start = ((bf16[4,144,256]{2,1,0:T(8,128)(2,1)}), bf16[4,144,256]{2,1,0:T(8,128)(2,1)S(1)}, u32[]{:S(2)}, u32[]{:S(2)}) async-start(bf16[4,144,256]{2,1,0:T(8,128)(2,1)} %get-tuple-element.14), calls=%async_computation | async-start | bytes 589824 | tf_op jit(solution)/shard_map/all_to_all | solution.py:38
  26.8 7.3 %all-to-all-done.parts_ref = bf16[4,144,256]{2,1,0:T(8,128)(2,1)S(1)} async-done(((bf16[4,144,256]{2,1,0:T(8,128)(2,1)}), bf16[4,144,256]{2,1,0:T(8,128)(2,1)S(1)}, u32[]{:S(2)}, u32[]{:S(2)}) %all-to-all-start) | async-done | bytes 294944 | tf_op jit(solution)/shard_map/all_to_all | solution.py:38
  35.0 3.5 %all-to-all-start.1 = ((bf16[4,2,144,256]{3,2,1,0:T(8,128)(2,1)}), bf16[4,2,144,256]{3,2,1,0:T(8,128)(2,1)S(1)}, u32[]{:S(2)}, u32[]{:S(2)}) async-start(bf16[4,2,144,256]{3,2,1,0:T(8,128)(2,1)} %shard_map.57), calls=%async_computation.1 | async-start | bytes 1179648 | tf_op jit(solution)/shard_map/all_to_all | solution.py:38
  38.5 2.5 %collective-permute-start.5 = (bf16[448,1792]{1,0:T(8,128)(2,1)S(1)}, bf16[448,1792]{1,0:T(8,128)(2,1)}, u32[]{:S(2)}, u32[]{:S(2)}) collective-permute-start(bf16[448,1792]{1,0:T(8,128)(2,1)S(1)} %bitcast.20), channel_id=1, source_target_pairs={{0,128},{128,0},{1,129},{129,1},{2,130},{130,2},{3,131},{131,3},{4... | collective-permute-start | bytes 4816904 | tf_op jit(solution)/shard_map/ppermute | solution.py:46
  41.2 12.7 %all-to-all-done.1.both_ref = bf16[4,2,144,256]{3,2,1,0:T(8,128)(2,1)S(1)} async-done(((bf16[4,2,144,256]{3,2,1,0:T(8,128)(2,1)}), bf16[4,2,144,256]{3,2,1,0:T(8,128)(2,1)S(1)}, u32[]{:S(2)}, u32[]{:S(2)}) %all-to-all-start.1) | async-done | bytes 589856 | tf_op jit(solution)/shard_map/all_to_all | solution.py:38
  54.7 2.8 %collective-permute-start.4 = (bf16[144,1792]{1,0:T(8,128)(2,1)S(1)}, bf16[144,1792]{1,0:T(8,128)(2,1)}, u32[]{:S(2)}, u32[]{:S(2)}) collective-permute-start(bf16[144,1792]{1,0:T(8,128)(2,1)S(1)} %shard_map.58.a_ref), channel_id=1, source_target_pairs={{0,24},{8,16},{16,8},{24,0},{1,25},{9,17},{17,9},{25,1},{2,26},{10... | collective-permute-start | bytes 1548296 | tf_op jit(solution)/shard_map/ppermute | solution.py:283
  57.5 3.1 %collective-permute-start.3 = (bf16[144,1792]{1,0:T(8,128)(2,1)S(1)}, bf16[144,1792]{1,0:T(8,128)(2,1)}, u32[]{:S(2)}, u32[]{:S(2)}) collective-permute-start(bf16[144,1792]{1,0:T(8,128)(2,1)S(1)} %shard_map.58.a_ref), channel_id=1, source_target_pairs={{0,16},{8,24},{16,0},{24,8},{1,17},{9,25},{17,1},{25,9},{2,18},{10... | collective-permute-start | bytes 1548296 | tf_op jit(solution)/shard_map/ppermute | solution.py:283
  60.6 3.1 %collective-permute-start.2 = (bf16[144,1792]{1,0:T(8,128)(2,1)S(1)}, bf16[144,1792]{1,0:T(8,128)(2,1)}, u32[]{:S(2)}, u32[]{:S(2)}) collective-permute-start(bf16[144,1792]{1,0:T(8,128)(2,1)S(1)} %shard_map.58.a_ref), channel_id=1, source_target_pairs={{0,8},{8,0},{16,24},{24,16},{1,9},{9,1},{17,25},{25,17},{2,10},{10... | collective-permute-start | bytes 1548296 | tf_op jit(solution)/shard_map/ppermute | solution.py:283
  65.2 6.2 %all-to-all-start.2 = ((bf16[16,80,128]{2,1,0:T(8,128)(2,1)}), bf16[16,80,128]{2,1,0:T(8,128)(2,1)S(1)}, u32[]{:S(2)}, u32[]{:S(2)}) async-start(bf16[16,80,128]{2,1,0:T(8,128)(2,1)} %shard_map.60), calls=%async_computation.2 | async-start | bytes 655360 | tf_op jit(solution)/shard_map/all_to_all | solution.py:38
  71.4 9.3 %collective-permute-done.4.d_ref = bf16[144,1792]{1,0:T(8,128)(2,1)} collective-permute-done((bf16[144,1792]{1,0:T(8,128)(2,1)S(1)}, bf16[144,1792]{1,0:T(8,128)(2,1)}, u32[]{:S(2)}, u32[]{:S(2)}) %collective-permute-start.4) | collective-permute-done | bytes 516128 | tf_op jit(solution)/shard_map/ppermute | solution.py:283
  80.8 2.3 %collective-permute-done.2.b_ref = bf16[144,1792]{1,0:T(8,128)(2,1)} collective-permute-done((bf16[144,1792]{1,0:T(8,128)(2,1)S(1)}, bf16[144,1792]{1,0:T(8,128)(2,1)}, u32[]{:S(2)}, u32[]{:S(2)}) %collective-permute-start.2) | collective-permute-done | bytes 516128 | tf_op jit(solution)/shard_map/ppermute | solution.py:283
  83.1 4.2 %shard_map.59 = bf16[4,72,448]{2,1,0:T(8,128)(2,1)} custom-call(s32[8]{0:T(128)S(1)} %stack.50.where_ref, bf16[144,1792]{1,0:T(8,128)(2,1)S(1)} %shard_map.58.a_ref, bf16[144,1792]{1,0:T(8,128)(2,1)} %collective-permute-done.2.b_ref, bf16[144,1792]{1,0:T(8,128)(2,1)} %collective-permute-done.3.c_ref, bf16[144,1792]{1,0:T(8,128)(2,1)} %collective-permute-done.4.d_ref, ...), custom_call_target="tpu_custom_call" | custom-call | flops 30000001024 | bytes 1000000 | tf_op jit(solution)/shard_map/pallas_call | solution.py:168
  87.3 4.0 %all-to-all-start.3 = ((bf16[4,72,448]{2,1,0:T(8,128)(2,1)}), bf16[4,72,448]{2,1,0:T(8,128)(2,1)S(1)}, u32[]{:S(2)}, u32[]{:S(2)}) async-start(bf16[4,72,448]{2,1,0:T(8,128)(2,1)} %shard_map.59), calls=%async_computation.3 | async-start | bytes 589824 | tf_op jit(solution)/shard_map/all_to_all | solution.py:38
  91.4 5.6 %all-to-all-done.3.parts_ref = bf16[4,72,448]{2,1,0:T(8,128)(2,1)S(1)} async-done(((bf16[4,72,448]{2,1,0:T(8,128)(2,1)}), bf16[4,72,448]{2,1,0:T(8,128)(2,1)S(1)}, u32[]{:S(2)}, u32[]{:S(2)}) %all-to-all-start.3) | async-done | bytes 258080 | tf_op jit(solution)/shard_map/all_to_all | solution.py:38
  97.0 8.5 %collective-permute-start.6 = (bf16[72,448]{1,0:T(8,128)(2,1)S(1)}, bf16[72,448]{1,0:T(8,128)(2,1)S(1)}, u32[]{:S(2)}, u32[]{:S(2)}) collective-permute-start(bf16[72,448]{1,0:T(8,128)(2,1)S(1)} %shard_map.61.one_ref), channel_id=1, source_target_pairs={{0,256},{256,0},{1,257},{257,1},{2,258},{258,2},{3,259},{259,3},{4... | collective-permute-start | bytes 193544 | tf_op jit(solution)/shard_map/ppermute | solution.py:46
  107.5 3.8 %collective-permute-start.9 = (bf16[2,152,256]{2,1,0:T(8,128)(2,1)S(1)}, bf16[2,152,256]{2,1,0:T(8,128)(2,1)S(1)}, u32[]{:S(2)}, u32[]{:S(2)}) collective-permute-start(bf16[2,152,256]{2,1,0:T(8,128)(2,1)S(1)} %shard_map.62), channel_id=1, source_target_pairs={{0,16},{8,24},{16,0},{24,8},{1,17},{9,25},{17,1},{25,9},{2,18},{10... | collective-permute-start | bytes 466952 | tf_op jit(solution)/shard_map/ppermute | solution.py:283
  111.3 3.3 %collective-permute-start.8 = (bf16[2,152,256]{2,1,0:T(8,128)(2,1)S(1)}, bf16[2,152,256]{2,1,0:T(8,128)(2,1)S(1)}, u32[]{:S(2)}, u32[]{:S(2)}) collective-permute-start(bf16[2,152,256]{2,1,0:T(8,128)(2,1)S(1)} %shard_map.62), channel_id=1, source_target_pairs={{0,8},{8,0},{16,24},{24,16},{1,9},{9,1},{17,25},{25,17},{2,10},{10... | collective-permute-start | bytes 466952 | tf_op jit(solution)/shard_map/ppermute | solution.py:283
  115.3 3.5 %all-to-all-start.4 = ((bf16[4,72,448]{2,1,0:T(8,128)(2,1)}), bf16[4,72,448]{2,1,0:T(8,128)(2,1)S(1)}, u32[]{:S(2)}, u32[]{:S(2)}) async-start(bf16[4,72,448]{2,1,0:T(8,128)(2,1)} %shard_map.63), calls=%async_computation.4 | async-start | bytes 589824 | tf_op jit(solution)/shard_map/all_to_all | solution.py:38
  118.9 8.2 %collective-permute-start.11 = (bf16[4,2,152,256]{3,2,1,0:T(8,128)(2,1)S(1)}, bf16[4,2,152,256]{3,2,1,0:T(8,128)(2,1)S(1)}, u32[]{:S(2)}, u32[]{:S(2)}) collective-permute-start(bf16[4,2,152,256]{3,2,1,0:T(8,128)(2,1)S(1)} %pad_maximum_fusion.own_ref), channel_id=1, source_target_pairs={{0,128},{128,0},{1,129},{129,1},{2,130},{130,2},{3,131},{131,3},{4... | collective-permute-start | bytes 1867784 | tf_op jit(solution)/shard_map/ppermute | solution.py:46
  127.2 6.7 %collective-permute-start.7 = (bf16[2,144,448]{2,1,0:T(8,128)(2,1)S(1)}, bf16[2,144,448]{2,1,0:T(8,128)(2,1)S(1)}, u32[]{:S(2)}, u32[]{:S(2)}) collective-permute-start(bf16[2,144,448]{2,1,0:T(8,128)(2,1)S(1)} %bitcast.18), channel_id=1, source_target_pairs={{0,128},{128,0},{1,129},{129,1},{2,130},{130,2},{3,131},{131,3},{4... | collective-permute-start | bytes 774152 | tf_op jit(solution)/shard_map/ppermute | solution.py:46
  135.0 4.3 %shard_map.66 = f32[448,1024]{1,0:T(8,128)} custom-call(s32[8]{0:T(128)S(1)} %stack.50.where_ref, bf16[2,448,144]{2,1,0:T(8,128)(2,1)S(1)} %shard_map.64.own_ref, bf16[2,144,448]{2,1,0:T(8,128)(2,1)S(1)} %collective-permute-done.7.other_ref, bf16[4,144,1024]{2,1,0:T(8,128)(2,1)S(1)} %get-tuple-element.19.in_ref, ...), custom_call_target="tpu_custom_call" | custom-call | tf_op jit(solution)/shard_map/pallas_call | solution.py:243
  (28 shorter events, 7.5 us)
Async XLA Ops:
  2.8 23.9 %collective-permute-start.1 = (bf16[144,256]{1,0:T(8,128)(2,1)}, bf16[144,256]{1,0:T(8,128)(2,1)S(1)}, u32[]{:S(2)}, u32[]{:S(2)}) collective-permute-start(bf16[144,256]{1,0:T(8,128)(2,1)} %get-tuple-element.13), channel_id=1, source_target_pairs={{0,4},{1,5},{2,6},{3,7},{4,0},{5,1},{6,2},{7,3},{8,12},{9,13},{10,... | collective-permute-start | bytes 221192 | tf_op jit(solution)/shard_map/ppermute | solution.py:302
  15.5 11.3 %collective-permute-start = (bf16[144,256]{1,0:T(8,128)(2,1)}, bf16[144,256]{1,0:T(8,128)(2,1)S(1)}, u32[]{:S(2)}, u32[]{:S(2)}) collective-permute-start(bf16[144,256]{1,0:T(8,128)(2,1)} %get-tuple-element.13), channel_id=1, source_target_pairs={{0,0},{1,1},{2,2},{3,3},{4,4},{5,5},{6,6},{7,7},{8,8},{9,9},{10,10... | collective-permute-start | bytes 221192 | tf_op jit(solution)/shard_map/ppermute | solution.py:301
  23.3 10.8 %all-to-all-start = ((bf16[4,144,256]{2,1,0:T(8,128)(2,1)}), bf16[4,144,256]{2,1,0:T(8,128)(2,1)S(1)}, u32[]{:S(2)}, u32[]{:S(2)}) async-start(bf16[4,144,256]{2,1,0:T(8,128)(2,1)} %get-tuple-element.14), calls=%async_computation | async-start | bytes 589824 | tf_op jit(solution)/shard_map/all_to_all | solution.py:38
  26.8 11.7 %copy-start = (bf16[1,1792,448]{1,2,0:T(8,128)(2,1)S(1)}, bf16[1,1792,448]{1,2,0:T(8,128)(2,1)}, u32[]{:S(2)}) copy-start(bf16[1,1792,448]{1,2,0:T(8,128)(2,1)} %param.8) | copy-start | bytes 4816900
  26.8 14.3 %copy-start.1 = (s32[1,2]{1,0:T(1,128)S(1)}, s32[1,2]{1,0:T(1,128)}, u32[]{:S(2)}) copy-start(s32[1,2]{1,0:T(1,128)} %len_ref.1) | copy-start | bytes 28
  35.0 18.9 %all-to-all-start.1 = ((bf16[4,2,144,256]{3,2,1,0:T(8,128)(2,1)}), bf16[4,2,144,256]{3,2,1,0:T(8,128)(2,1)S(1)}, u32[]{:S(2)}, u32[]{:S(2)}) async-start(bf16[4,2,144,256]{3,2,1,0:T(8,128)(2,1)} %shard_map.57), calls=%async_computation.1 | async-start | bytes 1179648 | tf_op jit(solution)/shard_map/all_to_all | solution.py:38
  38.5 32.9 %collective-permute-start.5 = (bf16[448,1792]{1,0:T(8,128)(2,1)S(1)}, bf16[448,1792]{1,0:T(8,128)(2,1)}, u32[]{:S(2)}, u32[]{:S(2)}) collective-permute-start(bf16[448,1792]{1,0:T(8,128)(2,1)S(1)} %bitcast.20), channel_id=1, source_target_pairs={{0,128},{128,0},{1,129},{129,1},{2,130},{130,2},{3,131},{131,3},{4... | collective-permute-start | bytes 4816904 | tf_op jit(solution)/shard_map/ppermute | solution.py:46
  54.7 26.1 %collective-permute-start.4 = (bf16[144,1792]{1,0:T(8,128)(2,1)S(1)}, bf16[144,1792]{1,0:T(8,128)(2,1)}, u32[]{:S(2)}, u32[]{:S(2)}) collective-permute-start(bf16[144,1792]{1,0:T(8,128)(2,1)S(1)} %shard_map.58.a_ref), channel_id=1, source_target_pairs={{0,24},{8,16},{16,8},{24,0},{1,25},{9,17},{17,9},{25,1},{2,26},{10... | collective-permute-start | bytes 1548296 | tf_op jit(solution)/shard_map/ppermute | solution.py:283
  57.5 23.3 %collective-permute-start.3 = (bf16[144,1792]{1,0:T(8,128)(2,1)S(1)}, bf16[144,1792]{1,0:T(8,128)(2,1)}, u32[]{:S(2)}, u32[]{:S(2)}) collective-permute-start(bf16[144,1792]{1,0:T(8,128)(2,1)S(1)} %shard_map.58.a_ref), channel_id=1, source_target_pairs={{0,16},{8,24},{16,0},{24,8},{1,17},{9,25},{17,1},{25,9},{2,18},{10... | collective-permute-start | bytes 1548296 | tf_op jit(solution)/shard_map/ppermute | solution.py:283
  60.6 22.5 %collective-permute-start.2 = (bf16[144,1792]{1,0:T(8,128)(2,1)S(1)}, bf16[144,1792]{1,0:T(8,128)(2,1)}, u32[]{:S(2)}, u32[]{:S(2)}) collective-permute-start(bf16[144,1792]{1,0:T(8,128)(2,1)S(1)} %shard_map.58.a_ref), channel_id=1, source_target_pairs={{0,8},{8,0},{16,24},{24,16},{1,9},{9,1},{17,25},{25,17},{2,10},{10... | collective-permute-start | bytes 1548296 | tf_op jit(solution)/shard_map/ppermute | solution.py:283
  65.2 22.0 %all-to-all-start.2 = ((bf16[16,80,128]{2,1,0:T(8,128)(2,1)}), bf16[16,80,128]{2,1,0:T(8,128)(2,1)S(1)}, u32[]{:S(2)}, u32[]{:S(2)}) async-start(bf16[16,80,128]{2,1,0:T(8,128)(2,1)} %shard_map.60), calls=%async_computation.2 | async-start | bytes 655360 | tf_op jit(solution)/shard_map/all_to_all | solution.py:38
  87.3 9.7 %all-to-all-start.3 = ((bf16[4,72,448]{2,1,0:T(8,128)(2,1)}), bf16[4,72,448]{2,1,0:T(8,128)(2,1)S(1)}, u32[]{:S(2)}, u32[]{:S(2)}) async-start(bf16[4,72,448]{2,1,0:T(8,128)(2,1)} %shard_map.59), calls=%async_computation.3 | async-start | bytes 589824 | tf_op jit(solution)/shard_map/all_to_all | solution.py:38
  97.0 17.5 %collective-permute-start.6 = (bf16[72,448]{1,0:T(8,128)(2,1)S(1)}, bf16[72,448]{1,0:T(8,128)(2,1)S(1)}, u32[]{:S(2)}, u32[]{:S(2)}) collective-permute-start(bf16[72,448]{1,0:T(8,128)(2,1)S(1)} %shard_map.61.one_ref), channel_id=1, source_target_pairs={{0,256},{256,0},{1,257},{257,1},{2,258},{258,2},{3,259},{259,3},{4... | collective-permute-start | bytes 193544 | tf_op jit(solution)/shard_map/ppermute | solution.py:46
  105.6 13.2 %collective-permute-start.10 = (bf16[2,152,256]{2,1,0:T(8,128)(2,1)S(1)}, bf16[2,152,256]{2,1,0:T(8,128)(2,1)S(1)}, u32[]{:S(2)}, u32[]{:S(2)}) collective-permute-start(bf16[2,152,256]{2,1,0:T(8,128)(2,1)S(1)} %shard_map.62), channel_id=1, source_target_pairs={{0,24},{8,16},{16,8},{24,0},{1,25},{9,17},{17,9},{25,1},{2,26},{10... | collective-permute-start | bytes 466952 | tf_op jit(solution)/shard_map/ppermute | solution.py:283
  107.5 11.3 %collective-permute-start.9 = (bf16[2,152,256]{2,1,0:T(8,128)(2,1)S(1)}, bf16[2,152,256]{2,1,0:T(8,128)(2,1)S(1)}, u32[]{:S(2)}, u32[]{:S(2)}) collective-permute-start(bf16[2,152,256]{2,1,0:T(8,128)(2,1)S(1)} %shard_map.62), channel_id=1, source_target_pairs={{0,16},{8,24},{16,0},{24,8},{1,17},{9,25},{17,1},{25,9},{2,18},{10... | collective-permute-start | bytes 466952 | tf_op jit(solution)/shard_map/ppermute | solution.py:283
  111.3 7.5 %collective-permute-start.8 = (bf16[2,152,256]{2,1,0:T(8,128)(2,1)S(1)}, bf16[2,152,256]{2,1,0:T(8,128)(2,1)S(1)}, u32[]{:S(2)}, u32[]{:S(2)}) collective-permute-start(bf16[2,152,256]{2,1,0:T(8,128)(2,1)S(1)} %shard_map.62), channel_id=1, source_target_pairs={{0,8},{8,0},{16,24},{24,16},{1,9},{9,1},{17,25},{25,17},{2,10},{10... | collective-permute-start | bytes 466952 | tf_op jit(solution)/shard_map/ppermute | solution.py:283
  115.3 11.8 %all-to-all-start.4 = ((bf16[4,72,448]{2,1,0:T(8,128)(2,1)}), bf16[4,72,448]{2,1,0:T(8,128)(2,1)S(1)}, u32[]{:S(2)}, u32[]{:S(2)}) async-start(bf16[4,72,448]{2,1,0:T(8,128)(2,1)} %shard_map.63), calls=%async_computation.4 | async-start | bytes 589824 | tf_op jit(solution)/shard_map/all_to_all | solution.py:38
  118.9 15.1 %collective-permute-start.11 = (bf16[4,2,152,256]{3,2,1,0:T(8,128)(2,1)S(1)}, bf16[4,2,152,256]{3,2,1,0:T(8,128)(2,1)S(1)}, u32[]{:S(2)}, u32[]{:S(2)}) collective-permute-start(bf16[4,2,152,256]{3,2,1,0:T(8,128)(2,1)S(1)} %pad_maximum_fusion.own_ref), channel_id=1, source_target_pairs={{0,128},{128,0},{1,129},{129,1},{2,130},{130,2},{3,131},{131,3},{4... | collective-permute-start | bytes 1867784 | tf_op jit(solution)/shard_map/ppermute | solution.py:46
  127.2 7.9 %collective-permute-start.7 = (bf16[2,144,448]{2,1,0:T(8,128)(2,1)S(1)}, bf16[2,144,448]{2,1,0:T(8,128)(2,1)S(1)}, u32[]{:S(2)}, u32[]{:S(2)}) collective-permute-start(bf16[2,144,448]{2,1,0:T(8,128)(2,1)S(1)} %bitcast.18), channel_id=1, source_target_pairs={{0,128},{128,0},{1,129},{129,1},{2,130},{130,2},{3,131},{131,3},{4... | collective-permute-start | bytes 774152 | tf_op jit(solution)/shard_map/ppermute | solution.py:46

commit v11 on v10

--- a/solution.py
+++ b/solution.py
@@ -97,15 +97,12 @@
             )
 
 
-def sort_kernel(where_ref, both_ref, out_ref):
+def sort_kernel(where_ref, both_ref, out_ref, in_ref):
     zh, crossed = where_ref[0], where_ref[1]
     for f in range(8):
         far = (jnp.int32(f // 4) != zh).astype(jnp.int32) ^ crossed
         at = (f % 4) ^ (3 * (far & crossed))
         out_ref[:, f * FEAT : (f + 1) * FEAT] = both_ref[at, far][:, :FEAT]
-
-
-def pack_kernel(where_ref, both_ref, in_ref):
     sums = []
     for w in range(2):
         total = both_ref[0, w][:, FEAT:].astype(F32)
@@ -162,7 +159,7 @@
 
 def project(where, lines, basis, other_basis):
     cols, rows = basis.shape
-    deep = rows // 2
+    deep = rows
     line = pl.BlockSpec((VALID, deep), lambda k: (0, k))
     rotated = pl.BlockSpec((cols, deep), lambda k: (0, k))
     return pl.pallas_call(
@@ -224,7 +221,7 @@
                 left_ref[2 * at] = first
                 left_ref[2 * at + 1] = lines - first
 
-    rows = 224
+    rows = 112
     for o in range(448 // rows):
         total = jnp.zeros((rows, eig_ref.shape[1]), F32)
         for s in range(8):
@@ -238,7 +235,7 @@
 
 
 def squares(where, left, other, ins, masks):
-    cols, wide, tile = left.shape[1], ins.shape[2], 256
+    cols, wide, tile = left.shape[1], ins.shape[2], ins.shape[2]
     whole = lambda x: pl.BlockSpec(x.shape, lambda i: (0, 0, 0))
     return pl.pallas_call(
         square_kernel,
@@ -307,8 +304,7 @@
     both = call(pair_kernel, like(2, VALID, WIDE), near, far, scalars=0, cost=HINT)
     both = call(join_kernel, like(4, 2, VALID, WIDE), both, partial, scalars=0)
     both = exchange(both, "zq")
-    lines = call(sort_kernel, like(VALID, 8 * FEAT), where, both)
-    ins = call(pack_kernel, like(16, 80, 128), where, both)
+    lines, ins = call(sort_kernel, [like(VALID, 8 * FEAT), like(16, 80, 128)], where, both)
     lines = [lines] + others(lines, "y")
     ins = exchange(ins, ("zhi", "zh", "zq"))
     part = project(where, lines, basis, other_basis)

time: 140 us -> 139 us (level)
  waiting for transfers between devices: 37.5 us -> 39.1 us
  starting transfers between devices: 84.9 us -> 83.4 us
    ppermute x6, waiting for transfers between devices: 11.7 us -> 13.2 us  [others(): lax.ppermute(x, axis, [(i, i ^ k) for i in range(n)])]
    ppermute x4, starting transfers between devices: 26 us -> 24.5 us  [swap(): return lax.ppermute(x, axis, [(0, 1), (1, 0)])]
    pallas_call x9 -> x8, Pallas kernels: 5.08 us -> 4.48 us  [call(): pl.pallas_call(kernel, in_specs=[smem] * scalars + [vmem] * (len(args) -...]
  transfers between devices with their start and end apart: 17 -> 17, of which waited for: 6 -> 6; matrix products, arithmetic and copies ran while one was open for 0% -> 0% of each run, Pallas kernels for 6% -> 5%
where the time goes in v11:
time: 139 us
  starting transfers between devices  83.4 us (60%)
  waiting for transfers between devices  39.1 us (28%)
  Pallas kernels  15.6 us (11%)
    all_to_all x5, waiting for transfers between devices, exchange(): return lax.all_to_all(x, axis, 0, 0, tiled=True)  25.6 us
    ppermute x4, starting transfers between devices, swap(): return lax.ppermute(x, axis, [(0, 1), (1, 0)])  24.5 us
    all_to_all x5, starting transfers between devices, exchange(): return lax.all_to_all(x, axis, 0, 0, tiled=True)  20.6 us
    ppermute x6, starting transfers between devices, others(): lax.ppermute(x, axis, [(i, i ^ k) for i in range(n)])  17.9 us
    ppermute x6, waiting for transfers between devices, others(): lax.ppermute(x, axis, [(i, i ^ k) for i in range(n)])  13.2 us
    ppermute x1, starting transfers between devices, per_device(): far = lax.ppermute(lines, PLANE, to_basis(True))  12.7 us
    ppermute x1, starting transfers between devices, per_device(): near = lax.ppermute(lines, PLANE, to_basis(False))  7.77 us
    pallas_call x8, Pallas kernels, call(): pl.pallas_call(kernel, in_specs=[smem] * scalars + [vmem] * (len(args) -...  4.48 us
  transfers between devices with their start and end apart: 17, of which 6 were waited for; matrix products, arithmetic and copies ran while one was open for 0% of the time, Pallas kernels for 5%

profile of v11, /device:TPU:1, one launch (start us, length us, event | category | flops | bytes accessed | tf_op | source)
XLA Modules:
  0.0 138.6 jit_solution(705751140809365649)
XLA Ops:
  0.0 2.8 %shard_map.55 = (bf16[144,256]{1,0:T(8,128)(2,1)}, bf16[4,144,256]{2,1,0:T(8,128)(2,1)}) custom-call(s32[1,2]{1,0:T(1,128)} %len_ref.1, bf16[192,224]{1,0:T(8,128)(2,1)} %grads_hbm.1, bf16[192,256]{1,0:T(8,128)(2,1)} %acts_hbm.1, bf16[256,1024]{1,0:T(8,128)(2,1)} %basis_hbm.1), custom_call_target="tpu_custom_call" | custom-call | tf_op jit(solution)/shard_map/pallas_call | solution.py:289
  2.9 12.7 %collective-permute-start.1 = (bf16[144,256]{1,0:T(8,128)(2,1)}, bf16[144,256]{1,0:T(8,128)(2,1)S(1)}, u32[]{:S(2)}, u32[]{:S(2)}) collective-permute-start(bf16[144,256]{1,0:T(8,128)(2,1)} %get-tuple-element.15), channel_id=1, source_target_pairs={{0,4},{1,5},{2,6},{3,7},{4,0},{5,1},{6,2},{7,3},{8,12},{9,13},{10,... | collective-permute-start | bytes 221192 | tf_op jit(solution)/shard_map/ppermute | solution.py:299
  15.5 7.8 %collective-permute-start = (bf16[144,256]{1,0:T(8,128)(2,1)}, bf16[144,256]{1,0:T(8,128)(2,1)S(1)}, u32[]{:S(2)}, u32[]{:S(2)}) collective-permute-start(bf16[144,256]{1,0:T(8,128)(2,1)} %get-tuple-element.15), channel_id=1, source_target_pairs={{0,0},{1,1},{2,2},{3,3},{4,4},{5,5},{6,6},{7,7},{8,8},{9,9},{10,10... | collective-permute-start | bytes 221192 | tf_op jit(solution)/shard_map/ppermute | solution.py:298
  23.3 3.5 %all-to-all-start = ((bf16[4,144,256]{2,1,0:T(8,128)(2,1)}), bf16[4,144,256]{2,1,0:T(8,128)(2,1)S(1)}, u32[]{:S(2)}, u32[]{:S(2)}) async-start(bf16[4,144,256]{2,1,0:T(8,128)(2,1)} %get-tuple-element.16), calls=%async_computation | async-start | bytes 589824 | tf_op jit(solution)/shard_map/all_to_all | solution.py:38
  26.8 7.3 %all-to-all-done.parts_ref = bf16[4,144,256]{2,1,0:T(8,128)(2,1)S(1)} async-done(((bf16[4,144,256]{2,1,0:T(8,128)(2,1)}), bf16[4,144,256]{2,1,0:T(8,128)(2,1)S(1)}, u32[]{:S(2)}, u32[]{:S(2)}) %all-to-all-start) | async-done | bytes 294944 | tf_op jit(solution)/shard_map/all_to_all | solution.py:38
  35.0 3.5 %all-to-all-start.1 = ((bf16[4,2,144,256]{3,2,1,0:T(8,128)(2,1)}), bf16[4,2,144,256]{3,2,1,0:T(8,128)(2,1)S(1)}, u32[]{:S(2)}, u32[]{:S(2)}) async-start(bf16[4,2,144,256]{3,2,1,0:T(8,128)(2,1)} %shard_map.57), calls=%async_computation.1 | async-start | bytes 1179648 | tf_op jit(solution)/shard_map/all_to_all | solution.py:38
  38.5 2.5 %collective-permute-start.5 = (bf16[448,1792]{1,0:T(8,128)(2,1)S(1)}, bf16[448,1792]{1,0:T(8,128)(2,1)}, u32[]{:S(2)}, u32[]{:S(2)}) collective-permute-start(bf16[448,1792]{1,0:T(8,128)(2,1)S(1)} %bitcast.20), channel_id=1, source_target_pairs={{0,128},{128,0},{1,129},{129,1},{2,130},{130,2},{3,131},{131,3},{4... | collective-permute-start | bytes 4816904 | tf_op jit(solution)/shard_map/ppermute | solution.py:46
  41.2 12.7 %all-to-all-done.1.both_ref = bf16[4,2,144,256]{3,2,1,0:T(8,128)(2,1)S(1)} async-done(((bf16[4,2,144,256]{3,2,1,0:T(8,128)(2,1)}), bf16[4,2,144,256]{3,2,1,0:T(8,128)(2,1)S(1)}, u32[]{:S(2)}, u32[]{:S(2)}) %all-to-all-start.1) | async-done | bytes 589856 | tf_op jit(solution)/shard_map/all_to_all | solution.py:38
  55.6 2.8 %collective-permute-start.4 = (bf16[144,1792]{1,0:T(8,128)(2,1)S(1)}, bf16[144,1792]{1,0:T(8,128)(2,1)}, u32[]{:S(2)}, u32[]{:S(2)}) collective-permute-start(bf16[144,1792]{1,0:T(8,128)(2,1)S(1)} %get-tuple-element.17.a_ref), channel_id=1, source_target_pairs={{0,24},{8,16},{16,8},{24,0},{1,25},{9,17},{17,9},{25,1},{2,26},{10... | collective-permute-start | bytes 1548296 | tf_op jit(solution)/shard_map/ppermute | solution.py:280
  58.4 3.1 %collective-permute-start.3 = (bf16[144,1792]{1,0:T(8,128)(2,1)S(1)}, bf16[144,1792]{1,0:T(8,128)(2,1)}, u32[]{:S(2)}, u32[]{:S(2)}) collective-permute-start(bf16[144,1792]{1,0:T(8,128)(2,1)S(1)} %get-tuple-element.17.a_ref), channel_id=1, source_target_pairs={{0,16},{8,24},{16,0},{24,8},{1,17},{9,25},{17,1},{25,9},{2,18},{10... | collective-permute-start | bytes 1548296 | tf_op jit(solution)/shard_map/ppermute | solution.py:280
  61.5 3.1 %collective-permute-start.2 = (bf16[144,1792]{1,0:T(8,128)(2,1)S(1)}, bf16[144,1792]{1,0:T(8,128)(2,1)}, u32[]{:S(2)}, u32[]{:S(2)}) collective-permute-start(bf16[144,1792]{1,0:T(8,128)(2,1)S(1)} %get-tuple-element.17.a_ref), channel_id=1, source_target_pairs={{0,8},{8,0},{16,24},{24,16},{1,9},{9,1},{17,25},{25,17},{2,10},{10... | collective-permute-start | bytes 1548296 | tf_op jit(solution)/shard_map/ppermute | solution.py:280
  64.6 6.2 %all-to-all-start.2 = ((bf16[16,80,128]{2,1,0:T(8,128)(2,1)}), bf16[16,80,128]{2,1,0:T(8,128)(2,1)S(1)}, u32[]{:S(2)}, u32[]{:S(2)}) async-start(bf16[16,80,128]{2,1,0:T(8,128)(2,1)} %get-tuple-element.18), calls=%async_computation.2 | async-start | bytes 655360 | tf_op jit(solution)/shard_map/all_to_all | solution.py:38
  70.8 10.9 %collective-permute-done.4.d_ref = bf16[144,1792]{1,0:T(8,128)(2,1)} collective-permute-done((bf16[144,1792]{1,0:T(8,128)(2,1)S(1)}, bf16[144,1792]{1,0:T(8,128)(2,1)}, u32[]{:S(2)}, u32[]{:S(2)}) %collective-permute-start.4) | collective-permute-done | bytes 516128 | tf_op jit(solution)/shard_map/ppermute | solution.py:280
  81.7 2.3 %collective-permute-done.2.b_ref = bf16[144,1792]{1,0:T(8,128)(2,1)} collective-permute-done((bf16[144,1792]{1,0:T(8,128)(2,1)S(1)}, bf16[144,1792]{1,0:T(8,128)(2,1)}, u32[]{:S(2)}, u32[]{:S(2)}) %collective-permute-start.2) | collective-permute-done | bytes 516128 | tf_op jit(solution)/shard_map/ppermute | solution.py:280
  84.0 4.1 %shard_map.59 = bf16[4,72,448]{2,1,0:T(8,128)(2,1)} custom-call(s32[8]{0:T(128)S(1)} %stack.50.where_ref, bf16[144,1792]{1,0:T(8,128)(2,1)S(1)} %get-tuple-element.17.a_ref, bf16[144,1792]{1,0:T(8,128)(2,1)} %collective-permute-done.2.b_ref, bf16[144,1792]{1,0:T(8,128)(2,1)} %collective-permute-done.3.c_ref, bf16[144,1792]{1,0:T(8,128)(2,1)} %collective-permute-done.4.d_ref, ...), custom_call_target="tpu_custom_call" | custom-call | flops 30000001024 | bytes 1000000 | tf_op jit(solution)/shard_map/pallas_call | solution.py:165
  88.1 4.0 %all-to-all-start.3 = ((bf16[4,72,448]{2,1,0:T(8,128)(2,1)}), bf16[4,72,448]{2,1,0:T(8,128)(2,1)S(1)}, u32[]{:S(2)}, u32[]{:S(2)}) async-start(bf16[4,72,448]{2,1,0:T(8,128)(2,1)} %shard_map.59), calls=%async_computation.3 | async-start | bytes 589824 | tf_op jit(solution)/shard_map/all_to_all | solution.py:38
  92.3 5.6 %all-to-all-done.3.parts_ref = bf16[4,72,448]{2,1,0:T(8,128)(2,1)S(1)} async-done(((bf16[4,72,448]{2,1,0:T(8,128)(2,1)}), bf16[4,72,448]{2,1,0:T(8,128)(2,1)S(1)}, u32[]{:S(2)}, u32[]{:S(2)}) %all-to-all-start.3) | async-done | bytes 258080 | tf_op jit(solution)/shard_map/all_to_all | solution.py:38
  97.9 7.1 %collective-permute-start.6 = (bf16[72,448]{1,0:T(8,128)(2,1)S(1)}, bf16[72,448]{1,0:T(8,128)(2,1)S(1)}, u32[]{:S(2)}, u32[]{:S(2)}) collective-permute-start(bf16[72,448]{1,0:T(8,128)(2,1)S(1)} %shard_map.60.one_ref), channel_id=1, source_target_pairs={{0,256},{256,0},{1,257},{257,1},{2,258},{258,2},{3,259},{259,3},{4... | collective-permute-start | bytes 193544 | tf_op jit(solution)/shard_map/ppermute | solution.py:46
  106.9 3.8 %collective-permute-start.9 = (bf16[2,152,256]{2,1,0:T(8,128)(2,1)S(1)}, bf16[2,152,256]{2,1,0:T(8,128)(2,1)S(1)}, u32[]{:S(2)}, u32[]{:S(2)}) collective-permute-start(bf16[2,152,256]{2,1,0:T(8,128)(2,1)S(1)} %shard_map.61), channel_id=1, source_target_pairs={{0,16},{8,24},{16,0},{24,8},{1,17},{9,25},{17,1},{25,9},{2,18},{10... | collective-permute-start | bytes 466952 | tf_op jit(solution)/shard_map/ppermute | solution.py:280
  110.7 3.3 %collective-permute-start.8 = (bf16[2,152,256]{2,1,0:T(8,128)(2,1)S(1)}, bf16[2,152,256]{2,1,0:T(8,128)(2,1)S(1)}, u32[]{:S(2)}, u32[]{:S(2)}) collective-permute-start(bf16[2,152,256]{2,1,0:T(8,128)(2,1)S(1)} %shard_map.61), channel_id=1, source_target_pairs={{0,8},{8,0},{16,24},{24,16},{1,9},{9,1},{17,25},{25,17},{2,10},{10... | collective-permute-start | bytes 466952 | tf_op jit(solution)/shard_map/ppermute | solution.py:280
  114.7 3.5 %all-to-all-start.4 = ((bf16[4,72,448]{2,1,0:T(8,128)(2,1)}), bf16[4,72,448]{2,1,0:T(8,128)(2,1)S(1)}, u32[]{:S(2)}, u32[]{:S(2)}) async-start(bf16[4,72,448]{2,1,0:T(8,128)(2,1)} %shard_map.62), calls=%async_computation.4 | async-start | bytes 589824 | tf_op jit(solution)/shard_map/all_to_all | solution.py:38
  118.3 8.2 %collective-permute-start.11 = (bf16[4,2,152,256]{3,2,1,0:T(8,128)(2,1)S(1)}, bf16[4,2,152,256]{3,2,1,0:T(8,128)(2,1)S(1)}, u32[]{:S(2)}, u32[]{:S(2)}) collective-permute-start(bf16[4,2,152,256]{3,2,1,0:T(8,128)(2,1)S(1)} %pad_maximum_fusion.own_ref), channel_id=1, source_target_pairs={{0,128},{128,0},{1,129},{129,1},{2,130},{130,2},{3,131},{131,3},{4... | collective-permute-start | bytes 1867784 | tf_op jit(solution)/shard_map/ppermute | solution.py:46
  126.6 6.7 %collective-permute-start.7 = (bf16[2,144,448]{2,1,0:T(8,128)(2,1)S(1)}, bf16[2,144,448]{2,1,0:T(8,128)(2,1)S(1)}, u32[]{:S(2)}, u32[]{:S(2)}) collective-permute-start(bf16[2,144,448]{2,1,0:T(8,128)(2,1)S(1)} %bitcast.18), channel_id=1, source_target_pairs={{0,128},{128,0},{1,129},{129,1},{2,130},{130,2},{3,131},{131,3},{4... | collective-permute-start | bytes 774152 | tf_op jit(solution)/shard_map/ppermute | solution.py:46
  134.4 4.2 %shard_map.65 = f32[448,1024]{1,0:T(8,128)} custom-call(s32[8]{0:T(128)S(1)} %stack.50.where_ref, bf16[2,448,144]{2,1,0:T(8,128)(2,1)S(1)} %shard_map.63.own_ref, bf16[2,144,448]{2,1,0:T(8,128)(2,1)S(1)} %collective-permute-done.7.other_ref, bf16[4,144,1024]{2,1,0:T(8,128)(2,1)S(1)} %get-tuple-element.23.in_ref, ...), custom_call_target="tpu_custom_call" | custom-call | tf_op jit(solution)/shard_map/pallas_call | solution.py:240
  (27 shorter events, 6.9 us)
Async XLA Ops:
  2.9 23.9 %collective-permute-start.1 = (bf16[144,256]{1,0:T(8,128)(2,1)}, bf16[144,256]{1,0:T(8,128)(2,1)S(1)}, u32[]{:S(2)}, u32[]{:S(2)}) collective-permute-start(bf16[144,256]{1,0:T(8,128)(2,1)} %get-tuple-element.15), channel_id=1, source_target_pairs={{0,4},{1,5},{2,6},{3,7},{4,0},{5,1},{6,2},{7,3},{8,12},{9,13},{10,... | collective-permute-start | bytes 221192 | tf_op jit(solution)/shard_map/ppermute | solution.py:299
  15.5 11.3 %collective-permute-start = (bf16[144,256]{1,0:T(8,128)(2,1)}, bf16[144,256]{1,0:T(8,128)(2,1)S(1)}, u32[]{:S(2)}, u32[]{:S(2)}) collective-permute-start(bf16[144,256]{1,0:T(8,128)(2,1)} %get-tuple-element.15), channel_id=1, source_target_pairs={{0,0},{1,1},{2,2},{3,3},{4,4},{5,5},{6,6},{7,7},{8,8},{9,9},{10,10... | collective-permute-start | bytes 221192 | tf_op jit(solution)/shard_map/ppermute | solution.py:298
  23.3 10.8 %all-to-all-start = ((bf16[4,144,256]{2,1,0:T(8,128)(2,1)}), bf16[4,144,256]{2,1,0:T(8,128)(2,1)S(1)}, u32[]{:S(2)}, u32[]{:S(2)}) async-start(bf16[4,144,256]{2,1,0:T(8,128)(2,1)} %get-tuple-element.16), calls=%async_computation | async-start | bytes 589824 | tf_op jit(solution)/shard_map/all_to_all | solution.py:38
  26.8 11.7 %copy-start = (bf16[1,1792,448]{1,2,0:T(8,128)(2,1)S(1)}, bf16[1,1792,448]{1,2,0:T(8,128)(2,1)}, u32[]{:S(2)}) copy-start(bf16[1,1792,448]{1,2,0:T(8,128)(2,1)} %param.8) | copy-start | bytes 4816900
  26.8 14.3 %copy-start.1 = (s32[1,2]{1,0:T(1,128)S(1)}, s32[1,2]{1,0:T(1,128)}, u32[]{:S(2)}) copy-start(s32[1,2]{1,0:T(1,128)} %len_ref.1) | copy-start | bytes 28
  35.0 18.9 %all-to-all-start.1 = ((bf16[4,2,144,256]{3,2,1,0:T(8,128)(2,1)}), bf16[4,2,144,256]{3,2,1,0:T(8,128)(2,1)S(1)}, u32[]{:S(2)}, u32[]{:S(2)}) async-start(bf16[4,2,144,256]{3,2,1,0:T(8,128)(2,1)} %shard_map.57), calls=%async_computation.1 | async-start | bytes 1179648 | tf_op jit(solution)/shard_map/all_to_all | solution.py:38
  38.5 32.3 %collective-permute-start.5 = (bf16[448,1792]{1,0:T(8,128)(2,1)S(1)}, bf16[448,1792]{1,0:T(8,128)(2,1)}, u32[]{:S(2)}, u32[]{:S(2)}) collective-permute-start(bf16[448,1792]{1,0:T(8,128)(2,1)S(1)} %bitcast.20), channel_id=1, source_target_pairs={{0,128},{128,0},{1,129},{129,1},{2,130},{130,2},{3,131},{131,3},{4... | collective-permute-start | bytes 4816904 | tf_op jit(solution)/shard_map/ppermute | solution.py:46
  55.6 26.1 %collective-permute-start.4 = (bf16[144,1792]{1,0:T(8,128)(2,1)S(1)}, bf16[144,1792]{1,0:T(8,128)(2,1)}, u32[]{:S(2)}, u32[]{:S(2)}) collective-permute-start(bf16[144,1792]{1,0:T(8,128)(2,1)S(1)} %get-tuple-element.17.a_ref), channel_id=1, source_target_pairs={{0,24},{8,16},{16,8},{24,0},{1,25},{9,17},{17,9},{25,1},{2,26},{10... | collective-permute-start | bytes 1548296 | tf_op jit(solution)/shard_map/ppermute | solution.py:280
  58.4 23.3 %collective-permute-start.3 = (bf16[144,1792]{1,0:T(8,128)(2,1)S(1)}, bf16[144,1792]{1,0:T(8,128)(2,1)}, u32[]{:S(2)}, u32[]{:S(2)}) collective-permute-start(bf16[144,1792]{1,0:T(8,128)(2,1)S(1)} %get-tuple-element.17.a_ref), channel_id=1, source_target_pairs={{0,16},{8,24},{16,0},{24,8},{1,17},{9,25},{17,1},{25,9},{2,18},{10... | collective-permute-start | bytes 1548296 | tf_op jit(solution)/shard_map/ppermute | solution.py:280
  61.5 22.5 %collective-permute-start.2 = (bf16[144,1792]{1,0:T(8,128)(2,1)S(1)}, bf16[144,1792]{1,0:T(8,128)(2,1)}, u32[]{:S(2)}, u32[]{:S(2)}) collective-permute-start(bf16[144,1792]{1,0:T(8,128)(2,1)S(1)} %get-tuple-element.17.a_ref), channel_id=1, source_target_pairs={{0,8},{8,0},{16,24},{24,16},{1,9},{9,1},{17,25},{25,17},{2,10},{10... | collective-permute-start | bytes 1548296 | tf_op jit(solution)/shard_map/ppermute | solution.py:280
  64.6 23.5 %all-to-all-start.2 = ((bf16[16,80,128]{2,1,0:T(8,128)(2,1)}), bf16[16,80,128]{2,1,0:T(8,128)(2,1)S(1)}, u32[]{:S(2)}, u32[]{:S(2)}) async-start(bf16[16,80,128]{2,1,0:T(8,128)(2,1)} %get-tuple-element.18), calls=%async_computation.2 | async-start | bytes 655360 | tf_op jit(solution)/shard_map/all_to_all | solution.py:38
  88.1 9.7 %all-to-all-start.3 = ((bf16[4,72,448]{2,1,0:T(8,128)(2,1)}), bf16[4,72,448]{2,1,0:T(8,128)(2,1)S(1)}, u32[]{:S(2)}, u32[]{:S(2)}) async-start(bf16[4,72,448]{2,1,0:T(8,128)(2,1)} %shard_map.59), calls=%async_computation.3 | async-start | bytes 589824 | tf_op jit(solution)/shard_map/all_to_all | solution.py:38
  97.9 16.1 %collective-permute-start.6 = (bf16[72,448]{1,0:T(8,128)(2,1)S(1)}, bf16[72,448]{1,0:T(8,128)(2,1)S(1)}, u32[]{:S(2)}, u32[]{:S(2)}) collective-permute-start(bf16[72,448]{1,0:T(8,128)(2,1)S(1)} %shard_map.60.one_ref), channel_id=1, source_target_pairs={{0,256},{256,0},{1,257},{257,1},{2,258},{258,2},{3,259},{259,3},{4... | collective-permute-start | bytes 193544 | tf_op jit(solution)/shard_map/ppermute | solution.py:46
  105.0 13.2 %collective-permute-start.10 = (bf16[2,152,256]{2,1,0:T(8,128)(2,1)S(1)}, bf16[2,152,256]{2,1,0:T(8,128)(2,1)S(1)}, u32[]{:S(2)}, u32[]{:S(2)}) collective-permute-start(bf16[2,152,256]{2,1,0:T(8,128)(2,1)S(1)} %shard_map.61), channel_id=1, source_target_pairs={{0,24},{8,16},{16,8},{24,0},{1,25},{9,17},{17,9},{25,1},{2,26},{10... | collective-permute-start | bytes 466952 | tf_op jit(solution)/shard_map/ppermute | solution.py:280
  106.9 11.3 %collective-permute-start.9 = (bf16[2,152,256]{2,1,0:T(8,128)(2,1)S(1)}, bf16[2,152,256]{2,1,0:T(8,128)(2,1)S(1)}, u32[]{:S(2)}, u32[]{:S(2)}) collective-permute-start(bf16[2,152,256]{2,1,0:T(8,128)(2,1)S(1)} %shard_map.61), channel_id=1, source_target_pairs={{0,16},{8,24},{16,0},{24,8},{1,17},{9,25},{17,1},{25,9},{2,18},{10... | collective-permute-start | bytes 466952 | tf_op jit(solution)/shard_map/ppermute | solution.py:280
  110.7 7.5 %collective-permute-start.8 = (bf16[2,152,256]{2,1,0:T(8,128)(2,1)S(1)}, bf16[2,152,256]{2,1,0:T(8,128)(2,1)S(1)}, u32[]{:S(2)}, u32[]{:S(2)}) collective-permute-start(bf16[2,152,256]{2,1,0:T(8,128)(2,1)S(1)} %shard_map.61), channel_id=1, source_target_pairs={{0,8},{8,0},{16,24},{24,16},{1,9},{9,1},{17,25},{25,17},{2,10},{10... | collective-permute-start | bytes 466952 | tf_op jit(solution)/shard_map/ppermute | solution.py:280
  114.7 11.8 %all-to-all-start.4 = ((bf16[4,72,448]{2,1,0:T(8,128)(2,1)}), bf16[4,72,448]{2,1,0:T(8,128)(2,1)S(1)}, u32[]{:S(2)}, u32[]{:S(2)}) async-start(bf16[4,72,448]{2,1,0:T(8,128)(2,1)} %shard_map.62), calls=%async_computation.4 | async-start | bytes 589824 | tf_op jit(solution)/shard_map/all_to_all | solution.py:38
  118.3 15.1 %collective-permute-start.11 = (bf16[4,2,152,256]{3,2,1,0:T(8,128)(2,1)S(1)}, bf16[4,2,152,256]{3,2,1,0:T(8,128)(2,1)S(1)}, u32[]{:S(2)}, u32[]{:S(2)}) collective-permute-start(bf16[4,2,152,256]{3,2,1,0:T(8,128)(2,1)S(1)} %pad_maximum_fusion.own_ref), channel_id=1, source_target_pairs={{0,128},{128,0},{1,129},{129,1},{2,130},{130,2},{3,131},{131,3},{4... | collective-permute-start | bytes 1867784 | tf_op jit(solution)/shard_map/ppermute | solution.py:46
  126.6 7.9 %collective-permute-start.7 = (bf16[2,144,448]{2,1,0:T(8,128)(2,1)S(1)}, bf16[2,144,448]{2,1,0:T(8,128)(2,1)S(1)}, u32[]{:S(2)}, u32[]{:S(2)}) collective-permute-start(bf16[2,144,448]{2,1,0:T(8,128)(2,1)S(1)} %bitcast.18), channel_id=1, source_target_pairs={{0,128},{128,0},{1,129},{129,1},{2,130},{130,2},{3,131},{131,3},{4... | collective-permute-start | bytes 774152 | tf_op jit(solution)/shard_map/ppermute | solution.py:46

commit v12 on v11

--- a/solution.py
+++ b/solution.py
@@ -207,8 +207,8 @@
         left_ref[t] = lines_ref[t].T
 
 
-def square_kernel(where_ref, own_ref, other_ref, in_ref, mask_ref, eig_ref, left_ref):
-    core = where_ref[3]
+def square_kernel(own_ref, other_ref, in_ref, mask_ref, eig_ref, left_ref):
+    core = lax.axis_index("core")
 
     @pl.when(pl.program_id(0) == 0)
     def _():
@@ -231,17 +231,16 @@
                 preferred_element_type=F32,
             )
             total += block * block
-        eig_ref[o * rows : (o + 1) * rows] = total / 768.0
-
-
-def squares(where, left, other, ins, masks):
+        eig_ref[o * rows : (o + 1) * rows] = total * (1.0 / 768.0)
+
+
+def squares(left, other, ins, masks):
     cols, wide, tile = left.shape[1], ins.shape[2], ins.shape[2]
     whole = lambda x: pl.BlockSpec(x.shape, lambda i: (0, 0, 0))
     return pl.pallas_call(
         square_kernel,
         grid=(wide // tile,),
         in_specs=[
-            pl.BlockSpec(memory_space=pltpu.SMEM),
             whole(left),
             whole(other),
             pl.BlockSpec((4, VALID, tile), lambda i: (0, 0, i)),
@@ -251,7 +250,7 @@
         out_shape=like(cols, wide, dtype=F32),
         scratch_shapes=[pltpu.VMEM((8, cols, VALID), BF)],
         compiler_params=PARAMS,
-    )(where, left, other, ins, masks)
+    )(left, other, ins, masks)
 
 
 def call(kernel, out, *args, scalars=1, scratch=(), cost=None):
@@ -326,7 +325,7 @@
         other_ins,
     )
     left = call(left_kernel, like(2, cols, VALID), outs, scalars=0, cost=HINT)
-    return squares(where, left, swap(outs, "core"), ins, masks)
+    return squares(left, swap(outs, "core"), ins, masks)
 
 
 def solution(mesh):

time: 139 us -> 139 us (level)
  no operation moved by 1% of the time
where the time goes in v12:
time: 139 us; the launch traced here: 138 us
  starting transfers between devices  83.4 us (60%)
  waiting for transfers between devices  39.1 us (28%)
  Pallas kernels  15.2 us (11%)
    all_to_all x5, waiting for transfers between devices, exchange(): return lax.all_to_all(x, axis, 0, 0, tiled=True)  25.6 us
    ppermute x4, starting transfers between devices, swap(): return lax.ppermute(x, axis, [(0, 1), (1, 0)])  24.5 us
    all_to_all x5, starting transfers between devices, exchange(): return lax.all_to_all(x, axis, 0, 0, tiled=True)  20.6 us
    ppermute x6, starting transfers between devices, others(): lax.ppermute(x, axis, [(i, i ^ k) for i in range(n)])  17.9 us
    ppermute x6, waiting for transfers between devices, others(): lax.ppermute(x, axis, [(i, i ^ k) for i in range(n)])  13.2 us
    ppermute x1, starting transfers between devices, per_device(): far = lax.ppermute(lines, PLANE, to_basis(True))  12.7 us
    ppermute x1, starting transfers between devices, per_device(): near = lax.ppermute(lines, PLANE, to_basis(False))  7.77 us
    pallas_call x8, Pallas kernels, call(): pl.pallas_call(kernel, in_specs=[smem] * scalars + [vmem] * (len(args) -...  4.48 us
  transfers between devices with their start and end apart: 17, of which 6 were waited for; matrix products, arithmetic and copies ran while one was open for 0% of the time, Pallas kernels for 5%

profile of v12, /device:TPU:1, one launch (start us, length us, event | category | flops | bytes accessed | tf_op | source)
XLA Modules:
  0.0 138.2 jit_solution(5141007592031885335)
XLA Ops:
  0.0 2.8 %shard_map.55 = (bf16[144,256]{1,0:T(8,128)(2,1)}, bf16[4,144,256]{2,1,0:T(8,128)(2,1)}) custom-call(s32[1,2]{1,0:T(1,128)} %len_ref.1, bf16[192,224]{1,0:T(8,128)(2,1)} %grads_hbm.1, bf16[192,256]{1,0:T(8,128)(2,1)} %acts_hbm.1, bf16[256,1024]{1,0:T(8,128)(2,1)} %basis_hbm.1), custom_call_target="tpu_custom_call" | custom-call | tf_op jit(solution)/shard_map/pallas_call | solution.py:288
  2.9 12.7 %collective-permute-start.1 = (bf16[144,256]{1,0:T(8,128)(2,1)}, bf16[144,256]{1,0:T(8,128)(2,1)S(1)}, u32[]{:S(2)}, u32[]{:S(2)}) collective-permute-start(bf16[144,256]{1,0:T(8,128)(2,1)} %get-tuple-element.15), channel_id=1, source_target_pairs={{0,4},{1,5},{2,6},{3,7},{4,0},{5,1},{6,2},{7,3},{8,12},{9,13},{10,... | collective-permute-start | bytes 221192 | tf_op jit(solution)/shard_map/ppermute | solution.py:298
  15.5 7.8 %collective-permute-start = (bf16[144,256]{1,0:T(8,128)(2,1)}, bf16[144,256]{1,0:T(8,128)(2,1)S(1)}, u32[]{:S(2)}, u32[]{:S(2)}) collective-permute-start(bf16[144,256]{1,0:T(8,128)(2,1)} %get-tuple-element.15), channel_id=1, source_target_pairs={{0,0},{1,1},{2,2},{3,3},{4,4},{5,5},{6,6},{7,7},{8,8},{9,9},{10,10... | collective-permute-start | bytes 221192 | tf_op jit(solution)/shard_map/ppermute | solution.py:297
  23.3 3.5 %all-to-all-start = ((bf16[4,144,256]{2,1,0:T(8,128)(2,1)}), bf16[4,144,256]{2,1,0:T(8,128)(2,1)S(1)}, u32[]{:S(2)}, u32[]{:S(2)}) async-start(bf16[4,144,256]{2,1,0:T(8,128)(2,1)} %get-tuple-element.16), calls=%async_computation | async-start | bytes 589824 | tf_op jit(solution)/shard_map/all_to_all | solution.py:38
  26.8 7.3 %all-to-all-done.parts_ref = bf16[4,144,256]{2,1,0:T(8,128)(2,1)S(1)} async-done(((bf16[4,144,256]{2,1,0:T(8,128)(2,1)}), bf16[4,144,256]{2,1,0:T(8,128)(2,1)S(1)}, u32[]{:S(2)}, u32[]{:S(2)}) %all-to-all-start) | async-done | bytes 294944 | tf_op jit(solution)/shard_map/all_to_all | solution.py:38
  35.0 3.5 %all-to-all-start.1 = ((bf16[4,2,144,256]{3,2,1,0:T(8,128)(2,1)}), bf16[4,2,144,256]{3,2,1,0:T(8,128)(2,1)S(1)}, u32[]{:S(2)}, u32[]{:S(2)}) async-start(bf16[4,2,144,256]{3,2,1,0:T(8,128)(2,1)} %shard_map.57), calls=%async_computation.1 | async-start | bytes 1179648 | tf_op jit(solution)/shard_map/all_to_all | solution.py:38
  38.5 2.5 %collective-permute-start.5 = (bf16[448,1792]{1,0:T(8,128)(2,1)S(1)}, bf16[448,1792]{1,0:T(8,128)(2,1)}, u32[]{:S(2)}, u32[]{:S(2)}) collective-permute-start(bf16[448,1792]{1,0:T(8,128)(2,1)S(1)} %bitcast.20), channel_id=1, source_target_pairs={{0,128},{128,0},{1,129},{129,1},{2,130},{130,2},{3,131},{131,3},{4... | collective-permute-start | bytes 4816904 | tf_op jit(solution)/shard_map/ppermute | solution.py:46
  41.2 12.7 %all-to-all-done.1.both_ref = bf16[4,2,144,256]{3,2,1,0:T(8,128)(2,1)S(1)} async-done(((bf16[4,2,144,256]{3,2,1,0:T(8,128)(2,1)}), bf16[4,2,144,256]{3,2,1,0:T(8,128)(2,1)S(1)}, u32[]{:S(2)}, u32[]{:S(2)}) %all-to-all-start.1) | async-done | bytes 589856 | tf_op jit(solution)/shard_map/all_to_all | solution.py:38
  55.6 2.8 %collective-permute-start.4 = (bf16[144,1792]{1,0:T(8,128)(2,1)S(1)}, bf16[144,1792]{1,0:T(8,128)(2,1)}, u32[]{:S(2)}, u32[]{:S(2)}) collective-permute-start(bf16[144,1792]{1,0:T(8,128)(2,1)S(1)} %get-tuple-element.17.a_ref), channel_id=1, source_target_pairs={{0,24},{8,16},{16,8},{24,0},{1,25},{9,17},{17,9},{25,1},{2,26},{10... | collective-permute-start | bytes 1548296 | tf_op jit(solution)/shard_map/ppermute | solution.py:279
  58.4 3.1 %collective-permute-start.3 = (bf16[144,1792]{1,0:T(8,128)(2,1)S(1)}, bf16[144,1792]{1,0:T(8,128)(2,1)}, u32[]{:S(2)}, u32[]{:S(2)}) collective-permute-start(bf16[144,1792]{1,0:T(8,128)(2,1)S(1)} %get-tuple-element.17.a_ref), channel_id=1, source_target_pairs={{0,16},{8,24},{16,0},{24,8},{1,17},{9,25},{17,1},{25,9},{2,18},{10... | collective-permute-start | bytes 1548296 | tf_op jit(solution)/shard_map/ppermute | solution.py:279
  61.5 3.1 %collective-permute-start.2 = (bf16[144,1792]{1,0:T(8,128)(2,1)S(1)}, bf16[144,1792]{1,0:T(8,128)(2,1)}, u32[]{:S(2)}, u32[]{:S(2)}) collective-permute-start(bf16[144,1792]{1,0:T(8,128)(2,1)S(1)} %get-tuple-element.17.a_ref), channel_id=1, source_target_pairs={{0,8},{8,0},{16,24},{24,16},{1,9},{9,1},{17,25},{25,17},{2,10},{10... | collective-permute-start | bytes 1548296 | tf_op jit(solution)/shard_map/ppermute | solution.py:279
  64.6 6.2 %all-to-all-start.2 = ((bf16[16,80,128]{2,1,0:T(8,128)(2,1)}), bf16[16,80,128]{2,1,0:T(8,128)(2,1)S(1)}, u32[]{:S(2)}, u32[]{:S(2)}) async-start(bf16[16,80,128]{2,1,0:T(8,128)(2,1)} %get-tuple-element.18), calls=%async_computation.2 | async-start | bytes 655360 | tf_op jit(solution)/shard_map/all_to_all | solution.py:38
  70.8 10.9 %collective-permute-done.4.d_ref = bf16[144,1792]{1,0:T(8,128)(2,1)} collective-permute-done((bf16[144,1792]{1,0:T(8,128)(2,1)S(1)}, bf16[144,1792]{1,0:T(8,128)(2,1)}, u32[]{:S(2)}, u32[]{:S(2)}) %collective-permute-start.4) | collective-permute-done | bytes 516128 | tf_op jit(solution)/shard_map/ppermute | solution.py:279
  81.7 2.3 %collective-permute-done.2.b_ref = bf16[144,1792]{1,0:T(8,128)(2,1)} collective-permute-done((bf16[144,1792]{1,0:T(8,128)(2,1)S(1)}, bf16[144,1792]{1,0:T(8,128)(2,1)}, u32[]{:S(2)}, u32[]{:S(2)}) %collective-permute-start.2) | collective-permute-done | bytes 516128 | tf_op jit(solution)/shard_map/ppermute | solution.py:279
  84.0 4.1 %shard_map.59 = bf16[4,72,448]{2,1,0:T(8,128)(2,1)} custom-call(s32[8]{0:T(128)S(1)} %stack.50.where_ref, bf16[144,1792]{1,0:T(8,128)(2,1)S(1)} %get-tuple-element.17.a_ref, bf16[144,1792]{1,0:T(8,128)(2,1)} %collective-permute-done.2.b_ref, bf16[144,1792]{1,0:T(8,128)(2,1)} %collective-permute-done.3.c_ref, bf16[144,1792]{1,0:T(8,128)(2,1)} %collective-permute-done.4.d_ref, ...), custom_call_target="tpu_custom_call" | custom-call | flops 30000001024 | bytes 1000000 | tf_op jit(solution)/shard_map/pallas_call | solution.py:165
  88.1 4.0 %all-to-all-start.3 = ((bf16[4,72,448]{2,1,0:T(8,128)(2,1)}), bf16[4,72,448]{2,1,0:T(8,128)(2,1)S(1)}, u32[]{:S(2)}, u32[]{:S(2)}) async-start(bf16[4,72,448]{2,1,0:T(8,128)(2,1)} %shard_map.59), calls=%async_computation.3 | async-start | bytes 589824 | tf_op jit(solution)/shard_map/all_to_all | solution.py:38
  92.3 5.6 %all-to-all-done.3.parts_ref = bf16[4,72,448]{2,1,0:T(8,128)(2,1)S(1)} async-done(((bf16[4,72,448]{2,1,0:T(8,128)(2,1)}), bf16[4,72,448]{2,1,0:T(8,128)(2,1)S(1)}, u32[]{:S(2)}, u32[]{:S(2)}) %all-to-all-start.3) | async-done | bytes 258080 | tf_op jit(solution)/shard_map/all_to_all | solution.py:38
  97.9 7.1 %collective-permute-start.6 = (bf16[72,448]{1,0:T(8,128)(2,1)S(1)}, bf16[72,448]{1,0:T(8,128)(2,1)S(1)}, u32[]{:S(2)}, u32[]{:S(2)}) collective-permute-start(bf16[72,448]{1,0:T(8,128)(2,1)S(1)} %shard_map.60.one_ref), channel_id=1, source_target_pairs={{0,256},{256,0},{1,257},{257,1},{2,258},{258,2},{3,259},{259,3},{4... | collective-permute-start | bytes 193544 | tf_op jit(solution)/shard_map/ppermute | solution.py:46
  106.9 3.8 %collective-permute-start.9 = (bf16[2,152,256]{2,1,0:T(8,128)(2,1)S(1)}, bf16[2,152,256]{2,1,0:T(8,128)(2,1)S(1)}, u32[]{:S(2)}, u32[]{:S(2)}) collective-permute-start(bf16[2,152,256]{2,1,0:T(8,128)(2,1)S(1)} %shard_map.61), channel_id=1, source_target_pairs={{0,16},{8,24},{16,0},{24,8},{1,17},{9,25},{17,1},{25,9},{2,18},{10... | collective-permute-start | bytes 466952 | tf_op jit(solution)/shard_map/ppermute | solution.py:279
  110.7 3.3 %collective-permute-start.8 = (bf16[2,152,256]{2,1,0:T(8,128)(2,1)S(1)}, bf16[2,152,256]{2,1,0:T(8,128)(2,1)S(1)}, u32[]{:S(2)}, u32[]{:S(2)}) collective-permute-start(bf16[2,152,256]{2,1,0:T(8,128)(2,1)S(1)} %shard_map.61), channel_id=1, source_target_pairs={{0,8},{8,0},{16,24},{24,16},{1,9},{9,1},{17,25},{25,17},{2,10},{10... | collective-permute-start | bytes 466952 | tf_op jit(solution)/shard_map/ppermute | solution.py:279
  114.7 3.5 %all-to-all-start.4 = ((bf16[4,72,448]{2,1,0:T(8,128)(2,1)}), bf16[4,72,448]{2,1,0:T(8,128)(2,1)S(1)}, u32[]{:S(2)}, u32[]{:S(2)}) async-start(bf16[4,72,448]{2,1,0:T(8,128)(2,1)} %shard_map.62), calls=%async_computation.4 | async-start | bytes 589824 | tf_op jit(solution)/shard_map/all_to_all | solution.py:38
  118.3 8.2 %collective-permute-start.11 = (bf16[4,2,152,256]{3,2,1,0:T(8,128)(2,1)S(1)}, bf16[4,2,152,256]{3,2,1,0:T(8,128)(2,1)S(1)}, u32[]{:S(2)}, u32[]{:S(2)}) collective-permute-start(bf16[4,2,152,256]{3,2,1,0:T(8,128)(2,1)S(1)} %pad_maximum_fusion.own_ref), channel_id=1, source_target_pairs={{0,128},{128,0},{1,129},{129,1},{2,130},{130,2},{3,131},{131,3},{4... | collective-permute-start | bytes 1867784 | tf_op jit(solution)/shard_map/ppermute | solution.py:46
  126.6 6.7 %collective-permute-start.7 = (bf16[2,144,448]{2,1,0:T(8,128)(2,1)S(1)}, bf16[2,144,448]{2,1,0:T(8,128)(2,1)S(1)}, u32[]{:S(2)}, u32[]{:S(2)}) collective-permute-start(bf16[2,144,448]{2,1,0:T(8,128)(2,1)S(1)} %bitcast.18), channel_id=1, source_target_pairs={{0,128},{128,0},{1,129},{129,1},{2,130},{130,2},{3,131},{131,3},{4... | collective-permute-start | bytes 774152 | tf_op jit(solution)/shard_map/ppermute | solution.py:46
  134.4 3.7 %shard_map.65 = f32[448,1024]{1,0:T(8,128)} custom-call(bf16[2,448,144]{2,1,0:T(8,128)(2,1)S(1)} %shard_map.63.own_ref, bf16[2,144,448]{2,1,0:T(8,128)(2,1)S(1)} %collective-permute-done.7.other_ref, bf16[4,144,1024]{2,1,0:T(8,128)(2,1)S(1)} %get-tuple-element.23.in_ref, bf16[4,8,144]{2,1,0:T(8,128)(2,1)S(1)} %get-tuple-element.24.mask_ref), custom_call_target="tpu_custom_call" | custom-call | tf_op jit(solution)/shard_map/pallas_call | solution.py:240
  (27 shorter events, 6.9 us)
Async XLA Ops:
  2.9 23.9 %collective-permute-start.1 = (bf16[144,256]{1,0:T(8,128)(2,1)}, bf16[144,256]{1,0:T(8,128)(2,1)S(1)}, u32[]{:S(2)}, u32[]{:S(2)}) collective-permute-start(bf16[144,256]{1,0:T(8,128)(2,1)} %get-tuple-element.15), channel_id=1, source_target_pairs={{0,4},{1,5},{2,6},{3,7},{4,0},{5,1},{6,2},{7,3},{8,12},{9,13},{10,... | collective-permute-start | bytes 221192 | tf_op jit(solution)/shard_map/ppermute | solution.py:298
  15.5 11.3 %collective-permute-start = (bf16[144,256]{1,0:T(8,128)(2,1)}, bf16[144,256]{1,0:T(8,128)(2,1)S(1)}, u32[]{:S(2)}, u32[]{:S(2)}) collective-permute-start(bf16[144,256]{1,0:T(8,128)(2,1)} %get-tuple-element.15), channel_id=1, source_target_pairs={{0,0},{1,1},{2,2},{3,3},{4,4},{5,5},{6,6},{7,7},{8,8},{9,9},{10,10... | collective-permute-start | bytes 221192 | tf_op jit(solution)/shard_map/ppermute | solution.py:297
  23.3 10.8 %all-to-all-start = ((bf16[4,144,256]{2,1,0:T(8,128)(2,1)}), bf16[4,144,256]{2,1,0:T(8,128)(2,1)S(1)}, u32[]{:S(2)}, u32[]{:S(2)}) async-start(bf16[4,144,256]{2,1,0:T(8,128)(2,1)} %get-tuple-element.16), calls=%async_computation | async-start | bytes 589824 | tf_op jit(solution)/shard_map/all_to_all | solution.py:38
  26.8 11.7 %copy-start = (bf16[1,1792,448]{1,2,0:T(8,128)(2,1)S(1)}, bf16[1,1792,448]{1,2,0:T(8,128)(2,1)}, u32[]{:S(2)}) copy-start(bf16[1,1792,448]{1,2,0:T(8,128)(2,1)} %param.8) | copy-start | bytes 4816900
  26.8 14.3 %copy-start.1 = (s32[1,2]{1,0:T(1,128)S(1)}, s32[1,2]{1,0:T(1,128)}, u32[]{:S(2)}) copy-start(s32[1,2]{1,0:T(1,128)} %len_ref.1) | copy-start | bytes 28
  35.0 18.9 %all-to-all-start.1 = ((bf16[4,2,144,256]{3,2,1,0:T(8,128)(2,1)}), bf16[4,2,144,256]{3,2,1,0:T(8,128)(2,1)S(1)}, u32[]{:S(2)}, u32[]{:S(2)}) async-start(bf16[4,2,144,256]{3,2,1,0:T(8,128)(2,1)} %shard_map.57), calls=%async_computation.1 | async-start | bytes 1179648 | tf_op jit(solution)/shard_map/all_to_all | solution.py:38
  38.5 32.3 %collective-permute-start.5 = (bf16[448,1792]{1,0:T(8,128)(2,1)S(1)}, bf16[448,1792]{1,0:T(8,128)(2,1)}, u32[]{:S(2)}, u32[]{:S(2)}) collective-permute-start(bf16[448,1792]{1,0:T(8,128)(2,1)S(1)} %bitcast.20), channel_id=1, source_target_pairs={{0,128},{128,0},{1,129},{129,1},{2,130},{130,2},{3,131},{131,3},{4... | collective-permute-start | bytes 4816904 | tf_op jit(solution)/shard_map/ppermute | solution.py:46
  55.6 26.1 %collective-permute-start.4 = (bf16[144,1792]{1,0:T(8,128)(2,1)S(1)}, bf16[144,1792]{1,0:T(8,128)(2,1)}, u32[]{:S(2)}, u32[]{:S(2)}) collective-permute-start(bf16[144,1792]{1,0:T(8,128)(2,1)S(1)} %get-tuple-element.17.a_ref), channel_id=1, source_target_pairs={{0,24},{8,16},{16,8},{24,0},{1,25},{9,17},{17,9},{25,1},{2,26},{10... | collective-permute-start | bytes 1548296 | tf_op jit(solution)/shard_map/ppermute | solution.py:279
  58.4 23.3 %collective-permute-start.3 = (bf16[144,1792]{1,0:T(8,128)(2,1)S(1)}, bf16[144,1792]{1,0:T(8,128)(2,1)}, u32[]{:S(2)}, u32[]{:S(2)}) collective-permute-start(bf16[144,1792]{1,0:T(8,128)(2,1)S(1)} %get-tuple-element.17.a_ref), channel_id=1, source_target_pairs={{0,16},{8,24},{16,0},{24,8},{1,17},{9,25},{17,1},{25,9},{2,18},{10... | collective-permute-start | bytes 1548296 | tf_op jit(solution)/shard_map/ppermute | solution.py:279
  61.5 22.5 %collective-permute-start.2 = (bf16[144,1792]{1,0:T(8,128)(2,1)S(1)}, bf16[144,1792]{1,0:T(8,128)(2,1)}, u32[]{:S(2)}, u32[]{:S(2)}) collective-permute-start(bf16[144,1792]{1,0:T(8,128)(2,1)S(1)} %get-tuple-element.17.a_ref), channel_id=1, source_target_pairs={{0,8},{8,0},{16,24},{24,16},{1,9},{9,1},{17,25},{25,17},{2,10},{10... | collective-permute-start | bytes 1548296 | tf_op jit(solution)/shard_map/ppermute | solution.py:279
  64.6 23.5 %all-to-all-start.2 = ((bf16[16,80,128]{2,1,0:T(8,128)(2,1)}), bf16[16,80,128]{2,1,0:T(8,128)(2,1)S(1)}, u32[]{:S(2)}, u32[]{:S(2)}) async-start(bf16[16,80,128]{2,1,0:T(8,128)(2,1)} %get-tuple-element.18), calls=%async_computation.2 | async-start | bytes 655360 | tf_op jit(solution)/shard_map/all_to_all | solution.py:38
  88.1 9.7 %all-to-all-start.3 = ((bf16[4,72,448]{2,1,0:T(8,128)(2,1)}), bf16[4,72,448]{2,1,0:T(8,128)(2,1)S(1)}, u32[]{:S(2)}, u32[]{:S(2)}) async-start(bf16[4,72,448]{2,1,0:T(8,128)(2,1)} %shard_map.59), calls=%async_computation.3 | async-start | bytes 589824 | tf_op jit(solution)/shard_map/all_to_all | solution.py:38
  97.9 16.1 %collective-permute-start.6 = (bf16[72,448]{1,0:T(8,128)(2,1)S(1)}, bf16[72,448]{1,0:T(8,128)(2,1)S(1)}, u32[]{:S(2)}, u32[]{:S(2)}) collective-permute-start(bf16[72,448]{1,0:T(8,128)(2,1)S(1)} %shard_map.60.one_ref), channel_id=1, source_target_pairs={{0,256},{256,0},{1,257},{257,1},{2,258},{258,2},{3,259},{259,3},{4... | collective-permute-start | bytes 193544 | tf_op jit(solution)/shard_map/ppermute | solution.py:46
  105.0 13.2 %collective-permute-start.10 = (bf16[2,152,256]{2,1,0:T(8,128)(2,1)S(1)}, bf16[2,152,256]{2,1,0:T(8,128)(2,1)S(1)}, u32[]{:S(2)}, u32[]{:S(2)}) collective-permute-start(bf16[2,152,256]{2,1,0:T(8,128)(2,1)S(1)} %shard_map.61), channel_id=1, source_target_pairs={{0,24},{8,16},{16,8},{24,0},{1,25},{9,17},{17,9},{25,1},{2,26},{10... | collective-permute-start | bytes 466952 | tf_op jit(solution)/shard_map/ppermute | solution.py:279
  106.9 11.3 %collective-permute-start.9 = (bf16[2,152,256]{2,1,0:T(8,128)(2,1)S(1)}, bf16[2,152,256]{2,1,0:T(8,128)(2,1)S(1)}, u32[]{:S(2)}, u32[]{:S(2)}) collective-permute-start(bf16[2,152,256]{2,1,0:T(8,128)(2,1)S(1)} %shard_map.61), channel_id=1, source_target_pairs={{0,16},{8,24},{16,0},{24,8},{1,17},{9,25},{17,1},{25,9},{2,18},{10... | collective-permute-start | bytes 466952 | tf_op jit(solution)/shard_map/ppermute | solution.py:279
  110.7 7.5 %collective-permute-start.8 = (bf16[2,152,256]{2,1,0:T(8,128)(2,1)S(1)}, bf16[2,152,256]{2,1,0:T(8,128)(2,1)S(1)}, u32[]{:S(2)}, u32[]{:S(2)}) collective-permute-start(bf16[2,152,256]{2,1,0:T(8,128)(2,1)S(1)} %shard_map.61), channel_id=1, source_target_pairs={{0,8},{8,0},{16,24},{24,16},{1,9},{9,1},{17,25},{25,17},{2,10},{10... | collective-permute-start | bytes 466952 | tf_op jit(solution)/shard_map/ppermute | solution.py:279
  114.7 11.8 %all-to-all-start.4 = ((bf16[4,72,448]{2,1,0:T(8,128)(2,1)}), bf16[4,72,448]{2,1,0:T(8,128)(2,1)S(1)}, u32[]{:S(2)}, u32[]{:S(2)}) async-start(bf16[4,72,448]{2,1,0:T(8,128)(2,1)} %shard_map.62), calls=%async_computation.4 | async-start | bytes 589824 | tf_op jit(solution)/shard_map/all_to_all | solution.py:38
  118.3 15.1 %collective-permute-start.11 = (bf16[4,2,152,256]{3,2,1,0:T(8,128)(2,1)S(1)}, bf16[4,2,152,256]{3,2,1,0:T(8,128)(2,1)S(1)}, u32[]{:S(2)}, u32[]{:S(2)}) collective-permute-start(bf16[4,2,152,256]{3,2,1,0:T(8,128)(2,1)S(1)} %pad_maximum_fusion.own_ref), channel_id=1, source_target_pairs={{0,128},{128,0},{1,129},{129,1},{2,130},{130,2},{3,131},{131,3},{4... | collective-permute-start | bytes 1867784 | tf_op jit(solution)/shard_map/ppermute | solution.py:46
  126.6 7.9 %collective-permute-start.7 = (bf16[2,144,448]{2,1,0:T(8,128)(2,1)S(1)}, bf16[2,144,448]{2,1,0:T(8,128)(2,1)S(1)}, u32[]{:S(2)}, u32[]{:S(2)}) collective-permute-start(bf16[2,144,448]{2,1,0:T(8,128)(2,1)S(1)} %bitcast.18), channel_id=1, source_target_pairs={{0,128},{128,0},{1,129},{129,1},{2,130},{130,2},{3,131},{131,3},{4... | collective-permute-start | bytes 774152 | tf_op jit(solution)/shard_map/ppermute | solution.py:46

commit v13 on v12

--- a/solution.py
+++ b/solution.py
@@ -97,8 +97,9 @@
             )
 
 
-def sort_kernel(where_ref, both_ref, out_ref, in_ref):
-    zh, crossed = where_ref[0], where_ref[1]
+def sort_kernel(len_ref, both_ref, out_ref, in_ref):
+    zh = lax.axis_index("zh")
+    crossed = (lax.axis_index("core") != lax.axis_index("zhi")).astype(jnp.int32)
     for f in range(8):
         far = (jnp.int32(f // 4) != zh).astype(jnp.int32) ^ crossed
         at = (f % 4) ^ (3 * (far & crossed))
@@ -111,7 +112,7 @@
         sums.append(total)
     half = VALID // 2
     packed = jnp.concatenate([x[i : i + half] for i in (0, half) for x in sums], axis=1)
-    count = jnp.full((8, 128), where_ref[2], jnp.int32).astype(F32).astype(BF)
+    count = jnp.broadcast_to(len_ref[:, :1].astype(F32), (8, 128)).astype(BF)
     for copy in range(16):
         in_ref[copy, :half] = packed.astype(BF)
         in_ref[copy, half:] = count
@@ -131,10 +132,11 @@
 
 
 def project_kernel(
-    where_ref, a_ref, b_ref, c_ref, d_ref, own_ref, other_ref, out_ref, held, total_ref
+    a_ref, b_ref, c_ref, d_ref, own_ref, other_ref, out_ref, held, total_ref
 ):
-    step = pl.program_id(0)
-    tokens, same = where_ref[7], where_ref[3] == where_ref[6]
+    step, y = pl.program_id(0), lax.axis_index("y")
+    tokens = (y >> 1) ^ lax.axis_index("zhi")
+    same = lax.axis_index("core") == (y & 1) ^ tokens
     for left_ref, right_ref, t in ((a_ref, b_ref, tokens), (d_ref, c_ref, 1 - tokens)):
         left, right = left_ref[...], right_ref[...]
         held[0, t] = jnp.where(same, left, right)
@@ -157,7 +159,7 @@
             out_ref[h] = total_ref[h * 72 : (h + 1) * 72].astype(BF)
 
 
-def project(where, lines, basis, other_basis):
+def project(lines, basis, other_basis):
     cols, rows = basis.shape
     deep = rows
     line = pl.BlockSpec((VALID, deep), lambda k: (0, k))
@@ -165,13 +167,13 @@
     return pl.pallas_call(
         project_kernel,
         grid=(rows // deep,),
-        in_specs=[pl.BlockSpec(memory_space=pltpu.SMEM)] + [line] * 4 + [rotated] * 2,
+        in_specs=[line] * 4 + [rotated] * 2,
         out_specs=pl.BlockSpec((4, 72, cols), lambda k: (0, 0, 0)),
         out_shape=like(4, 72, cols),
         scratch_shapes=[pltpu.VMEM((2, 2, VALID, deep), BF), pltpu.VMEM((2 * VALID, cols), F32)],
         compiler_params=PARAMS,
         cost_estimate=LONG,
-    )(where, *lines, basis, other_basis)
+    )(*lines, basis, other_basis)
 
 
 def sum_kernel(parts_ref, out_ref):
@@ -187,15 +189,15 @@
         out_ref[x] = total
 
 
-def arrange_kernel(where_ref, own_ref, other_ref, out_ref, mask_ref):
-    core = where_ref[3]
+def arrange_kernel(own_ref, other_ref, out_ref, mask_ref):
+    core, own_y = lax.axis_index("core"), lax.axis_index("y")
     slot = lax.broadcasted_iota(jnp.int32, (8, VALID), 1).astype(F32)
     for zhi in range(2):
         for c in range(2):
             mine = core == c
             g = zhi * 2 + c
             for y in range(4):
-                k = y ^ where_ref[5]
+                k = y ^ own_y
                 block = jnp.where(mine, own_ref[k, zhi], other_ref[k, zhi])
                 out_ref[g, :, y * WIDE : (y + 1) * WIDE] = block[:VALID]
             count = block[VALID:, :VALID].astype(F32)
@@ -281,10 +283,6 @@
 
 
 def per_device(acts, grads, basis_in, basis_out, lengths):
-    zhi, core, y, zh, zq = (lax.axis_index(a) for a in ("zhi", "core", "y", "zh", "zq"))
-    crossed = (core != zhi).astype(jnp.int32)
-    tokens = (y >> 1) ^ zhi
-    where = jnp.stack([zh, crossed, lengths[0, 0], core, zq, y, (y & 1) ^ tokens, tokens])
     lines, partial = pl.pallas_call(
         start_kernel,
         in_specs=[pl.BlockSpec(memory_space=pltpu.SMEM)] + [pl.BlockSpec(memory_space=pl.ANY)] * 3,
@@ -303,10 +301,10 @@
     both = call(pair_kernel, like(2, VALID, WIDE), near, far, scalars=0, cost=HINT)
     both = call(join_kernel, like(4, 2, VALID, WIDE), both, partial, scalars=0)
     both = exchange(both, "zq")
-    lines, ins = call(sort_kernel, [like(VALID, 8 * FEAT), like(16, 80, 128)], where, both)
+    lines, ins = call(sort_kernel, [like(VALID, 8 * FEAT), like(16, 80, 128)], lengths, both, scalars=0)
     lines = [lines] + others(lines, "y")
     ins = exchange(ins, ("zhi", "zh", "zq"))
-    part = project(where, lines, basis, other_basis)
+    part = project(lines, basis, other_basis)
     part, ins = lax.optimization_barrier((part, ins))
     ins = call(merge_kernel, like(2, VALID + 8, WIDE), ins, scalars=0)
     part = exchange(part, "x")
@@ -320,9 +318,9 @@
     ins, masks = call(
         arrange_kernel,
         [like(4, VALID, 1024), like(4, 8, VALID)],
-        where,
         ins,
         other_ins,
+        scalars=0,
     )
     left = call(left_kernel, like(2, cols, VALID), outs, scalars=0, cost=HINT)
     return squares(left, swap(outs, "core"), ins, masks)

time: 139 us -> 138 us (level)
  no operation moved by 1% of the time
where the time goes in v13:
time: 138 us
  starting transfers between devices  83.6 us (61%)
  waiting for transfers between devices  39.8 us (29%)
  Pallas kernels  13.9 us (10%)
    all_to_all x5, waiting for transfers between devices, exchange(): return lax.all_to_all(x, axis, 0, 0, tiled=True)  25.7 us
    ppermute x4, starting transfers between devices, swap(): return lax.ppermute(x, axis, [(0, 1), (1, 0)])  24.6 us
    all_to_all x5, starting transfers between devices, exchange(): return lax.all_to_all(x, axis, 0, 0, tiled=True)  20.6 us
    ppermute x6, starting transfers between devices, others(): lax.ppermute(x, axis, [(i, i ^ k) for i in range(n)])  17.9 us
    ppermute x6, waiting for transfers between devices, others(): lax.ppermute(x, axis, [(i, i ^ k) for i in range(n)])  13.2 us
    ppermute x1, starting transfers between devices, per_device(): far = lax.ppermute(lines, PLANE, to_basis(True))  12.7 us
    ppermute x1, starting transfers between devices, per_device(): near = lax.ppermute(lines, PLANE, to_basis(False))  7.77 us
    pallas_call x1, Pallas kernels, project(): pl.pallas_call(project_kernel, grid=(rows // deep,), in_specs=[line] * 4...  3.97 us
  transfers between devices with their start and end apart: 17, of which 6 were waited for; matrix products, arithmetic and copies ran while one was open for 0% of the time, Pallas kernels for 5%

profile of v13, /device:TPU:1, one launch (start us, length us, event | category | flops | bytes accessed | tf_op | source)
XLA Modules:
  0.0 137.6 jit_solution(517449955551147889)
XLA Ops:
  0.0 2.8 %shard_map.55 = (bf16[144,256]{1,0:T(8,128)(2,1)}, bf16[4,144,256]{2,1,0:T(8,128)(2,1)}) custom-call(s32[1,2]{1,0:T(1,128)} %len_ref.3, bf16[192,224]{1,0:T(8,128)(2,1)} %grads_hbm.1, bf16[192,256]{1,0:T(8,128)(2,1)} %acts_hbm.1, bf16[256,1024]{1,0:T(8,128)(2,1)} %basis_hbm.1), custom_call_target="tpu_custom_call" | custom-call | tf_op jit(solution)/shard_map/pallas_call | solution.py:286
  2.9 12.7 %collective-permute-start.1 = (bf16[144,256]{1,0:T(8,128)(2,1)}, bf16[144,256]{1,0:T(8,128)(2,1)S(1)}, u32[]{:S(2)}, u32[]{:S(2)}) collective-permute-start(bf16[144,256]{1,0:T(8,128)(2,1)} %get-tuple-element.15), channel_id=1, source_target_pairs={{0,4},{1,5},{2,6},{3,7},{4,0},{5,1},{6,2},{7,3},{8,12},{9,13},{10,... | collective-permute-start | bytes 221192 | tf_op jit(solution)/shard_map/ppermute | solution.py:296
  15.5 7.8 %collective-permute-start = (bf16[144,256]{1,0:T(8,128)(2,1)}, bf16[144,256]{1,0:T(8,128)(2,1)S(1)}, u32[]{:S(2)}, u32[]{:S(2)}) collective-permute-start(bf16[144,256]{1,0:T(8,128)(2,1)} %get-tuple-element.15), channel_id=1, source_target_pairs={{0,0},{1,1},{2,2},{3,3},{4,4},{5,5},{6,6},{7,7},{8,8},{9,9},{10,10... | collective-permute-start | bytes 221192 | tf_op jit(solution)/shard_map/ppermute | solution.py:295
  23.3 3.5 %all-to-all-start = ((bf16[4,144,256]{2,1,0:T(8,128)(2,1)}), bf16[4,144,256]{2,1,0:T(8,128)(2,1)S(1)}, u32[]{:S(2)}, u32[]{:S(2)}) async-start(bf16[4,144,256]{2,1,0:T(8,128)(2,1)} %get-tuple-element.16), calls=%async_computation | async-start | bytes 589824 | tf_op jit(solution)/shard_map/all_to_all | solution.py:38
  26.8 7.3 %all-to-all-done.parts_ref = bf16[4,144,256]{2,1,0:T(8,128)(2,1)S(1)} async-done(((bf16[4,144,256]{2,1,0:T(8,128)(2,1)}), bf16[4,144,256]{2,1,0:T(8,128)(2,1)S(1)}, u32[]{:S(2)}, u32[]{:S(2)}) %all-to-all-start) | async-done | bytes 294944 | tf_op jit(solution)/shard_map/all_to_all | solution.py:38
  35.0 3.5 %all-to-all-start.1 = ((bf16[4,2,144,256]{3,2,1,0:T(8,128)(2,1)}), bf16[4,2,144,256]{3,2,1,0:T(8,128)(2,1)S(1)}, u32[]{:S(2)}, u32[]{:S(2)}) async-start(bf16[4,2,144,256]{3,2,1,0:T(8,128)(2,1)} %shard_map.57), calls=%async_computation.1 | async-start | bytes 1179648 | tf_op jit(solution)/shard_map/all_to_all | solution.py:38
  38.5 2.5 %collective-permute-start.5 = (bf16[448,1792]{1,0:T(8,128)(2,1)S(1)}, bf16[448,1792]{1,0:T(8,128)(2,1)}, u32[]{:S(2)}, u32[]{:S(2)}) collective-permute-start(bf16[448,1792]{1,0:T(8,128)(2,1)S(1)} %bitcast.11), channel_id=1, source_target_pairs={{0,128},{128,0},{1,129},{129,1},{2,130},{130,2},{3,131},{131,3},{4... | collective-permute-start | bytes 4816904 | tf_op jit(solution)/shard_map/ppermute | solution.py:46
  41.1 12.9 %all-to-all-done.1.both_ref = bf16[4,2,144,256]{3,2,1,0:T(8,128)(2,1)S(1)} async-done(((bf16[4,2,144,256]{3,2,1,0:T(8,128)(2,1)}), bf16[4,2,144,256]{3,2,1,0:T(8,128)(2,1)S(1)}, u32[]{:S(2)}, u32[]{:S(2)}) %all-to-all-start.1) | async-done | bytes 589856 | tf_op jit(solution)/shard_map/all_to_all | solution.py:38
  55.1 2.8 %collective-permute-start.4 = (bf16[144,1792]{1,0:T(8,128)(2,1)S(1)}, bf16[144,1792]{1,0:T(8,128)(2,1)S(1)}, u32[]{:S(2)}, u32[]{:S(2)}) collective-permute-start(bf16[144,1792]{1,0:T(8,128)(2,1)S(1)} %get-tuple-element.17.a_ref), channel_id=1, source_target_pairs={{0,24},{8,16},{16,8},{24,0},{1,25},{9,17},{17,9},{25,1},{2,26},{10... | collective-permute-start | bytes 1548296 | tf_op jit(solution)/shard_map/ppermute | solution.py:281
  57.9 3.1 %collective-permute-start.3 = (bf16[144,1792]{1,0:T(8,128)(2,1)S(1)}, bf16[144,1792]{1,0:T(8,128)(2,1)}, u32[]{:S(2)}, u32[]{:S(2)}) collective-permute-start(bf16[144,1792]{1,0:T(8,128)(2,1)S(1)} %get-tuple-element.17.a_ref), channel_id=1, source_target_pairs={{0,16},{8,24},{16,0},{24,8},{1,17},{9,25},{17,1},{25,9},{2,18},{10... | collective-permute-start | bytes 1548296 | tf_op jit(solution)/shard_map/ppermute | solution.py:281
  61.0 3.1 %collective-permute-start.2 = (bf16[144,1792]{1,0:T(8,128)(2,1)S(1)}, bf16[144,1792]{1,0:T(8,128)(2,1)}, u32[]{:S(2)}, u32[]{:S(2)}) collective-permute-start(bf16[144,1792]{1,0:T(8,128)(2,1)S(1)} %get-tuple-element.17.a_ref), channel_id=1, source_target_pairs={{0,8},{8,0},{16,24},{24,16},{1,9},{9,1},{17,25},{25,17},{2,10},{10... | collective-permute-start | bytes 1548296 | tf_op jit(solution)/shard_map/ppermute | solution.py:281
  64.1 6.2 %all-to-all-start.2 = ((bf16[16,80,128]{2,1,0:T(8,128)(2,1)}), bf16[16,80,128]{2,1,0:T(8,128)(2,1)S(1)}, u32[]{:S(2)}, u32[]{:S(2)}) async-start(bf16[16,80,128]{2,1,0:T(8,128)(2,1)} %get-tuple-element.18), calls=%async_computation.2 | async-start | bytes 655360 | tf_op jit(solution)/shard_map/all_to_all | solution.py:38
  70.3 10.8 %collective-permute-done.4.d_ref = bf16[144,1792]{1,0:T(8,128)(2,1)S(1)} collective-permute-done((bf16[144,1792]{1,0:T(8,128)(2,1)S(1)}, bf16[144,1792]{1,0:T(8,128)(2,1)S(1)}, u32[]{:S(2)}, u32[]{:S(2)}) %collective-permute-start.4) | collective-permute-done | bytes 516128 | tf_op jit(solution)/shard_map/ppermute | solution.py:281
  81.1 2.4 %collective-permute-done.2.b_ref = bf16[144,1792]{1,0:T(8,128)(2,1)} collective-permute-done((bf16[144,1792]{1,0:T(8,128)(2,1)S(1)}, bf16[144,1792]{1,0:T(8,128)(2,1)}, u32[]{:S(2)}, u32[]{:S(2)}) %collective-permute-start.2) | collective-permute-done | bytes 516128 | tf_op jit(solution)/shard_map/ppermute | solution.py:281
  83.5 4.0 %shard_map.59 = bf16[4,72,448]{2,1,0:T(8,128)(2,1)} custom-call(bf16[144,1792]{1,0:T(8,128)(2,1)S(1)} %get-tuple-element.17.a_ref, bf16[144,1792]{1,0:T(8,128)(2,1)} %collective-permute-done.2.b_ref, bf16[144,1792]{1,0:T(8,128)(2,1)} %collective-permute-done.3.c_ref, bf16[144,1792]{1,0:T(8,128)(2,1)S(1)} %collective-permute-done.4.d_ref, ...), custom_call_target="tpu_custom_call" | custom-call | flops 30000001024 | bytes 1000000 | tf_op jit(solution)/shard_map/pallas_call | solution.py:167
  87.5 4.0 %all-to-all-start.3 = ((bf16[4,72,448]{2,1,0:T(8,128)(2,1)}), bf16[4,72,448]{2,1,0:T(8,128)(2,1)S(1)}, u32[]{:S(2)}, u32[]{:S(2)}) async-start(bf16[4,72,448]{2,1,0:T(8,128)(2,1)} %shard_map.59), calls=%async_computation.3 | async-start | bytes 589824 | tf_op jit(solution)/shard_map/all_to_all | solution.py:38
  91.6 5.6 %all-to-all-done.3.parts_ref = bf16[4,72,448]{2,1,0:T(8,128)(2,1)S(1)} async-done(((bf16[4,72,448]{2,1,0:T(8,128)(2,1)}), bf16[4,72,448]{2,1,0:T(8,128)(2,1)S(1)}, u32[]{:S(2)}, u32[]{:S(2)}) %all-to-all-start.3) | async-done | bytes 258080 | tf_op jit(solution)/shard_map/all_to_all | solution.py:38
  97.2 7.2 %collective-permute-start.6 = (bf16[72,448]{1,0:T(8,128)(2,1)S(1)}, bf16[72,448]{1,0:T(8,128)(2,1)S(1)}, u32[]{:S(2)}, u32[]{:S(2)}) collective-permute-start(bf16[72,448]{1,0:T(8,128)(2,1)S(1)} %shard_map.60.one_ref), channel_id=1, source_target_pairs={{0,256},{256,0},{1,257},{257,1},{2,258},{258,2},{3,259},{259,3},{4... | collective-permute-start | bytes 193544 | tf_op jit(solution)/shard_map/ppermute | solution.py:46
  106.4 3.8 %collective-permute-start.9 = (bf16[2,152,256]{2,1,0:T(8,128)(2,1)S(1)}, bf16[2,152,256]{2,1,0:T(8,128)(2,1)S(1)}, u32[]{:S(2)}, u32[]{:S(2)}) collective-permute-start(bf16[2,152,256]{2,1,0:T(8,128)(2,1)S(1)} %shard_map.61), channel_id=1, source_target_pairs={{0,16},{8,24},{16,0},{24,8},{1,17},{9,25},{17,1},{25,9},{2,18},{10... | collective-permute-start | bytes 466952 | tf_op jit(solution)/shard_map/ppermute | solution.py:281
  110.1 3.3 %collective-permute-start.8 = (bf16[2,152,256]{2,1,0:T(8,128)(2,1)S(1)}, bf16[2,152,256]{2,1,0:T(8,128)(2,1)S(1)}, u32[]{:S(2)}, u32[]{:S(2)}) collective-permute-start(bf16[2,152,256]{2,1,0:T(8,128)(2,1)S(1)} %shard_map.61), channel_id=1, source_target_pairs={{0,8},{8,0},{16,24},{24,16},{1,9},{9,1},{17,25},{25,17},{2,10},{10... | collective-permute-start | bytes 466952 | tf_op jit(solution)/shard_map/ppermute | solution.py:281
  114.2 3.5 %all-to-all-start.4 = ((bf16[4,72,448]{2,1,0:T(8,128)(2,1)}), bf16[4,72,448]{2,1,0:T(8,128)(2,1)S(1)}, u32[]{:S(2)}, u32[]{:S(2)}) async-start(bf16[4,72,448]{2,1,0:T(8,128)(2,1)} %shard_map.62), calls=%async_computation.4 | async-start | bytes 589824 | tf_op jit(solution)/shard_map/all_to_all | solution.py:38
  117.8 8.2 %collective-permute-start.11 = (bf16[4,2,152,256]{3,2,1,0:T(8,128)(2,1)S(1)}, bf16[4,2,152,256]{3,2,1,0:T(8,128)(2,1)S(1)}, u32[]{:S(2)}, u32[]{:S(2)}) collective-permute-start(bf16[4,2,152,256]{3,2,1,0:T(8,128)(2,1)S(1)} %pad_maximum_fusion.own_ref), channel_id=1, source_target_pairs={{0,128},{128,0},{1,129},{129,1},{2,130},{130,2},{3,131},{131,3},{4... | collective-permute-start | bytes 1867784 | tf_op jit(solution)/shard_map/ppermute | solution.py:46
  126.0 6.7 %collective-permute-start.7 = (bf16[2,144,448]{2,1,0:T(8,128)(2,1)S(1)}, bf16[2,144,448]{2,1,0:T(8,128)(2,1)S(1)}, u32[]{:S(2)}, u32[]{:S(2)}) collective-permute-start(bf16[2,144,448]{2,1,0:T(8,128)(2,1)S(1)} %bitcast.9), channel_id=1, source_target_pairs={{0,128},{128,0},{1,129},{129,1},{2,130},{130,2},{3,131},{131,3},{4... | collective-permute-start | bytes 774152 | tf_op jit(solution)/shard_map/ppermute | solution.py:46
  133.9 3.7 %shard_map.65 = f32[448,1024]{1,0:T(8,128)} custom-call(bf16[2,448,144]{2,1,0:T(8,128)(2,1)S(1)} %shard_map.63.own_ref, bf16[2,144,448]{2,1,0:T(8,128)(2,1)S(1)} %collective-permute-done.7.other_ref, bf16[4,144,1024]{2,1,0:T(8,128)(2,1)S(1)} %get-tuple-element.23.in_ref, bf16[4,8,144]{2,1,0:T(8,128)(2,1)S(1)} %get-tuple-element.24.mask_ref), custom_call_target="tpu_custom_call" | custom-call | tf_op jit(solution)/shard_map/pallas_call | solution.py:242
  (26 shorter events, 6.2 us)
Async XLA Ops:
  2.9 23.9 %collective-permute-start.1 = (bf16[144,256]{1,0:T(8,128)(2,1)}, bf16[144,256]{1,0:T(8,128)(2,1)S(1)}, u32[]{:S(2)}, u32[]{:S(2)}) collective-permute-start(bf16[144,256]{1,0:T(8,128)(2,1)} %get-tuple-element.15), channel_id=1, source_target_pairs={{0,4},{1,5},{2,6},{3,7},{4,0},{5,1},{6,2},{7,3},{8,12},{9,13},{10,... | collective-permute-start | bytes 221192 | tf_op jit(solution)/shard_map/ppermute | solution.py:296
  15.5 11.3 %collective-permute-start = (bf16[144,256]{1,0:T(8,128)(2,1)}, bf16[144,256]{1,0:T(8,128)(2,1)S(1)}, u32[]{:S(2)}, u32[]{:S(2)}) collective-permute-start(bf16[144,256]{1,0:T(8,128)(2,1)} %get-tuple-element.15), channel_id=1, source_target_pairs={{0,0},{1,1},{2,2},{3,3},{4,4},{5,5},{6,6},{7,7},{8,8},{9,9},{10,10... | collective-permute-start | bytes 221192 | tf_op jit(solution)/shard_map/ppermute | solution.py:295
  23.3 10.8 %all-to-all-start = ((bf16[4,144,256]{2,1,0:T(8,128)(2,1)}), bf16[4,144,256]{2,1,0:T(8,128)(2,1)S(1)}, u32[]{:S(2)}, u32[]{:S(2)}) async-start(bf16[4,144,256]{2,1,0:T(8,128)(2,1)} %get-tuple-element.16), calls=%async_computation | async-start | bytes 589824 | tf_op jit(solution)/shard_map/all_to_all | solution.py:38
  26.8 11.7 %copy-start.1 = (bf16[1,1792,448]{1,2,0:T(8,128)(2,1)S(1)}, bf16[1,1792,448]{1,2,0:T(8,128)(2,1)}, u32[]{:S(2)}) copy-start(bf16[1,1792,448]{1,2,0:T(8,128)(2,1)} %param.8) | copy-start | bytes 4816900
  26.8 27.1 %copy-start = (s32[1,2]{1,0:T(1,128)S(1)}, s32[1,2]{1,0:T(1,128)}, u32[]{:S(2)}) copy-start(s32[1,2]{1,0:T(1,128)} %len_ref.3) | copy-start | bytes 28
  35.0 18.9 %all-to-all-start.1 = ((bf16[4,2,144,256]{3,2,1,0:T(8,128)(2,1)}), bf16[4,2,144,256]{3,2,1,0:T(8,128)(2,1)S(1)}, u32[]{:S(2)}, u32[]{:S(2)}) async-start(bf16[4,2,144,256]{3,2,1,0:T(8,128)(2,1)} %shard_map.57), calls=%async_computation.1 | async-start | bytes 1179648 | tf_op jit(solution)/shard_map/all_to_all | solution.py:38
  38.5 31.7 %collective-permute-start.5 = (bf16[448,1792]{1,0:T(8,128)(2,1)S(1)}, bf16[448,1792]{1,0:T(8,128)(2,1)}, u32[]{:S(2)}, u32[]{:S(2)}) collective-permute-start(bf16[448,1792]{1,0:T(8,128)(2,1)S(1)} %bitcast.11), channel_id=1, source_target_pairs={{0,128},{128,0},{1,129},{129,1},{2,130},{130,2},{3,131},{131,3},{4... | collective-permute-start | bytes 4816904 | tf_op jit(solution)/shard_map/ppermute | solution.py:46
  55.1 26.0 %collective-permute-start.4 = (bf16[144,1792]{1,0:T(8,128)(2,1)S(1)}, bf16[144,1792]{1,0:T(8,128)(2,1)S(1)}, u32[]{:S(2)}, u32[]{:S(2)}) collective-permute-start(bf16[144,1792]{1,0:T(8,128)(2,1)S(1)} %get-tuple-element.17.a_ref), channel_id=1, source_target_pairs={{0,24},{8,16},{16,8},{24,0},{1,25},{9,17},{17,9},{25,1},{2,26},{10... | collective-permute-start | bytes 1548296 | tf_op jit(solution)/shard_map/ppermute | solution.py:281
  57.9 23.2 %collective-permute-start.3 = (bf16[144,1792]{1,0:T(8,128)(2,1)S(1)}, bf16[144,1792]{1,0:T(8,128)(2,1)}, u32[]{:S(2)}, u32[]{:S(2)}) collective-permute-start(bf16[144,1792]{1,0:T(8,128)(2,1)S(1)} %get-tuple-element.17.a_ref), channel_id=1, source_target_pairs={{0,16},{8,24},{16,0},{24,8},{1,17},{9,25},{17,1},{25,9},{2,18},{10... | collective-permute-start | bytes 1548296 | tf_op jit(solution)/shard_map/ppermute | solution.py:281
  61.0 22.5 %collective-permute-start.2 = (bf16[144,1792]{1,0:T(8,128)(2,1)S(1)}, bf16[144,1792]{1,0:T(8,128)(2,1)}, u32[]{:S(2)}, u32[]{:S(2)}) collective-permute-start(bf16[144,1792]{1,0:T(8,128)(2,1)S(1)} %get-tuple-element.17.a_ref), channel_id=1, source_target_pairs={{0,8},{8,0},{16,24},{24,16},{1,9},{9,1},{17,25},{25,17},{2,10},{10... | collective-permute-start | bytes 1548296 | tf_op jit(solution)/shard_map/ppermute | solution.py:281
  64.1 23.4 %all-to-all-start.2 = ((bf16[16,80,128]{2,1,0:T(8,128)(2,1)}), bf16[16,80,128]{2,1,0:T(8,128)(2,1)S(1)}, u32[]{:S(2)}, u32[]{:S(2)}) async-start(bf16[16,80,128]{2,1,0:T(8,128)(2,1)} %get-tuple-element.18), calls=%async_computation.2 | async-start | bytes 655360 | tf_op jit(solution)/shard_map/all_to_all | solution.py:38
  87.5 9.7 %all-to-all-start.3 = ((bf16[4,72,448]{2,1,0:T(8,128)(2,1)}), bf16[4,72,448]{2,1,0:T(8,128)(2,1)S(1)}, u32[]{:S(2)}, u32[]{:S(2)}) async-start(bf16[4,72,448]{2,1,0:T(8,128)(2,1)} %shard_map.59), calls=%async_computation.3 | async-start | bytes 589824 | tf_op jit(solution)/shard_map/all_to_all | solution.py:38
  97.2 16.2 %collective-permute-start.6 = (bf16[72,448]{1,0:T(8,128)(2,1)S(1)}, bf16[72,448]{1,0:T(8,128)(2,1)S(1)}, u32[]{:S(2)}, u32[]{:S(2)}) collective-permute-start(bf16[72,448]{1,0:T(8,128)(2,1)S(1)} %shard_map.60.one_ref), channel_id=1, source_target_pairs={{0,256},{256,0},{1,257},{257,1},{2,258},{258,2},{3,259},{259,3},{4... | collective-permute-start | bytes 193544 | tf_op jit(solution)/shard_map/ppermute | solution.py:46
  104.4 13.2 %collective-permute-start.10 = (bf16[2,152,256]{2,1,0:T(8,128)(2,1)S(1)}, bf16[2,152,256]{2,1,0:T(8,128)(2,1)S(1)}, u32[]{:S(2)}, u32[]{:S(2)}) collective-permute-start(bf16[2,152,256]{2,1,0:T(8,128)(2,1)S(1)} %shard_map.61), channel_id=1, source_target_pairs={{0,24},{8,16},{16,8},{24,0},{1,25},{9,17},{17,9},{25,1},{2,26},{10... | collective-permute-start | bytes 466952 | tf_op jit(solution)/shard_map/ppermute | solution.py:281
  106.4 11.3 %collective-permute-start.9 = (bf16[2,152,256]{2,1,0:T(8,128)(2,1)S(1)}, bf16[2,152,256]{2,1,0:T(8,128)(2,1)S(1)}, u32[]{:S(2)}, u32[]{:S(2)}) collective-permute-start(bf16[2,152,256]{2,1,0:T(8,128)(2,1)S(1)} %shard_map.61), channel_id=1, source_target_pairs={{0,16},{8,24},{16,0},{24,8},{1,17},{9,25},{17,1},{25,9},{2,18},{10... | collective-permute-start | bytes 466952 | tf_op jit(solution)/shard_map/ppermute | solution.py:281
  110.1 7.5 %collective-permute-start.8 = (bf16[2,152,256]{2,1,0:T(8,128)(2,1)S(1)}, bf16[2,152,256]{2,1,0:T(8,128)(2,1)S(1)}, u32[]{:S(2)}, u32[]{:S(2)}) collective-permute-start(bf16[2,152,256]{2,1,0:T(8,128)(2,1)S(1)} %shard_map.61), channel_id=1, source_target_pairs={{0,8},{8,0},{16,24},{24,16},{1,9},{9,1},{17,25},{25,17},{2,10},{10... | collective-permute-start | bytes 466952 | tf_op jit(solution)/shard_map/ppermute | solution.py:281
  114.2 11.8 %all-to-all-start.4 = ((bf16[4,72,448]{2,1,0:T(8,128)(2,1)}), bf16[4,72,448]{2,1,0:T(8,128)(2,1)S(1)}, u32[]{:S(2)}, u32[]{:S(2)}) async-start(bf16[4,72,448]{2,1,0:T(8,128)(2,1)} %shard_map.62), calls=%async_computation.4 | async-start | bytes 589824 | tf_op jit(solution)/shard_map/all_to_all | solution.py:38
  117.8 15.1 %collective-permute-start.11 = (bf16[4,2,152,256]{3,2,1,0:T(8,128)(2,1)S(1)}, bf16[4,2,152,256]{3,2,1,0:T(8,128)(2,1)S(1)}, u32[]{:S(2)}, u32[]{:S(2)}) collective-permute-start(bf16[4,2,152,256]{3,2,1,0:T(8,128)(2,1)S(1)} %pad_maximum_fusion.own_ref), channel_id=1, source_target_pairs={{0,128},{128,0},{1,129},{129,1},{2,130},{130,2},{3,131},{131,3},{4... | collective-permute-start | bytes 1867784 | tf_op jit(solution)/shard_map/ppermute | solution.py:46
  126.0 7.9 %collective-permute-start.7 = (bf16[2,144,448]{2,1,0:T(8,128)(2,1)S(1)}, bf16[2,144,448]{2,1,0:T(8,128)(2,1)S(1)}, u32[]{:S(2)}, u32[]{:S(2)}) collective-permute-start(bf16[2,144,448]{2,1,0:T(8,128)(2,1)S(1)} %bitcast.9), channel_id=1, source_target_pairs={{0,128},{128,0},{1,129},{129,1},{2,130},{130,2},{3,131},{131,3},{4... | collective-permute-start | bytes 774152 | tf_op jit(solution)/shard_map/ppermute | solution.py:46
